TPU v7x, 32 devices: a whole 2x2x4 slice. The times are simulated.
32 devices in a mesh: dp: 8 (over z, x), tp: 4 (over y, core).
Axes of the slice: x: 2, y: 2, z: 4, core: 2. Of those that a mesh axis runs over, the one named last changes fastest.
Arguments:
- inputs: bfloat16 [4096, 768], P('dp'), may hold values from -6 to 6
- cotangent: bfloat16 [4096, 768], P('dp'), may hold values from -6 to 6
- seg_lengths: int32 [8, 4], P('dp'), may hold values from 1 to 256, 512 in all within a row
- bucket_ids: int32 [1023], replicated, may hold values from 0 to 31
- qkv_weight: float32 [3, 768, 768], P(None, 'dp', 'tp'), may hold values from -0.0625 to 0.0625
- qkv_first: float32 [3, 768, 768], P(None, 'dp', 'tp'), may hold values from -0.0009765625 to 0.0009765625
- qkv_second: float32 [3, 768, 768], P(None, 'dp', 'tp'), may hold values from 3.598771e-10 to 1.4280838e-09
- out_weight: float32 [768, 768], P('dp', 'tp'), may hold values from -3 to 3
- out_first: float32 [768, 768], P('dp', 'tp'), may hold values from -2.2888184e-05 to 2.2888184e-05
- out_second: float32 [768, 768], P('dp', 'tp'), may hold values from 1.8279472e-13 to 7.426035e-13
- ffn_in_weight: float32 [768, 3072], P('dp', 'tp'), may hold values from -0.21875 to 0.21875
- ffn_in_first: float32 [768, 3072], P('dp', 'tp'), may hold values from -0.00012207031 to 0.00012207031
- ffn_in_second: float32 [768, 3072], P('dp', 'tp'), may hold values from 6.854802e-12 to 2.7990442e-11
- ffn_down_weight: float32 [768, 3072], P('dp', 'tp'), may hold values from -0.109375 to 0.109375
- ffn_down_first: float32 [768, 3072], P('dp', 'tp'), may hold values from -0.00024414062 to 0.00024414062
- ffn_down_second: float32 [768, 3072], P('dp', 'tp'), may hold values from 2.8561674e-11 to 1.14246695e-10
- norm_gains: float32 [2, 768], replicated, may hold values from 0.5 to 1.5
- gains_first: float32 [2, 768], replicated, may hold values from -0.0004272461 to 0.0004272461
- gains_second: float32 [2, 768], replicated, may hold values from 6.854802e-11 to 2.7419209e-10
- bias_table: float32 [32, 12], P(None, 'tp'), may hold values from -4 to 4
- table_first: float32 [32, 12], P(None, 'tp'), may hold values from -0.00048828125 to 0.00048828125
- table_second: float32 [32, 12], P(None, 'tp'), may hold values from 7.997269e-11 to 3.3131542e-10
Outputs:
- block_out: bfloat16 [4096, 768], P(('dp', 'tp'))
- input_grad: float32 [4096, 768], P(('dp', 'tp'))
- grad_norm: float32 [], replicated
- qkv_new: float32 [3, 768, 768], P(None, 'dp', 'tp')
- qkv_first_new: float32 [3, 768, 768], P(None, 'dp', 'tp')
- qkv_second_new: float32 [3, 768, 768], P(None, 'dp', 'tp')
- qkv_low: bfloat16 [3, 768, 768], P(None, 'dp', 'tp')
- out_new: float32 [768, 768], P('dp', 'tp')
- out_first_new: float32 [768, 768], P('dp', 'tp')
- out_second_new: float32 [768, 768], P('dp', 'tp')
- out_low: bfloat16 [768, 768], P('dp', 'tp')
- ffn_in_new: float32 [768, 3072], P('dp', 'tp')
- ffn_in_first_new: float32 [768, 3072], P('dp', 'tp')
- ffn_in_second_new: float32 [768, 3072], P('dp', 'tp')
- ffn_in_low: bfloat16 [768, 3072], P('dp', 'tp')
- ffn_down_new: float32 [768, 3072], P('dp', 'tp')
- ffn_down_first_new: float32 [768, 3072], P('dp', 'tp')
- ffn_down_second_new: float32 [768, 3072], P('dp', 'tp')
- ffn_down_low: bfloat16 [768, 3072], P('dp', 'tp')
- gains_new: float32 [2, 768], replicated
- gains_first_new: float32 [2, 768], replicated
- gains_second_new: float32 [2, 768], replicated
- gains_grad: float32 [2, 768], replicated
- table_new: float32 [32, 12], P(None, 'tp')
- table_first_new: float32 [32, 12], P(None, 'tp')
- table_second_new: float32 [32, 12], P(None, 'tp')
Inputs may be any that keep to these rules, and one draw needn't show every extreme that they name: `seg_lengths`: each packed row's 4 lengths sum to 512, and one of them is exactly 256.
All inputs are finite; a program needn't handle non-finite values.
Results may differ from a plain program's by a relative error of at most 0.014.
Values may be sent and summed in bfloat16 or wider, within the bound.
No kernel may reach another device: no remote copies, remote signals or barrier semaphores. Data moves between devices by JAX's collectives and lax.ppermute only.
A program may use at most 320 MiB of HBM per device.

v0:
```python
import math

import jax
import jax.numpy as jnp
from jax import lax
from jax.sharding import PartitionSpec as P

HEADS = 12
HDIM = 64
BUCKETS = 32
LEN = 512


eps_norm = 1e-06
clip_norm = 1.0
beta_one = 0.9
beta_two = 0.999
adam_eps = 1e-08
decay_rate = 0.01
adam_step = 10.0
mask_fill = -1000000000.0
rate_small = 0.02
rate_large = 0.5
gelu_coef = 0.044715


def segment_ids(seg_lengths):
    ends = jnp.cumsum(seg_lengths, axis=1, dtype=jnp.int32)
    position = jnp.arange(LEN, dtype=jnp.int32)
    return jnp.sum((position[None, :, None] >= ends[:, None, :-1]).astype(jnp.int32), axis=2)


def norm_parts(values):
    scale = lax.rsqrt(jnp.mean(values * values, axis=-1, keepdims=True) + eps_norm)
    return (scale, values * scale)


def norm_back(normal_grad, normed, scale):
    return scale * (normal_grad - normed * jnp.mean(normal_grad * normed, axis=-1, keepdims=True))


def gelu_slope(values):
    root_coef = math.sqrt(2.0 / math.pi)
    tanh_part = jnp.tanh(root_coef * (values + gelu_coef * values * values * values))
    inner_slope = root_coef * (1.0 + 3.0 * gelu_coef * values * values)
    return 0.5 * (1.0 + tanh_part) + 0.5 * values * (1.0 - tanh_part * tanh_part) * inner_slope


def adamw_update(weight, gradient, moment_one, moment_two, rate):
    one_new = beta_one * moment_one + (1.0 - beta_one) * gradient
    two_new = beta_two * moment_two + (1.0 - beta_two) * gradient * gradient
    one_hat = one_new / (1.0 - beta_one**adam_step)
    two_hat = two_new / (1.0 - beta_two**adam_step)
    weight_new = weight - rate * (one_hat / (jnp.sqrt(two_hat) + adam_eps) + decay_rate * weight)
    return (weight_new, one_new, two_new)


def on_device(
    inputs,
    cotangent,
    seg_lengths,
    bucket_ids,
    qkv_weight,
    qkv_first,
    qkv_second,
    out_weight,
    out_first,
    out_second,
    ffn_in_weight,
    ffn_in_first,
    ffn_in_second,
    ffn_down_weight,
    ffn_down_first,
    ffn_down_second,
    norm_gains,
    gains_first,
    gains_second,
    bias_table,
    table_first,
    table_second,
):
    qkv_full, out_full, in_full, down_full = (
        lax.all_gather(qkv_weight.astype(jnp.bfloat16), "dp", axis=1, tiled=True),
        lax.all_gather(out_weight.astype(jnp.bfloat16), "dp", axis=0, tiled=True),
        lax.all_gather(ffn_in_weight.astype(jnp.bfloat16), "dp", axis=0, tiled=True),
        lax.all_gather(ffn_down_weight.astype(jnp.bfloat16), "dp", axis=0, tiled=True),
    )
    tokens = inputs.shape[0]
    seq_count = tokens // LEN
    share = tokens // lax.axis_size("tp")
    share_start = lax.axis_index("tp") * share
    local_width = qkv_full.shape[2]
    heads_here = local_width // HDIM
    contract_rows = (((0,), (0,)), ((), ()))
    contract_cols = (((1,), (1,)), ((), ()))
    segment = segment_ids(seg_lengths)
    position = jnp.arange(LEN, dtype=jnp.int32)
    offsets = position[None, :] - position[:, None] + (LEN - 1)
    bucket_onehot = (bucket_ids[:, None] == jnp.arange(BUCKETS, dtype=jnp.int32)[None, :]).astype(
        jnp.float32
    )
    bias_rows = jnp.dot(
        bucket_onehot,
        bias_table,
        precision=lax.Precision.HIGHEST,
        preferred_element_type=jnp.float32,
    )
    bias_full = jnp.transpose(bias_rows[offsets], (2, 0, 1))
    resid_in = inputs.astype(jnp.float32)
    grad_out = cotangent.astype(jnp.float32)
    scale_one, normed_one = norm_parts(resid_in)
    act_one = (normed_one * norm_gains[0]).astype(jnp.bfloat16)
    projected = jnp.einsum(
        "td,cde->cte", act_one, qkv_full, preferred_element_type=jnp.float32
    ).astype(jnp.bfloat16)
    heads_view = projected.reshape(3, seq_count, LEN, heads_here, HDIM)

    def masked_scores(query_rows, key_rows, seg_row):
        scores = (
            jnp.einsum("ihd,jhd->hij", query_rows, key_rows, preferred_element_type=jnp.float32)
            + bias_full
        )
        visible = seg_row[None, :, None] == seg_row[None, None, :]
        return jnp.where(visible, scores, mask_fill)

    def attend_fwd(block_rows):
        query_rows, key_rows, value_rows, seg_row = block_rows
        scores = masked_scores(query_rows, key_rows, seg_row)
        row_max = jnp.max(scores, axis=-1, keepdims=True)
        exp_scores = jnp.exp(scores - row_max)
        row_total = jnp.sum(exp_scores, axis=-1, keepdims=True)
        prob_low = (exp_scores / row_total).astype(jnp.bfloat16)
        mixed_rows = jnp.einsum(
            "hij,jhd->ihd", prob_low, value_rows, preferred_element_type=jnp.float32
        ).astype(jnp.bfloat16)
        return (mixed_rows, row_max[..., 0] + jnp.log(row_total[..., 0]))

    attn_mix, log_total = lax.map(
        attend_fwd, (heads_view[0], heads_view[1], heads_view[2], segment)
    )
    mix_flat = attn_mix.reshape(tokens, local_width)
    attn_part = lax.dot_general(
        mix_flat, out_full, contract_cols, preferred_element_type=jnp.float32
    )
    resid_one = resid_in + lax.psum(attn_part, "tp")
    scale_two, normed_two = norm_parts(resid_one)
    act_two = (normed_two * norm_gains[1]).astype(jnp.bfloat16)
    hidden_pre = jnp.dot(act_two, in_full, preferred_element_type=jnp.float32)
    hidden_act = jax.nn.gelu(hidden_pre, approximate=True).astype(jnp.bfloat16)
    ffn_part = lax.dot_general(
        hidden_act, down_full, contract_cols, preferred_element_type=jnp.float32
    )
    block_f32 = resid_one + lax.psum(ffn_part, "tp")
    block_out = lax.dynamic_slice_in_dim(block_f32, share_start, share, 0).astype(jnp.bfloat16)
    down_grad = lax.dot_general(
        cotangent, hidden_act, contract_rows, preferred_element_type=jnp.float32
    )
    hidden_grad = jnp.dot(cotangent, down_full, preferred_element_type=jnp.float32)
    pre_grad = (hidden_grad * gelu_slope(hidden_pre)).astype(jnp.bfloat16)
    in_grad = lax.dot_general(act_two, pre_grad, contract_rows, preferred_element_type=jnp.float32)
    act_two_grad = lax.dot_general(
        pre_grad, in_full, contract_cols, preferred_element_type=jnp.float32
    )
    gain_two_part = jnp.sum(act_two_grad * normed_two, axis=0)
    normal_two = lax.psum(act_two_grad, "tp")
    resid_grad = grad_out + norm_back(normal_two * norm_gains[1], normed_two, scale_two)
    resid_low = resid_grad.astype(jnp.bfloat16)
    out_grad = lax.dot_general(
        resid_low, mix_flat, contract_rows, preferred_element_type=jnp.float32
    )
    mix_grad = jnp.dot(resid_low, out_full, preferred_element_type=jnp.float32).astype(jnp.bfloat16)
    mix_grad = mix_grad.reshape(seq_count, LEN, heads_here, HDIM)

    def attend_back(bias_acc, block_rows):
        query_rows, key_rows, value_rows, seg_row, grad_rows, lse_rows = block_rows
        scores = masked_scores(query_rows, key_rows, seg_row)
        attn_prob = jnp.exp(scores - lse_rows[..., None])
        prob_low = attn_prob.astype(jnp.bfloat16)
        prob_grad = jnp.einsum(
            "ihd,jhd->hij", grad_rows, value_rows, preferred_element_type=jnp.float32
        )
        row_dot = jnp.sum(attn_prob * prob_grad, axis=-1, keepdims=True)
        score_grad = attn_prob * (prob_grad - row_dot)
        score_low = score_grad.astype(jnp.bfloat16)
        query_grad = jnp.einsum(
            "hij,jhd->ihd", score_low, key_rows, preferred_element_type=jnp.float32
        ).astype(jnp.bfloat16)
        key_grad = jnp.einsum(
            "hij,ihd->jhd", score_low, query_rows, preferred_element_type=jnp.float32
        ).astype(jnp.bfloat16)
        value_grad = jnp.einsum(
            "hij,ihd->jhd", prob_low, grad_rows, preferred_element_type=jnp.float32
        ).astype(jnp.bfloat16)
        return (bias_acc + score_grad, jnp.stack((query_grad, key_grad, value_grad)))

    bias_start = jnp.zeros((heads_here, LEN, LEN), jnp.float32)
    bias_grad, proj_stack = lax.scan(
        attend_back,
        bias_start,
        (heads_view[0], heads_view[1], heads_view[2], segment, mix_grad, log_total),
    )
    proj_low = jnp.moveaxis(proj_stack, 1, 0).reshape(3, tokens, local_width)
    qkv_grad = jnp.einsum("td,cte->cde", act_one, proj_low, preferred_element_type=jnp.float32)
    act_one_grad = jnp.einsum("cte,cde->td", proj_low, qkv_full, preferred_element_type=jnp.float32)
    gain_one_part = jnp.sum(act_one_grad * normed_one, axis=0)
    normal_one = lax.psum(act_one_grad.astype(jnp.bfloat16), "tp").astype(jnp.float32)
    input_full = resid_grad + norm_back(normal_one * norm_gains[0], normed_one, scale_one)
    input_grad = lax.dynamic_slice_in_dim(input_full, share_start, share, 0)
    diag_sum = jax.ops.segment_sum(
        bias_grad.reshape(heads_here, LEN * LEN).T, offsets.reshape(-1), num_segments=2 * LEN - 1
    )
    table_part = jnp.dot(
        bucket_onehot.T,
        diag_sum,
        precision=lax.Precision.HIGHEST,
        preferred_element_type=jnp.float32,
    )
    table_spread = lax.dynamic_update_slice_in_dim(
        jnp.zeros((BUCKETS, HEADS), jnp.float32), table_part, lax.axis_index("tp") * heads_here, 1
    )
    gains_part = jnp.stack((gain_one_part, gain_two_part))
    qkv_sum, out_sum, in_sum, down_sum = (
        lax.psum_scatter(qkv_grad, "dp", scatter_dimension=1, tiled=True),
        lax.psum_scatter(out_grad, "dp", scatter_dimension=0, tiled=True),
        lax.psum_scatter(in_grad, "dp", scatter_dimension=0, tiled=True),
        lax.psum_scatter(down_grad, "dp", scatter_dimension=0, tiled=True),
    )
    shard_squares = (
        jnp.sum(qkv_sum * qkv_sum)
        + jnp.sum(out_sum * out_sum)
        + jnp.sum(in_sum * in_sum)
        + jnp.sum(down_sum * down_sum)
    )
    gains_sum, table_whole, total_squares = lax.psum(
        (gains_part, table_spread, shard_squares), ("dp", "tp")
    )
    table_grad = lax.dynamic_slice_in_dim(
        table_whole, lax.axis_index("tp") * heads_here, heads_here, 1
    )
    grad_norm = jnp.sqrt(
        total_squares + jnp.sum(gains_sum * gains_sum) + jnp.sum(table_whole * table_whole)
    )
    factor = clip_norm / jnp.maximum(grad_norm, clip_norm)
    qkv_new, qkv_first_new, qkv_second_new = adamw_update(
        qkv_weight, qkv_sum * factor, qkv_first, qkv_second, rate_small
    )
    out_new, out_first_new, out_second_new = adamw_update(
        out_weight, out_sum * factor, out_first, out_second, rate_large
    )
    ffn_in_new, ffn_in_first_new, ffn_in_second_new = adamw_update(
        ffn_in_weight, in_sum * factor, ffn_in_first, ffn_in_second, rate_small
    )
    ffn_down_new, ffn_down_first_new, ffn_down_second_new = adamw_update(
        ffn_down_weight, down_sum * factor, ffn_down_first, ffn_down_second, rate_small
    )
    gains_grad = gains_sum * factor
    gains_new, gains_first_new, gains_second_new = adamw_update(
        norm_gains, gains_grad, gains_first, gains_second, rate_large
    )
    table_new, table_first_new, table_second_new = adamw_update(
        bias_table, table_grad * factor, table_first, table_second, rate_large
    )
    return (
        block_out,
        input_grad,
        grad_norm,
        qkv_new,
        qkv_first_new,
        qkv_second_new,
        qkv_new.astype(jnp.bfloat16),
        out_new,
        out_first_new,
        out_second_new,
        out_new.astype(jnp.bfloat16),
        ffn_in_new,
        ffn_in_first_new,
        ffn_in_second_new,
        ffn_in_new.astype(jnp.bfloat16),
        ffn_down_new,
        ffn_down_first_new,
        ffn_down_second_new,
        ffn_down_new.astype(jnp.bfloat16),
        gains_new,
        gains_first_new,
        gains_second_new,
        gains_grad,
        table_new,
        table_first_new,
        table_second_new,
    )


def solution(mesh):
    in_specs = (
        P("dp", None),
        P("dp", None),
        P("dp", None),
        P(),
        P(None, "dp", "tp"),
        P(None, "dp", "tp"),
        P(None, "dp", "tp"),
        P("dp", "tp"),
        P("dp", "tp"),
        P("dp", "tp"),
        P("dp", "tp"),
        P("dp", "tp"),
        P("dp", "tp"),
        P("dp", "tp"),
        P("dp", "tp"),
        P("dp", "tp"),
        P(),
        P(),
        P(),
        P(None, "tp"),
        P(None, "tp"),
        P(None, "tp"),
    )
    out_specs = (
        P(("dp", "tp"), None),
        P(("dp", "tp"), None),
        P(),
        P(None, "dp", "tp"),
        P(None, "dp", "tp"),
        P(None, "dp", "tp"),
        P(None, "dp", "tp"),
        P("dp", "tp"),
        P("dp", "tp"),
        P("dp", "tp"),
        P("dp", "tp"),
        P("dp", "tp"),
        P("dp", "tp"),
        P("dp", "tp"),
        P("dp", "tp"),
        P("dp", "tp"),
        P("dp", "tp"),
        P("dp", "tp"),
        P("dp", "tp"),
        P(),
        P(),
        P(),
        P(),
        P(None, "tp"),
        P(None, "tp"),
        P(None, "tp"),
    )
    return jax.shard_map(
        on_device, mesh=mesh, in_specs=in_specs, out_specs=out_specs, check_vma=False
    )
```

profile of v0, /device:TPU:0, one launch (start us, length us, event | category | flops | bytes accessed | tf_op | source)
XLA Modules:
  0.0 2757.5 jit_solution(18333481309932703680)
XLA Ops:
  8.2 1.0 convert_element_type.117
  9.3 38.8 %all_gather.12 = bf16[3,768,192]{2,0,1:T(4,128)(2,1)S(1)} all-gather(bf16[3,96,192]{2,0,1:T(4,128)(2,1)S(1)} %copy.126), channel_id=1, replica_groups=mesh['dp'=8,'tp'=4] {'dp'}, dimensions={1}, use_global_device_ids=true | all-gather | bytes 995328 | tf_op jit(solution)/shard_map/all_gather | solution.py:83
  48.2 2.1 copy.127
  51.1 1.9 fusion.48
  55.3 861.6 %gather_fusion = f32[262144,3]{1,0:T(8,128)} fusion(f32[1023,3]{1,0:T(8,128)S(1)} %fusion.34, s32[262144]{0:T(1024)S(1)} %broadcast_clamp_fusion), kind=kCustom, calls=%fused_computation | custom fusion | bytes 7340032 | tf_op jit(solution)/shard_map/gather | solution.py:108
  916.9 71.3 %copy.130 = f32[512,512,3]{0,1,2:T(8,128)} copy(f32[512,512,3]{2,1,0:T(8,128)} %bitcast.8) | data formatting | bytes 6291456 | tf_op jit(solution)/shard_map/gather | solution.py:108
  988.8 31.2 %all_gather.13 = bf16[768,192]{1,0:T(8,128)(2,1)S(1)} all-gather(bf16[96,192]{1,0:T(8,128)(2,1)S(1)} %convert_element_type.124), channel_id=1, replica_groups=mesh['dp'=8,'tp'=4] {'dp'}, dimensions={0}, use_global_device_ids=true | all-gather | bytes 331776 | tf_op jit(solution)/shard_map/all_gather | solution.py:84
  1020.0 2.9 fusion.71
  1025.2 1.6 fusion.72
  1026.8 1.6 convert_element_type.126
  1028.5 1.6 convert_element_type.128
  1030.2 38.5 %all-reduce.6.cloned.1.call-done = f32[512,768]{1,0:T(8,128)} async-done(((f32[512,768]{1,0:T(8,128)}), f32[512,768]{1,0:T(8,128)}) %all-reduce.6.cloned.1.call-update) | async-done | bytes 1572880 | tf_op jit(solution)/shard_map/psum | solution.py:145
  1068.8 3.0 multiply_reduce_fusion.4
  1071.8 3.7 fusion.56
  1075.5 37.5 %all-gather.5.cloned.1.call-done = bf16[768,768]{1,0:T(8,128)(2,1)} async-done(((bf16[96,768]{1,0:T(8,128)(2,1)}), bf16[768,768]{1,0:T(8,128)(2,1)}) %all-gather.5.cloned.1.call-update) | async-done | bytes 1179664 | tf_op jit(solution)/shard_map/all_gather | solution.py:86
  1113.0 3.5 fusion.19
  1116.5 2.0 fusion.73
  1119.1 2.2 fusion.58
  1122.3 66.3 %all-reduce.10.cloned.1.call-done = (f32[512,768]{1,0:T(8,128)}, f32[512,768]{1,0:T(8,128)}) async-done(((f32[512,768]{1,0:T(8,128)}, f32[512,768]{1,0:T(8,128)}), (f32[512,768]{1,0:T(8,128)}, f32[512,768]{1,0:T(8,128)})) %all-reduce.10.cloned.1.call-update) | async-done | bytes 3145744 | tf_op jit(solution)/shard_map/psum | solution.py:153
  1188.6 3.6 multiply_reduce_fusion.1
  1196.4 1.0 copy-done
  1198.7 2.3 bitcast_convert_fusion
  1201.1 1.3 fusion.37
  1202.4 3.5 fusion.55
  1206.0 1.4 copy-done.13
  1207.6 2.5 convolution_bitcast_fusion
  1211.3 2.0 convolution_bitcast_fusion.1
  1213.4 3.0 copy.155
  1216.3 2.8 reshape.268
  1220.5 1.3 copy.158
  1221.8 1.9 copy.139
  1223.7 1.8 copy.140
  1225.5 2.3 copy.137
  1227.8 6.0 copy.159
  1233.9 58.4 %copy.138 = f32[262144,3]{1,0:T(8,128)} copy(f32[262144,3]{0,1:T(4,128)} %bitcast.79) | data formatting | bytes 6291456 | tf_op jit(solution)/shard_map/transpose | solution.py:210
  1292.3 1386.6 %scatter_custom_fusion = f32[1023,3]{1,0:T(8,128)S(1)} fusion(s32[262144]{0:T(1024)} %bitcast.91, f32[262144,3]{1,0:T(8,128)} %copy.138, f32[]{:T(128)} %constant.42.clone.1), kind=kCustom, calls=%fused_computation.92 | custom fusion | flops 786432 | bytes 12788 | tf_op jit(solution)/shard_map/scatter-add | solution.py:209
  2679.7 1.8 fusion.36
  2681.5 3.3 fusion.22
  2684.9 1.5 multiply_reduce_fusion.8
  2686.4 1.6 multiply_reduce_fusion.6
  2688.1 1.6 multiply_reduce_fusion.5
  2689.7 1.2 reshape.269
  2694.4 2.0 dynamic-slice_add_fusion
  2696.4 39.9 %all-reduce = (f32[]{:T(128)}, f32[2,768]{1,0:T(2,128)S(1)}, f32[32,12]{0,1:T(8,128)S(1)}) all-reduce(f32[]{:T(128)S(6)} %add.256, f32[2,768]{1,0:T(2,128)S(1)} %pad_maximum_fusion.3, f32[32,12]{0,1:T(8,128)S(1)} %dynamic_update_slice.12), channel_id=1, replica_groups=mesh['dp'=8,'tp'=4] {'dp','tp'}, use_global_device_ids=true, to_apply=%region_21.22 | all-reduce | flops 1921 | bytes 15368 | tf_op jit(solution)/shard_map/psum | solution.py:234
  2743.4 1.3 multiply_subtract_fusion.4
  2744.7 1.3 multiply_subtract_fusion.5
  2746.0 1.7 fusion.66
  2747.8 1.4 fusion.62
  (185 shorter events, 23.0 us)
Async XLA Ops:
  8.0 1060.7 %all-reduce.6.cloned.1.call-start = ((), (), s32[]{:S(2)}) async-start(), calls=%async_computation.4 | async-start | bytes 3145728 | tf_op jit(solution)/shard_map/psum | solution.py:145
  48.1 2.1 copy-start.45
  48.1 2.7 copy-start.6
  50.8 2.2 copy-start.49
  51.1 2.0 copy-start.54
  916.9 71.4 %copy-start.57 = (s32[1,4]{1,0:T(1,128)S(1)}, s32[1,4]{1,0:T(1,128)}, u32[]{:S(2)}) copy-start(s32[1,4]{1,0:T(1,128)} %param.24) | copy-start | bytes 52
  916.9 71.9 %copy-start.30 = (f32[96,192]{1,0:T(8,128)S(1)}, f32[96,192]{1,0:T(8,128)}, u32[]{:S(2)}) copy-start(f32[96,192]{1,0:T(8,128)} %param.29) | copy-start | bytes 221188
  1026.8 45.0 %all-gather.3.cloned.1.call-start = ((), (), s32[]{:S(2)}) async-start(), calls=%async_computation.5 | async-start | bytes 1327104 | tf_op jit(solution)/shard_map/all_gather | solution.py:85
  1028.5 84.5 %all-gather.5.cloned.1.call-start = ((), (), s32[]{:S(2)}) async-start(), calls=%async_computation.6 | async-start | bytes 1327104 | tf_op jit(solution)/shard_map/all_gather | solution.py:86
  1030.2 41.6 %copy-start.41 = (f32[768]{0:T(1024)S(1)}, f32[768]{0:T(1024)}, u32[]{:S(2)}) copy-start(f32[768]{0:T(1024)} %get-tuple-element.214) | copy-start | bytes 9220
  1030.2 158.4 %all-reduce.10.cloned.1.call-start = ((), (), s32[]{:S(2)}) async-start(), calls=%async_computation.12 | async-start | bytes 6291456 | tf_op jit(solution)/shard_map/psum | solution.py:153
  1113.0 3.5 copy-start.20
  1116.5 2.0 copy-start.25
  1116.5 2.0 copy-start.12
  1116.5 2.6 copy-start.56
  1121.4 1560.1 %all-reduce.8.cloned.1.call-start = ((), (), s32[]{:S(2)}) async-start(), calls=%async_computation.7 | async-start | bytes 1572864 | tf_op jit(solution)/shard_map/psum | solution.py:206
  1188.6 3.6 copy-start.2
  1188.6 3.6 copy-start.9
  1188.6 3.6 copy-start.28
  1195.8 1.7 copy-start
  1195.8 1.7 copy-start.10
  1197.9 3.1 copy-start.39
  1198.7 2.4 copy-start.5
  1198.7 2.4 copy-start.27
  1201.0 1483.9 %reduce-scatter.7.cloned.1.call-start = ((), (), s32[]{:S(2)}) async-start(), calls=%async_computation.8 | async-start | bytes 884736 | tf_op jit(solution)/shard_map/reduce_scatter | solution.py:224
  1202.4 1484.1 %reduce-scatter.9.cloned.1.call-start = ((), (), s32[]{:S(2)}) async-start(), calls=%async_computation.9 | async-start | bytes 2654208 | tf_op jit(solution)/shard_map/reduce_scatter | solution.py:225
  1205.9 1.7 copy-start.29
  1206.0 1482.1 %reduce-scatter.11.cloned.1.call-start = ((), (), s32[]{:S(2)}) async-start(), calls=%async_computation.10 | async-start | bytes 2654208 | tf_op jit(solution)/shard_map/reduce_scatter | solution.py:226
  1210.1 1479.6 %reduce-scatter.13.cloned.1.call-start = ((), (), s32[]{:S(2)}) async-start(), calls=%async_computation.11 | async-start | bytes 2211840
  1220.5 5.0 copy-start.1
  1225.5 2.3 copy-start.51
  1233.9 1445.0 %copy-start.48 = (s32[1023]{0:T(1024)S(1)}, s32[1023]{0:T(1024)}, u32[]{:S(2)}) copy-start(s32[1023]{0:T(1024)} %param.25) | copy-start | bytes 12280
  1292.3 1389.2 %copy-start.8 = (bf16[512,768]{1,0:T(8,128)(2,1)S(1)}, bf16[512,768]{1,0:T(8,128)(2,1)}, u32[]{:S(2)}) copy-start(bf16[512,768]{1,0:T(8,128)(2,1)} %param.22) | copy-start | bytes 2359300
  2689.7 49.8 %copy-start.18 = (f32[3,96,192]{1,2,0:T(8,128)S(1)}, f32[3,96,192]{1,2,0:T(8,128)}, u32[]{:S(2)}) copy-start(f32[3,96,192]{1,2,0:T(8,128)} %copy.139) | copy-start | bytes 663556
  2689.7 49.8 %copy-start.19 = (f32[3,96,192]{1,2,0:T(8,128)S(1)}, f32[3,96,192]{1,2,0:T(8,128)}, u32[]{:S(2)}) copy-start(f32[3,96,192]{1,2,0:T(8,128)} %copy.140) | copy-start | bytes 663556
  2736.3 3.2 copy-start.52
  2739.5 3.8 copy-start.46
  2739.6 6.5 copy-start.42
  2739.8 6.2 copy-start.31
  2739.8 6.2 copy-start.32
  2739.8 7.9 copy-start.14
  2739.9 7.8 copy-start.15
  2739.9 7.8 copy-start.16
  2739.9 7.8 copy-start.17
  2739.9 7.8 copy-start.33
  2739.9 7.8 copy-start.34
  2739.9 7.8 copy-start.35
  2740.8 6.9 copy-start.36
  (19 other events, 19.7 us)
Sparse Core Ops, SparseCore 0:
  1026.9 41.8 all-reduce.5
  1121.5 67.1 all-reduce.9
  1201.1 34.8 all-reduce.7
Sparse Core Ops, SparseCore 1:
  1030.0 40.3 all-gather.2
  1073.0 40.0 all-gather.4
  1204.8 62.7 reduce-scatter.6
  1271.4 68.2 reduce-scatter.8
  1343.6 68.3 reduce-scatter.10
  1415.8 66.4 reduce-scatter.12
where the time goes:
time: 2760 us
  other arithmetic  1420 us (51%)
  local copies, waits for them, and re-layouts  1030 us (37%)
  waiting for transfers between devices  143 us (5%)
  blocking collectives  110 us (4%)
  matrix products  33.9 us (1%)
    scatter-add x1, other arithmetic, on_device(): jax.ops.segment_sum(bias_grad.reshape(heads_here, LEN * LEN).T, offsets.r...  1390 us
    gather x2, local copies, waits for them, and re-layouts, on_device(): bias_full = jnp.transpose(bias_rows[offsets], (2, 0, 1))  933 us
    psum x1, waiting for transfers between devices, on_device(): block_f32 = resid_one + lax.psum(ffn_part, 'tp')  66.3 us
    transpose x1, local copies, waits for them, and re-layouts, on_device(): bias_grad.reshape(heads_here, LEN * LEN)  58.4 us
  transfers between devices with their start and end apart: 9, of which 3 were waited for; matrix products, arithmetic and copies ran while one was open for 54% of the time, Pallas kernels for 0%

commit v1 on v0

v1 whole, which is shorter than its diff:
```python
import functools
import math

import jax
import jax.numpy as jnp
from jax import lax
from jax.experimental import pallas as pl
from jax.experimental.pallas import tpu as pltpu
from jax.sharding import PartitionSpec as P

HEADS = 12
HDIM = 64
BUCKETS = 32
LEN = 512
BLK = 128
WIN = LEN + BLK


eps_norm = 1e-06
clip_norm = 1.0
beta_one = 0.9
beta_two = 0.999
adam_eps = 1e-08
decay_rate = 0.01
adam_step = 10.0
mask_fill = -1000000000.0
rate_small = 0.02
rate_large = 0.5
gelu_coef = 0.044715
root_coef = math.sqrt(2.0 / math.pi)

f32 = jnp.float32
bf16 = jnp.bfloat16
sds = jax.ShapeDtypeStruct


def dot_nn(a, b):
    return lax.dot_general(a, b, (((1,), (0,)), ((), ())), preferred_element_type=f32)


def dot_nt(a, b):
    return lax.dot_general(a, b, (((1,), (1,)), ((), ())), preferred_element_type=f32)


def dot_tn(a, b):
    return lax.dot_general(a, b, (((0,), (0,)), ((), ())), preferred_element_type=f32)


def call(body, outs, args, name, flops=0, smem=(), scratch=(), limit=28):
    moved = sum(a.size * a.dtype.itemsize for a in (*args, *outs))
    return pl.pallas_call(
        body,
        out_shape=tuple(outs),
        in_specs=[
            pl.BlockSpec(memory_space=pltpu.SMEM if i in smem else pltpu.VMEM)
            for i in range(len(args))
        ],
        out_specs=tuple(pl.BlockSpec(memory_space=pltpu.VMEM) for _ in outs),
        scratch_shapes=list(scratch),
        compiler_params=pltpu.CompilerParams(vmem_limit_bytes=limit << 20),
        cost_estimate=pl.CostEstimate(flops=flops, bytes_accessed=moved, transcendentals=0),
        name=name,
    )(*args)


def assemble(into, blocks):
    if len(blocks) == 1:
        into[...] = blocks[0][...]
        return
    me = lax.axis_index("dp")
    rows = blocks[0].shape[0]
    for e, block in enumerate(blocks):
        start = pl.multiple_of((me ^ e) * rows, 32)
        into[pl.ds(start, rows), :] = block[...]


def spread(grad, outs):
    if len(outs) == 1:
        outs[0][...] = grad[...].astype(bf16)
        return
    me = lax.axis_index("dp")
    rows = outs[0].shape[1]
    for b, out in enumerate(outs):
        for k in range(out.shape[0]):
            start = pl.multiple_of((me ^ (2 * k + b)) * rows, 32)
            out[k] = grad[pl.ds(start, rows), :].astype(bf16)


def spread_shapes(dp, width, cols):
    if dp == 8:
        return [sds((dp // 2, width // dp, cols), bf16)] * 2
    return [sds((width, cols), bf16)]


def half_rows():
    core = lax.axis_index("tp") & 1
    for half in range(2):
        for at in range(2):
            start = pl.multiple_of(((core ^ half) + 2 * at) * BLK, BLK)
            yield half, at, pl.ds(start, BLK)


def pack_kernel(qkv, out, packed):
    for part in range(3):
        packed[:, part * 192 : part * 192 + 192] = qkv[part].astype(bf16)
    packed[:, 576:768] = out[...].astype(bf16)


def prep_kernel(seg, table, bucket, x, gains, act, act_t, bias):
    values = x[...].astype(f32)
    scale = lax.rsqrt(jnp.mean(values * values, axis=-1, keepdims=True) + eps_norm)
    low = (values * scale * gains[0:1, :]).astype(bf16)
    act[...] = low
    act_t[...] = low.T
    ends = [seg[0, 0]]
    for k in (1, 2):
        ends.append(ends[-1] + seg[0, k])

    def segment_of(position):
        return sum((position >= end).astype(jnp.int32) for end in ends)

    seg_cols = segment_of(lax.broadcasted_iota(jnp.int32, (1, LEN), 1))
    heads = bias.shape[0]
    lines = []
    for h in range(heads):
        line = jnp.zeros((1, 2 * LEN), f32)
        for b in range(BUCKETS):
            line = jnp.where(bucket[...] == b, table[b, h], line)
        lines.append(line)
    for r in range(LEN // BLK):
        seg_rows = segment_of(lax.broadcasted_iota(jnp.int32, (BLK, 1), 0) + r * BLK)
        visible = seg_rows == seg_cols
        low_at = LEN - BLK - r * BLK
        for h in range(heads):
            window = jnp.broadcast_to(lines[h][:, low_at : low_at + WIN], (BLK, WIN))
            turned = pltpu.roll(window, 1, 1, stride=1, stride_axis=0)
            bias[h, r * BLK : (r + 1) * BLK, :] = jnp.where(visible, turned[:, BLK:], mask_fill)


def attend_kernel(n_blocks, act, bias, *rest):
    blocks = rest[:n_blocks]
    weights, qkv, prob, mixed, keep, send = rest[n_blocks:]
    assemble(weights, blocks)
    width = qkv.shape[1] // 3
    qkv[...] = dot_nn(act[...], weights[:, : 3 * width]).astype(bf16)
    for h in range(bias.shape[0]):
        cols = slice(h * HDIM, (h + 1) * HDIM)
        query, key, value = (qkv[:, s * width + h * HDIM : s * width + (h + 1) * HDIM] for s in range(3))
        scores = dot_nt(query, key) + bias[h]
        top = jnp.max(scores, axis=-1, keepdims=True)
        exps = jnp.exp(scores - top)
        total = jnp.sum(exps, axis=-1, keepdims=True)
        low = (exps * (1.0 / total)).astype(bf16)
        prob[h] = low
        mixed[:, cols] = dot_nn(low, value).astype(bf16)
    out_cols = weights[:, 3 * width :]
    for half, at, rows in half_rows():
        to = send if half else keep
        to[at * BLK : (at + 1) * BLK, :] = dot_nt(mixed[rows, :], out_cols).astype(bf16)


def dhid_kernel(n_blocks, dy, *rest):
    blocks = rest[:n_blocks]
    weights, hidden_grad = rest[n_blocks:]
    assemble(weights, blocks)
    hidden_grad[...] = dot_nn(dy[...], weights[...])


def ffn_kernel(n_blocks, x, gains, hidden_grad, own_a, own_b, other_a, other_b, *rest):
    blocks = rest[:n_blocks]
    resid, act, hidden, pre_grad, keep, send, weights = rest[n_blocks:]
    assemble(weights, blocks)
    for half, at, rows in half_rows():
        here = slice(at * BLK, (at + 1) * BLK)
        part_a, part_b = ((own_a, own_b), (other_a, other_b))[half]
        values = x[rows, :].astype(f32) + (part_a[here, :].astype(f32) + part_b[here, :].astype(f32))
        resid[rows, :] = values
        scale = lax.rsqrt(jnp.mean(values * values, axis=-1, keepdims=True) + eps_norm)
        low = (values * scale * gains[1:2, :]).astype(bf16)
        act[rows, :] = low
        u = dot_nn(low, weights[...])
        square = u * u
        tanh_part = jnp.tanh(root_coef * (u + gelu_coef * square * u))
        hidden[rows, :] = (0.5 * u * (1.0 + tanh_part)).astype(bf16)
        inner = root_coef * (1.0 + 3.0 * gelu_coef * square)
        slope = 0.5 * (1.0 + tanh_part) + 0.5 * u * (1.0 - tanh_part * tanh_part) * inner
        du = (hidden_grad[rows, :] * slope).astype(bf16)
        pre_grad[rows, :] = du
        (send if half else keep)[here, :] = dot_nt(du, weights[...]).astype(bf16)


def weight_grad_kernel(left, right, *rest):
    outs, grad = rest[:-1], rest[-1]
    grad[...] = dot_tn(left[...], right[...])
    spread(grad, outs)


def ffn_out_kernel(hidden, weights, keep, send):
    for half, at, rows in half_rows():
        to = send if half else keep
        to[at * BLK : (at + 1) * BLK, :] = dot_nt(hidden[rows, :], weights[...]).astype(bf16)


def attend_back_kernel(
    n_outs, resid, dy, gains, own_a, own_b, other_a, other_b, weights, qkv, prob, mixed, act_t, *rest
):
    outs = rest[:n_outs]
    share_grad, gain_part, score_grad, proj_grad, resid_low, grad = rest[n_outs:]
    chip = lax.axis_index("tp") >> 1
    width = qkv.shape[1] // 3
    for half, at, rows in half_rows():
        here = slice(at * BLK, (at + 1) * BLK)
        part_a, part_b = ((own_a, own_b), (other_a, other_b))[half]
        act_grad = part_a[here, :].astype(f32) + part_b[here, :].astype(f32)
        values = resid[rows, :]
        scale = lax.rsqrt(jnp.mean(values * values, axis=-1, keepdims=True) + eps_norm)
        normed = values * scale
        normal_grad = act_grad * gains[1:2, :]
        mean_part = jnp.mean(normal_grad * normed, axis=-1, keepdims=True)
        total = dy[rows, :].astype(f32) + scale * (normal_grad - normed * mean_part)
        resid_low[rows, :] = total.astype(bf16)
        if half == 0:

            @pl.when(chip == at)
            def _():
                share_grad[...] = total
                gain_part[...] = jnp.sum(act_grad * normed, axis=0, keepdims=True)

    mix_grad = dot_nn(resid_low[...], weights[:, 3 * width :]).astype(bf16)
    for h in range(prob.shape[0]):
        query, key, value = (qkv[:, s * width + h * HDIM : s * width + (h + 1) * HDIM] for s in range(3))
        grad_rows = mix_grad[:, h * HDIM : (h + 1) * HDIM]
        prob_grad = dot_nt(grad_rows, value)
        prob_here = prob[h].astype(f32)
        row_dot = jnp.sum(prob_here * prob_grad, axis=-1, keepdims=True)
        low = (prob_here * (prob_grad - row_dot)).astype(bf16)
        score_grad[h] = low
        for s, part in enumerate((dot_nn(low, key), dot_tn(low, query), dot_tn(prob[h], grad_rows))):
            proj_grad[:, s * width + h * HDIM : s * width + (h + 1) * HDIM] = part.astype(bf16)
    grad[:, : 3 * width] = dot_nn(act_t[...], proj_grad[...])
    grad[:, 3 * width :] = dot_tn(resid_low[...], mixed[...])
    spread(grad, outs)


def tail_kernel(score_grad, proj_grad, weights, bucket, keep, send, table_part, diag):
    width = proj_grad.shape[1]
    for half, at, rows in half_rows():
        to = send if half else keep
        to[at * BLK : (at + 1) * BLK, :] = dot_nt(proj_grad[rows, :], weights[:, :width]).astype(bf16)
    row = lax.broadcasted_iota(jnp.int32, (BLK, BLK), 0)
    col = lax.broadcasted_iota(jnp.int32, (BLK, BLK), 1)
    flip = (row + col == BLK - 1).astype(f32).astype(bf16)
    onehot = lax.broadcasted_iota(jnp.int32, (BUCKETS, 2 * LEN), 0) == bucket[...]
    diag[...] = jnp.zeros_like(diag)
    for h in range(score_grad.shape[0]):
        for r in range(LEN // BLK):
            flipped = dot_nn(flip, score_grad[h, r * BLK : (r + 1) * BLK, :])
            wide = jnp.concatenate([flipped, jnp.zeros((BLK, BLK), f32)], axis=1)
            turned = pltpu.roll(wide, 0, 1, stride=1, stride_axis=0)
            low_at = LEN - BLK - r * BLK
            diag[h : h + 1, low_at : low_at + WIN] += jnp.sum(turned, axis=0, keepdims=True)
        table_part[:, h : h + 1] = jnp.sum(
            jnp.where(onehot, diag[h : h + 1, :], 0.0), axis=1, keepdims=True
        )


def core_add_kernel(keep, got, mine, theirs):
    chip = lax.axis_index("tp") >> 1
    for to, index in ((mine, chip), (theirs, 1 - chip)):
        rows = pl.ds(pl.multiple_of(index * BLK, BLK), BLK)
        to[...] = (keep[rows, :].astype(f32) + got[rows, :].astype(f32)).astype(bf16)


def share_ds():
    return pl.ds(pl.multiple_of(lax.axis_index("tp") * BLK, BLK), BLK)


def block_out_kernel(resid, mine, got, out):
    out[...] = (resid[share_ds(), :] + (mine[...].astype(f32) + got[...].astype(f32))).astype(bf16)


def input_grad_kernel(x, gains, share_grad, mine, got, out, gain_part):
    values = x[share_ds(), :].astype(f32)
    scale = lax.rsqrt(jnp.mean(values * values, axis=-1, keepdims=True) + eps_norm)
    normed = values * scale
    act_grad = mine[...].astype(f32) + got[...].astype(f32)
    normal_grad = act_grad * gains[0:1, :]
    mean_part = jnp.mean(normal_grad * normed, axis=-1, keepdims=True)
    out[...] = share_grad[...] + scale * (normal_grad - normed * mean_part)
    gain_part[...] = jnp.sum(act_grad * normed, axis=0, keepdims=True)


def pair_add_kernel(keep, got, *outs):
    for k, out in enumerate(outs):
        out[...] = (keep[k].astype(f32) + got[k].astype(f32)).astype(bf16)


def fold(values):
    rows, cols = values.shape
    squares = values * values
    lanes = sum(squares[:, c : c + BLK] for c in range(0, cols, BLK))
    return jnp.sum(lanes, axis=0, keepdims=True)


def sum_kernel(n_parts, *rest):
    parts, (grad, squares) = rest[:n_parts], rest[n_parts:]
    total = sum(part[...].astype(f32) for part in parts)
    grad[...] = total
    squares[...] = fold(total)


def last_sum_kernel(n_parts, *rest):
    parts, (extra_a, extra_b, grad, payload) = rest[:n_parts], rest[n_parts:]
    total = sum(part[...].astype(f32) for part in parts)
    grad[...] = total
    squares = fold(total) + extra_a[...] + extra_b[...]
    payload[...] = jnp.broadcast_to(squares[None] * 0.125, payload.shape)


def adamw(weight, gradient, moment_one, moment_two, rate):
    one_new = beta_one * moment_one + (1.0 - beta_one) * gradient
    two_new = beta_two * moment_two + (1.0 - beta_two) * gradient * gradient
    one_hat = one_new / (1.0 - beta_one**adam_step)
    two_hat = two_new / (1.0 - beta_two**adam_step)
    weight_new = weight - rate * (one_hat / (jnp.sqrt(two_hat) + adam_eps) + decay_rate * weight)
    return (weight_new, one_new, two_new)


def adam_kernel(*refs):
    (
        sums,
        gains_sum,
        table_whole,
        table_grad,
        grad_qkvo,
        grad_in,
        grad_down,
        *state,
    ) = refs[:25]
    outs = refs[25:]
    qkv, out, ffn_in, ffn_down, gains, table = (state[i : i + 3] for i in range(0, 18, 3))
    norm_ref, qkv_o, out_o, in_o, down_o, gains_o, gains_grad, table_o = (
        outs[0],
        outs[1:5],
        outs[5:9],
        outs[9:13],
        outs[13:17],
        outs[17:20],
        outs[20],
        outs[21:24],
    )
    squares = (
        jnp.sum(sums[...])
        + jnp.sum(gains_sum[...] * gains_sum[...])
        + jnp.sum(table_whole[...] * table_whole[...])
    )
    norm = jnp.sqrt(jnp.full((1, 1), squares, f32))
    norm_ref[...] = norm
    factor = clip_norm / jnp.maximum(norm, clip_norm)

    def update(state_refs, gradient, to, rate, at=...):
        new = adamw(state_refs[0][at], gradient * factor, state_refs[1][at], state_refs[2][at], rate)
        for ref, value in zip(to, new):
            ref[at] = value
        if len(to) == 4:
            to[3][at] = new[0].astype(bf16)

    width = qkv[0].shape[2]
    for part in range(3):
        update(qkv, grad_qkvo[:, part * width : (part + 1) * width], qkv_o, rate_small, part)
    update(out, grad_qkvo[:, 3 * width :], out_o, rate_large)
    update(ffn_in, grad_in[...], in_o, rate_small)
    update(ffn_down, grad_down[...], down_o, rate_small)
    update(gains, gains_sum[...], gains_o, rate_large)
    gains_grad[...] = gains_sum[...] * factor
    update(table, table_grad[...], table_o, rate_large)


def on_device(
    dp,
    inputs,
    cotangent,
    seg_lengths,
    bucket_ids,
    qkv_weight,
    qkv_first,
    qkv_second,
    out_weight,
    out_first,
    out_second,
    ffn_in_weight,
    ffn_in_first,
    ffn_in_second,
    ffn_down_weight,
    ffn_down_first,
    ffn_down_second,
    norm_gains,
    gains_first,
    gains_second,
    bias_table,
    table_first,
    table_second,
):
    tokens, model = inputs.shape
    rows, local = out_weight.shape
    hidden = ffn_in_weight.shape[1]
    heads_here = local // HDIM
    tp = lax.axis_size("tp")
    packed_cols = 4 * local
    direct = dp == 8

    def swap_dp(value, distance):
        return lax.ppermute(value, "dp", [(i, i ^ distance) for i in range(dp)])

    def swap_tp(value, distance):
        return lax.ppermute(value, "tp", [(i, i ^ distance) for i in range(tp)])

    def gather(block):
        if not direct:
            return [lax.all_gather(block, "dp", axis=0, tiled=True)]
        along = [block] + [swap_dp(block, 2 * k) for k in range(1, dp // 2)]
        return [b for own in along for b in (own, swap_dp(own, 1))]

    def scatter(parts):
        if not direct:
            return [lax.psum_scatter(parts[0].astype(f32), "dp", scatter_dimension=0, tiled=True)]
        keep, send = parts
        outs = [sds(keep.shape[1:], bf16)] * keep.shape[0]
        folded = call(pair_add_kernel, outs, (keep, swap_dp(send, 1)), "pair_add")
        return [folded[0]] + [swap_dp(folded[k], 2 * k) for k in range(1, len(folded))]

    def sum_halves(keep, send):
        first = keep + swap_tp(send, 1)
        other_first = swap_tp(first, 1)
        second = swap_tp(first, 2)
        return (first, second, other_first, swap_tp(second, 1))

    def share_sum(keep, send):
        outs = [sds((BLK, model), bf16)] * 2
        mine, theirs = call(core_add_kernel, outs, (keep, swap_tp(send, 1)), "core_add")
        return mine, swap_tp(theirs, 2)

    half_shape = [sds((tokens // 2, model), bf16)] * 2
    (packed,) = call(
        pack_kernel, [sds((rows, packed_cols), bf16)], (qkv_weight, out_weight), "pack"
    )
    qkvo_blocks = gather(packed)
    down_blocks = gather(ffn_down_weight.astype(bf16))
    in_blocks = gather(ffn_in_weight.astype(bf16))
    n_blocks = len(qkvo_blocks)

    bucket_row = jnp.pad(bucket_ids, (0, 1))[None, :]
    act_one, act_one_t, bias = call(
        prep_kernel,
        [
            sds((tokens, model), bf16),
            sds((model, tokens), bf16),
            sds((heads_here, LEN, LEN), f32),
        ],
        (seg_lengths, bias_table, bucket_row, inputs, norm_gains),
        "prep",
        flops=20 * tokens * model,
        smem=(0, 1),
    )
    weights_one, qkv, prob, mixed, attn_keep, attn_send = call(
        functools.partial(attend_kernel, n_blocks),
        [
            sds((model, packed_cols), bf16),
            sds((tokens, 3 * local), bf16),
            sds((heads_here, LEN, LEN), bf16),
            sds((tokens, local), bf16),
            *half_shape,
        ],
        (act_one, bias, *qkvo_blocks),
        "attend",
        flops=2 * tokens * model * packed_cols + 4 * tokens * LEN * local,
    )
    down_full, hidden_grad = call(
        functools.partial(dhid_kernel, n_blocks),
        [sds((model, hidden), bf16), sds((tokens, hidden), f32)],
        (cotangent, *down_blocks),
        "dhid",
        flops=2 * tokens * model * hidden,
    )
    attn_sums = sum_halves(attn_keep, attn_send)
    resid, act_two, hidden_act, pre_grad, back_keep, back_send = call(
        functools.partial(ffn_kernel, n_blocks),
        [
            sds((tokens, model), f32),
            sds((tokens, model), bf16),
            sds((tokens, hidden), bf16),
            sds((tokens, hidden), bf16),
            *half_shape,
        ],
        (inputs, norm_gains, hidden_grad, *attn_sums, *in_blocks),
        "ffn",
        flops=4 * tokens * model * hidden,
        scratch=[pltpu.VMEM((model, hidden), bf16)],
    )
    back_sums = sum_halves(back_keep, back_send)
    grad_scratch = [pltpu.VMEM((model, hidden), f32)]
    down_parts = call(
        weight_grad_kernel,
        spread_shapes(dp, model, hidden),
        (cotangent, hidden_act),
        "down_grad",
        flops=2 * tokens * model * hidden,
        scratch=grad_scratch,
    )
    in_parts = call(
        weight_grad_kernel,
        spread_shapes(dp, model, hidden),
        (act_two, pre_grad),
        "in_grad",
        flops=2 * tokens * model * hidden,
        scratch=grad_scratch,
    )
    ffn_halves = call(
        ffn_out_kernel,
        half_shape,
        (hidden_act, down_full),
        "ffn_out",
        flops=2 * tokens * model * hidden,
    )
    qkvo_shapes = spread_shapes(dp, model, packed_cols)
    *qkvo_parts, share_grad, gain_two_part, score_grad, proj_grad = call(
        functools.partial(attend_back_kernel, len(qkvo_shapes)),
        [
            *qkvo_shapes,
            sds((BLK, model), f32),
            sds((1, model), f32),
            sds((heads_here, LEN, LEN), bf16),
            sds((tokens, 3 * local), bf16),
        ],
        (
            resid,
            cotangent,
            norm_gains,
            *back_sums,
            weights_one,
            qkv,
            prob,
            mixed,
            act_one_t,
        ),
        "attend_back",
        flops=2 * tokens * model * (packed_cols + local) + 10 * tokens * LEN * local,
        scratch=[pltpu.VMEM((tokens, model), bf16), pltpu.VMEM((model, packed_cols), f32)],
        limit=40,
    )
    act_keep, act_send, table_part = call(
        tail_kernel,
        [*half_shape, sds((BUCKETS, heads_here), f32)],
        (score_grad, proj_grad, weights_one, bucket_row),
        "tail",
        flops=2 * tokens * model * 3 * local,
        scratch=[pltpu.VMEM((8, 2 * LEN), f32)],
    )
    (block_out,) = call(
        block_out_kernel,
        [sds((BLK, model), bf16)],
        (resid, *share_sum(*ffn_halves)),
        "block_out",
    )
    input_grad, gain_one_part = call(
        input_grad_kernel,
        [sds((BLK, model), f32), sds((1, model), f32)],
        (inputs, norm_gains, share_grad, *share_sum(act_keep, act_send)),
        "input_grad",
    )

    everyone = dp * tp
    table_spread = lax.dynamic_update_slice_in_dim(
        jnp.zeros((BUCKETS, HEADS), f32), table_part, lax.axis_index("tp") * heads_here, 1
    )
    small = jnp.concatenate(
        (gain_one_part, gain_two_part, table_spread.reshape(1, -1)), axis=1
    ).reshape(-1, BLK)
    small = jnp.pad(small, ((0, 16 - small.shape[0]), (0, 0)))
    gathered = lax.all_to_all(
        jnp.broadcast_to(small[None], (everyone, 16, BLK)), ("dp", "tp"), 0, 0
    )
    small_sum = jnp.sum(gathered, axis=0).reshape(-1)
    gains_sum = small_sum[: 2 * model].reshape(2, model)
    table_whole = small_sum[2 * model : 2 * model + BUCKETS * HEADS].reshape(BUCKETS, HEADS)
    table_grad = lax.dynamic_slice_in_dim(
        table_whole, lax.axis_index("tp") * heads_here, heads_here, 1
    )

    def summed(parts):
        return call(
            functools.partial(sum_kernel, len(parts)),
            [sds((rows, parts[0].shape[1]), f32), sds((1, BLK), f32)],
            parts,
            "sum_parts",
        )

    down_grad, down_squares = summed(scatter(down_parts))
    in_grad, in_squares = summed(scatter(in_parts))
    last_parts = scatter(qkvo_parts)
    qkvo_grad, payload = call(
        functools.partial(last_sum_kernel, len(last_parts)),
        [sds((rows, packed_cols), f32), sds((everyone, 8, BLK), f32)],
        (*last_parts, down_squares, in_squares),
        "last_sum",
    )
    squares = lax.all_to_all(payload, ("dp", "tp"), 0, 0)
    matrix = [sds((rows, hidden), f32)] * 3 + [sds((rows, hidden), bf16)]
    state = (
        qkv_weight,
        qkv_first,
        qkv_second,
        out_weight,
        out_first,
        out_second,
        ffn_in_weight,
        ffn_in_first,
        ffn_in_second,
        ffn_down_weight,
        ffn_down_first,
        ffn_down_second,
        norm_gains,
        gains_first,
        gains_second,
        bias_table,
        table_first,
        table_second,
    )
    norm, *updated = call(
        adam_kernel,
        [
            sds((1, 1), f32),
            *[sds(qkv_weight.shape, f32)] * 3,
            sds(qkv_weight.shape, bf16),
            *[sds(out_weight.shape, f32)] * 3,
            sds(out_weight.shape, bf16),
            *matrix,
            *matrix,
            *[sds(norm_gains.shape, f32)] * 4,
            *[sds(bias_table.shape, f32)] * 3,
        ],
        (
            squares,
            gains_sum,
            table_whole,
            table_grad,
            qkvo_grad,
            in_grad,
            down_grad,
            *state,
        ),
        "adam",
    )
    return (block_out, input_grad, norm.reshape(()), *updated)


def solution(mesh):
    row = P("dp", None)
    matrix = P("dp", "tp")
    stack = P(None, "dp", "tp")
    table = P(None, "tp")
    share = P(("dp", "tp"), None)
    in_specs = (
        *(row,) * 3,
        P(),
        *(stack,) * 3,
        *(matrix,) * 9,
        *(P(),) * 3,
        *(table,) * 3,
    )
    out_specs = (
        *(share,) * 2,
        P(),
        *(stack,) * 4,
        *(matrix,) * 12,
        *(P(),) * 4,
        *(table,) * 3,
    )
    return jax.shard_map(
        functools.partial(on_device, mesh.shape["dp"]),
        mesh=mesh,
        in_specs=in_specs,
        out_specs=out_specs,
        check_vma=False,
    )
```

time: 2760 us -> 209 us (0.08)
  other arithmetic: 1420 us -> 1.24 us
  local copies, waits for them, and re-layouts: 1030 us -> 29.1 us
  blocking collectives: 110 us -> 0 us
  waiting for transfers between devices: 143 us -> 70.8 us
  starting transfers between devices: 0.79 us -> 69.4 us
  Pallas kernels: 0 us -> 35.9 us
  matrix products: 33.9 us -> 0 us
    scatter-add x1 -> x0, other arithmetic: 1390 us -> none  [on_device(): jax.ops.segment_sum(bias_grad.reshape(heads_here, LEN * LEN).T, offsets.r...]
    gather x2 -> x0, local copies, waits for them, and re-layouts: 933 us -> none  [on_device(): bias_full = jnp.transpose(bias_rows[offsets], (2, 0, 1))]
    psum x3 -> x0, waiting for transfers between devices: 105 us -> none  [the longest x1 66.3 us: on_device(): block_f32 = resid_one + lax.psum(ffn_part, 'tp')]
    all_gather x2 -> x0, blocking collectives: 70 us -> none  [the longest x1 38.8 us: on_device(): lax.all_gather(qkv_weight.astype(jnp.bfloat16), 'dp', axis=1, tiled=True)]
    ppermute x0 -> x45, waiting for transfers between devices: none -> 65.6 us  [the longest x33 49.6 us: swap_dp(): return lax.ppermute(value, 'dp', [(i, i ^ distance) for i in range(dp)])]
    transpose x1 -> x0, local copies, waits for them, and re-layouts: 58.4 us -> none  [on_device(): bias_grad.reshape(heads_here, LEN * LEN)]
    ppermute x0 -> x45, starting transfers between devices: none -> 58 us  [the longest x33 54 us: swap_dp(): return lax.ppermute(value, 'dp', [(i, i ^ distance) for i in range(dp)])]
    psum x1 -> x0, blocking collectives: 39.9 us -> none  [on_device(): lax.psum((gains_part, table_spread, shard_squares), ('dp', 'tp'))]
  transfers between devices with their start and end apart: 9 -> 47, of which waited for: 3 -> 18; matrix products, arithmetic and copies ran while one was open for 54% -> 3% of each run, Pallas kernels for 0% -> 9%
where the time goes in v1:
time: 209 us; the launch traced here: 208 us
  waiting for transfers between devices  70.8 us (34%)
  starting transfers between devices  69.4 us (33%)
  Pallas kernels  35.9 us (17%)
  local copies, waits for them, and re-layouts  29.1 us (14%)
    ppermute x33, starting transfers between devices, swap_dp(): return lax.ppermute(value, 'dp', [(i, i ^ distance) for i in range(dp)])  54 us
    ppermute x33, waiting for transfers between devices, swap_dp(): return lax.ppermute(value, 'dp', [(i, i ^ distance) for i in range(dp)])  49.6 us
    pallas_call x21, Pallas kernels, call(): pl.pallas_call(body, out_shape=tuple(outs), in_specs=[pl.BlockSpec(memory...  35.9 us
    unnamed x94, local copies, waits for them, and re-layouts  24.7 us
    ppermute x12, waiting for transfers between devices, swap_tp(): return lax.ppermute(value, 'tp', [(i, i ^ distance) for i in range(tp)])  16 us
    all_to_all x1, starting transfers between devices, on_device(): lax.all_to_all(jnp.broadcast_to(small[None], (everyone, 16, BLK)), ('dp',...  7.4 us
    all_to_all x1, waiting for transfers between devices, on_device(): squares = lax.all_to_all(payload, ('dp', 'tp'), 0, 0)  5.18 us
  transfers between devices with their start and end apart: 47, of which 18 were waited for; matrix products, arithmetic and copies ran while one was open for 3% of the time, Pallas kernels for 9%

profile of v1, /device:TPU:0, one launch (start us, length us, event | category | flops | bytes accessed | tf_op | source)
XLA Modules:
  0.0 207.6 jit_solution(2438366800504728729)
XLA Ops:
  2.6 3.1 %collective-permute-start.8 = (bf16[96,768]{1,0:T(8,128)(2,1)S(1)}, bf16[96,768]{1,0:T(8,128)(2,1)S(1)}, u32[]{:S(2)}, u32[]{:S(2)}) collective-permute-start(bf16[96,768]{1,0:T(8,128)(2,1)S(1)} %pack.1.rest_0_), channel_id=1, source_target_pairs={{0,8},{4,12},{8,0},{12,4},{16,24},{20,28},{24,16},{28,20},{1,9},{5... | collective-permute-start | bytes 442376 | tf_op jit(solution)/shard_map/ppermute | solution.py:413
  5.7 2.6 %collective-permute-start.10 = (bf16[96,768]{1,0:T(8,128)(2,1)S(1)}, bf16[96,768]{1,0:T(8,128)(2,1)S(1)}, u32[]{:S(2)}, u32[]{:S(2)}) collective-permute-start(bf16[96,768]{1,0:T(8,128)(2,1)S(1)} %pack.1.rest_0_), channel_id=1, source_target_pairs={{0,16},{4,20},{8,24},{12,28},{16,0},{20,4},{24,8},{28,12},{1,17},{... | collective-permute-start | bytes 442376 | tf_op jit(solution)/shard_map/ppermute | solution.py:413
  8.3 1.7 collective-permute-start.7
  10.0 1.6 collective-permute-done.8.rest_2_
  11.6 1.7 collective-permute-start.9
  13.3 6.4 %collective-permute-done.10.rest_4_ = bf16[96,768]{1,0:T(8,128)(2,1)S(1)} collective-permute-done((bf16[96,768]{1,0:T(8,128)(2,1)S(1)}, bf16[96,768]{1,0:T(8,128)(2,1)S(1)}, u32[]{:S(2)}, u32[]{:S(2)}) %collective-permute-start.10) | collective-permute-done | bytes 147488 | tf_op jit(solution)/shard_map/ppermute | solution.py:413
  25.7 1.7 prep.1
  27.5 2.9 %attend.1 = (bf16[768,768]{1,0:T(8,128)(2,1)S(1)}, bf16[512,576]{1,0:T(8,128)(2,1)S(1)}, bf16[3,512,512]{2,1,0:T(8,128)(2,1)S(1)}, bf16[512,192]{1,0:T(8,128)(2,...) custom-call(bf16[512,768]{1,0:T(8,128)(2,1)S(1)} %get-tuple-element.107.act, ...), custom_call_target="tpu_custom_call" | custom-call | flops 805306368 | bytes 9437184 | tf_op jit(solution)/shard_map/attend/pallas_call | solution.py:51
  30.5 1.7 collective-permute-done.14
  32.4 1.6 collective-permute-start.15
  34.0 1.6 collective-permute-start
  36.3 2.0 collective-permute-start.3
  38.4 1.5 collective-permute-start.5
  41.1 1.8 collective-permute-done.1.rest_2_
  43.1 7.3 %collective-permute-done.3.rest_4_ = bf16[96,768]{1,0:T(8,128)(2,1)S(1)} collective-permute-done((bf16[96,768]{1,0:T(8,128)(2,1)S(1)}, bf16[96,768]{1,0:T(8,128)(2,1)S(1)}, u32[]{:S(2)}, u32[]{:S(2)}) %collective-permute-start.3) | collective-permute-done | bytes 147488 | tf_op jit(solution)/shard_map/ppermute | solution.py:413
  50.4 2.5 %collective-permute-start.23 = (bf16[96,768]{1,0:T(8,128)(2,1)S(1)}, bf16[96,768]{1,0:T(8,128)(2,1)S(1)}, u32[]{:S(2)}, u32[]{:S(2)}) collective-permute-start(bf16[96,768]{1,0:T(8,128)(2,1)S(1)} %convert_element_type.9.rest_0_), channel_id=1, source_target_pairs={{0,24},{4,28},{8,16},{12,20},{16,8},{20,12},{24,0},{28,4},{1,25},{... | collective-permute-start | bytes 442376 | tf_op jit(solution)/shard_map/ppermute | solution.py:413
  53.4 1.5 collective-permute-start.2
  54.9 8.0 %collective-permute-done.21.rest_4_ = bf16[96,768]{1,0:T(8,128)(2,1)S(1)} collective-permute-done((bf16[96,768]{1,0:T(8,128)(2,1)S(1)}, bf16[96,768]{1,0:T(8,128)(2,1)S(1)}, u32[]{:S(2)}, u32[]{:S(2)}) %collective-permute-start.21) | collective-permute-done | bytes 147488 | tf_op jit(solution)/shard_map/ppermute | solution.py:413
  66.4 3.3 %collective-permute-done.4.rest_5_ = bf16[96,768]{1,0:T(8,128)(2,1)S(1)} collective-permute-done((bf16[96,768]{1,0:T(8,128)(2,1)S(1)}, bf16[96,768]{1,0:T(8,128)(2,1)S(1)}, u32[]{:S(2)}, u32[]{:S(2)}) %collective-permute-start.4) | collective-permute-done | bytes 147488 | tf_op jit(solution)/shard_map/ppermute | solution.py:413
  71.2 1.7 collective-permute-done.6.rest_7_
  76.3 1.7 collective-permute-done.24.rest_7_
  78.0 3.0 %ffn.1 = (f32[512,768]{1,0:T(8,128)S(1)}, bf16[512,768]{1,0:T(8,128)(2,1)S(1)}, bf16[512,768]{1,0:T(8,128)(2,1)S(1)}, bf16[512,768]{1,0:T(8,128)(2,1)S(1)}, bf16...) custom-call(bf16[512,768]{1,0:T(8,128)(2,1)S(1)} %copy-done.1, f32[2,768]{1,0:T(2,128)S(1)} %copy-done.32, ...), custom_call_target="tpu_custom_call" | custom-call | flops 1207959552 | bytes 9836544 | tf_op jit(solution)/shard_map/ffn/pallas_call | solution.py:51
  81.1 1.7 collective-permute-done.27
  83.5 10.6 %collective-permute-done.28.own_b = bf16[256,768]{1,0:T(8,128)(2,1)S(1)} collective-permute-done((bf16[256,768]{1,0:T(8,128)(2,1)S(1)}, bf16[256,768]{1,0:T(8,128)(2,1)S(1)}, u32[]{:S(2)}, u32[]{:S(2)}) %collective-permute-start.28) | collective-permute-done | bytes 393248 | tf_op jit(solution)/shard_map/ppermute | solution.py:416
  94.1 1.7 collective-permute-done.30.other_b
  95.9 6.2 %attend_back.1 = (bf16[4,96,768]{2,1,0:T(8,128)(2,1)S(1)}, bf16[4,96,768]{2,1,0:T(8,128)(2,1)}, f32[128,768]{1,0:T(8,128)S(1)}, f32[1,768]{1,0:T(1,128)S(1)}, bf...) custom-call(f32[512,768]{1,0:T(8,128)S(1)} %get-tuple-element.111.resid, bf16[512,768]{1,0:T(8,128)(2,1)S(1)} %copy-done.6, ...), custom_call_target="tpu_custom_call" | custom-call | flops 1258291200 | bytes 12002304 | tf_op jit(solution)/shard_map/attend_back/pallas_call | solution.py:51
  102.1 2.6 %tail.1 = (bf16[256,768]{1,0:T(8,128)(2,1)S(1)}, bf16[256,768]{1,0:T(8,128)(2,1)S(1)}, f32[32,3]{1,0:T(8,128)S(1)}) custom-call(bf16[3,512,512]{2,1,0:T(8,128)(2,1)S(1)} %get-tuple-element.126.score_grad, bf16[512,576]{1,0:T(8,128)(2,1)S(1)} %get-tuple-element.127.proj_grad, bf16[768,768]{1,0:T(8,128)(2,1)S(1)} %get-tuple-element.120.weights, ...), custom_call_target="tpu_custom_call" | custom-call | flops 452984832 | bytes 4133248 | tf_op jit(solution)/shard_map/tail/pallas_call | solution.py:51
  104.9 1.8 down_grad.1
  107.5 1.5 collective-permute-start.37
  109.0 1.8 in_grad.1
  115.5 2.4 %ffn_out.1 = (bf16[256,768]{1,0:T(8,128)(2,1)S(1)}, bf16[256,768]{1,0:T(8,128)(2,1)}) custom-call(bf16[512,768]{1,0:T(8,128)(2,1)S(1)} %get-tuple-element.112.hidden.right, bf16[768,768]{1,0:T(8,128)(2,1)S(1)} %get-tuple-element.113.weights), custom_call_target="tpu_custom_call" | custom-call | flops 603979776 | bytes 2752512 | tf_op jit(solution)/shard_map/ffn_out/pallas_call | solution.py:51
  123.6 1.9 input_grad.1
  126.3 7.4 %all-to-all-start.1 = ((f32[32,16,128]{2,1,0:T(8,128)}), f32[32,16,128]{2,1,0:T(8,128)}, u32[]{:S(2)}, u32[]{:S(2)}) async-start(f32[32,16,128]{2,1,0:T(8,128)} %broadcast_in_dim.14), calls=%async_computation.1 | async-start | bytes 524288 | tf_op jit(solution)/shard_map/all_to_all | solution.py:580
  136.0 1.8 collective-permute-start.38
  137.8 2.4 %collective-permute-start.39 = (bf16[96,768]{1,0:T(8,128)(2,1)S(1)}, bf16[96,768]{1,0:T(8,128)(2,1)S(1)}, u32[]{:S(2)}, u32[]{:S(2)}) collective-permute-start(bf16[96,768]{1,0:T(8,128)(2,1)S(1)} %get-tuple-element.143), channel_id=1, source_target_pairs={{0,16},{4,20},{8,24},{12,28},{16,0},{20,4},{24,8},{28,12},{1,17},{... | collective-permute-start | bytes 442376 | tf_op jit(solution)/shard_map/ppermute | solution.py:413
  141.7 4.8 %collective-permute-start.42 = (bf16[96,768]{1,0:T(8,128)(2,1)S(1)}, bf16[96,768]{1,0:T(8,128)(2,1)S(1)}, u32[]{:S(2)}, u32[]{:S(2)}) collective-permute-start(bf16[96,768]{1,0:T(8,128)(2,1)S(1)} %get-tuple-element.151), channel_id=1, source_target_pairs={{0,8},{4,12},{8,0},{12,4},{16,24},{20,28},{24,16},{28,20},{1,9},{5... | collective-permute-start | bytes 442376 | tf_op jit(solution)/shard_map/ppermute | solution.py:413
  146.5 4.6 %collective-permute-done.33.got = bf16[4,96,768]{2,1,0:T(8,128)(2,1)} collective-permute-done((bf16[4,96,768]{2,1,0:T(8,128)(2,1)}, bf16[4,96,768]{2,1,0:T(8,128)(2,1)}, u32[]{:S(2)}, u32[]{:S(2)}) %collective-permute-start.33) | collective-permute-done | bytes 589856 | tf_op jit(solution)/shard_map/ppermute | solution.py:413
  151.1 6.0 %collective-permute-start.43 = (bf16[96,768]{1,0:T(8,128)(2,1)S(1)}, bf16[96,768]{1,0:T(8,128)(2,1)S(1)}, u32[]{:S(2)}, u32[]{:S(2)}) collective-permute-start(bf16[96,768]{1,0:T(8,128)(2,1)S(1)} %get-tuple-element.152), channel_id=1, source_target_pairs={{0,16},{4,20},{8,24},{12,28},{16,0},{20,4},{24,8},{28,12},{1,17},{... | collective-permute-start | bytes 442376 | tf_op jit(solution)/shard_map/ppermute | solution.py:413
  158.3 2.0 collective-permute-start.44
  160.3 2.4 %collective-permute-start.35 = (bf16[96,768]{1,0:T(8,128)(2,1)S(1)}, bf16[96,768]{1,0:T(8,128)(2,1)S(1)}, u32[]{:S(2)}, u32[]{:S(2)}) collective-permute-start(bf16[96,768]{1,0:T(8,128)(2,1)S(1)} %get-tuple-element.137), channel_id=1, source_target_pairs={{0,16},{4,20},{8,24},{12,28},{16,0},{20,4},{24,8},{28,12},{1,17},{... | collective-permute-start | bytes 442376 | tf_op jit(solution)/shard_map/ppermute | solution.py:413
  162.8 1.9 collective-permute-start.36
  164.7 1.7 core_add.2
  166.4 2.9 %collective-permute-done.43.rest_2_ = bf16[96,768]{1,0:T(8,128)(2,1)S(1)} collective-permute-done((bf16[96,768]{1,0:T(8,128)(2,1)S(1)}, bf16[96,768]{1,0:T(8,128)(2,1)S(1)}, u32[]{:S(2)}, u32[]{:S(2)}) %collective-permute-start.43) | collective-permute-done | bytes 147488 | tf_op jit(solution)/shard_map/ppermute | solution.py:413
  171.5 9.2 %collective-permute-done.35.rest_2_ = bf16[96,768]{1,0:T(8,128)(2,1)S(1)} collective-permute-done((bf16[96,768]{1,0:T(8,128)(2,1)S(1)}, bf16[96,768]{1,0:T(8,128)(2,1)S(1)}, u32[]{:S(2)}, u32[]{:S(2)}) %collective-permute-start.35) | collective-permute-done | bytes 147488 | tf_op jit(solution)/shard_map/ppermute | solution.py:413
  182.2 4.1 %all-to-all-start = ((f32[32,8,128]{2,1,0:T(8,128)}), f32[32,8,128]{2,1,0:T(8,128)S(1)}, u32[]{:S(2)}, u32[]{:S(2)}) async-start(f32[32,8,128]{2,1,0:T(8,128)} %copy-done.35), calls=%async_computation | async-start | bytes 262144 | tf_op jit(solution)/shard_map/all_to_all | solution.py:607
  186.5 1.7 block_out.1
  189.4 5.2 %all-to-all-done.refs_0_ = f32[32,8,128]{2,1,0:T(8,128)S(1)} async-done(((f32[32,8,128]{2,1,0:T(8,128)}), f32[32,8,128]{2,1,0:T(8,128)S(1)}, u32[]{:S(2)}, u32[]{:S(2)}) %all-to-all-start) | async-done | bytes 131104 | tf_op jit(solution)/shard_map/all_to_all | solution.py:607
  203.1 2.5 %adam.1 = (f32[1,1]{1,0:T(1,128)}, f32[3,96,192]{2,1,0:T(8,128)}, f32[3,96,192]{2,1,0:T(8,128)}, f32[3,96,192]{2,1,0:T(8,128)}, bf16[3,96,192]{2,1,0:T(8,128)(2,...) custom-call(f32[32,8,128]{2,1,0:T(8,128)S(1)} %all-to-all-done.refs_, ...), custom_call_target="tpu_custom_call" | custom-call | bytes 6819972 | tf_op jit(solution)/shard_map/adam/pallas_call | solution.py:51
  (177 shorter events, 52.7 us)
Async XLA Ops:
  2.6 8.9 %collective-permute-start.8 = (bf16[96,768]{1,0:T(8,128)(2,1)S(1)}, bf16[96,768]{1,0:T(8,128)(2,1)S(1)}, u32[]{:S(2)}, u32[]{:S(2)}) collective-permute-start(bf16[96,768]{1,0:T(8,128)(2,1)S(1)} %pack.1.rest_0_), channel_id=1, source_target_pairs={{0,8},{4,12},{8,0},{12,4},{16,24},{20,28},{24,16},{28,20},{1,9},{5... | collective-permute-start | bytes 442376 | tf_op jit(solution)/shard_map/ppermute | solution.py:413
  5.7 14.0 %collective-permute-start.10 = (bf16[96,768]{1,0:T(8,128)(2,1)S(1)}, bf16[96,768]{1,0:T(8,128)(2,1)S(1)}, u32[]{:S(2)}, u32[]{:S(2)}) collective-permute-start(bf16[96,768]{1,0:T(8,128)(2,1)S(1)} %pack.1.rest_0_), channel_id=1, source_target_pairs={{0,16},{4,20},{8,24},{12,28},{16,0},{20,4},{24,8},{28,12},{1,17},{... | collective-permute-start | bytes 442376 | tf_op jit(solution)/shard_map/ppermute | solution.py:413
  8.3 12.9 %collective-permute-start.12 = (bf16[96,768]{1,0:T(8,128)(2,1)S(1)}, bf16[96,768]{1,0:T(8,128)(2,1)S(1)}, u32[]{:S(2)}, u32[]{:S(2)}) collective-permute-start(bf16[96,768]{1,0:T(8,128)(2,1)S(1)} %pack.1.rest_0_), channel_id=1, source_target_pairs={{0,24},{4,28},{8,16},{12,20},{16,8},{20,12},{24,0},{28,4},{1,25},{... | collective-permute-start | bytes 442376 | tf_op jit(solution)/shard_map/ppermute | solution.py:413
  8.3 19.1 %collective-permute-start.7 = (bf16[96,768]{1,0:T(8,128)(2,1)S(1)}, bf16[96,768]{1,0:T(8,128)(2,1)S(1)}, u32[]{:S(2)}, u32[]{:S(2)}) collective-permute-start(bf16[96,768]{1,0:T(8,128)(2,1)S(1)} %pack.1.rest_0_), channel_id=1, source_target_pairs={{0,4},{4,0},{8,12},{12,8},{16,20},{20,16},{24,28},{28,24},{1,5},{5... | collective-permute-start | bytes 442376 | tf_op jit(solution)/shard_map/ppermute | solution.py:413
  11.6 15.9 %collective-permute-start.9 = (bf16[96,768]{1,0:T(8,128)(2,1)S(1)}, bf16[96,768]{1,0:T(8,128)(2,1)S(1)}, u32[]{:S(2)}, u32[]{:S(2)}) collective-permute-start(bf16[96,768]{1,0:T(8,128)(2,1)S(1)} %collective-permute-done.8.rest_2_), channel_id=1, source_target_pairs={{0,4},{4,0},{8,12},{12,8},{16,20},{20,16},{24,28},{28,24},{1,5},{5... | collective-permute-start | bytes 442376 | tf_op jit(solution)/shard_map/ppermute | solution.py:413
  19.7 7.7 %collective-permute-start.11 = (bf16[96,768]{1,0:T(8,128)(2,1)S(1)}, bf16[96,768]{1,0:T(8,128)(2,1)S(1)}, u32[]{:S(2)}, u32[]{:S(2)}) collective-permute-start(bf16[96,768]{1,0:T(8,128)(2,1)S(1)} %collective-permute-done.10.rest_4_), channel_id=1, source_target_pairs={{0,4},{4,0},{8,12},{12,8},{16,20},{20,16},{24,28},{28,24},{1,5},{5... | collective-permute-start | bytes 442376 | tf_op jit(solution)/shard_map/ppermute | solution.py:413
  21.2 6.2 %collective-permute-start.13 = (bf16[96,768]{1,0:T(8,128)(2,1)S(1)}, bf16[96,768]{1,0:T(8,128)(2,1)S(1)}, u32[]{:S(2)}, u32[]{:S(2)}) collective-permute-start(bf16[96,768]{1,0:T(8,128)(2,1)S(1)} %collective-permute-done.12.rest_6_), channel_id=1, source_target_pairs={{0,4},{4,0},{8,12},{12,8},{16,20},{20,16},{24,28},{28,24},{1,5},{5... | collective-permute-start | bytes 442376 | tf_op jit(solution)/shard_map/ppermute | solution.py:413
  30.5 1.8 collective-permute-start.14
  32.3 45.6 %copy-start.1 = (bf16[512,768]{1,0:T(8,128)(2,1)S(1)}, bf16[512,768]{1,0:T(8,128)(2,1)}, u32[]{:S(2)}) copy-start(bf16[512,768]{1,0:T(8,128)(2,1)} %x.9) | copy-start | bytes 2359300
  32.4 20.5 %collective-permute-start.15 = (bf16[256,768]{1,0:T(8,128)(2,1)S(1)}, bf16[256,768]{1,0:T(8,128)(2,1)S(1)}, u32[]{:S(2)}, u32[]{:S(2)}) collective-permute-start(bf16[256,768]{1,0:T(8,128)(2,1)S(1)} %add.14.own_a), channel_id=1, source_target_pairs={{0,2},{1,3},{2,0},{3,1},{4,6},{5,7},{6,4},{7,5},{8,10},{9,11},{10,... | collective-permute-start | bytes 1179656 | tf_op jit(solution)/shard_map/ppermute | solution.py:416
  34.0 6.0 %collective-permute-start = (bf16[96,768]{1,0:T(8,128)(2,1)S(1)}, bf16[96,768]{1,0:T(8,128)(2,1)S(1)}, u32[]{:S(2)}, u32[]{:S(2)}) collective-permute-start(bf16[96,768]{1,0:T(8,128)(2,1)S(1)} %convert_element_type.8.rest_0_), channel_id=1, source_target_pairs={{0,4},{4,0},{8,12},{12,8},{16,20},{20,16},{24,28},{28,24},{1,5},{5... | collective-permute-start | bytes 442376 | tf_op jit(solution)/shard_map/ppermute | solution.py:413
  35.5 7.4 %collective-permute-start.1 = (bf16[96,768]{1,0:T(8,128)(2,1)S(1)}, bf16[96,768]{1,0:T(8,128)(2,1)S(1)}, u32[]{:S(2)}, u32[]{:S(2)}) collective-permute-start(bf16[96,768]{1,0:T(8,128)(2,1)S(1)} %convert_element_type.8.rest_0_), channel_id=1, source_target_pairs={{0,8},{4,12},{8,0},{12,4},{16,24},{20,28},{24,16},{28,20},{1,9},{5... | collective-permute-start | bytes 442376 | tf_op jit(solution)/shard_map/ppermute | solution.py:413
  36.3 14.0 %collective-permute-start.3 = (bf16[96,768]{1,0:T(8,128)(2,1)S(1)}, bf16[96,768]{1,0:T(8,128)(2,1)S(1)}, u32[]{:S(2)}, u32[]{:S(2)}) collective-permute-start(bf16[96,768]{1,0:T(8,128)(2,1)S(1)} %convert_element_type.8.rest_0_), channel_id=1, source_target_pairs={{0,16},{4,20},{8,24},{12,28},{16,0},{20,4},{24,8},{28,12},{1,17},{... | collective-permute-start | bytes 442376 | tf_op jit(solution)/shard_map/ppermute | solution.py:413
  38.4 12.0 %collective-permute-start.5 = (bf16[96,768]{1,0:T(8,128)(2,1)S(1)}, bf16[96,768]{1,0:T(8,128)(2,1)S(1)}, u32[]{:S(2)}, u32[]{:S(2)}) collective-permute-start(bf16[96,768]{1,0:T(8,128)(2,1)S(1)} %convert_element_type.8.rest_0_), channel_id=1, source_target_pairs={{0,24},{4,28},{8,16},{12,20},{16,8},{20,12},{24,0},{28,4},{1,25},{... | collective-permute-start | bytes 442376 | tf_op jit(solution)/shard_map/ppermute | solution.py:413
  40.0 12.9 %collective-permute-start.18 = (bf16[96,768]{1,0:T(8,128)(2,1)S(1)}, bf16[96,768]{1,0:T(8,128)(2,1)S(1)}, u32[]{:S(2)}, u32[]{:S(2)}) collective-permute-start(bf16[96,768]{1,0:T(8,128)(2,1)S(1)} %convert_element_type.9.rest_0_), channel_id=1, source_target_pairs={{0,4},{4,0},{8,12},{12,8},{16,20},{20,16},{24,28},{28,24},{1,5},{5... | collective-permute-start | bytes 442376 | tf_op jit(solution)/shard_map/ppermute | solution.py:413
  42.9 10.4 %collective-permute-start.19 = (bf16[96,768]{1,0:T(8,128)(2,1)S(1)}, bf16[96,768]{1,0:T(8,128)(2,1)S(1)}, u32[]{:S(2)}, u32[]{:S(2)}) collective-permute-start(bf16[96,768]{1,0:T(8,128)(2,1)S(1)} %convert_element_type.9.rest_0_), channel_id=1, source_target_pairs={{0,8},{4,12},{8,0},{12,4},{16,24},{20,28},{24,16},{28,20},{1,9},{5... | collective-permute-start | bytes 442376 | tf_op jit(solution)/shard_map/ppermute | solution.py:413
  50.4 12.5 %collective-permute-start.21 = (bf16[96,768]{1,0:T(8,128)(2,1)S(1)}, bf16[96,768]{1,0:T(8,128)(2,1)S(1)}, u32[]{:S(2)}, u32[]{:S(2)}) collective-permute-start(bf16[96,768]{1,0:T(8,128)(2,1)S(1)} %convert_element_type.9.rest_0_), channel_id=1, source_target_pairs={{0,16},{4,20},{8,24},{12,28},{16,0},{20,4},{24,8},{28,12},{1,17},{... | collective-permute-start | bytes 442376 | tf_op jit(solution)/shard_map/ppermute | solution.py:413
  50.4 14.0 %collective-permute-start.23 = (bf16[96,768]{1,0:T(8,128)(2,1)S(1)}, bf16[96,768]{1,0:T(8,128)(2,1)S(1)}, u32[]{:S(2)}, u32[]{:S(2)}) collective-permute-start(bf16[96,768]{1,0:T(8,128)(2,1)S(1)} %convert_element_type.9.rest_0_), channel_id=1, source_target_pairs={{0,24},{4,28},{8,16},{12,20},{16,8},{20,12},{24,0},{28,4},{1,25},{... | collective-permute-start | bytes 442376 | tf_op jit(solution)/shard_map/ppermute | solution.py:413
  52.8 25.1 %collective-permute-start.16 = (bf16[256,768]{1,0:T(8,128)(2,1)S(1)}, bf16[256,768]{1,0:T(8,128)(2,1)S(1)}, u32[]{:S(2)}, u32[]{:S(2)}) collective-permute-start(bf16[256,768]{1,0:T(8,128)(2,1)S(1)} %add.14.own_a), channel_id=1, source_target_pairs={{0,1},{1,0},{2,3},{3,2},{4,5},{5,4},{6,7},{7,6},{8,9},{9,8},{10,11... | collective-permute-start | bytes 1179656 | tf_op jit(solution)/shard_map/ppermute | solution.py:416
  52.9 25.1 %collective-permute-start.17 = (bf16[256,768]{1,0:T(8,128)(2,1)S(1)}, bf16[256,768]{1,0:T(8,128)(2,1)S(1)}, u32[]{:S(2)}, u32[]{:S(2)}) collective-permute-start(bf16[256,768]{1,0:T(8,128)(2,1)S(1)} %collective-permute-done.15.own_b), channel_id=1, source_target_pairs={{0,1},{1,0},{2,3},{3,2},{4,5},{5,4},{6,7},{7,6},{8,9},{9,8},{10,11... | collective-permute-start | bytes 1179656 | tf_op jit(solution)/shard_map/ppermute | solution.py:416
  53.4 11.6 %collective-permute-start.2 = (bf16[96,768]{1,0:T(8,128)(2,1)S(1)}, bf16[96,768]{1,0:T(8,128)(2,1)S(1)}, u32[]{:S(2)}, u32[]{:S(2)}) collective-permute-start(bf16[96,768]{1,0:T(8,128)(2,1)S(1)} %collective-permute-done.1.rest_2_), channel_id=1, source_target_pairs={{0,4},{4,0},{8,12},{12,8},{16,20},{20,16},{24,28},{28,24},{1,5},{5... | collective-permute-start | bytes 442376 | tf_op jit(solution)/shard_map/ppermute | solution.py:413
  62.9 6.8 %collective-permute-start.4 = (bf16[96,768]{1,0:T(8,128)(2,1)S(1)}, bf16[96,768]{1,0:T(8,128)(2,1)S(1)}, u32[]{:S(2)}, u32[]{:S(2)}) collective-permute-start(bf16[96,768]{1,0:T(8,128)(2,1)S(1)} %collective-permute-done.3.rest_4_), channel_id=1, source_target_pairs={{0,4},{4,0},{8,12},{12,8},{16,20},{20,16},{24,28},{28,24},{1,5},{5... | collective-permute-start | bytes 442376 | tf_op jit(solution)/shard_map/ppermute | solution.py:413
  64.4 8.5 %collective-permute-start.6 = (bf16[96,768]{1,0:T(8,128)(2,1)S(1)}, bf16[96,768]{1,0:T(8,128)(2,1)S(1)}, u32[]{:S(2)}, u32[]{:S(2)}) collective-permute-start(bf16[96,768]{1,0:T(8,128)(2,1)S(1)} %collective-permute-done.5.rest_6_), channel_id=1, source_target_pairs={{0,4},{4,0},{8,12},{12,8},{16,20},{20,16},{24,28},{28,24},{1,5},{5... | collective-permute-start | bytes 442376 | tf_op jit(solution)/shard_map/ppermute | solution.py:413
  64.9 10.3 %collective-permute-start.20 = (bf16[96,768]{1,0:T(8,128)(2,1)S(1)}, bf16[96,768]{1,0:T(8,128)(2,1)S(1)}, u32[]{:S(2)}, u32[]{:S(2)}) collective-permute-start(bf16[96,768]{1,0:T(8,128)(2,1)S(1)} %collective-permute-done.19.rest_2_), channel_id=1, source_target_pairs={{0,4},{4,0},{8,12},{12,8},{16,20},{20,16},{24,28},{28,24},{1,5},{5... | collective-permute-start | bytes 442376 | tf_op jit(solution)/shard_map/ppermute | solution.py:413
  69.7 6.6 %collective-permute-start.22 = (bf16[96,768]{1,0:T(8,128)(2,1)S(1)}, bf16[96,768]{1,0:T(8,128)(2,1)S(1)}, u32[]{:S(2)}, u32[]{:S(2)}) collective-permute-start(bf16[96,768]{1,0:T(8,128)(2,1)S(1)} %collective-permute-done.21.rest_4_), channel_id=1, source_target_pairs={{0,4},{4,0},{8,12},{12,8},{16,20},{20,16},{24,28},{28,24},{1,5},{5... | collective-permute-start | bytes 442376 | tf_op jit(solution)/shard_map/ppermute | solution.py:413
  72.8 5.1 %collective-permute-start.24 = (bf16[96,768]{1,0:T(8,128)(2,1)S(1)}, bf16[96,768]{1,0:T(8,128)(2,1)S(1)}, u32[]{:S(2)}, u32[]{:S(2)}) collective-permute-start(bf16[96,768]{1,0:T(8,128)(2,1)S(1)} %collective-permute-done.23.rest_6_), channel_id=1, source_target_pairs={{0,4},{4,0},{8,12},{12,8},{16,20},{20,16},{24,28},{28,24},{1,5},{5... | collective-permute-start | bytes 442376 | tf_op jit(solution)/shard_map/ppermute | solution.py:413
  81.0 1.8 collective-permute-start.27
  82.9 11.2 %collective-permute-start.28 = (bf16[256,768]{1,0:T(8,128)(2,1)S(1)}, bf16[256,768]{1,0:T(8,128)(2,1)S(1)}, u32[]{:S(2)}, u32[]{:S(2)}) collective-permute-start(bf16[256,768]{1,0:T(8,128)(2,1)S(1)} %add.15.own_a), channel_id=1, source_target_pairs={{0,2},{1,3},{2,0},{3,1},{4,6},{5,7},{6,4},{7,5},{8,10},{9,11},{10,... | collective-permute-start | bytes 1179656 | tf_op jit(solution)/shard_map/ppermute | solution.py:416
  83.5 10.7 %collective-permute-start.29 = (bf16[256,768]{1,0:T(8,128)(2,1)S(1)}, bf16[256,768]{1,0:T(8,128)(2,1)S(1)}, u32[]{:S(2)}, u32[]{:S(2)}) collective-permute-start(bf16[256,768]{1,0:T(8,128)(2,1)S(1)} %add.15.own_a), channel_id=1, source_target_pairs={{0,1},{1,0},{2,3},{3,2},{4,5},{5,4},{6,7},{7,6},{8,9},{9,8},{10,11... | collective-permute-start | bytes 1179656 | tf_op jit(solution)/shard_map/ppermute | solution.py:416
  94.1 1.7 collective-permute-start.30
  104.7 8.9 %collective-permute-start.31 = (bf16[256,768]{1,0:T(8,128)(2,1)S(1)}, bf16[256,768]{1,0:T(8,128)(2,1)S(1)}, u32[]{:S(2)}, u32[]{:S(2)}) collective-permute-start(bf16[256,768]{1,0:T(8,128)(2,1)S(1)} %get-tuple-element.129), channel_id=1, source_target_pairs={{0,1},{1,0},{2,3},{3,2},{4,5},{5,4},{6,7},{7,6},{8,9},{9,8},{10,11... | collective-permute-start | bytes 1179656 | tf_op jit(solution)/shard_map/ppermute | solution.py:416
  107.5 26.2 %collective-permute-start.37 = (bf16[4,96,768]{2,1,0:T(8,128)(2,1)}, bf16[4,96,768]{2,1,0:T(8,128)(2,1)}, u32[]{:S(2)}, u32[]{:S(2)}) collective-permute-start(bf16[4,96,768]{2,1,0:T(8,128)(2,1)} %get-tuple-element.140), channel_id=1, source_target_pairs={{0,4},{4,0},{8,12},{12,8},{16,20},{20,16},{24,28},{28,24},{1,5},{5... | collective-permute-start | bytes 1769480 | tf_op jit(solution)/shard_map/ppermute | solution.py:413
  111.6 28.6 %collective-permute-start.41 = (bf16[4,96,768]{2,1,0:T(8,128)(2,1)}, bf16[4,96,768]{2,1,0:T(8,128)(2,1)}, u32[]{:S(2)}, u32[]{:S(2)}) collective-permute-start(bf16[4,96,768]{2,1,0:T(8,128)(2,1)} %get-tuple-element.149), channel_id=1, source_target_pairs={{0,4},{4,0},{8,12},{12,8},{16,20},{20,16},{24,28},{28,24},{1,5},{5... | collective-permute-start | bytes 1769480 | tf_op jit(solution)/shard_map/ppermute | solution.py:413
  112.1 39.0 %collective-permute-start.33 = (bf16[4,96,768]{2,1,0:T(8,128)(2,1)}, bf16[4,96,768]{2,1,0:T(8,128)(2,1)}, u32[]{:S(2)}, u32[]{:S(2)}) collective-permute-start(bf16[4,96,768]{2,1,0:T(8,128)(2,1)} %get-tuple-element.134), channel_id=1, source_target_pairs={{0,4},{4,0},{8,12},{12,8},{16,20},{20,16},{24,28},{28,24},{1,5},{5... | collective-permute-start | bytes 1769480 | tf_op jit(solution)/shard_map/ppermute | solution.py:413
  115.0 6.6 %collective-permute-start.32 = (bf16[128,768]{1,0:T(8,128)(2,1)}, bf16[128,768]{1,0:T(8,128)(2,1)}, u32[]{:S(2)}, u32[]{:S(2)}) collective-permute-start(bf16[128,768]{1,0:T(8,128)(2,1)} %get-tuple-element.131), channel_id=1, source_target_pairs={{0,2},{1,3},{2,0},{3,1},{4,6},{5,7},{6,4},{7,5},{8,10},{9,11},{10,... | collective-permute-start | bytes 589832 | tf_op jit(solution)/shard_map/ppermute | solution.py:416
  118.7 23.0 %collective-permute-start.25 = (bf16[256,768]{1,0:T(8,128)(2,1)}, bf16[256,768]{1,0:T(8,128)(2,1)}, u32[]{:S(2)}, u32[]{:S(2)}) collective-permute-start(bf16[256,768]{1,0:T(8,128)(2,1)} %get-tuple-element.115), channel_id=1, source_target_pairs={{0,1},{1,0},{2,3},{3,2},{4,5},{5,4},{6,7},{7,6},{8,9},{9,8},{10,11... | collective-permute-start | bytes 1179656 | tf_op jit(solution)/shard_map/ppermute | solution.py:416
  126.3 55.3 %all-to-all-start.1 = ((f32[32,16,128]{2,1,0:T(8,128)}), f32[32,16,128]{2,1,0:T(8,128)}, u32[]{:S(2)}, u32[]{:S(2)}) async-start(f32[32,16,128]{2,1,0:T(8,128)} %broadcast_in_dim.14), calls=%async_computation.1 | async-start | bytes 524288 | tf_op jit(solution)/shard_map/all_to_all | solution.py:580
  136.0 22.3 %collective-permute-start.38 = (bf16[96,768]{1,0:T(8,128)(2,1)S(1)}, bf16[96,768]{1,0:T(8,128)(2,1)S(1)}, u32[]{:S(2)}, u32[]{:S(2)}) collective-permute-start(bf16[96,768]{1,0:T(8,128)(2,1)S(1)} %get-tuple-element.142), channel_id=1, source_target_pairs={{0,8},{4,12},{8,0},{12,4},{16,24},{20,28},{24,16},{28,20},{1,9},{5... | collective-permute-start | bytes 442376 | tf_op jit(solution)/shard_map/ppermute | solution.py:413
  137.8 22.6 %collective-permute-start.39 = (bf16[96,768]{1,0:T(8,128)(2,1)S(1)}, bf16[96,768]{1,0:T(8,128)(2,1)S(1)}, u32[]{:S(2)}, u32[]{:S(2)}) collective-permute-start(bf16[96,768]{1,0:T(8,128)(2,1)S(1)} %get-tuple-element.143), channel_id=1, source_target_pairs={{0,16},{4,20},{8,24},{12,28},{16,0},{20,4},{24,8},{28,12},{1,17},{... | collective-permute-start | bytes 442376 | tf_op jit(solution)/shard_map/ppermute | solution.py:413
  140.2 20.1 %collective-permute-start.40 = (bf16[96,768]{1,0:T(8,128)(2,1)S(1)}, bf16[96,768]{1,0:T(8,128)(2,1)S(1)}, u32[]{:S(2)}, u32[]{:S(2)}) collective-permute-start(bf16[96,768]{1,0:T(8,128)(2,1)S(1)} %get-tuple-element.144), channel_id=1, source_target_pairs={{0,24},{4,28},{8,16},{12,20},{16,8},{20,12},{24,0},{28,4},{1,25},{... | collective-permute-start | bytes 442376 | tf_op jit(solution)/shard_map/ppermute | solution.py:413
  141.7 21.1 %collective-permute-start.42 = (bf16[96,768]{1,0:T(8,128)(2,1)S(1)}, bf16[96,768]{1,0:T(8,128)(2,1)S(1)}, u32[]{:S(2)}, u32[]{:S(2)}) collective-permute-start(bf16[96,768]{1,0:T(8,128)(2,1)S(1)} %get-tuple-element.151), channel_id=1, source_target_pairs={{0,8},{4,12},{8,0},{12,4},{16,24},{20,28},{24,16},{28,20},{1,9},{5... | collective-permute-start | bytes 442376 | tf_op jit(solution)/shard_map/ppermute | solution.py:413
  151.1 18.2 %collective-permute-start.43 = (bf16[96,768]{1,0:T(8,128)(2,1)S(1)}, bf16[96,768]{1,0:T(8,128)(2,1)S(1)}, u32[]{:S(2)}, u32[]{:S(2)}) collective-permute-start(bf16[96,768]{1,0:T(8,128)(2,1)S(1)} %get-tuple-element.152), channel_id=1, source_target_pairs={{0,16},{4,20},{8,24},{12,28},{16,0},{20,4},{24,8},{28,12},{1,17},{... | collective-permute-start | bytes 442376 | tf_op jit(solution)/shard_map/ppermute | solution.py:413
  158.3 12.3 %collective-permute-start.44 = (bf16[96,768]{1,0:T(8,128)(2,1)S(1)}, bf16[96,768]{1,0:T(8,128)(2,1)S(1)}, u32[]{:S(2)}, u32[]{:S(2)}) collective-permute-start(bf16[96,768]{1,0:T(8,128)(2,1)S(1)} %get-tuple-element.153), channel_id=1, source_target_pairs={{0,24},{4,28},{8,16},{12,20},{16,8},{20,12},{24,0},{28,4},{1,25},{... | collective-permute-start | bytes 442376 | tf_op jit(solution)/shard_map/ppermute | solution.py:413
  160.3 11.1 %collective-permute-start.34 = (bf16[96,768]{1,0:T(8,128)(2,1)S(1)}, bf16[96,768]{1,0:T(8,128)(2,1)S(1)}, u32[]{:S(2)}, u32[]{:S(2)}) collective-permute-start(bf16[96,768]{1,0:T(8,128)(2,1)S(1)} %get-tuple-element.136), channel_id=1, source_target_pairs={{0,8},{4,12},{8,0},{12,4},{16,24},{20,28},{24,16},{28,20},{1,9},{5... | collective-permute-start | bytes 442376 | tf_op jit(solution)/shard_map/ppermute | solution.py:413
  160.3 20.4 %collective-permute-start.35 = (bf16[96,768]{1,0:T(8,128)(2,1)S(1)}, bf16[96,768]{1,0:T(8,128)(2,1)S(1)}, u32[]{:S(2)}, u32[]{:S(2)}) collective-permute-start(bf16[96,768]{1,0:T(8,128)(2,1)S(1)} %get-tuple-element.137), channel_id=1, source_target_pairs={{0,16},{4,20},{8,24},{12,28},{16,0},{20,4},{24,8},{28,12},{1,17},{... | collective-permute-start | bytes 442376 | tf_op jit(solution)/shard_map/ppermute | solution.py:413
  162.8 17.9 %collective-permute-start.36 = (bf16[96,768]{1,0:T(8,128)(2,1)S(1)}, bf16[96,768]{1,0:T(8,128)(2,1)S(1)}, u32[]{:S(2)}, u32[]{:S(2)}) collective-permute-start(bf16[96,768]{1,0:T(8,128)(2,1)S(1)} %get-tuple-element.138), channel_id=1, source_target_pairs={{0,24},{4,28},{8,16},{12,20},{16,8},{20,12},{24,0},{28,4},{1,25},{... | collective-permute-start | bytes 442376 | tf_op jit(solution)/shard_map/ppermute | solution.py:413
  169.3 17.2 %collective-permute-start.26 = (bf16[128,768]{1,0:T(8,128)(2,1)}, bf16[128,768]{1,0:T(8,128)(2,1)}, u32[]{:S(2)}, u32[]{:S(2)}) collective-permute-start(bf16[128,768]{1,0:T(8,128)(2,1)} %get-tuple-element.117), channel_id=1, source_target_pairs={{0,2},{1,3},{2,0},{3,1},{4,6},{5,7},{6,4},{7,5},{8,10},{9,11},{10,... | collective-permute-start | bytes 589832 | tf_op jit(solution)/shard_map/ppermute | solution.py:416
  182.2 12.3 %all-to-all-start = ((f32[32,8,128]{2,1,0:T(8,128)}), f32[32,8,128]{2,1,0:T(8,128)S(1)}, u32[]{:S(2)}, u32[]{:S(2)}) async-start(f32[32,8,128]{2,1,0:T(8,128)} %copy-done.35), calls=%async_computation | async-start | bytes 262144 | tf_op jit(solution)/shard_map/all_to_all | solution.py:607
  (43 other events, 348.9 us)

commit v2 on v1

v2 whole, which is shorter than its diff:
```python
import functools
import math

import jax
import jax.numpy as jnp
from jax import lax
from jax.experimental import pallas as pl
from jax.experimental.pallas import tpu as pltpu
from jax.sharding import PartitionSpec as P

HEADS = 12
HDIM = 64
BUCKETS = 32
LEN = 512
BLK = 128
WIN = LEN + BLK
SMALL = 16


eps_norm = 1e-06
clip_norm = 1.0
beta_one = 0.9
beta_two = 0.999
adam_eps = 1e-08
decay_rate = 0.01
adam_step = 10.0
mask_fill = -1000000000.0
rate_small = 0.02
rate_large = 0.5
gelu_coef = 0.044715
root_coef = math.sqrt(2.0 / math.pi)

f32 = jnp.float32
bf16 = jnp.bfloat16
sds = jax.ShapeDtypeStruct


def dot_nn(a, b):
    return lax.dot_general(a, b, (((1,), (0,)), ((), ())), preferred_element_type=f32)


def dot_nt(a, b):
    return lax.dot_general(a, b, (((1,), (1,)), ((), ())), preferred_element_type=f32)


def dot_tn(a, b):
    return lax.dot_general(a, b, (((0,), (0,)), ((), ())), preferred_element_type=f32)


def after(value, *deps):
    return lax.optimization_barrier((value, *deps))[0]


def call(body, outs, args, name, hbm=(), scratch=(), limit=16, behind=()):
    spaces = [pl.ANY if i in hbm else pltpu.VMEM for i in range(len(args))]
    args = [after(args[0], *behind), *args[1:]] if behind else args
    args = [
        pltpu.with_memory_space_constraint(a, pltpu.HBM) if i in hbm else a for i, a in enumerate(args)
    ]
    return pl.pallas_call(
        body,
        out_shape=tuple(outs),
        in_specs=[pl.BlockSpec(memory_space=space) for space in spaces],
        out_specs=tuple(
            pl.BlockSpec(memory_space=pl.ANY if hasattr(o, "memory_space") else pltpu.VMEM) for o in outs
        ),
        scratch_shapes=list(scratch),
        compiler_params=pltpu.CompilerParams(vmem_limit_bytes=limit << 20),
        cost_estimate=pl.CostEstimate(flops=0, bytes_accessed=0, transcendentals=0),
        name=name,
    )(*args)


def to_hbm(staged, out, sem):
    copy = pltpu.make_async_copy(staged, out, sem)
    copy.start()
    copy.wait()


def assemble(into, blocks, start_col=0):
    cols = slice(start_col, start_col + into.shape[1])
    if len(blocks) == 1:
        into[...] = blocks[0][:, cols]
        return
    me = lax.axis_index("dp")
    rows = blocks[0].shape[0]
    for e, block in enumerate(blocks):
        start = pl.multiple_of((me ^ e) * rows, 32)
        into[pl.ds(start, rows), :] = block[:, cols]


def spread(grad, outs, order=(1, 2, 4)):
    if len(outs) == 1:
        outs[0][...] = grad[...].astype(bf16)
        return
    me = lax.axis_index("dp")
    rows = outs[0].shape[1]
    keep, high, low = outs
    for b in range(2):
        for k in range(4):
            out, at = ((low, high)[k >> 1], k & 1) if b else (keep, k)
            apart = b * order[0] ^ (k >> 1) * order[1] ^ (k & 1) * order[2]
            start = pl.multiple_of((me ^ apart) * rows, 32)
            out[at] = grad[pl.ds(start, rows), :].astype(bf16)


def spread_shapes(dp, width, cols):
    if dp == 8:
        return [sds((n, width // dp, cols), bf16) for n in (4, 2, 2)]
    return [sds((width, cols), bf16)]


def half_rows():
    core = lax.axis_index("tp") & 1
    for half in range(2):
        for at in range(2):
            start = pl.multiple_of(((core ^ half) + 2 * at) * BLK, BLK)
            yield half, at, pl.ds(start, BLK)


def pack_kernel(qkv, out, down, ffn_in, packed, packed_ffn, *scratch):
    *landed, sems = scratch
    copies = [
        pltpu.make_async_copy(source, to, sems.at[i])
        for i, (source, to) in enumerate(zip((qkv, out, down, ffn_in), landed))
    ]
    for copy in copies:
        copy.start()
    local = out.shape[1]
    copies[0].wait()
    copies[1].wait()
    for part in range(3):
        packed[:, part * local : (part + 1) * local] = landed[0][part].astype(bf16)
    packed[:, 3 * local :] = landed[1][...].astype(bf16)
    width = down.shape[1]
    for i in (2, 3):
        copies[i].wait()
        packed_ffn[:, (i - 2) * width : (i - 1) * width] = landed[i][...].astype(bf16)


def prep_kernel(
    seg_in, table_in, bucket_in, x_in, gains_in, dy_in, act, act_t, bias, bucket, x, gains, dy, seg, table, ids, sems
):
    sources = (x_in, gains_in, bucket_in, seg_in, table_in, dy_in)
    copies = [
        pltpu.make_async_copy(source, to, sems.at[i])
        for i, (source, to) in enumerate(zip(sources, (x, gains, ids, seg, table, dy)))
    ]
    for copy in copies:
        copy.start()
    copies[0].wait()
    copies[1].wait()
    values = x[...].astype(f32)
    scale = lax.rsqrt(jnp.mean(values * values, axis=-1, keepdims=True) + eps_norm)
    low = (values * scale * gains[0:1, :]).astype(bf16)
    act[...] = low
    act_t[...] = low.T
    for copy in copies[2:]:
        copy.wait()
    ends = [seg[0, 0]]
    for k in (1, 2):
        ends.append(ends[-1] + seg[0, k])

    def segment_of(position):
        return sum((position >= end).astype(jnp.int32) for end in ends)

    seg_cols = segment_of(lax.broadcasted_iota(jnp.int32, (1, LEN), 1))
    heads = bias.shape[0]
    bucket[...] = jnp.zeros_like(bucket)
    bucket[:, : 2 * LEN - 1] = ids[...]
    lines = []
    for h in range(heads):
        line = jnp.zeros((1, 2 * LEN), f32)
        for b in range(BUCKETS):
            line = jnp.where(bucket[...] == b, table[h, b], line)
        lines.append(line)
    for r in range(LEN // BLK):
        seg_rows = segment_of(lax.broadcasted_iota(jnp.int32, (BLK, 1), 0) + r * BLK)
        visible = seg_rows == seg_cols
        low_at = LEN - BLK - r * BLK
        for h in range(heads):
            window = jnp.broadcast_to(lines[h][:, low_at : low_at + WIN], (BLK, WIN))
            turned = pltpu.roll(window, 1, 1, stride=1, stride_axis=0)
            bias[h, r * BLK : (r + 1) * BLK, :] = jnp.where(visible, turned[:, BLK:], mask_fill)


def attend_kernel(n_blocks, act, bias, *rest):
    blocks = rest[:n_blocks]
    weights, qkv, prob, mixed, keep, send = rest[n_blocks:]
    assemble(weights, blocks)
    width = qkv.shape[1] // 3
    qkv[...] = dot_nn(act[...], weights[:, : 3 * width]).astype(bf16)
    for h in range(bias.shape[0]):
        cols = slice(h * HDIM, (h + 1) * HDIM)
        query, key, value = (qkv[:, s * width + h * HDIM : s * width + (h + 1) * HDIM] for s in range(3))
        scores = dot_nt(query, key) + bias[h]
        top = jnp.max(scores, axis=-1, keepdims=True)
        exps = jnp.exp(scores - top)
        total = jnp.sum(exps, axis=-1, keepdims=True)
        low = (exps * (1.0 / total)).astype(bf16)
        prob[h] = low
        mixed[:, cols] = dot_nn(low, value).astype(bf16)
    out_cols = weights[:, 3 * width :]
    for half, at, rows in half_rows():
        to = send if half else keep
        to[at * BLK : (at + 1) * BLK, :] = dot_nt(mixed[rows, :], out_cols).astype(bf16)


def ffn_kernel(n_blocks, x, gains, dy, own, other, *rest):
    blocks = rest[:n_blocks]
    resid, act, hidden, pre_grad, keep, send, down, weights, hidden_grad = rest[n_blocks:]
    assemble(down, blocks)
    assemble(weights, blocks, down.shape[1])
    hidden_grad[...] = dot_nn(dy[...], down[...])
    for half, at, rows in half_rows():
        here = slice(at * BLK, (at + 1) * BLK)
        values = x[rows, :].astype(f32) + (other if half else own)[here, :].astype(f32)
        resid[rows, :] = values
        scale = lax.rsqrt(jnp.mean(values * values, axis=-1, keepdims=True) + eps_norm)
        low = (values * scale * gains[1:2, :]).astype(bf16)
        act[rows, :] = low
        u = dot_nn(low, weights[...])
        square = u * u
        tanh_part = jnp.tanh(root_coef * (u + gelu_coef * square * u))
        hidden[rows, :] = (0.5 * u * (1.0 + tanh_part)).astype(bf16)
        inner = root_coef * (1.0 + 3.0 * gelu_coef * square)
        slope = 0.5 * (1.0 + tanh_part) + 0.5 * u * (1.0 - tanh_part * tanh_part) * inner
        du = (hidden_grad[rows, :] * slope).astype(bf16)
        pre_grad[rows, :] = du
        (send if half else keep)[here, :] = dot_nt(du, weights[...]).astype(bf16)


def weight_grad_kernel(order, left, right, *rest):
    outs, grad = rest[:-1], rest[-1]
    grad[...] = dot_tn(left[...], right[...])
    spread(grad, outs, order)


def ffn_out_kernel(hidden, weights, keep, send):
    for half, at, rows in half_rows():
        to = send if half else keep
        to[at * BLK : (at + 1) * BLK, :] = dot_nt(hidden[rows, :], weights[...]).astype(bf16)


def attend_back_kernel(
    n_outs, resid, dy, gains, own, other, weights, qkv, prob, mixed, act_t, *rest
):
    outs = rest[:n_outs]
    share_grad, gain_part, score_grad, proj_grad, resid_low, grad = rest[n_outs:]
    chip = lax.axis_index("tp") >> 1
    width = qkv.shape[1] // 3
    for half, at, rows in half_rows():
        here = slice(at * BLK, (at + 1) * BLK)
        act_grad = (other if half else own)[here, :].astype(f32)
        values = resid[rows, :]
        scale = lax.rsqrt(jnp.mean(values * values, axis=-1, keepdims=True) + eps_norm)
        normed = values * scale
        normal_grad = act_grad * gains[1:2, :]
        mean_part = jnp.mean(normal_grad * normed, axis=-1, keepdims=True)
        total = dy[rows, :].astype(f32) + scale * (normal_grad - normed * mean_part)
        resid_low[rows, :] = total.astype(bf16)
        if half == 0:

            @pl.when(chip == at)
            def _():
                share_grad[...] = total
                gain_part[...] = jnp.sum(act_grad * normed, axis=0, keepdims=True)

    mix_grad = dot_nn(resid_low[...], weights[:, 3 * width :]).astype(bf16)
    for h in range(prob.shape[0]):
        query, key, value = (qkv[:, s * width + h * HDIM : s * width + (h + 1) * HDIM] for s in range(3))
        grad_rows = mix_grad[:, h * HDIM : (h + 1) * HDIM]
        prob_grad = dot_nt(grad_rows, value)
        prob_here = prob[h].astype(f32)
        row_dot = jnp.sum(prob_here * prob_grad, axis=-1, keepdims=True)
        low = (prob_here * (prob_grad - row_dot)).astype(bf16)
        score_grad[h] = low
        for s, part in enumerate((dot_nn(low, key), dot_tn(low, query), dot_tn(prob[h], grad_rows))):
            proj_grad[:, s * width + h * HDIM : s * width + (h + 1) * HDIM] = part.astype(bf16)
    grad[:, : 3 * width] = dot_nn(act_t[...], proj_grad[...])
    grad[:, 3 * width :] = dot_tn(resid_low[...], mixed[...])
    spread(grad, outs)


def tail_kernel(score_grad, proj_grad, weights, bucket, x, gain_two, *rest):
    *high, keep, send, small, diag = rest
    width = proj_grad.shape[1]
    gain_one = jnp.zeros(gain_two.shape, f32)
    for half, at, rows in half_rows():
        to = send if half else keep
        act_grad = dot_nt(proj_grad[rows, :], weights[:, :width])
        to[at * BLK : (at + 1) * BLK, :] = act_grad.astype(bf16)
        values = x[rows, :].astype(f32)
        scale = lax.rsqrt(jnp.mean(values * values, axis=-1, keepdims=True) + eps_norm)
        gain_one = gain_one + jnp.sum(act_grad * (values * scale), axis=0, keepdims=True)
    row = lax.broadcasted_iota(jnp.int32, (BLK, BLK), 0)
    col = lax.broadcasted_iota(jnp.int32, (BLK, BLK), 1)
    flip = (row + col == BLK - 1).astype(f32).astype(bf16)
    onehot = (lax.broadcasted_iota(jnp.int32, (BUCKETS, 2 * LEN), 0) == bucket[...]).astype(f32)
    diag[...] = jnp.zeros_like(diag)
    heads = score_grad.shape[0]
    for h in range(heads):
        for r in range(LEN // BLK):
            flipped = dot_nn(flip, score_grad[h, r * BLK : (r + 1) * BLK, :])
            wide = jnp.concatenate([flipped, jnp.zeros((BLK, BLK), f32)], axis=1)
            turned = pltpu.roll(wide, 0, 1, stride=1, stride_axis=0)
            low_at = LEN - BLK - r * BLK
            diag[h : h + 1, low_at : low_at + WIN] += jnp.sum(turned, axis=0, keepdims=True)
    by_bucket = lax.dot_general(
        diag[...],
        onehot,
        (((1,), (1,)), ((), ())),
        precision=lax.Precision.HIGHEST,
        preferred_element_type=f32,
    )
    first = lax.axis_index("tp") * heads
    cells = [
        sum(jnp.where(first + h == head, by_bucket[h : h + 1, :], 0.0) for h in range(heads))
        for head in range(HEADS)
    ]
    cells.append(jnp.zeros((1, gain_one.shape[1] - HEADS * BUCKETS), f32))
    lines = (gain_one, gain_two[...], jnp.concatenate(cells, axis=1))
    whole = jnp.concatenate((*lines, jnp.zeros((SMALL - 3, gain_one.shape[1]), f32)), axis=0)
    if high:
        rows = high[0].shape[1]
        small[:rows, :] = high[0][0]
        small[rows : 2 * rows, :] = high[0][1]
        small[2 * rows :, :] = whole.astype(bf16)
    else:
        small[...] = whole


def core_add_kernel(keep, got, mine, theirs):
    chip = lax.axis_index("tp") >> 1
    for to, index in ((mine, chip), (theirs, 1 - chip)):
        rows = pl.ds(pl.multiple_of(index * BLK, BLK), BLK)
        to[...] = (keep[rows, :].astype(f32) + got[rows, :].astype(f32)).astype(bf16)


def share_ds():
    return pl.ds(pl.multiple_of(lax.axis_index("tp") * BLK, BLK), BLK)


def block_out_kernel(resid, mine, got, out):
    out[...] = (resid[share_ds(), :] + (mine[...].astype(f32) + got[...].astype(f32))).astype(bf16)


def input_grad_kernel(x, gains, share_grad, mine, got, out):
    values = x[share_ds(), :].astype(f32)
    scale = lax.rsqrt(jnp.mean(values * values, axis=-1, keepdims=True) + eps_norm)
    normed = values * scale
    normal_grad = (mine[...].astype(f32) + got[...].astype(f32)) * gains[0:1, :]
    mean_part = jnp.mean(normal_grad * normed, axis=-1, keepdims=True)
    out[...] = share_grad[...] + scale * (normal_grad - normed * mean_part)


def add_kernel(one, two, out):
    out[...] = (one[...].astype(f32) + two[...].astype(f32)).astype(bf16)


def high_add_kernel(keep, got, theirs):
    for k in range(2):
        theirs[k] = (keep[k + 2].astype(f32) + got[k].astype(f32)).astype(bf16)


def last_high_kernel(keep, sent, got, out, out_small):
    rows = keep.shape[1]
    out[...] = (keep[2].astype(f32) + got[:rows, :].astype(f32)).astype(bf16)
    out_small[:rows, :] = (keep[3].astype(f32) + got[rows : 2 * rows, :].astype(f32)).astype(bf16)
    small = slice(2 * rows, None)
    out_small[rows:, :] = (sent[small, :].astype(f32) + got[small, :].astype(f32)).astype(bf16)


def last_late_kernel(keep, got_low, sent, got, out):
    rows = keep.shape[1]
    block = keep[1].astype(f32) + got_low[1].astype(f32) + got[:rows, :].astype(f32)
    out[:rows, :] = block.astype(bf16)
    out[rows:, :] = (sent[rows:, :].astype(f32) + got[rows:, :].astype(f32)).astype(bf16)


def late_add_kernel(keep, got_low, got, mine, theirs):
    for k, to in enumerate((mine, theirs)):
        to[...] = (keep[k].astype(f32) + got_low[k].astype(f32) + got[k].astype(f32)).astype(bf16)


def fold(values):
    rows, cols = values.shape
    squares = values * values
    lanes = sum(squares[:, c : c + BLK] for c in range(0, cols, BLK))
    return jnp.sum(lanes, axis=0, keepdims=True)


def sum_kernel(n_parts, *rest):
    parts, (grad, squares) = rest[:n_parts], rest[n_parts:]
    total = sum(part[...].astype(f32) for part in parts)
    grad[...] = total
    squares[...] = fold(total)


def last_sum_kernel(direct, extra_a, extra_b, *rest):
    *parts, grad, out, payload, lines, sem = rest
    if direct:
        keep, got_low, got_block, sent, got = parts
        rows = keep.shape[1]
        total = keep[0].astype(f32) + got_low[0].astype(f32)
        total = total + (got_block[...].astype(f32) + got[:rows, :].astype(f32))
        small = sent[rows:, :].astype(f32) + got[rows:, :].astype(f32)
    else:
        total, small = (part[...] for part in parts)
    grad[...] = total
    per_row = total.shape[1] // BLK
    lines[...] = jnp.zeros_like(lines)
    for line in range(SMALL):
        row, at = divmod(line, per_row)
        lines[line : line + 1, :] = small[row : row + 1, at * BLK : (at + 1) * BLK]
    me = lax.axis_index("dp")
    start = pl.multiple_of(jnp.minimum(2 * me, SMALL), 2)
    squares = fold(total) + extra_a[...] + extra_b[...]
    told = jnp.concatenate((squares, lines[pl.ds(start, 2), :], jnp.zeros((5, BLK), f32)), axis=0)
    payload[...] = jnp.broadcast_to(told[None], payload.shape)
    to_hbm(payload, out, sem)


def adamw(weight, gradient, moment_one, moment_two, rate):
    one_new = beta_one * moment_one + (1.0 - beta_one) * gradient
    two_new = beta_two * moment_two + (1.0 - beta_two) * gradient * gradient
    one_hat = one_new / (1.0 - beta_one**adam_step)
    two_hat = two_new / (1.0 - beta_two**adam_step)
    weight_new = weight - rate * (one_hat / (jnp.sqrt(two_hat) + adam_eps) + decay_rate * weight)
    return (weight_new, one_new, two_new)


def adam_kernel(*refs):
    told, grad_qkvo, grad_in, grad_down, *state = refs[:22]
    outs = refs[22:46]
    *landed, gains_sum, table_grad, sems = refs[46:]
    copies = [pltpu.make_async_copy(state[i], landed[i], sems.at[i]) for i in range(12)]
    for copy in copies:
        copy.start()
    qkv, out, ffn_in, ffn_down = (landed[i : i + 3] for i in range(0, 12, 3))
    gains, table = state[12:15], state[15:18]
    norm_ref, qkv_o, out_o, in_o, down_o, gains_o, gains_grad, table_o = (
        outs[0],
        outs[1:5],
        outs[5:9],
        outs[9:13],
        outs[13:17],
        outs[17:20],
        outs[20],
        outs[21:24],
    )
    tp = lax.axis_size("tp")
    squares = told[0, 0:1, :]
    for i in range(1, told.shape[0]):
        squares = squares + told[i, 0:1, :]
    model = gains_sum.shape[1]
    per_row = model // BLK
    per_line = BLK // BUCKETS
    first = lax.axis_index("tp") * table_grad.shape[0]
    for line in range(2 * per_row + HEADS // per_line):
        index, at = divmod(line, 2)
        value = told[index * tp, at + 1 : at + 2, :]
        for i in range(1, tp):
            value = value + told[index * tp + i, at + 1 : at + 2, :]
        squares = squares + value * value
        row, at = divmod(line, per_row)
        if row < 2:
            gains_sum[row : row + 1, at * BLK : (at + 1) * BLK] = value
            continue
        for i in range(per_line):
            head = at * per_line + i
            cell = value[:, i * BUCKETS : (i + 1) * BUCKETS]
            for h in range(table_grad.shape[0]):

                @pl.when(first + h == head)
                def _():
                    table_grad[h : h + 1, :] = cell

    norm = jnp.sqrt(jnp.sum(squares, axis=1, keepdims=True))
    norm_ref[...] = norm
    factor = clip_norm / jnp.maximum(norm, clip_norm)

    def update(state_refs, gradient, to, rate, at=...):
        new = adamw(state_refs[0][at], gradient * factor, state_refs[1][at], state_refs[2][at], rate)
        for ref, value in zip(to, new):
            ref[at] = value
        if len(to) == 4:
            to[3][at] = new[0].astype(bf16)

    update(gains, gains_sum[...], gains_o, rate_large)
    gains_grad[...] = gains_sum[...] * factor
    update(table, table_grad[...], table_o, rate_large)
    width = qkv[0].shape[2]
    for copy in copies[:3]:
        copy.wait()
    for part in range(3):
        update(qkv, grad_qkvo[:, part * width : (part + 1) * width], qkv_o, rate_small, part)
    for copy in copies[3:6]:
        copy.wait()
    update(out, grad_qkvo[:, 3 * width :], out_o, rate_large)
    for copy in copies[6:9]:
        copy.wait()
    update(ffn_in, grad_in[...], in_o, rate_small)
    for copy in copies[9:]:
        copy.wait()
    update(ffn_down, grad_down[...], down_o, rate_small)


def on_device(
    dp,
    inputs,
    cotangent,
    seg_lengths,
    bucket_ids,
    qkv_weight,
    qkv_first,
    qkv_second,
    out_weight,
    out_first,
    out_second,
    ffn_in_weight,
    ffn_in_first,
    ffn_in_second,
    ffn_down_weight,
    ffn_down_first,
    ffn_down_second,
    norm_gains,
    gains_first,
    gains_second,
    bias_table,
    table_first,
    table_second,
):
    tokens, model = inputs.shape
    rows, local = out_weight.shape
    hidden = ffn_in_weight.shape[1]
    heads_here = local // HDIM
    tp = lax.axis_size("tp")
    packed_cols = 4 * local
    direct = dp == 8

    def swap_dp(value, distance):
        return lax.ppermute(value, "dp", [(i, i ^ distance) for i in range(dp)])

    def swap_tp(value, distance):
        return lax.ppermute(value, "tp", [(i, i ^ distance) for i in range(tp)])

    def add(one, two, behind=()):
        (out,) = call(add_kernel, [sds(one.shape, bf16)], (one, two), "add", limit=4, behind=behind)
        return out

    def high_add(keep, got, behind):
        (out,) = call(
            high_add_kernel,
            [sds((2, *keep.shape[1:]), bf16)],
            (keep, got),
            "high_add",
            limit=4,
            behind=behind,
        )
        return out

    def late_add(keep, got_low, got, behind):
        return call(
            late_add_kernel,
            [sds(keep.shape[1:], bf16)] * 2,
            (keep, got_low, got),
            "late_add",
            limit=4,
            behind=behind,
        )

    half_shape = [sds((tokens // 2, model), bf16)] * 2
    matrices = (qkv_weight, out_weight, ffn_down_weight, ffn_in_weight)
    packed, packed_ffn = call(
        pack_kernel,
        [sds((rows, packed_cols), bf16), sds((rows, 2 * hidden), bf16)],
        matrices,
        "pack",
        hbm=(0, 1, 2, 3),
        scratch=[*(pltpu.VMEM(m.shape, f32) for m in matrices), pltpu.SemaphoreType.DMA((4,))],
    )
    ids = bucket_ids[None, :]
    act_one, act_one_t, bias, bucket_row, inputs, norm_gains_here, cotangent = call(
        prep_kernel,
        [
            sds((tokens, model), bf16),
            sds((model, tokens), bf16),
            sds((heads_here, LEN, LEN), f32),
            sds((1, 2 * LEN), jnp.int32),
            sds(inputs.shape, bf16),
            sds(norm_gains.shape, f32),
            sds(inputs.shape, bf16),
        ],
        (seg_lengths, bias_table.T, ids, inputs, norm_gains, cotangent),
        "prep",
        hbm=range(6),
        scratch=[
            pltpu.SMEM(seg_lengths.shape, jnp.int32),
            pltpu.SMEM((heads_here, BUCKETS), f32),
            pltpu.VMEM(ids.shape, jnp.int32),
            pltpu.SemaphoreType.DMA((6,)),
        ],
    )
    if direct:
        one, two, own = swap_dp(packed, 2), swap_dp(packed, 4), swap_dp(packed, 1)
        ffn_own = swap_dp(packed_ffn, 1)
        one_across = swap_dp(after(one, act_one, ffn_own), 1)
        three = swap_dp(after(two, one, own), 2)
        ffn_two = swap_dp(after(packed_ffn, two, one), 4)
        two_across = swap_dp(two, 1)
        ffn_one = swap_dp(after(packed_ffn, two, one), 2)
        three_across = swap_dp(after(three, one_across), 1)
        qkvo_blocks = [packed, own, one, one_across, two, two_across, three, three_across]
        ffn_three = swap_dp(ffn_two, 2)
        ffn_blocks = [packed_ffn, ffn_own]
        for block in (ffn_one, ffn_two, ffn_three):
            ffn_blocks += [block, swap_dp(block, 1)]
        bias = after(bias, ffn_one, ffn_two)
        ffn_early = (ffn_blocks[3], ffn_blocks[5], ffn_three)
    else:
        qkvo_blocks = [lax.all_gather(packed, "dp", axis=0, tiled=True)]
        ffn_blocks = ffn_early = [lax.all_gather(packed_ffn, "dp", axis=0, tiled=True)]
    n_blocks = len(qkvo_blocks)

    weights_one, qkv, prob, mixed, attn_keep, attn_send = call(
        functools.partial(attend_kernel, n_blocks),
        [
            sds((model, packed_cols), bf16),
            sds((tokens, 3 * local), bf16),
            sds((heads_here, LEN, LEN), bf16),
            sds((tokens, local), bf16),
            *half_shape,
        ],
        (act_one, bias, *qkvo_blocks),
        "attend",
    )
    attn_first = add(attn_keep, swap_tp(attn_send, 1))
    attn_sum = add(attn_first, swap_tp(attn_first, 2), ffn_early)
    resid, act_two, hidden_act, pre_grad, back_keep, back_send, down_full = call(
        functools.partial(ffn_kernel, n_blocks),
        [
            sds((tokens, model), f32),
            sds((tokens, model), bf16),
            sds((tokens, hidden), bf16),
            sds((tokens, hidden), bf16),
            *half_shape,
            sds((model, hidden), bf16),
        ],
        (inputs, norm_gains_here, cotangent, attn_sum, swap_tp(attn_sum, 1), *ffn_blocks),
        "ffn",
        scratch=[pltpu.VMEM((model, hidden), bf16), pltpu.VMEM((tokens, hidden), f32)],
    )
    back_first = add(back_keep, swap_tp(back_send, 1))
    back_got = swap_tp(back_first, 2)
    down_order, in_order = (1, 2, 4), (2, 4, 1)
    grad_scratch = [pltpu.VMEM((model, hidden), f32)]
    down_parts = call(
        functools.partial(weight_grad_kernel, down_order),
        spread_shapes(dp, model, hidden),
        (cotangent, after(hidden_act, back_first)),
        "down_grad",
        scratch=grad_scratch,
    )
    in_parts = call(
        functools.partial(weight_grad_kernel, in_order),
        spread_shapes(dp, model, hidden),
        (act_two, after(pre_grad, down_parts[0])),
        "in_grad",
        scratch=grad_scratch,
    )
    if direct:
        down_keep, down_high, down_low = down_parts
        in_keep, in_high, in_low = in_parts
        down_got, in_got = swap_dp(down_high, down_order[0]), swap_dp(in_high, in_order[0])
        back_sum = add(back_first, back_got, (down_got, in_got))
        down_one = high_add(down_keep, down_got, (back_sum,))
        in_one = high_add(in_keep, in_got, (down_one,))
        back_behind = (in_one,)
    else:
        back_sum = add(back_first, back_got, in_parts)
        back_behind = (back_sum,)
    qkvo_shapes = spread_shapes(dp, model, packed_cols)
    *qkvo_parts, share_grad, gain_two_part, score_grad, proj_grad = call(
        functools.partial(attend_back_kernel, len(qkvo_shapes)),
        [
            *qkvo_shapes,
            sds((BLK, model), f32),
            sds((1, model), f32),
            sds((heads_here, LEN, LEN), bf16),
            sds((tokens, 3 * local), bf16),
        ],
        (
            resid,
            cotangent,
            norm_gains_here,
            back_sum,
            swap_tp(back_sum, 1),
            weights_one,
            qkv,
            prob,
            mixed,
            act_one_t,
        ),
        "attend_back",
        scratch=[pltpu.VMEM((tokens, model), bf16), pltpu.VMEM((model, packed_cols), f32)],
        behind=back_behind,
    )
    everyone = dp * tp
    share_shape = [sds((BLK, model), bf16)] * 2
    small_rows = 2 * rows + SMALL if direct else SMALL
    act_keep, act_send, small = call(
        tail_kernel,
        [*half_shape, sds((small_rows, model), bf16 if direct else f32)],
        (score_grad, proj_grad, weights_one, bucket_row, inputs, gain_two_part, *qkvo_parts[1:2]),
        "tail",
        scratch=[pltpu.VMEM((8, 2 * LEN), f32)],
    )
    if direct:
        keep, _, send_low = qkvo_parts
        single = sds((rows, packed_cols), bf16)
        longer = sds((rows + SMALL, packed_cols), bf16)
        got_high, got_low = swap_dp(small, 1), swap_dp(send_low, 1)
        down_two = late_add(
            down_keep, swap_dp(down_low, down_order[0]), swap_dp(down_one, down_order[1]), (act_keep,)
        )
        high, high_small = call(
            last_high_kernel, [single, longer], (keep, small, got_high), "last_high", behind=down_two
        )
        got_block, got_small = swap_dp(high, 2), swap_dp(high_small, 2)
        in_two = late_add(in_keep, swap_dp(in_low, in_order[0]), swap_dp(in_one, in_order[1]), (high,))
        ffn_behind = in_two
    else:
        ffn_behind = (small,)
    ffn_keep, ffn_send = call(
        ffn_out_kernel, half_shape, (hidden_act, down_full), "ffn_out", behind=ffn_behind
    )
    if direct:
        (late,) = call(
            last_late_kernel, [longer], (keep, got_low, high_small, got_small), "last_late", behind=(ffn_keep,)
        )
        last_parts = (keep, got_low, got_block, late, swap_dp(late, 4))
        down_sums = (down_two[0], swap_dp(down_two[1], down_order[2]))
        in_sums = (in_two[0], swap_dp(in_two[1], in_order[2]))
        share_behind = (late,)
    else:
        qkvo_sums, down_sums, in_sums = (
            (lax.psum_scatter(p[0].astype(f32), "dp", scatter_dimension=0, tiled=True),)
            for p in (qkvo_parts, down_parts, in_parts)
        )
        last_parts = (*qkvo_sums, lax.psum(small, "dp"))
        share_behind = (ffn_keep,)
    ffn_mine, ffn_theirs = call(
        core_add_kernel, share_shape, (ffn_keep, swap_tp(ffn_send, 1)), "core_add", behind=share_behind
    )
    act_mine, act_theirs = call(
        core_add_kernel, share_shape, (act_keep, swap_tp(act_send, 1)), "core_add", behind=(ffn_mine,)
    )

    def summed(parts, behind):
        return call(
            functools.partial(sum_kernel, len(parts)),
            [sds((rows, parts[0].shape[1]), f32), sds((1, BLK), f32)],
            parts,
            "sum_parts",
            behind=behind,
        )

    down_grad, down_squares = summed(down_sums, (act_mine,))
    (block_out,) = call(
        block_out_kernel,
        [sds((BLK, model), bf16)],
        (resid, ffn_mine, swap_tp(ffn_theirs, 2)),
        "block_out",
        behind=(down_grad,),
    )
    (input_grad,) = call(
        input_grad_kernel,
        [sds((BLK, model), f32)],
        (inputs, norm_gains_here, share_grad, act_mine, swap_tp(act_theirs, 2)),
        "input_grad",
        behind=(block_out,),
    )
    in_grad, in_squares = summed(in_sums, (input_grad,))
    qkvo_grad, payload = call(
        functools.partial(last_sum_kernel, direct),
        [sds((rows, packed_cols), f32), pltpu.HBM((everyone, 8, BLK), f32)],
        (down_squares, in_squares, *last_parts),
        "last_sum",
        scratch=[
            pltpu.VMEM((everyone, 8, BLK), f32),
            pltpu.VMEM((SMALL + 8, BLK), f32),
            pltpu.SemaphoreType.DMA,
        ],
        behind=(in_grad,),
    )
    told = lax.all_to_all(payload, ("dp", "tp"), 0, 0)
    matrix = [sds((rows, hidden), f32)] * 3 + [sds((rows, hidden), bf16)]
    state = (
        qkv_weight,
        qkv_first,
        qkv_second,
        out_weight,
        out_first,
        out_second,
        ffn_in_weight,
        ffn_in_first,
        ffn_in_second,
        ffn_down_weight,
        ffn_down_first,
        ffn_down_second,
        norm_gains,
        gains_first,
        gains_second,
        bias_table.T,
        table_first.T,
        table_second.T,
    )
    norm, *updated = call(
        adam_kernel,
        [
            sds((1, 1), f32),
            *[sds(qkv_weight.shape, f32)] * 3,
            sds(qkv_weight.shape, bf16),
            *[sds(out_weight.shape, f32)] * 3,
            sds(out_weight.shape, bf16),
            *matrix,
            *matrix,
            *[sds(norm_gains.shape, f32)] * 4,
            *[sds((heads_here, BUCKETS), f32)] * 3,
        ],
        (
            told,
            qkvo_grad,
            in_grad,
            down_grad,
            *state,
        ),
        "adam",
        hbm=range(4, 16),
        scratch=[
            *(pltpu.VMEM(m.shape, f32) for m in state[:12]),
            pltpu.VMEM(norm_gains.shape, f32),
            pltpu.VMEM((heads_here, BUCKETS), f32),
            pltpu.SemaphoreType.DMA((12,)),
        ],
    )
    return (block_out, input_grad, norm.reshape(()), *updated[:-3], *(t.T for t in updated[-3:]))


def solution(mesh):
    row = P("dp", None)
    matrix = P("dp", "tp")
    stack = P(None, "dp", "tp")
    table = P(None, "tp")
    share = P(("dp", "tp"), None)
    in_specs = (
        *(row,) * 3,
        P(),
        *(stack,) * 3,
        *(matrix,) * 9,
        *(P(),) * 3,
        *(table,) * 3,
    )
    out_specs = (
        *(share,) * 2,
        P(),
        *(stack,) * 4,
        *(matrix,) * 12,
        *(P(),) * 4,
        *(table,) * 3,
    )
    return jax.shard_map(
        functools.partial(on_device, mesh.shape["dp"]),
        mesh=mesh,
        in_specs=in_specs,
        out_specs=out_specs,
        check_vma=False,
    )
```

time: 209 us -> 161 us (0.77)
  starting transfers between devices: 69.4 us -> 37.1 us
  local copies, waits for them, and re-layouts: 29.1 us -> 0.03 us
  blocking collectives: 0 us -> 12.8 us
  waiting for transfers between devices: 70.8 us -> 80.6 us
  Pallas kernels: 35.9 us -> 29.1 us
    unnamed x94 -> x12, local copies, waits for them, and re-layouts: 24.7 us -> 0.03 us
    ppermute x33 -> x27, waiting for transfers between devices: 49.6 us -> 73.2 us  [swap_dp(): return lax.ppermute(value, 'dp', [(i, i ^ distance) for i in range(dp)])]
    ppermute x33 -> x27, starting transfers between devices: 54 us -> 31.9 us  [swap_dp(): return lax.ppermute(value, 'dp', [(i, i ^ distance) for i in range(dp)])]
    all_to_all x0 -> x1, blocking collectives: none -> 12.8 us  [on_device(): told = lax.all_to_all(payload, ('dp', 'tp'), 0, 0)]
    all_to_all x2 -> x0, starting transfers between devices: 11.4 us -> none  [the longest x1 7.4 us: on_device(): lax.all_to_all(jnp.broadcast_to(small[None], (everyone, 16, BLK)), ('dp',...]
    ppermute x12 -> x10, waiting for transfers between devices: 16 us -> 7.41 us  [swap_tp(): return lax.ppermute(value, 'tp', [(i, i ^ distance) for i in range(tp)])]
    pallas_call x21 -> x27, Pallas kernels: 35.9 us -> 29.1 us  [call(): pl.pallas_call(body, out_shape=tuple(outs), in_specs=[pl.BlockSpec(memory...]
    all_to_all x2 -> x0, waiting for transfers between devices: 5.19 us -> none  [the longest x1 5.18 us: on_device(): squares = lax.all_to_all(payload, ('dp', 'tp'), 0, 0)]
  transfers between devices with their start and end apart: 47 -> 37, of which waited for: 18 -> 21; matrix products, arithmetic and copies ran while one was open for 3% -> 0% of each run, Pallas kernels for 9% -> 4%
where the time goes in v2:
time: 161 us
  waiting for transfers between devices  80.6 us (50%)
  starting transfers between devices  37.1 us (23%)
  Pallas kernels  29.1 us (18%)
  blocking collectives  12.8 us (8%)
    ppermute x27, waiting for transfers between devices, swap_dp(): return lax.ppermute(value, 'dp', [(i, i ^ distance) for i in range(dp)])  73.2 us
    ppermute x27, starting transfers between devices, swap_dp(): return lax.ppermute(value, 'dp', [(i, i ^ distance) for i in range(dp)])  31.9 us
    pallas_call x27, Pallas kernels, call(): pl.pallas_call(body, out_shape=tuple(outs), in_specs=[pl.BlockSpec(memory...  29.1 us
    all_to_all x1, blocking collectives, on_device(): told = lax.all_to_all(payload, ('dp', 'tp'), 0, 0)  12.8 us
    ppermute x10, waiting for transfers between devices, swap_tp(): return lax.ppermute(value, 'tp', [(i, i ^ distance) for i in range(tp)])  7.41 us
    ppermute x10, starting transfers between devices, swap_tp(): return lax.ppermute(value, 'tp', [(i, i ^ distance) for i in range(tp)])  5.18 us
  transfers between devices with their start and end apart: 37, of which 21 were waited for; matrix products, arithmetic and copies ran while one was open for 0% of the time, Pallas kernels for 4%

profile of v2, /device:TPU:0, one launch (start us, length us, event | category | flops | bytes accessed | tf_op | source)
XLA Modules:
  0.0 160.7 jit_solution(1056589106105081558)
XLA Ops:
  0.7 1.2 pack.1
  1.9 3.0 %collective-permute-start.5 = (bf16[96,1536]{1,0:T(8,128)(2,1)S(1)}, bf16[96,1536]{1,0:T(8,128)(2,1)S(1)}, u32[]{:S(2)}, u32[]{:S(2)}) collective-permute-start(bf16[96,1536]{1,0:T(8,128)(2,1)S(1)} %get-tuple-element.137.rest_0_), channel_id=1, source_target_pairs={{0,4},{4,0},{8,12},{12,8},{16,20},{20,16},{24,28},{28,24},{1,5},{5... | collective-permute-start | bytes 884744 | tf_op jit(solution)/shard_map/ppermute | solution.py:543
  4.9 1.6 collective-permute-start.1
  6.5 2.6 %collective-permute-start = (bf16[96,768]{1,0:T(8,128)(2,1)S(1)}, bf16[96,768]{1,0:T(8,128)(2,1)S(1)}, u32[]{:S(2)}, u32[]{:S(2)}) collective-permute-start(bf16[96,768]{1,0:T(8,128)(2,1)S(1)} %get-tuple-element.136.rest_0_), channel_id=1, source_target_pairs={{0,16},{4,20},{8,24},{12,28},{16,0},{20,4},{24,8},{28,12},{1,17},{... | collective-permute-start | bytes 442376 | tf_op jit(solution)/shard_map/ppermute | solution.py:543
  9.6 2.2 %prep.1 = (bf16[512,768]{1,0:T(8,128)(2,1)S(1)}, bf16[768,512]{1,0:T(8,128)(2,1)S(1)}, f32[3,512,512]{2,1,0:T(8,128)S(1)}, s32[1,1024]{1,0:T(1,128)S(1)}, bf16[5...) custom-call(s32[1,4]{1,0:T(1,128)} %seg_in.1, f32[3,32]{1,0:T(4,128)} %bitcast.8, ...), custom_call_target="tpu_custom_call" | custom-call | tf_op jit(solution)/shard_map/prep/pallas_call | solution.py:60
  11.8 0.8 collective-permute-done.1.rest_2_
  12.6 3.0 %collective-permute-done.rest_4_ = bf16[96,768]{1,0:T(8,128)(2,1)S(1)} collective-permute-done((bf16[96,768]{1,0:T(8,128)(2,1)S(1)}, bf16[96,768]{1,0:T(8,128)(2,1)S(1)}, u32[]{:S(2)}, u32[]{:S(2)}) %collective-permute-start) | collective-permute-done | bytes 147488 | tf_op jit(solution)/shard_map/ppermute | solution.py:543
  15.9 2.8 %collective-permute-start.2 = (bf16[96,1536]{1,0:T(8,128)(2,1)S(1)}, bf16[96,1536]{1,0:T(8,128)(2,1)S(1)}, u32[]{:S(2)}, u32[]{:S(2)}) collective-permute-start(bf16[96,1536]{1,0:T(8,128)(2,1)S(1)} %get-tuple-element.137.rest_0_), channel_id=1, source_target_pairs={{0,8},{4,12},{8,0},{12,4},{16,24},{20,28},{24,16},{28,20},{1,9},{5... | collective-permute-start | bytes 884744 | tf_op jit(solution)/shard_map/ppermute | solution.py:543
  19.3 1.5 collective-permute-start.7
  20.8 11.0 %collective-permute-done.8.rest_6_ = bf16[96,768]{1,0:T(8,128)(2,1)S(1)} collective-permute-done((bf16[96,768]{1,0:T(8,128)(2,1)S(1)}, bf16[96,768]{1,0:T(8,128)(2,1)S(1)}, u32[]{:S(2)}, u32[]{:S(2)}) %collective-permute-start.8) | collective-permute-done | bytes 147488 | tf_op jit(solution)/shard_map/ppermute | solution.py:543
  32.3 4.6 %collective-permute-done.9.rest_7_ = bf16[96,768]{1,0:T(8,128)(2,1)S(1)} collective-permute-done((bf16[96,768]{1,0:T(8,128)(2,1)S(1)}, bf16[96,768]{1,0:T(8,128)(2,1)S(1)}, u32[]{:S(2)}, u32[]{:S(2)}) %collective-permute-start.9) | collective-permute-done | bytes 147488 | tf_op jit(solution)/shard_map/ppermute | solution.py:543
  36.9 3.0 %attend.1 = (bf16[768,768]{1,0:T(8,128)(2,1)S(1)}, bf16[512,576]{1,0:T(8,128)(2,1)S(1)}, bf16[3,512,512]{2,1,0:T(8,128)(2,1)S(1)}, bf16[512,192]{1,0:T(8,128)(2,...) custom-call(bf16[512,768]{1,0:T(8,128)(2,1)S(1)} %get-tuple-element.133.act, ...), custom_call_target="tpu_custom_call" | custom-call | tf_op jit(solution)/shard_map/attend/pallas_call | solution.py:60
  40.0 1.7 %collective-permute-done.10.two = bf16[256,768]{1,0:T(8,128)(2,1)S(1)} collective-permute-done((bf16[256,768]{1,0:T(8,128)(2,1)S(1)}, bf16[256,768]{1,0:T(8,128)(2,1)S(1)}, u32[]{:S(2)}, u32[]{:S(2)}) %collective-permute-start.10) | collective-permute-done | bytes 393248 | tf_op jit(solution)/shard_map/ppermute | solution.py:546
  41.8 1.6 collective-permute-start.14
  43.4 1.8 %collective-permute-start.13 = (bf16[96,1536]{1,0:T(8,128)(2,1)S(1)}, bf16[96,1536]{1,0:T(8,128)(2,1)S(1)}, u32[]{:S(2)}, u32[]{:S(2)}) collective-permute-start(bf16[96,1536]{1,0:T(8,128)(2,1)S(1)} %collective-permute-done.3.rest_4_), channel_id=1, source_target_pairs={{0,8},{4,12},{8,0},{12,4},{16,24},{20,28},{24,16},{28,20},{1,9},{5... | collective-permute-start | bytes 884744 | tf_op jit(solution)/shard_map/ppermute | solution.py:543
  45.8 1.5 collective-permute-start.11
  47.2 5.0 %collective-permute-done.13.rest_6_ = bf16[96,1536]{1,0:T(8,128)(2,1)S(1)} collective-permute-done((bf16[96,1536]{1,0:T(8,128)(2,1)S(1)}, bf16[96,1536]{1,0:T(8,128)(2,1)S(1)}, u32[]{:S(2)}, u32[]{:S(2)}) %collective-permute-start.13) | collective-permute-done | bytes 294944 | tf_op jit(solution)/shard_map/ppermute | solution.py:543
  52.2 2.9 %collective-permute-done.12.rest_5_ = bf16[96,1536]{1,0:T(8,128)(2,1)S(1)} collective-permute-done((bf16[96,1536]{1,0:T(8,128)(2,1)S(1)}, bf16[96,1536]{1,0:T(8,128)(2,1)S(1)}, u32[]{:S(2)}, u32[]{:S(2)}) %collective-permute-start.12) | collective-permute-done | bytes 294944 | tf_op jit(solution)/shard_map/ppermute | solution.py:543
  55.2 4.9 %collective-permute-done.11.rest_3_ = bf16[96,1536]{1,0:T(8,128)(2,1)S(1)} collective-permute-done((bf16[96,1536]{1,0:T(8,128)(2,1)S(1)}, bf16[96,1536]{1,0:T(8,128)(2,1)S(1)}, u32[]{:S(2)}, u32[]{:S(2)}) %collective-permute-start.11) | collective-permute-done | bytes 294944 | tf_op jit(solution)/shard_map/ppermute | solution.py:543
  60.8 8.8 %collective-permute-done.16.rest_7_ = bf16[96,1536]{1,0:T(8,128)(2,1)S(1)} collective-permute-done((bf16[96,1536]{1,0:T(8,128)(2,1)S(1)}, bf16[96,1536]{1,0:T(8,128)(2,1)S(1)}, u32[]{:S(2)}, u32[]{:S(2)}) %collective-permute-start.16) | collective-permute-done | bytes 294944 | tf_op jit(solution)/shard_map/ppermute | solution.py:543
  69.6 3.5 %ffn.1 = (f32[512,768]{1,0:T(8,128)S(1)}, bf16[512,768]{1,0:T(8,128)(2,1)S(1)}, bf16[512,768]{1,0:T(8,128)(2,1)S(1)}, bf16[512,768]{1,0:T(8,128)(2,1)S(1)}, bf16...) custom-call(bf16[512,768]{1,0:T(8,128)(2,1)S(1)} %get-tuple-element.200.x, ...), custom_call_target="tpu_custom_call" | custom-call | tf_op jit(solution)/shard_map/ffn/pallas_call | solution.py:60
  73.2 1.7 %collective-permute-done.17.two = bf16[256,768]{1,0:T(8,128)(2,1)S(1)} collective-permute-done((bf16[256,768]{1,0:T(8,128)(2,1)S(1)}, bf16[256,768]{1,0:T(8,128)(2,1)S(1)}, u32[]{:S(2)}, u32[]{:S(2)}) %collective-permute-start.17) | collective-permute-done | bytes 393248 | tf_op jit(solution)/shard_map/ppermute | solution.py:546
  75.6 0.9 down_grad.1
  76.5 0.9 in_grad.1
  78.4 8.0 %collective-permute-done.19.got = bf16[2,96,768]{2,1,0:T(8,128)(2,1)S(1)} collective-permute-done((bf16[2,96,768]{2,1,0:T(8,128)(2,1)S(1)}, bf16[2,96,768]{2,1,0:T(8,128)(2,1)S(1)}, u32[]{:S(2)}, u32[]{:S(2)}) %collective-permute-start.19) | collective-permute-done | bytes 294944 | tf_op jit(solution)/shard_map/ppermute | solution.py:543
  86.7 1.6 collective-permute-done.21.other
  88.3 5.4 %attend_back.1 = (bf16[4,96,768]{2,1,0:T(8,128)(2,1)S(1)}, bf16[2,96,768]{2,1,0:T(8,128)(2,1)S(1)}, bf16[2,96,768]{2,1,0:T(8,128)(2,1)S(1)}, f32[128,768]{1,0:T(...) custom-call(f32[512,768]{1,0:T(8,128)S(1)} %get-tuple-element.198.resid, ...), custom_call_target="tpu_custom_call" | custom-call | tf_op jit(solution)/shard_map/attend_back/pallas_call | solution.py:60
  93.7 2.5 %tail.1 = (bf16[256,768]{1,0:T(8,128)(2,1)S(1)}, bf16[256,768]{1,0:T(8,128)(2,1)S(1)}, bf16[208,768]{1,0:T(8,128)(2,1)S(1)}) custom-call(bf16[3,512,512]{2,1,0:T(8,128)(2,1)S(1)} %get-tuple-element.166.score_grad, bf16[512,576]{1,0:T(8,128)(2,1)S(1)} %get-tuple-element.167.proj_grad, bf16[768,768]{1,0:T(8,128)(2,1)S(1)} %get-tuple-element.161.weights, ...), custom_call_target="tpu_custom_call" | custom-call | tf_op jit(solution)/shard_map/tail/pallas_call | solution.py:60
  96.8 1.5 collective-permute-start.22
  98.3 1.7 %collective-permute-start.23 = (bf16[2,96,768]{2,1,0:T(8,128)(2,1)S(1)}, bf16[2,96,768]{2,1,0:T(8,128)(2,1)S(1)}, u32[]{:S(2)}, u32[]{:S(2)}) collective-permute-start(bf16[2,96,768]{2,1,0:T(8,128)(2,1)S(1)} %high_add.2), channel_id=1, source_target_pairs={{0,8},{4,12},{8,0},{12,4},{16,24},{20,28},{24,16},{28,20},{1,9},{5... | collective-permute-start | bytes 884744 | tf_op jit(solution)/shard_map/ppermute | solution.py:543
  100.4 2.0 %collective-permute-start.26 = (bf16[2,96,768]{2,1,0:T(8,128)(2,1)S(1)}, bf16[2,96,768]{2,1,0:T(8,128)(2,1)S(1)}, u32[]{:S(2)}, u32[]{:S(2)}) collective-permute-start(bf16[2,96,768]{2,1,0:T(8,128)(2,1)S(1)} %high_add.3), channel_id=1, source_target_pairs={{0,16},{4,20},{8,24},{12,28},{16,0},{20,4},{24,8},{28,12},{1,17},{... | collective-permute-start | bytes 884744 | tf_op jit(solution)/shard_map/ppermute | solution.py:543
  102.4 9.8 %collective-permute-done.22.got_low = bf16[2,96,768]{2,1,0:T(8,128)(2,1)S(1)} collective-permute-done((bf16[2,96,768]{2,1,0:T(8,128)(2,1)S(1)}, bf16[2,96,768]{2,1,0:T(8,128)(2,1)S(1)}, u32[]{:S(2)}, u32[]{:S(2)}) %collective-permute-start.22) | collective-permute-done | bytes 294944 | tf_op jit(solution)/shard_map/ppermute | solution.py:543
  112.2 2.4 %collective-permute-done.23.got = bf16[2,96,768]{2,1,0:T(8,128)(2,1)S(1)} collective-permute-done((bf16[2,96,768]{2,1,0:T(8,128)(2,1)S(1)}, bf16[2,96,768]{2,1,0:T(8,128)(2,1)S(1)}, u32[]{:S(2)}, u32[]{:S(2)}) %collective-permute-start.23) | collective-permute-done | bytes 294944 | tf_op jit(solution)/shard_map/ppermute | solution.py:543
  114.8 4.6 %collective-permute-done.25.got_low = bf16[2,96,768]{2,1,0:T(8,128)(2,1)S(1)} collective-permute-done((bf16[2,96,768]{2,1,0:T(8,128)(2,1)S(1)}, bf16[2,96,768]{2,1,0:T(8,128)(2,1)S(1)}, u32[]{:S(2)}, u32[]{:S(2)}) %collective-permute-start.25) | collective-permute-done | bytes 294944 | tf_op jit(solution)/shard_map/ppermute | solution.py:543
  119.6 1.6 %ffn_out.1 = (bf16[256,768]{1,0:T(8,128)(2,1)S(1)}, bf16[256,768]{1,0:T(8,128)(2,1)S(1)}) custom-call(bf16[512,768]{1,0:T(8,128)(2,1)S(1)} %get-tuple-element.184.right.hidden, bf16[768,768]{1,0:T(8,128)(2,1)S(1)} %get-tuple-element.185.weights), custom_call_target="tpu_custom_call" | custom-call | tf_op jit(solution)/shard_map/ffn_out/pallas_call | solution.py:60
  122.3 2.1 %collective-permute-start.28 = (bf16[112,768]{1,0:T(8,128)(2,1)S(1)}, bf16[112,768]{1,0:T(8,128)(2,1)S(1)}, u32[]{:S(2)}, u32[]{:S(2)}) collective-permute-start(bf16[112,768]{1,0:T(8,128)(2,1)S(1)} %get-tuple-element.189.sent), channel_id=1, source_target_pairs={{0,8},{4,12},{8,0},{12,4},{16,24},{20,28},{24,16},{28,20},{1,9},{5... | collective-permute-start | bytes 516104 | tf_op jit(solution)/shard_map/ppermute | solution.py:543
  124.9 5.9 %collective-permute-done.27.got_low.rest_1_ = bf16[2,96,768]{2,1,0:T(8,128)(2,1)S(1)} collective-permute-done((bf16[2,96,768]{2,1,0:T(8,128)(2,1)S(1)}, bf16[2,96,768]{2,1,0:T(8,128)(2,1)S(1)}, u32[]{:S(2)}, u32[]{:S(2)}) %collective-permute-start.27) | collective-permute-done | bytes 294944 | tf_op jit(solution)/shard_map/ppermute | solution.py:543
  130.8 1.0 collective-permute-done.28.got
  132.0 1.6 collective-permute-start.32
  134.2 1.6 collective-permute-start.36
  136.3 1.8 %collective-permute-start.35 = (bf16[96,768]{1,0:T(8,128)(2,1)S(1)}, bf16[96,768]{1,0:T(8,128)(2,1)S(1)}, u32[]{:S(2)}, u32[]{:S(2)}) collective-permute-start(bf16[96,768]{1,0:T(8,128)(2,1)S(1)} %get-tuple-element.179), channel_id=1, source_target_pairs={{0,8},{4,12},{8,0},{12,4},{16,24},{20,28},{24,16},{28,20},{1,9},{5... | collective-permute-start | bytes 442376 | tf_op jit(solution)/shard_map/ppermute | solution.py:543
  138.2 1.1 collective-permute-done.32.got
  139.3 0.8 block_out.1
  140.0 1.4 collective-permute-done.33.got
  141.4 1.0 input_grad.1
  142.9 0.8 last_sum.1
  143.7 12.8 %all_to_all.5.refs_0_ = f32[32,8,128]{2,1,0:T(8,128)S(1)} all-to-all(f32[32,8,128]{2,1,0:T(8,128)} %get-tuple-element.208), channel_id=1, replica_groups=mesh['dp'=8,'tp'=4] {'dp','tp'}, dimensions={0} | all-to-all | bytes 262144 | tf_op jit(solution)/shard_map/all_to_all | solution.py:797
  156.6 3.9 %adam.1 = (f32[1,1]{1,0:T(1,128)}, f32[3,96,192]{2,1,0:T(8,128)}, f32[3,96,192]{2,1,0:T(8,128)}, f32[3,96,192]{2,1,0:T(8,128)}, bf16[3,96,192]{2,1,0:T(8,128)(2,...) custom-call(f32[32,8,128]{2,1,0:T(8,128)S(1)} %all_to_all.5.refs_0_,, ...), custom_call_target="tpu_custom_call" | custom-call | tf_op jit(solution)/shard_map/adam/pallas_call | solution.py:60
  (66 shorter events, 10.2 us)
Async XLA Ops:
  1.9 16.8 %collective-permute-start.5 = (bf16[96,1536]{1,0:T(8,128)(2,1)S(1)}, bf16[96,1536]{1,0:T(8,128)(2,1)S(1)}, u32[]{:S(2)}, u32[]{:S(2)}) collective-permute-start(bf16[96,1536]{1,0:T(8,128)(2,1)S(1)} %get-tuple-element.137.rest_0_), channel_id=1, source_target_pairs={{0,4},{4,0},{8,12},{12,8},{16,20},{20,16},{24,28},{28,24},{1,5},{5... | collective-permute-start | bytes 884744 | tf_op jit(solution)/shard_map/ppermute | solution.py:543
  4.9 7.7 %collective-permute-start.1 = (bf16[96,768]{1,0:T(8,128)(2,1)S(1)}, bf16[96,768]{1,0:T(8,128)(2,1)S(1)}, u32[]{:S(2)}, u32[]{:S(2)}) collective-permute-start(bf16[96,768]{1,0:T(8,128)(2,1)S(1)} %get-tuple-element.136.rest_0_), channel_id=1, source_target_pairs={{0,8},{4,12},{8,0},{12,4},{16,24},{20,28},{24,16},{28,20},{1,9},{5... | collective-permute-start | bytes 442376 | tf_op jit(solution)/shard_map/ppermute | solution.py:543
  6.5 9.1 %collective-permute-start = (bf16[96,768]{1,0:T(8,128)(2,1)S(1)}, bf16[96,768]{1,0:T(8,128)(2,1)S(1)}, u32[]{:S(2)}, u32[]{:S(2)}) collective-permute-start(bf16[96,768]{1,0:T(8,128)(2,1)S(1)} %get-tuple-element.136.rest_0_), channel_id=1, source_target_pairs={{0,16},{4,20},{8,24},{12,28},{16,0},{20,4},{24,8},{28,12},{1,17},{... | collective-permute-start | bytes 442376 | tf_op jit(solution)/shard_map/ppermute | solution.py:543
  9.1 9.6 %collective-permute-start.4 = (bf16[96,768]{1,0:T(8,128)(2,1)S(1)}, bf16[96,768]{1,0:T(8,128)(2,1)S(1)}, u32[]{:S(2)}, u32[]{:S(2)}) collective-permute-start(bf16[96,768]{1,0:T(8,128)(2,1)S(1)} %get-tuple-element.136.rest_0_), channel_id=1, source_target_pairs={{0,4},{4,0},{8,12},{12,8},{16,20},{20,16},{24,28},{28,24},{1,5},{5... | collective-permute-start | bytes 442376 | tf_op jit(solution)/shard_map/ppermute | solution.py:543
  15.6 16.7 %collective-permute-start.3 = (bf16[96,1536]{1,0:T(8,128)(2,1)S(1)}, bf16[96,1536]{1,0:T(8,128)(2,1)S(1)}, u32[]{:S(2)}, u32[]{:S(2)}) collective-permute-start(bf16[96,1536]{1,0:T(8,128)(2,1)S(1)} %get-tuple-element.137.rest_0_), channel_id=1, source_target_pairs={{0,16},{4,20},{8,24},{12,28},{16,0},{20,4},{24,8},{28,12},{1,17},{... | collective-permute-start | bytes 884744 | tf_op jit(solution)/shard_map/ppermute | solution.py:543
  15.9 16.4 %collective-permute-start.2 = (bf16[96,1536]{1,0:T(8,128)(2,1)S(1)}, bf16[96,1536]{1,0:T(8,128)(2,1)S(1)}, u32[]{:S(2)}, u32[]{:S(2)}) collective-permute-start(bf16[96,1536]{1,0:T(8,128)(2,1)S(1)} %get-tuple-element.137.rest_0_), channel_id=1, source_target_pairs={{0,8},{4,12},{8,0},{12,4},{16,24},{20,28},{24,16},{28,20},{1,9},{5... | collective-permute-start | bytes 884744 | tf_op jit(solution)/shard_map/ppermute | solution.py:543
  18.7 13.1 %collective-permute-start.8 = (bf16[96,768]{1,0:T(8,128)(2,1)S(1)}, bf16[96,768]{1,0:T(8,128)(2,1)S(1)}, u32[]{:S(2)}, u32[]{:S(2)}) collective-permute-start(bf16[96,768]{1,0:T(8,128)(2,1)S(1)} %collective-permute-done.rest_4_), channel_id=1, source_target_pairs={{0,8},{4,12},{8,0},{12,4},{16,24},{20,28},{24,16},{28,20},{1,9},{5... | collective-permute-start | bytes 442376 | tf_op jit(solution)/shard_map/ppermute | solution.py:543
  18.7 13.0 %collective-permute-start.6 = (bf16[96,768]{1,0:T(8,128)(2,1)S(1)}, bf16[96,768]{1,0:T(8,128)(2,1)S(1)}, u32[]{:S(2)}, u32[]{:S(2)}) collective-permute-start(bf16[96,768]{1,0:T(8,128)(2,1)S(1)} %collective-permute-done.1.rest_2_), channel_id=1, source_target_pairs={{0,4},{4,0},{8,12},{12,8},{16,20},{20,16},{24,28},{28,24},{1,5},{5... | collective-permute-start | bytes 442376 | tf_op jit(solution)/shard_map/ppermute | solution.py:543
  19.3 13.0 %collective-permute-start.7 = (bf16[96,768]{1,0:T(8,128)(2,1)S(1)}, bf16[96,768]{1,0:T(8,128)(2,1)S(1)}, u32[]{:S(2)}, u32[]{:S(2)}) collective-permute-start(bf16[96,768]{1,0:T(8,128)(2,1)S(1)} %collective-permute-done.rest_4_), channel_id=1, source_target_pairs={{0,4},{4,0},{8,12},{12,8},{16,20},{20,16},{24,28},{28,24},{1,5},{5... | collective-permute-start | bytes 442376 | tf_op jit(solution)/shard_map/ppermute | solution.py:543
  31.8 5.1 %collective-permute-start.9 = (bf16[96,768]{1,0:T(8,128)(2,1)S(1)}, bf16[96,768]{1,0:T(8,128)(2,1)S(1)}, u32[]{:S(2)}, u32[]{:S(2)}) collective-permute-start(bf16[96,768]{1,0:T(8,128)(2,1)S(1)} %collective-permute-done.8.rest_6_), channel_id=1, source_target_pairs={{0,4},{4,0},{8,12},{12,8},{16,20},{20,16},{24,28},{28,24},{1,5},{5... | collective-permute-start | bytes 442376 | tf_op jit(solution)/shard_map/ppermute | solution.py:543
  40.0 1.8 %collective-permute-start.10 = (bf16[256,768]{1,0:T(8,128)(2,1)S(1)}, bf16[256,768]{1,0:T(8,128)(2,1)S(1)}, u32[]{:S(2)}, u32[]{:S(2)}) collective-permute-start(bf16[256,768]{1,0:T(8,128)(2,1)S(1)} %get-tuple-element.143), channel_id=1, source_target_pairs={{0,1},{1,0},{2,3},{3,2},{4,5},{5,4},{6,7},{7,6},{8,9},{9,8},{10,11... | collective-permute-start | bytes 1179656 | tf_op jit(solution)/shard_map/ppermute | solution.py:546
  41.8 18.2 %collective-permute-start.14 = (bf16[256,768]{1,0:T(8,128)(2,1)S(1)}, bf16[256,768]{1,0:T(8,128)(2,1)S(1)}, u32[]{:S(2)}, u32[]{:S(2)}) collective-permute-start(bf16[256,768]{1,0:T(8,128)(2,1)S(1)} %add.4.one), channel_id=1, source_target_pairs={{0,2},{1,3},{2,0},{3,1},{4,6},{5,7},{6,4},{7,5},{8,10},{9,11},{10,... | collective-permute-start | bytes 1179656 | tf_op jit(solution)/shard_map/ppermute | solution.py:546
  43.4 8.8 %collective-permute-start.13 = (bf16[96,1536]{1,0:T(8,128)(2,1)S(1)}, bf16[96,1536]{1,0:T(8,128)(2,1)S(1)}, u32[]{:S(2)}, u32[]{:S(2)}) collective-permute-start(bf16[96,1536]{1,0:T(8,128)(2,1)S(1)} %collective-permute-done.3.rest_4_), channel_id=1, source_target_pairs={{0,8},{4,12},{8,0},{12,4},{16,24},{20,28},{24,16},{28,20},{1,9},{5... | collective-permute-start | bytes 884744 | tf_op jit(solution)/shard_map/ppermute | solution.py:543
  45.2 9.9 %collective-permute-start.12 = (bf16[96,1536]{1,0:T(8,128)(2,1)S(1)}, bf16[96,1536]{1,0:T(8,128)(2,1)S(1)}, u32[]{:S(2)}, u32[]{:S(2)}) collective-permute-start(bf16[96,1536]{1,0:T(8,128)(2,1)S(1)} %collective-permute-done.3.rest_4_), channel_id=1, source_target_pairs={{0,4},{4,0},{8,12},{12,8},{16,20},{20,16},{24,28},{28,24},{1,5},{5... | collective-permute-start | bytes 884744 | tf_op jit(solution)/shard_map/ppermute | solution.py:543
  45.8 14.3 %collective-permute-start.11 = (bf16[96,1536]{1,0:T(8,128)(2,1)S(1)}, bf16[96,1536]{1,0:T(8,128)(2,1)S(1)}, u32[]{:S(2)}, u32[]{:S(2)}) collective-permute-start(bf16[96,1536]{1,0:T(8,128)(2,1)S(1)} %collective-permute-done.2.rest_2_), channel_id=1, source_target_pairs={{0,4},{4,0},{8,12},{12,8},{16,20},{20,16},{24,28},{28,24},{1,5},{5... | collective-permute-start | bytes 884744 | tf_op jit(solution)/shard_map/ppermute | solution.py:543
  60.1 9.5 %collective-permute-start.15 = (bf16[256,768]{1,0:T(8,128)(2,1)S(1)}, bf16[256,768]{1,0:T(8,128)(2,1)S(1)}, u32[]{:S(2)}, u32[]{:S(2)}) collective-permute-start(bf16[256,768]{1,0:T(8,128)(2,1)S(1)} %add.5.own), channel_id=1, source_target_pairs={{0,1},{1,0},{2,3},{3,2},{4,5},{5,4},{6,7},{7,6},{8,9},{9,8},{10,11... | collective-permute-start | bytes 1179656 | tf_op jit(solution)/shard_map/ppermute | solution.py:546
  60.2 9.4 %collective-permute-start.16 = (bf16[96,1536]{1,0:T(8,128)(2,1)S(1)}, bf16[96,1536]{1,0:T(8,128)(2,1)S(1)}, u32[]{:S(2)}, u32[]{:S(2)}) collective-permute-start(bf16[96,1536]{1,0:T(8,128)(2,1)S(1)} %collective-permute-done.13.rest_6_), channel_id=1, source_target_pairs={{0,4},{4,0},{8,12},{12,8},{16,20},{20,16},{24,28},{28,24},{1,5},{5... | collective-permute-start | bytes 884744 | tf_op jit(solution)/shard_map/ppermute | solution.py:543
  73.1 1.8 %collective-permute-start.17 = (bf16[256,768]{1,0:T(8,128)(2,1)S(1)}, bf16[256,768]{1,0:T(8,128)(2,1)S(1)}, u32[]{:S(2)}, u32[]{:S(2)}) collective-permute-start(bf16[256,768]{1,0:T(8,128)(2,1)S(1)} %get-tuple-element.148), channel_id=1, source_target_pairs={{0,1},{1,0},{2,3},{3,2},{4,5},{5,4},{6,7},{7,6},{8,9},{9,8},{10,11... | collective-permute-start | bytes 1179656 | tf_op jit(solution)/shard_map/ppermute | solution.py:546
  75.0 11.4 %collective-permute-start.20 = (bf16[256,768]{1,0:T(8,128)(2,1)S(1)}, bf16[256,768]{1,0:T(8,128)(2,1)S(1)}, u32[]{:S(2)}, u32[]{:S(2)}) collective-permute-start(bf16[256,768]{1,0:T(8,128)(2,1)S(1)} %add.6.one), channel_id=1, source_target_pairs={{0,2},{1,3},{2,0},{3,1},{4,6},{5,7},{6,4},{7,5},{8,10},{9,11},{10,... | collective-permute-start | bytes 1179656 | tf_op jit(solution)/shard_map/ppermute | solution.py:546
  77.5 8.8 %collective-permute-start.19 = (bf16[2,96,768]{2,1,0:T(8,128)(2,1)S(1)}, bf16[2,96,768]{2,1,0:T(8,128)(2,1)S(1)}, u32[]{:S(2)}, u32[]{:S(2)}) collective-permute-start(bf16[2,96,768]{2,1,0:T(8,128)(2,1)S(1)} %get-tuple-element.156), channel_id=1, source_target_pairs={{0,8},{4,12},{8,0},{12,4},{16,24},{20,28},{24,16},{28,20},{1,9},{5... | collective-permute-start | bytes 884744 | tf_op jit(solution)/shard_map/ppermute | solution.py:543
  77.8 8.6 %collective-permute-start.18 = (bf16[2,96,768]{2,1,0:T(8,128)(2,1)S(1)}, bf16[2,96,768]{2,1,0:T(8,128)(2,1)S(1)}, u32[]{:S(2)}, u32[]{:S(2)}) collective-permute-start(bf16[2,96,768]{2,1,0:T(8,128)(2,1)S(1)} %get-tuple-element.155), channel_id=1, source_target_pairs={{0,4},{4,0},{8,12},{12,8},{16,20},{20,16},{24,28},{28,24},{1,5},{5... | collective-permute-start | bytes 884744 | tf_op jit(solution)/shard_map/ppermute | solution.py:543
  86.5 1.8 %collective-permute-start.21 = (bf16[256,768]{1,0:T(8,128)(2,1)S(1)}, bf16[256,768]{1,0:T(8,128)(2,1)S(1)}, u32[]{:S(2)}, u32[]{:S(2)}) collective-permute-start(bf16[256,768]{1,0:T(8,128)(2,1)S(1)} %add.7.own), channel_id=1, source_target_pairs={{0,1},{1,0},{2,3},{3,2},{4,5},{5,4},{6,7},{7,6},{8,9},{9,8},{10,11... | collective-permute-start | bytes 1179656 | tf_op jit(solution)/shard_map/ppermute | solution.py:546
  96.2 18.5 %collective-permute-start.24 = (bf16[208,768]{1,0:T(8,128)(2,1)S(1)}, bf16[208,768]{1,0:T(8,128)(2,1)S(1)}, u32[]{:S(2)}, u32[]{:S(2)}) collective-permute-start(bf16[208,768]{1,0:T(8,128)(2,1)S(1)} %get-tuple-element.178.sent), channel_id=1, source_target_pairs={{0,4},{4,0},{8,12},{12,8},{16,20},{20,16},{24,28},{28,24},{1,5},{5... | collective-permute-start | bytes 958472 | tf_op jit(solution)/shard_map/ppermute | solution.py:543
  96.8 15.4 %collective-permute-start.22 = (bf16[2,96,768]{2,1,0:T(8,128)(2,1)S(1)}, bf16[2,96,768]{2,1,0:T(8,128)(2,1)S(1)}, u32[]{:S(2)}, u32[]{:S(2)}) collective-permute-start(bf16[2,96,768]{2,1,0:T(8,128)(2,1)S(1)} %get-tuple-element.173), channel_id=1, source_target_pairs={{0,4},{4,0},{8,12},{12,8},{16,20},{20,16},{24,28},{28,24},{1,5},{5... | collective-permute-start | bytes 884744 | tf_op jit(solution)/shard_map/ppermute | solution.py:543
  98.3 16.3 %collective-permute-start.23 = (bf16[2,96,768]{2,1,0:T(8,128)(2,1)S(1)}, bf16[2,96,768]{2,1,0:T(8,128)(2,1)S(1)}, u32[]{:S(2)}, u32[]{:S(2)}) collective-permute-start(bf16[2,96,768]{2,1,0:T(8,128)(2,1)S(1)} %high_add.2), channel_id=1, source_target_pairs={{0,8},{4,12},{8,0},{12,4},{16,24},{20,28},{24,16},{28,20},{1,9},{5... | collective-permute-start | bytes 884744 | tf_op jit(solution)/shard_map/ppermute | solution.py:543
  100.0 19.4 %collective-permute-start.25 = (bf16[2,96,768]{2,1,0:T(8,128)(2,1)S(1)}, bf16[2,96,768]{2,1,0:T(8,128)(2,1)S(1)}, u32[]{:S(2)}, u32[]{:S(2)}) collective-permute-start(bf16[2,96,768]{2,1,0:T(8,128)(2,1)S(1)} %get-tuple-element.181), channel_id=1, source_target_pairs={{0,8},{4,12},{8,0},{12,4},{16,24},{20,28},{24,16},{28,20},{1,9},{5... | collective-permute-start | bytes 884744 | tf_op jit(solution)/shard_map/ppermute | solution.py:543
  100.4 19.1 %collective-permute-start.26 = (bf16[2,96,768]{2,1,0:T(8,128)(2,1)S(1)}, bf16[2,96,768]{2,1,0:T(8,128)(2,1)S(1)}, u32[]{:S(2)}, u32[]{:S(2)}) collective-permute-start(bf16[2,96,768]{2,1,0:T(8,128)(2,1)S(1)} %high_add.3), channel_id=1, source_target_pairs={{0,16},{4,20},{8,24},{12,28},{16,0},{20,4},{24,8},{28,12},{1,17},{... | collective-permute-start | bytes 884744 | tf_op jit(solution)/shard_map/ppermute | solution.py:543
  121.2 10.6 %collective-permute-start.29 = (bf16[256,768]{1,0:T(8,128)(2,1)S(1)}, bf16[256,768]{1,0:T(8,128)(2,1)S(1)}, u32[]{:S(2)}, u32[]{:S(2)}) collective-permute-start(bf16[256,768]{1,0:T(8,128)(2,1)S(1)} %get-tuple-element.191), channel_id=1, source_target_pairs={{0,1},{1,0},{2,3},{3,2},{4,5},{5,4},{6,7},{7,6},{8,9},{9,8},{10,11... | collective-permute-start | bytes 1179656 | tf_op jit(solution)/shard_map/ppermute | solution.py:546
  121.3 12.3 %collective-permute-start.30 = (bf16[256,768]{1,0:T(8,128)(2,1)S(1)}, bf16[256,768]{1,0:T(8,128)(2,1)S(1)}, u32[]{:S(2)}, u32[]{:S(2)}) collective-permute-start(bf16[256,768]{1,0:T(8,128)(2,1)S(1)} %get-tuple-element.194), channel_id=1, source_target_pairs={{0,1},{1,0},{2,3},{3,2},{4,5},{5,4},{6,7},{7,6},{8,9},{9,8},{10,11... | collective-permute-start | bytes 1179656 | tf_op jit(solution)/shard_map/ppermute | solution.py:546
  121.8 9.0 %collective-permute-start.27 = (bf16[2,96,768]{2,1,0:T(8,128)(2,1)S(1)}, bf16[2,96,768]{2,1,0:T(8,128)(2,1)S(1)}, u32[]{:S(2)}, u32[]{:S(2)}) collective-permute-start(bf16[2,96,768]{2,1,0:T(8,128)(2,1)S(1)} %get-tuple-element.188), channel_id=1, source_target_pairs={{0,4},{4,0},{8,12},{12,8},{16,20},{20,16},{24,28},{28,24},{1,5},{5... | collective-permute-start | bytes 884744 | tf_op jit(solution)/shard_map/ppermute | solution.py:543
  122.3 9.5 %collective-permute-start.28 = (bf16[112,768]{1,0:T(8,128)(2,1)S(1)}, bf16[112,768]{1,0:T(8,128)(2,1)S(1)}, u32[]{:S(2)}, u32[]{:S(2)}) collective-permute-start(bf16[112,768]{1,0:T(8,128)(2,1)S(1)} %get-tuple-element.189.sent), channel_id=1, source_target_pairs={{0,8},{4,12},{8,0},{12,4},{16,24},{20,28},{24,16},{28,20},{1,9},{5... | collective-permute-start | bytes 516104 | tf_op jit(solution)/shard_map/ppermute | solution.py:543
  124.4 11.9 %collective-permute-start.31 = (bf16[96,768]{1,0:T(8,128)(2,1)S(1)}, bf16[96,768]{1,0:T(8,128)(2,1)S(1)}, u32[]{:S(2)}, u32[]{:S(2)}) collective-permute-start(bf16[96,768]{1,0:T(8,128)(2,1)S(1)} %get-tuple-element.176), channel_id=1, source_target_pairs={{0,16},{4,20},{8,24},{12,28},{16,0},{20,4},{24,8},{28,12},{1,17},{... | collective-permute-start | bytes 442376 | tf_op jit(solution)/shard_map/ppermute | solution.py:543
  132.0 7.3 %collective-permute-start.32 = (bf16[128,768]{1,0:T(8,128)(2,1)S(1)}, bf16[128,768]{1,0:T(8,128)(2,1)S(1)}, u32[]{:S(2)}, u32[]{:S(2)}) collective-permute-start(bf16[128,768]{1,0:T(8,128)(2,1)S(1)} %get-tuple-element.199), channel_id=1, source_target_pairs={{0,2},{1,3},{2,0},{3,1},{4,6},{5,7},{6,4},{7,5},{8,10},{9,11},{10,... | collective-permute-start | bytes 589832 | tf_op jit(solution)/shard_map/ppermute | solution.py:546
  133.7 7.7 %collective-permute-start.33 = (bf16[128,768]{1,0:T(8,128)(2,1)S(1)}, bf16[128,768]{1,0:T(8,128)(2,1)S(1)}, u32[]{:S(2)}, u32[]{:S(2)}) collective-permute-start(bf16[128,768]{1,0:T(8,128)(2,1)S(1)} %get-tuple-element.202), channel_id=1, source_target_pairs={{0,2},{1,3},{2,0},{3,1},{4,6},{5,7},{6,4},{7,5},{8,10},{9,11},{10,... | collective-permute-start | bytes 589832 | tf_op jit(solution)/shard_map/ppermute | solution.py:546
  134.2 8.7 %collective-permute-start.36 = (bf16[112,768]{1,0:T(8,128)(2,1)S(1)}, bf16[112,768]{1,0:T(8,128)(2,1)S(1)}, u32[]{:S(2)}, u32[]{:S(2)}) collective-permute-start(bf16[112,768]{1,0:T(8,128)(2,1)S(1)} %last_late.1.rest_3_), channel_id=1, source_target_pairs={{0,16},{4,20},{8,24},{12,28},{16,0},{20,4},{24,8},{28,12},{1,17},{... | collective-permute-start | bytes 516104 | tf_op jit(solution)/shard_map/ppermute | solution.py:543
  135.8 6.6 %collective-permute-start.34 = (bf16[96,768]{1,0:T(8,128)(2,1)S(1)}, bf16[96,768]{1,0:T(8,128)(2,1)S(1)}, u32[]{:S(2)}, u32[]{:S(2)}) collective-permute-start(bf16[96,768]{1,0:T(8,128)(2,1)S(1)} %get-tuple-element.183), channel_id=1, source_target_pairs={{0,4},{4,0},{8,12},{12,8},{16,20},{20,16},{24,28},{28,24},{1,5},{5... | collective-permute-start | bytes 442376 | tf_op jit(solution)/shard_map/ppermute | solution.py:543
  136.3 6.2 %collective-permute-start.35 = (bf16[96,768]{1,0:T(8,128)(2,1)S(1)}, bf16[96,768]{1,0:T(8,128)(2,1)S(1)}, u32[]{:S(2)}, u32[]{:S(2)}) collective-permute-start(bf16[96,768]{1,0:T(8,128)(2,1)S(1)} %get-tuple-element.179), channel_id=1, source_target_pairs={{0,8},{4,12},{8,0},{12,4},{16,24},{20,28},{24,16},{28,20},{1,9},{5... | collective-permute-start | bytes 442376 | tf_op jit(solution)/shard_map/ppermute | solution.py:543
  141.4 15.1 %copy-start = (f32[2,768]{1,0:T(2,128)S(1)}, f32[2,768]{1,0:T(2,128)}, u32[]{:S(2)}) copy-start(f32[2,768]{1,0:T(2,128)} %refs_16_.1) | copy-start | bytes 18436
  141.4 15.1 %copy-start.1 = (f32[32,3]{0,1:T(4,128)S(1)}, f32[32,3]{0,1:T(4,128)}, u32[]{:S(2)}) copy-start(f32[32,3]{0,1:T(4,128)} %param.41) | copy-start | bytes 1156
  141.4 15.1 %copy-start.2 = (f32[2,768]{1,0:T(2,128)S(1)}, f32[2,768]{1,0:T(2,128)}, u32[]{:S(2)}) copy-start(f32[2,768]{1,0:T(2,128)} %refs_17_.1) | copy-start | bytes 18436
  141.4 15.1 %copy-start.3 = (f32[2,768]{1,0:T(2,128)S(1)}, f32[2,768]{1,0:T(2,128)}, u32[]{:S(2)}) copy-start(f32[2,768]{1,0:T(2,128)} %refs_18_.1) | copy-start | bytes 18436
  141.4 15.1 %copy-start.4 = (f32[32,3]{0,1:T(4,128)S(1)}, f32[32,3]{0,1:T(4,128)}, u32[]{:S(2)}) copy-start(f32[32,3]{0,1:T(4,128)} %param.42) | copy-start | bytes 1156
  141.4 15.1 %copy-start.5 = (f32[32,3]{0,1:T(4,128)S(1)}, f32[32,3]{0,1:T(4,128)}, u32[]{:S(2)}) copy-start(f32[32,3]{0,1:T(4,128)} %param.43) | copy-start | bytes 1156

commit v3 on v2

v3 whole, which is shorter than its diff:
```python
import functools
import math

import jax
import jax.numpy as jnp
from jax import lax
from jax.experimental import pallas as pl
from jax.experimental.pallas import tpu as pltpu
from jax.sharding import PartitionSpec as P

HEADS = 12
HDIM = 64
BUCKETS = 32
LEN = 512
BLK = 128
WIN = LEN + BLK
SMALL = 16


eps_norm = 1e-06
clip_norm = 1.0
beta_one = 0.9
beta_two = 0.999
adam_eps = 1e-08
decay_rate = 0.01
adam_step = 10.0
mask_fill = -1000000000.0
rate_small = 0.02
rate_large = 0.5
gelu_coef = 0.044715
root_coef = math.sqrt(2.0 / math.pi)

f32 = jnp.float32
bf16 = jnp.bfloat16
sds = jax.ShapeDtypeStruct


def dot_nn(a, b):
    return lax.dot_general(a, b, (((1,), (0,)), ((), ())), preferred_element_type=f32)


def dot_nt(a, b):
    return lax.dot_general(a, b, (((1,), (1,)), ((), ())), preferred_element_type=f32)


def dot_tn(a, b):
    return lax.dot_general(a, b, (((0,), (0,)), ((), ())), preferred_element_type=f32)


def after(value, *deps):
    return lax.optimization_barrier((value, *deps))[0]


def call(body, outs, args, name, hbm=(), scratch=(), limit=16, behind=()):
    spaces = [pl.ANY if i in hbm else pltpu.VMEM for i in range(len(args))]
    args = [after(args[0], *behind), *args[1:]] if behind else args
    args = [
        pltpu.with_memory_space_constraint(a, pltpu.HBM) if i in hbm else a for i, a in enumerate(args)
    ]
    return pl.pallas_call(
        body,
        out_shape=tuple(outs),
        in_specs=[pl.BlockSpec(memory_space=space) for space in spaces],
        out_specs=tuple(
            pl.BlockSpec(memory_space=pl.ANY if hasattr(o, "memory_space") else pltpu.VMEM) for o in outs
        ),
        scratch_shapes=list(scratch),
        compiler_params=pltpu.CompilerParams(vmem_limit_bytes=limit << 20),
        cost_estimate=pl.CostEstimate(flops=0, bytes_accessed=0, transcendentals=0),
        name=name,
    )(*args)


def to_hbm(staged, out, sem):
    copy = pltpu.make_async_copy(staged, out, sem)
    copy.start()
    copy.wait()


def assemble(into, blocks, start_col=0):
    cols = slice(start_col, start_col + into.shape[1])
    if len(blocks) == 1:
        into[...] = blocks[0][:, cols]
        return
    me = lax.axis_index("dp")
    rows = blocks[0].shape[0]
    for e, block in enumerate(blocks):
        start = pl.multiple_of((me ^ e) * rows, 32)
        into[pl.ds(start, rows), :] = block[:, cols]


def spread(grad, outs, order=(1, 2, 4)):
    if len(outs) == 1:
        outs[0][...] = grad[...].astype(bf16)
        return
    me = lax.axis_index("dp")
    rows = outs[0].shape[1]
    keep, *send = outs
    for b in range(2):
        for k in range(4):
            out, at = (keep, k) if b == 0 else (send[0], k) if len(send) == 1 else (send[1 - (k >> 1)], k & 1)
            apart = b * order[0] ^ (k >> 1) * order[1] ^ (k & 1) * order[2]
            start = pl.multiple_of((me ^ apart) * rows, 32)
            block = grad[pl.ds(start, rows), :].astype(bf16)
            if len(out.shape) == 2:
                out[at * rows : (at + 1) * rows, :] = block
            else:
                out[at] = block


def spread_shapes(dp, width, cols, lengths):
    if dp == 8:
        return [sds((n, width // dp, cols), bf16) for n in lengths]
    return [sds((width, cols), bf16)]


def half_rows():
    core = lax.axis_index("tp") & 1
    for half in range(2):
        for at in range(2):
            start = pl.multiple_of(((core ^ half) + 2 * at) * BLK, BLK)
            yield half, at, pl.ds(start, BLK)


def pack_kernel(qkv, out, down, ffn_in, packed, packed_ffn, *scratch):
    *landed, sems = scratch
    copies = [
        pltpu.make_async_copy(source, to, sems.at[i])
        for i, (source, to) in enumerate(zip((qkv, out, down, ffn_in), landed))
    ]
    for copy in copies:
        copy.start()
    local = out.shape[1]
    copies[0].wait()
    copies[1].wait()
    for part in range(3):
        packed[:, part * local : (part + 1) * local] = landed[0][part].astype(bf16)
    packed[:, 3 * local :] = landed[1][...].astype(bf16)
    width = down.shape[1]
    for i in (2, 3):
        copies[i].wait()
        packed_ffn[:, (i - 2) * width : (i - 1) * width] = landed[i][...].astype(bf16)


def prep_kernel(
    seg_in, table_in, bucket_in, x_in, gains_in, dy_in, act, act_t, bias, bucket, x, gains, dy, seg, table, ids, sems
):
    sources = (x_in, gains_in, bucket_in, seg_in, table_in, dy_in)
    copies = [
        pltpu.make_async_copy(source, to, sems.at[i])
        for i, (source, to) in enumerate(zip(sources, (x, gains, ids, seg, table, dy)))
    ]
    for copy in copies:
        copy.start()
    copies[0].wait()
    copies[1].wait()
    values = x[...].astype(f32)
    scale = lax.rsqrt(jnp.mean(values * values, axis=-1, keepdims=True) + eps_norm)
    low = (values * scale * gains[0:1, :]).astype(bf16)
    act[...] = low
    act_t[...] = low.T
    for copy in copies[2:]:
        copy.wait()
    ends = [seg[0, 0]]
    for k in (1, 2):
        ends.append(ends[-1] + seg[0, k])

    def segment_of(position):
        return sum((position >= end).astype(jnp.int32) for end in ends)

    seg_cols = segment_of(lax.broadcasted_iota(jnp.int32, (1, LEN), 1))
    heads = bias.shape[0]
    bucket[...] = jnp.zeros_like(bucket)
    bucket[:, : 2 * LEN - 1] = ids[...]
    lines = []
    for h in range(heads):
        line = jnp.zeros((1, 2 * LEN), f32)
        for b in range(BUCKETS):
            line = jnp.where(bucket[...] == b, table[h, b], line)
        lines.append(line)
    for r in range(LEN // BLK):
        seg_rows = segment_of(lax.broadcasted_iota(jnp.int32, (BLK, 1), 0) + r * BLK)
        visible = seg_rows == seg_cols
        low_at = LEN - BLK - r * BLK
        for h in range(heads):
            window = jnp.broadcast_to(lines[h][:, low_at : low_at + WIN], (BLK, WIN))
            turned = pltpu.roll(window, 1, 1, stride=1, stride_axis=0)
            bias[h, r * BLK : (r + 1) * BLK, :] = jnp.where(visible, turned[:, BLK:], mask_fill)


def attend_kernel(n_blocks, act, bias, *rest):
    blocks = rest[:n_blocks]
    weights, qkv, prob, mixed, keep, send = rest[n_blocks:]
    assemble(weights, blocks)
    width = qkv.shape[1] // 3
    qkv[...] = dot_nn(act[...], weights[:, : 3 * width]).astype(bf16)
    for h in range(bias.shape[0]):
        cols = slice(h * HDIM, (h + 1) * HDIM)
        query, key, value = (qkv[:, s * width + h * HDIM : s * width + (h + 1) * HDIM] for s in range(3))
        scores = dot_nt(query, key) + bias[h]
        top = jnp.max(scores, axis=-1, keepdims=True)
        exps = jnp.exp(scores - top)
        total = jnp.sum(exps, axis=-1, keepdims=True)
        low = (exps * (1.0 / total)).astype(bf16)
        prob[h] = low
        mixed[:, cols] = dot_nn(low, value).astype(bf16)
    out_cols = weights[:, 3 * width :]
    for half, at, rows in half_rows():
        to = send if half else keep
        to[at * BLK : (at + 1) * BLK, :] = dot_nt(mixed[rows, :], out_cols).astype(bf16)


def ffn_kernel(n_blocks, x, gains, dy, own_a, own_b, other_a, other_b, *rest):
    blocks = rest[:n_blocks]
    resid, act, hidden, pre_grad, keep, send, down, weights, hidden_grad = rest[n_blocks:]
    assemble(down, blocks)
    assemble(weights, blocks, down.shape[1])
    hidden_grad[...] = dot_nn(dy[...], down[...])
    for half, at, rows in half_rows():
        here = slice(at * BLK, (at + 1) * BLK)
        attn = ((own_a, own_b), (other_a, other_b))[half][at]
        values = x[rows, :].astype(f32) + attn[...].astype(f32)
        resid[rows, :] = values
        scale = lax.rsqrt(jnp.mean(values * values, axis=-1, keepdims=True) + eps_norm)
        low = (values * scale * gains[1:2, :]).astype(bf16)
        act[rows, :] = low
        u = dot_nn(low, weights[...])
        square = u * u
        tanh_part = jnp.tanh(root_coef * (u + gelu_coef * square * u))
        hidden[rows, :] = (0.5 * u * (1.0 + tanh_part)).astype(bf16)
        inner = root_coef * (1.0 + 3.0 * gelu_coef * square)
        slope = 0.5 * (1.0 + tanh_part) + 0.5 * u * (1.0 - tanh_part * tanh_part) * inner
        du = (hidden_grad[rows, :] * slope).astype(bf16)
        pre_grad[rows, :] = du
        (send if half else keep)[here, :] = dot_nt(du, weights[...]).astype(bf16)


def row_products(weights, grad):
    products = weights.astype(f32) * grad
    width = grad.shape[1]
    folded = sum(products[:, c : c + BLK] for c in range(0, width - BLK + 1, BLK))
    if width % BLK:
        rest = products[:, width - width % BLK :]
        wide = jnp.zeros((grad.shape[0], BLK - width % BLK), f32)
        folded = folded + jnp.concatenate([rest, wide], axis=1)
    return jnp.sum(folded.T, axis=0, keepdims=True)


def down_grad_kernel(order, left, right, *rest):
    outs, grad = rest[:-1], rest[-1]
    grad[...] = dot_tn(left[...], right[...])
    spread(grad, outs, order)


def in_grad_kernel(order, left, right, weights, gains, *rest):
    *outs, gain_part, grad = rest
    grad[...] = dot_tn(left[...], right[...])
    spread(grad, outs, order)
    gain_part[...] = row_products(weights[...], grad[...]) / gains[1:2, :]


def attend_back_kernel(
    n_outs, resid, dy, gains, own, other, weights, qkv, prob, mixed, act_t, bucket, gain_two, *rest
):
    outs = rest[:n_outs]
    share_grad, small, proj_grad, resid_low, grad, diag = rest[n_outs:]
    chip = lax.axis_index("tp") >> 1
    width = qkv.shape[1] // 3
    for half, at, rows in half_rows():
        here = slice(at * BLK, (at + 1) * BLK)
        act_grad = (other if half else own)[here, :].astype(f32)
        values = resid[rows, :]
        scale = lax.rsqrt(jnp.mean(values * values, axis=-1, keepdims=True) + eps_norm)
        normed = values * scale
        normal_grad = act_grad * gains[1:2, :]
        mean_part = jnp.mean(normal_grad * normed, axis=-1, keepdims=True)
        total = dy[rows, :].astype(f32) + scale * (normal_grad - normed * mean_part)
        resid_low[rows, :] = total.astype(bf16)
        if half == 0:

            @pl.when(chip == at)
            def _():
                share_grad[...] = total

    mix_grad = dot_nn(resid_low[...], weights[:, 3 * width :]).astype(bf16)
    heads = prob.shape[0]
    row = lax.broadcasted_iota(jnp.int32, (BLK, BLK), 0)
    col = lax.broadcasted_iota(jnp.int32, (BLK, BLK), 1)
    flip = (row + col == BLK - 1).astype(f32).astype(bf16)
    diag[...] = jnp.zeros_like(diag)
    for h in range(heads):
        query, key, value = (qkv[:, s * width + h * HDIM : s * width + (h + 1) * HDIM] for s in range(3))
        grad_rows = mix_grad[:, h * HDIM : (h + 1) * HDIM]
        prob_grad = dot_nt(grad_rows, value)
        prob_here = prob[h].astype(f32)
        row_dot = jnp.sum(prob_here * prob_grad, axis=-1, keepdims=True)
        low = (prob_here * (prob_grad - row_dot)).astype(bf16)
        for r in range(LEN // BLK):
            flipped = dot_nn(flip, low[r * BLK : (r + 1) * BLK, :])
            wide = jnp.concatenate([flipped, jnp.zeros((BLK, BLK), f32)], axis=1)
            turned = pltpu.roll(wide, 0, 1, stride=1, stride_axis=0)
            low_at = LEN - BLK - r * BLK
            diag[h : h + 1, low_at : low_at + WIN] += jnp.sum(turned, axis=0, keepdims=True)
        for s, part in enumerate((dot_nn(low, key), dot_tn(low, query), dot_tn(prob[h], grad_rows))):
            proj_grad[:, s * width + h * HDIM : s * width + (h + 1) * HDIM] = part.astype(bf16)
    grad[:, : 3 * width] = dot_nn(act_t[...], proj_grad[...])
    grad[:, 3 * width :] = dot_tn(resid_low[...], mixed[...])
    onehot = (lax.broadcasted_iota(jnp.int32, (BUCKETS, 2 * LEN), 0) == bucket[...]).astype(f32)
    by_bucket = lax.dot_general(
        diag[...],
        onehot,
        (((1,), (1,)), ((), ())),
        precision=lax.Precision.HIGHEST,
        preferred_element_type=f32,
    )
    first = lax.axis_index("tp") * heads
    cells = [
        sum(jnp.where(first + h == head, by_bucket[h : h + 1, :], 0.0) for h in range(heads))
        for head in range(HEADS)
    ]
    model = gains.shape[1]
    cells.append(jnp.zeros((1, model - HEADS * BUCKETS), f32))
    gain_one = row_products(weights[:, : 3 * width], grad[:, : 3 * width]) / gains[0:1, :]
    lines = (gain_one, gain_two[...], jnp.concatenate(cells, axis=1), jnp.zeros((SMALL - 3, model), f32))
    whole = jnp.concatenate(lines, axis=0)
    if n_outs == 1:
        spread(grad, outs)
        small[...] = whole
        return
    keep, low = outs
    rows = keep.shape[1]
    spread(grad, (keep, small, low))
    small[2 * rows :, :] = whole.astype(bf16)


def ffn_out_kernel(hidden, down, keep, send):
    for half, at, rows in half_rows():
        to = send if half else keep
        to[at * BLK : (at + 1) * BLK, :] = dot_nt(hidden[rows, :], down[...]).astype(bf16)


def act_grad_kernel(proj_grad, weights, keep, *send):
    width = proj_grad.shape[1]
    for half, at, rows in half_rows():
        block = dot_nt(proj_grad[rows, :], weights[:, :width]).astype(bf16)
        if half:
            send[at][...] = block
        else:
            keep[at * BLK : (at + 1) * BLK, :] = block


def core_add_kernel(ffn_keep, ffn_got, act_keep, act_got_a, act_got_b, mine, theirs):
    chip = lax.axis_index("tp") >> 1
    for at in range(2):
        here = slice(at * BLK, (at + 1) * BLK)
        ffn = (ffn_keep[here, :].astype(f32) + ffn_got[here, :].astype(f32)).astype(bf16)
        got = (act_got_a, act_got_b)[at]
        act = (act_keep[here, :].astype(f32) + got[...].astype(f32)).astype(bf16)

        @pl.when(chip == at)
        def _():
            mine[:BLK, :] = ffn
            mine[BLK:, :] = act

        @pl.when(chip != at)
        def _():
            theirs[:BLK, :] = ffn
            theirs[BLK:, :] = act


def share_out_kernel(resid, x, gains, share_grad, mine, got, block_out, input_grad):
    share = pl.ds(pl.multiple_of(lax.axis_index("tp") * BLK, BLK), BLK)
    first, second = slice(0, BLK), slice(BLK, 2 * BLK)
    ffn = mine[first, :].astype(f32) + got[first, :].astype(f32)
    block_out[...] = (resid[share, :] + ffn).astype(bf16)
    values = x[share, :].astype(f32)
    scale = lax.rsqrt(jnp.mean(values * values, axis=-1, keepdims=True) + eps_norm)
    normed = values * scale
    normal_grad = (mine[second, :].astype(f32) + got[second, :].astype(f32)) * gains[0:1, :]
    mean_part = jnp.mean(normal_grad * normed, axis=-1, keepdims=True)
    input_grad[...] = share_grad[...] + scale * (normal_grad - normed * mean_part)


def add_kernel(one, two, out):
    out[...] = (one[...].astype(f32) + two[...].astype(f32)).astype(bf16)


def split_add_kernel(one, two, *outs):
    for i, out in enumerate(outs):
        rows = slice(i * BLK, (i + 1) * BLK)
        out[...] = (one[rows, :].astype(f32) + two[rows, :].astype(f32)).astype(bf16)


def pair_add_kernel(keep, got, mine, theirs):
    for k in range(4):
        to = theirs if k >= 2 else mine
        to[k % 2] = (keep[k].astype(f32) + got[k].astype(f32)).astype(bf16)


def next_add_kernel(keep, got, mine, theirs):
    for k, to in enumerate((mine, theirs)):
        to[...] = (keep[k].astype(f32) + got[k].astype(f32)).astype(bf16)


def last_high_kernel(keep, sent, got, out):
    rows = keep.shape[1]
    for k in range(2):
        here = slice(k * rows, (k + 1) * rows)
        out[here, :] = (keep[k + 2].astype(f32) + got[here, :].astype(f32)).astype(bf16)
    small = slice(2 * rows, None)
    out[small, :] = (sent[small, :].astype(f32) + got[small, :].astype(f32)).astype(bf16)


def last_late_kernel(keep, got_low, sent, got, mine, out):
    rows = keep.shape[1]
    first, second, small = slice(0, rows), slice(rows, 2 * rows), slice(2 * rows, None)
    mine[...] = keep[0].astype(f32) + got_low[0].astype(f32) + got[first, :].astype(f32)
    block = keep[1].astype(f32) + got_low[1].astype(f32) + got[second, :].astype(f32)
    out[:rows, :] = block.astype(bf16)
    out[rows:, :] = (sent[small, :].astype(f32) + got[small, :].astype(f32)).astype(bf16)


def fold(values):
    rows, cols = values.shape
    squares = values * values
    lanes = sum(squares[:, c : c + BLK] for c in range(0, cols, BLK))
    return jnp.sum(lanes, axis=0, keepdims=True)


def sum_kernel(n_parts, *rest):
    parts, (grad, squares) = rest[:n_parts], rest[n_parts:]
    total = sum(part[...].astype(f32) for part in parts)
    grad[...] = total
    squares[...] = fold(total)


def last_sum_kernel(direct, extra_a, extra_b, *rest):
    *parts, grad, out, payload, lines, sem = rest
    if direct:
        mine, sent, got = parts
        rows = mine.shape[0]
        total = mine[...] + got[:rows, :].astype(f32)
        small = sent[rows:, :].astype(f32) + got[rows:, :].astype(f32)
    else:
        total, small = (part[...] for part in parts)
    grad[...] = total
    per_row = total.shape[1] // BLK
    lines[...] = jnp.zeros_like(lines)
    for line in range(SMALL):
        row, at = divmod(line, per_row)
        lines[line : line + 1, :] = small[row : row + 1, at * BLK : (at + 1) * BLK]
    me = lax.axis_index("dp")
    start = pl.multiple_of(jnp.minimum(2 * me, SMALL), 2)
    squares = fold(total) + extra_a[...] + extra_b[...]
    two = lines[pl.ds(start, 2), :]
    told = jnp.concatenate((squares, two[0:1, :], two[1:2, :]), axis=1)
    payload[...] = jnp.broadcast_to(told[None], payload.shape)
    to_hbm(payload, out, sem)


def adamw(weight, gradient, moment_one, moment_two, rate):
    one_new = beta_one * moment_one + (1.0 - beta_one) * gradient
    two_new = beta_two * moment_two + (1.0 - beta_two) * gradient * gradient
    one_hat = one_new / (1.0 - beta_one**adam_step)
    two_hat = two_new / (1.0 - beta_two**adam_step)
    weight_new = weight - rate * (one_hat / (jnp.sqrt(two_hat) + adam_eps) + decay_rate * weight)
    return (weight_new, one_new, two_new)


def adam_kernel(*refs):
    told, grad_qkvo, grad_in, grad_down, *state_in = refs[:22]
    norm_ref, *matrices, gains_a, gains_b, gains_c, gains_grad, table_a, table_b, table_c = refs[22:46]
    state, staged = refs[46:64], refs[64:80]
    gains_sum, table_grad, sems_in, sems = refs[80:]
    fetches = [pltpu.make_async_copy(state_in[i], state[i], sems_in.at[i]) for i in range(18)]
    for i in (*range(6, 12), *range(6), *range(12, 18)):
        fetches[i].start()
    gains_o, table_o = (gains_a, gains_b, gains_c), (table_a, table_b, table_c)
    qkv, out, ffn_in, ffn_down, gains, table = (state[i : i + 3] for i in range(0, 18, 3))
    qkv_o, out_o, in_o, down_o = (staged[i : i + 4] for i in range(0, 16, 4))
    tp = lax.axis_size("tp")
    squares = told[0, :, :BLK]
    for i in range(1, told.shape[0]):
        squares = squares + told[i, :, :BLK]
    model = gains_sum.shape[1]
    per_row = model // BLK
    per_line = BLK // BUCKETS
    first = lax.axis_index("tp") * table_grad.shape[0]
    for line in range(2 * per_row + HEADS // per_line):
        index, at = divmod(line, 2)
        cols = slice((at + 1) * BLK, (at + 2) * BLK)
        value = told[index * tp, :, cols]
        for i in range(1, tp):
            value = value + told[index * tp + i, :, cols]
        squares = squares + value * value
        row, at = divmod(line, per_row)
        if row < 2:
            gains_sum[row : row + 1, at * BLK : (at + 1) * BLK] = value
            continue
        for i in range(per_line):
            head = at * per_line + i
            cell = value[:, i * BUCKETS : (i + 1) * BUCKETS]
            for h in range(table_grad.shape[0]):

                @pl.when(first + h == head)
                def _():
                    table_grad[h : h + 1, :] = cell

    norm = jnp.sqrt(jnp.sum(squares, axis=1, keepdims=True))
    norm_ref[...] = norm
    factor = clip_norm / jnp.maximum(norm, clip_norm)

    def update(state_refs, gradient, to, rate, at=...):
        new = adamw(state_refs[0][at], gradient * factor, state_refs[1][at], state_refs[2][at], rate)
        for ref, value in zip(to, new):
            ref[at] = value
        if len(to) == 4:
            to[3][at] = new[0].astype(bf16)

    copies = []

    def arrived(first):
        for i in range(first, first + 3):
            fetches[i].wait()

    def send(first):
        for i in range(first, first + 4):
            copies.append(pltpu.make_async_copy(staged[i], matrices[i], sems.at[i]))
            copies[-1].start()

    arrived(6)
    update(ffn_in, grad_in[...], in_o, rate_small)
    send(8)
    arrived(9)
    update(ffn_down, grad_down[...], down_o, rate_small)
    send(12)
    arrived(0)
    width = qkv[0].shape[2]
    for part in range(3):
        update(qkv, grad_qkvo[:, part * width : (part + 1) * width], qkv_o, rate_small, part)
    send(0)
    arrived(3)
    update(out, grad_qkvo[:, 3 * width :], out_o, rate_large)
    send(4)
    arrived(12)
    update(gains, gains_sum[...], gains_o, rate_large)
    gains_grad[...] = gains_sum[...] * factor
    arrived(15)
    update(table, table_grad[...], table_o, rate_large)
    for copy in copies:
        copy.wait()


def on_device(
    dp,
    inputs,
    cotangent,
    seg_lengths,
    bucket_ids,
    qkv_weight,
    qkv_first,
    qkv_second,
    out_weight,
    out_first,
    out_second,
    ffn_in_weight,
    ffn_in_first,
    ffn_in_second,
    ffn_down_weight,
    ffn_down_first,
    ffn_down_second,
    norm_gains,
    gains_first,
    gains_second,
    bias_table,
    table_first,
    table_second,
):
    tokens, model = inputs.shape
    rows, local = out_weight.shape
    hidden = ffn_in_weight.shape[1]
    heads_here = local // HDIM
    tp = lax.axis_size("tp")
    packed_cols = 4 * local
    direct = dp == 8

    def swap_dp(value, distance):
        return lax.ppermute(value, "dp", [(i, i ^ distance) for i in range(dp)])

    def swap_tp(value, distance):
        return lax.ppermute(value, "tp", [(i, i ^ distance) for i in range(tp)])

    def add(one, two, behind=()):
        (out,) = call(add_kernel, [sds(one.shape, bf16)], (one, two), "add", limit=4, behind=behind)
        return out

    def pair_add(keep, got, behind):
        outs = [sds((2, *keep.shape[1:]), bf16)] * 2
        return call(pair_add_kernel, outs, (keep, got), "pair_add", limit=4, behind=behind)

    def next_add(keep, got, behind):
        outs = [sds(keep.shape[1:], bf16)] * 2
        return call(next_add_kernel, outs, (keep, got), "next_add", limit=4, behind=behind)

    half_shape = [sds((tokens // 2, model), bf16)] * 2
    matrices = (qkv_weight, out_weight, ffn_down_weight, ffn_in_weight)
    packed, packed_ffn = call(
        pack_kernel,
        [sds((rows, packed_cols), bf16), sds((rows, 2 * hidden), bf16)],
        matrices,
        "pack",
        hbm=(0, 1, 2, 3),
        scratch=[*(pltpu.VMEM(m.shape, f32) for m in matrices), pltpu.SemaphoreType.DMA((4,))],
    )
    ids = bucket_ids[None, :]
    act_one, act_one_t, bias, bucket_row, inputs, norm_gains_here, cotangent = call(
        prep_kernel,
        [
            sds((tokens, model), bf16),
            sds((model, tokens), bf16),
            sds((heads_here, LEN, LEN), f32),
            sds((1, 2 * LEN), jnp.int32),
            sds(inputs.shape, bf16),
            sds(norm_gains.shape, f32),
            sds(inputs.shape, bf16),
        ],
        (seg_lengths, bias_table.T, ids, inputs, norm_gains, cotangent),
        "prep",
        hbm=range(6),
        scratch=[
            pltpu.SMEM(seg_lengths.shape, jnp.int32),
            pltpu.SMEM((heads_here, BUCKETS), f32),
            pltpu.VMEM(ids.shape, jnp.int32),
            pltpu.SemaphoreType.DMA((6,)),
        ],
    )
    if direct:
        one, two = swap_dp(packed, 2), swap_dp(packed, 4)
        own, ffn_own = swap_dp(after(packed, act_one), 1), swap_dp(after(packed_ffn, act_one), 1)
        one_across = swap_dp(one, 1)
        three = swap_dp(two, 2)
        ffn_two = swap_dp(after(packed_ffn, two), 4)
        two_across = swap_dp(two, 1)
        ffn_one = swap_dp(after(packed_ffn, three, own, one_across), 2)
        three_across = swap_dp(three, 1)
        qkvo_blocks = [packed, own, one, one_across, two, two_across, three, three_across]
        ffn_three = swap_dp(after(ffn_two, ffn_one), 2)
        ffn_blocks = [packed_ffn, ffn_own, ffn_one, swap_dp(after(ffn_own, ffn_three), 2)]
        for block in (ffn_two, ffn_three):
            ffn_blocks += [block, swap_dp(block, 1)]
        bias = after(bias, ffn_own, ffn_two)
        ffn_early = (ffn_blocks[5], ffn_three)
    else:
        qkvo_blocks = [lax.all_gather(packed, "dp", axis=0, tiled=True)]
        ffn_blocks = ffn_early = [lax.all_gather(packed_ffn, "dp", axis=0, tiled=True)]
    n_blocks = len(qkvo_blocks)

    weights_one, qkv, prob, mixed, attn_keep, attn_send = call(
        functools.partial(attend_kernel, n_blocks),
        [
            sds((model, packed_cols), bf16),
            sds((tokens, 3 * local), bf16),
            sds((heads_here, LEN, LEN), bf16),
            sds((tokens, local), bf16),
            *half_shape,
        ],
        (act_one, bias, *qkvo_blocks),
        "attend",
    )
    half_blocks = [sds((BLK, model), bf16)] * 2
    attn_first = call(
        split_add_kernel, half_blocks, (attn_keep, swap_tp(attn_send, 1)), "split_add", limit=4
    )
    attn_own = [add(first, swap_tp(first, 2), ffn_early) for first in attn_first]
    attn_sums = (*attn_own, *(swap_tp(own, 1) for own in attn_own))
    resid, act_two, hidden_act, pre_grad, back_keep, back_send, down_full, in_full = call(
        functools.partial(ffn_kernel, n_blocks),
        [
            sds((tokens, model), f32),
            sds((tokens, model), bf16),
            sds((tokens, hidden), bf16),
            sds((tokens, hidden), bf16),
            *half_shape,
            *[sds((model, hidden), bf16)] * 2,
        ],
        (inputs, norm_gains_here, cotangent, *attn_sums, *ffn_blocks),
        "ffn",
        scratch=[pltpu.VMEM((tokens, hidden), f32)],
    )
    back_first = add(back_keep, swap_tp(back_send, 1))
    back_got = swap_tp(back_first, 2)
    down_order, in_order = (1, 2, 4), (2, 4, 1)
    grad_scratch = [pltpu.VMEM((model, hidden), f32)]
    down_parts = call(
        functools.partial(down_grad_kernel, down_order),
        spread_shapes(dp, model, hidden, (4, 4)),
        (cotangent, after(hidden_act, back_first)),
        "down_grad",
        scratch=grad_scratch,
    )
    *in_parts, gain_two_part = call(
        functools.partial(in_grad_kernel, in_order),
        [*spread_shapes(dp, model, hidden, (4, 4)), sds((1, model), f32)],
        (act_two, after(pre_grad, down_parts[0]), in_full, norm_gains_here),
        "in_grad",
        scratch=grad_scratch,
    )
    ffn_keep, ffn_send = call(
        ffn_out_kernel, half_shape, (hidden_act, down_full), "ffn_out", behind=(gain_two_part,)
    )
    back_sum = add(back_first, back_got, (ffn_keep,))
    everyone = dp * tp
    qkvo_shapes = spread_shapes(dp, model, packed_cols, (4, 2))
    small_shape = sds((2 * rows + SMALL, model), bf16) if direct else sds((SMALL, model), f32)
    *qkvo_parts, share_grad, small, proj_grad = call(
        functools.partial(attend_back_kernel, len(qkvo_shapes)),
        [*qkvo_shapes, sds((BLK, model), f32), small_shape, sds((tokens, 3 * local), bf16)],
        (
            resid,
            cotangent,
            norm_gains_here,
            back_sum,
            swap_tp(back_sum, 1),
            weights_one,
            qkv,
            prob,
            mixed,
            act_one_t,
            bucket_row,
            gain_two_part,
        ),
        "attend_back",
        scratch=[
            pltpu.VMEM((tokens, model), bf16),
            pltpu.VMEM((model, packed_cols), f32),
            pltpu.VMEM((8, 2 * LEN), f32),
        ],
    )
    def summed(parts, behind):
        return call(
            functools.partial(sum_kernel, len(parts)),
            [sds((rows, parts[0].shape[1]), f32), sds((1, BLK), f32)],
            parts,
            "sum_parts",
            limit=4,
            behind=behind,
        )

    def act_shares(behind):
        keep, *send = call(
            act_grad_kernel,
            [half_shape[0], *half_blocks],
            (proj_grad, weights_one),
            "act_grad",
            behind=behind,
        )
        return keep, [swap_tp(part, 1) for part in send]

    def share_sums(keep, got, behind):
        outs = [sds((2 * BLK, model), bf16)] * 2
        args = (ffn_keep, swap_tp(ffn_send, 1), keep, *got)
        return call(core_add_kernel, outs, args, "core_add", limit=4, behind=behind)

    if direct:
        keep, send_low = qkvo_parts
        down_keep, down_send = down_parts
        in_keep, in_send = in_parts
        in_one = pair_add(in_keep, swap_dp(in_send, in_order[0]), (proj_grad,))
        down_one = pair_add(down_keep, swap_dp(down_send, down_order[0]), in_one)
        got_high = swap_dp(after(small, *down_one), 1)
        share_own, share_got = act_shares(down_one)
        (high,) = call(
            last_high_kernel, [small_shape], (keep, small, got_high), "last_high", limit=4, behind=(share_own,)
        )
        got_low = swap_dp(after(send_low, high), 1)
        mine, theirs = share_sums(share_own, share_got, (high,))
        down_two = next_add(down_one[0], swap_dp(down_one[1], down_order[1]), (mine,))
        in_two = next_add(in_one[0], swap_dp(in_one[1], in_order[1]), down_two)
        down_grad, down_squares = summed((down_two[0], swap_dp(down_two[1], down_order[2])), in_two)
        in_grad, in_squares = summed((in_two[0], swap_dp(in_two[1], in_order[2])), (down_grad,))
        last, late = call(
            last_late_kernel,
            [sds((rows, packed_cols), f32), sds((rows + SMALL, packed_cols), bf16)],
            (keep, got_low, high, swap_dp(high, 2)),
            "last_late",
            limit=4,
            behind=(in_grad,),
        )
        last_parts = (last, late, swap_dp(late, 4))
        share_behind = (late,)
    else:
        qkvo_sums, down_sums, in_sums = (
            (lax.psum_scatter(p[0].astype(f32), "dp", scatter_dimension=0, tiled=True),)
            for p in (qkvo_parts, down_parts, in_parts)
        )
        last_parts = (*qkvo_sums, lax.psum(small, "dp"))
        down_grad, down_squares = summed(down_sums, ())
        in_grad, in_squares = summed(in_sums, ())
        mine, theirs = share_sums(*act_shares(()), ())
        share_behind = ()
    block_out, input_grad = call(
        share_out_kernel,
        [sds((BLK, model), bf16), sds((BLK, model), f32)],
        (resid, inputs, norm_gains_here, share_grad, mine, swap_tp(theirs, 2)),
        "share_out",
        behind=share_behind,
    )
    qkvo_grad, payload = call(
        functools.partial(last_sum_kernel, direct),
        [sds((rows, packed_cols), f32), pltpu.HBM((everyone, 1, 3 * BLK), f32)],
        (down_squares, in_squares, *last_parts),
        "last_sum",
        scratch=[
            pltpu.VMEM((everyone, 1, 3 * BLK), f32),
            pltpu.VMEM((SMALL + 8, BLK), f32),
            pltpu.SemaphoreType.DMA,
        ],
        behind=(block_out,),
    )
    told = lax.all_to_all(payload, ("dp", "tp"), 0, 0)
    matrices = (
        qkv_weight,
        qkv_first,
        qkv_second,
        out_weight,
        out_first,
        out_second,
        ffn_in_weight,
        ffn_in_first,
        ffn_in_second,
        ffn_down_weight,
        ffn_down_first,
        ffn_down_second,
    )
    vectors = (norm_gains, gains_first, gains_second, bias_table.T, table_first.T, table_second.T)
    state = matrices + vectors
    shapes = [(m.shape, kind) for m in matrices[::3] for kind in (f32, f32, f32, bf16)]
    norm, *updated = call(
        adam_kernel,
        [
            sds((1, 1), f32),
            *(pltpu.HBM(shape, kind) for shape, kind in shapes),
            *[sds(norm_gains.shape, f32)] * 4,
            *[sds((heads_here, BUCKETS), f32)] * 3,
        ],
        (told, qkvo_grad, in_grad, down_grad, *state),
        "adam",
        hbm=range(4, 22),
        scratch=[
            *(pltpu.VMEM(m.shape, f32) for m in state),
            *(pltpu.VMEM(shape, kind) for shape, kind in shapes),
            pltpu.VMEM(norm_gains.shape, f32),
            pltpu.VMEM((heads_here, BUCKETS), f32),
            pltpu.SemaphoreType.DMA((18,)),
            pltpu.SemaphoreType.DMA((16,)),
        ],
    )
    return (block_out, input_grad, norm.reshape(()), *updated[:-3], *(t.T for t in updated[-3:]))


def solution(mesh):
    row = P("dp", None)
    matrix = P("dp", "tp")
    stack = P(None, "dp", "tp")
    table = P(None, "tp")
    share = P(("dp", "tp"), None)
    in_specs = (
        *(row,) * 3,
        P(),
        *(stack,) * 3,
        *(matrix,) * 9,
        *(P(),) * 3,
        *(table,) * 3,
    )
    out_specs = (
        *(share,) * 2,
        P(),
        *(stack,) * 4,
        *(matrix,) * 12,
        *(P(),) * 4,
        *(table,) * 3,
    )
    return jax.shard_map(
        functools.partial(on_device, mesh.shape["dp"]),
        mesh=mesh,
        in_specs=in_specs,
        out_specs=out_specs,
        check_vma=False,
    )
```

time: 161 us -> 134 us (0.83)
  waiting for transfers between devices: 80.6 us -> 50.7 us
  starting transfers between devices: 37.1 us -> 41.6 us
    ppermute x27 -> x24, waiting for transfers between devices: 73.2 us -> 42.1 us  [swap_dp(): return lax.ppermute(value, 'dp', [(i, i ^ distance) for i in range(dp)])]
    ppermute x27 -> x24, starting transfers between devices: 31.9 us -> 35.4 us  [swap_dp(): return lax.ppermute(value, 'dp', [(i, i ^ distance) for i in range(dp)])]
    ppermute x10 -> x12, waiting for transfers between devices: 7.41 us -> 8.66 us  [swap_tp(): return lax.ppermute(value, 'tp', [(i, i ^ distance) for i in range(tp)])]
    ppermute x10 -> x12, starting transfers between devices: 5.18 us -> 6.19 us  [swap_tp(): return lax.ppermute(value, 'tp', [(i, i ^ distance) for i in range(tp)])]
    pallas_call x27 -> x26, Pallas kernels: 29.1 us -> 28.2 us  [call(): pl.pallas_call(body, out_shape=tuple(outs), in_specs=[pl.BlockSpec(memory...]
  transfers between devices with their start and end apart: 37 -> 36, of which waited for: 21 -> 20; matrix products, arithmetic and copies ran while one was open for 0% -> 0% of each run, Pallas kernels for 4% -> 14%
where the time goes in v3:
time: 134 us
  waiting for transfers between devices  50.7 us (38%)
  starting transfers between devices  41.6 us (31%)
  Pallas kernels  28.2 us (21%)
  blocking collectives  12 us (9%)
    ppermute x24, waiting for transfers between devices, swap_dp(): return lax.ppermute(value, 'dp', [(i, i ^ distance) for i in range(dp)])  42.1 us
    ppermute x24, starting transfers between devices, swap_dp(): return lax.ppermute(value, 'dp', [(i, i ^ distance) for i in range(dp)])  35.4 us
    pallas_call x26, Pallas kernels, call(): pl.pallas_call(body, out_shape=tuple(outs), in_specs=[pl.BlockSpec(memory...  28.2 us
    all_to_all x1, blocking collectives, on_device(): told = lax.all_to_all(payload, ('dp', 'tp'), 0, 0)  12 us
    ppermute x12, waiting for transfers between devices, swap_tp(): return lax.ppermute(value, 'tp', [(i, i ^ distance) for i in range(tp)])  8.66 us
    ppermute x12, starting transfers between devices, swap_tp(): return lax.ppermute(value, 'tp', [(i, i ^ distance) for i in range(tp)])  6.19 us
  transfers between devices with their start and end apart: 36, of which 20 were waited for; matrix products, arithmetic and copies ran while one was open for 0% of the time, Pallas kernels for 14%

profile of v3, /device:TPU:0, one launch (start us, length us, event | category | flops | bytes accessed | tf_op | source)
XLA Modules:
  0.0 133.6 jit_solution(12448728647306975596)
XLA Ops:
  0.7 1.2 pack.1
  1.9 4.1 %collective-permute-start.1 = (bf16[96,768]{1,0:T(8,128)(2,1)S(1)}, bf16[96,768]{1,0:T(8,128)(2,1)S(1)}, u32[]{:S(2)}, u32[]{:S(2)}) collective-permute-start(bf16[96,768]{1,0:T(8,128)(2,1)S(1)} %get-tuple-element.147.rest_0_), channel_id=1, source_target_pairs={{0,16},{4,20},{8,24},{12,28},{16,0},{20,4},{24,8},{28,12},{1,17},{... | collective-permute-start | bytes 442376 | tf_op jit(solution)/shard_map/ppermute | solution.py:588
  6.0 1.6 %collective-permute-start.4 = (bf16[96,768]{1,0:T(8,128)(2,1)S(1)}, bf16[96,768]{1,0:T(8,128)(2,1)S(1)}, u32[]{:S(2)}, u32[]{:S(2)}) collective-permute-start(bf16[96,768]{1,0:T(8,128)(2,1)S(1)} %get-tuple-element.147.rest_0_), channel_id=1, source_target_pairs={{0,8},{4,12},{8,0},{12,4},{16,24},{20,28},{24,16},{28,20},{1,9},{5... | collective-permute-start | bytes 442376 | tf_op jit(solution)/shard_map/ppermute | solution.py:588
  7.6 2.2 %prep.1 = (bf16[512,768]{1,0:T(8,128)(2,1)S(1)}, bf16[768,512]{1,0:T(8,128)(2,1)S(1)}, f32[3,512,512]{2,1,0:T(8,128)S(1)}, s32[1,1024]{1,0:T(1,128)S(1)}, bf16[5...) custom-call(s32[1,4]{1,0:T(1,128)} %seg_in.1, f32[3,32]{1,0:T(4,128)} %bitcast.8, ...), custom_call_target="tpu_custom_call" | custom-call | tf_op jit(solution)/shard_map/prep/pallas_call | solution.py:60
  9.8 1.6 %collective-permute-start = (bf16[96,1536]{1,0:T(8,128)(2,1)S(1)}, bf16[96,1536]{1,0:T(8,128)(2,1)S(1)}, u32[]{:S(2)}, u32[]{:S(2)}) collective-permute-start(bf16[96,1536]{1,0:T(8,128)(2,1)S(1)} %get-tuple-element.151.rest_0_), channel_id=1, source_target_pairs={{0,4},{4,0},{8,12},{12,8},{16,20},{20,16},{24,28},{28,24},{1,5},{5... | collective-permute-start | bytes 884744 | tf_op jit(solution)/shard_map/ppermute | solution.py:588
  11.4 1.8 %collective-permute-done.1.rest_4_ = bf16[96,768]{1,0:T(8,128)(2,1)S(1)} collective-permute-done((bf16[96,768]{1,0:T(8,128)(2,1)S(1)}, bf16[96,768]{1,0:T(8,128)(2,1)S(1)}, u32[]{:S(2)}, u32[]{:S(2)}) %collective-permute-start.1) | collective-permute-done | bytes 147488 | tf_op jit(solution)/shard_map/ppermute | solution.py:588
  13.7 1.5 %collective-permute-start.3 = (bf16[96,768]{1,0:T(8,128)(2,1)S(1)}, bf16[96,768]{1,0:T(8,128)(2,1)S(1)}, u32[]{:S(2)}, u32[]{:S(2)}) collective-permute-start(bf16[96,768]{1,0:T(8,128)(2,1)S(1)} %get-tuple-element.147.rest_0_), channel_id=1, source_target_pairs={{0,4},{4,0},{8,12},{12,8},{16,20},{20,16},{24,28},{28,24},{1,5},{5... | collective-permute-start | bytes 442376 | tf_op jit(solution)/shard_map/ppermute | solution.py:588
  15.2 3.4 %collective-permute-start.7 = (bf16[96,768]{1,0:T(8,128)(2,1)S(1)}, bf16[96,768]{1,0:T(8,128)(2,1)S(1)}, u32[]{:S(2)}, u32[]{:S(2)}) collective-permute-start(bf16[96,768]{1,0:T(8,128)(2,1)S(1)} %collective-permute-done.1.rest_4_), channel_id=1, source_target_pairs={{0,8},{4,12},{8,0},{12,4},{16,24},{20,28},{24,16},{28,20},{1,9},{5... | collective-permute-start | bytes 442376 | tf_op jit(solution)/shard_map/ppermute | solution.py:588
  19.2 2.8 %collective-permute-done.3.rest_1_ = bf16[96,768]{1,0:T(8,128)(2,1)S(1)} collective-permute-done((bf16[96,768]{1,0:T(8,128)(2,1)S(1)}, bf16[96,768]{1,0:T(8,128)(2,1)S(1)}, u32[]{:S(2)}, u32[]{:S(2)}) %collective-permute-start.3) | collective-permute-done | bytes 147488 | tf_op jit(solution)/shard_map/ppermute | solution.py:588
  22.0 2.5 %collective-permute-start.6 = (bf16[96,768]{1,0:T(8,128)(2,1)S(1)}, bf16[96,768]{1,0:T(8,128)(2,1)S(1)}, u32[]{:S(2)}, u32[]{:S(2)}) collective-permute-start(bf16[96,768]{1,0:T(8,128)(2,1)S(1)} %collective-permute-done.1.rest_4_), channel_id=1, source_target_pairs={{0,4},{4,0},{8,12},{12,8},{16,20},{20,16},{24,28},{28,24},{1,5},{5... | collective-permute-start | bytes 442376 | tf_op jit(solution)/shard_map/ppermute | solution.py:588
  25.4 1.6 %collective-permute-start.11 = (bf16[96,1536]{1,0:T(8,128)(2,1)S(1)}, bf16[96,1536]{1,0:T(8,128)(2,1)S(1)}, u32[]{:S(2)}, u32[]{:S(2)}) collective-permute-start(bf16[96,1536]{1,0:T(8,128)(2,1)S(1)} %get-tuple-element.151.rest_0_), channel_id=1, source_target_pairs={{0,8},{4,12},{8,0},{12,4},{16,24},{20,28},{24,16},{28,20},{1,9},{5... | collective-permute-start | bytes 884744 | tf_op jit(solution)/shard_map/ppermute | solution.py:588
  27.0 1.5 %collective-permute-done.2.rest_4_ = bf16[96,1536]{1,0:T(8,128)(2,1)S(1)} collective-permute-done((bf16[96,1536]{1,0:T(8,128)(2,1)S(1)}, bf16[96,1536]{1,0:T(8,128)(2,1)S(1)}, u32[]{:S(2)}, u32[]{:S(2)}) %collective-permute-start.2) | collective-permute-done | bytes 294944 | tf_op jit(solution)/shard_map/ppermute | solution.py:588
  29.1 1.6 %collective-permute-done.8.rest_7_ = bf16[96,768]{1,0:T(8,128)(2,1)S(1)} collective-permute-done((bf16[96,768]{1,0:T(8,128)(2,1)S(1)}, bf16[96,768]{1,0:T(8,128)(2,1)S(1)}, u32[]{:S(2)}, u32[]{:S(2)}) %collective-permute-start.8) | collective-permute-done | bytes 147488 | tf_op jit(solution)/shard_map/ppermute | solution.py:588
  30.7 3.1 %attend.1 = (bf16[768,768]{1,0:T(8,128)(2,1)S(1)}, bf16[512,576]{1,0:T(8,128)(2,1)S(1)}, bf16[3,512,512]{2,1,0:T(8,128)(2,1)S(1)}, bf16[512,192]{1,0:T(8,128)(2,...) custom-call(bf16[512,768]{1,0:T(8,128)(2,1)S(1)} %get-tuple-element.140.act, ...), custom_call_target="tpu_custom_call" | custom-call | tf_op jit(solution)/shard_map/attend/pallas_call | solution.py:60
  33.8 0.9 collective-permute-done.11.rest_2_
  35.3 1.5 %collective-permute-start.10 = (bf16[96,1536]{1,0:T(8,128)(2,1)S(1)}, bf16[96,1536]{1,0:T(8,128)(2,1)S(1)}, u32[]{:S(2)}, u32[]{:S(2)}) collective-permute-start(bf16[96,1536]{1,0:T(8,128)(2,1)S(1)} %collective-permute-done.2.rest_4_), channel_id=1, source_target_pairs={{0,4},{4,0},{8,12},{12,8},{16,20},{20,16},{24,28},{28,24},{1,5},{5... | collective-permute-start | bytes 884744 | tf_op jit(solution)/shard_map/ppermute | solution.py:588
  36.9 1.6 %collective-permute-start.13 = (bf16[128,768]{1,0:T(8,128)(2,1)S(1)}, bf16[128,768]{1,0:T(8,128)(2,1)S(1)}, u32[]{:S(2)}, u32[]{:S(2)}) collective-permute-start(bf16[128,768]{1,0:T(8,128)(2,1)S(1)} %get-tuple-element.153.one), channel_id=1, source_target_pairs={{0,2},{1,3},{2,0},{3,1},{4,6},{5,7},{6,4},{7,5},{8,10},{9,11},{10,... | collective-permute-start | bytes 589832 | tf_op jit(solution)/shard_map/ppermute | solution.py:591
  39.0 4.2 %collective-permute-done.12.rest_6_ = bf16[96,1536]{1,0:T(8,128)(2,1)S(1)} collective-permute-done((bf16[96,1536]{1,0:T(8,128)(2,1)S(1)}, bf16[96,1536]{1,0:T(8,128)(2,1)S(1)}, u32[]{:S(2)}, u32[]{:S(2)}) %collective-permute-start.12) | collective-permute-done | bytes 294944 | tf_op jit(solution)/shard_map/ppermute | solution.py:588
  43.3 1.5 %collective-permute-start.18 = (bf16[96,1536]{1,0:T(8,128)(2,1)S(1)}, bf16[96,1536]{1,0:T(8,128)(2,1)S(1)}, u32[]{:S(2)}, u32[]{:S(2)}) collective-permute-start(bf16[96,1536]{1,0:T(8,128)(2,1)S(1)} %collective-permute-done.12.rest_6_), channel_id=1, source_target_pairs={{0,4},{4,0},{8,12},{12,8},{16,20},{20,16},{24,28},{28,24},{1,5},{5... | collective-permute-start | bytes 884744 | tf_op jit(solution)/shard_map/ppermute | solution.py:588
  44.7 1.4 %collective-permute-start.17 = (bf16[96,1536]{1,0:T(8,128)(2,1)S(1)}, bf16[96,1536]{1,0:T(8,128)(2,1)S(1)}, u32[]{:S(2)}, u32[]{:S(2)}) collective-permute-start(bf16[96,1536]{1,0:T(8,128)(2,1)S(1)} %collective-permute-done.rest_1_), channel_id=1, source_target_pairs={{0,8},{4,12},{8,0},{12,4},{16,24},{20,28},{24,16},{28,20},{1,9},{5... | collective-permute-start | bytes 884744 | tf_op jit(solution)/shard_map/ppermute | solution.py:588
  46.3 1.6 %collective-permute-done.14.two = bf16[128,768]{1,0:T(8,128)(2,1)S(1)} collective-permute-done((bf16[128,768]{1,0:T(8,128)(2,1)S(1)}, bf16[128,768]{1,0:T(8,128)(2,1)S(1)}, u32[]{:S(2)}, u32[]{:S(2)}) %collective-permute-start.14) | collective-permute-done | bytes 196640 | tf_op jit(solution)/shard_map/ppermute | solution.py:591
  48.0 3.0 %collective-permute-done.18.rest_7_ = bf16[96,1536]{1,0:T(8,128)(2,1)S(1)} collective-permute-done((bf16[96,1536]{1,0:T(8,128)(2,1)S(1)}, bf16[96,1536]{1,0:T(8,128)(2,1)S(1)}, u32[]{:S(2)}, u32[]{:S(2)}) %collective-permute-start.18) | collective-permute-done | bytes 294944 | tf_op jit(solution)/shard_map/ppermute | solution.py:588
  51.0 1.7 %collective-permute-done.17.rest_3_ = bf16[96,1536]{1,0:T(8,128)(2,1)S(1)} collective-permute-done((bf16[96,1536]{1,0:T(8,128)(2,1)S(1)}, bf16[96,1536]{1,0:T(8,128)(2,1)S(1)}, u32[]{:S(2)}, u32[]{:S(2)}) %collective-permute-start.17) | collective-permute-done | bytes 294944 | tf_op jit(solution)/shard_map/ppermute | solution.py:588
  52.7 3.5 %ffn.1 = (f32[512,768]{1,0:T(8,128)S(1)}, bf16[512,768]{1,0:T(8,128)(2,1)S(1)}, bf16[512,768]{1,0:T(8,128)(2,1)S(1)}, bf16[512,768]{1,0:T(8,128)(2,1)S(1)}, bf16...) custom-call(bf16[512,768]{1,0:T(8,128)(2,1)S(1)} %get-tuple-element., ...), custom_call_target="tpu_custom_call" | custom-call | tf_op jit(solution)/shard_map/ffn/pallas_call | solution.py:60
  56.3 1.7 %collective-permute-done.19.two = bf16[256,768]{1,0:T(8,128)(2,1)S(1)} collective-permute-done((bf16[256,768]{1,0:T(8,128)(2,1)S(1)}, bf16[256,768]{1,0:T(8,128)(2,1)S(1)}, u32[]{:S(2)}, u32[]{:S(2)}) %collective-permute-start.19) | collective-permute-done | bytes 393248 | tf_op jit(solution)/shard_map/ppermute | solution.py:591
  58.1 1.6 %collective-permute-start.20 = (bf16[256,768]{1,0:T(8,128)(2,1)S(1)}, bf16[256,768]{1,0:T(8,128)(2,1)S(1)}, u32[]{:S(2)}, u32[]{:S(2)}) collective-permute-start(bf16[256,768]{1,0:T(8,128)(2,1)S(1)} %add.6.one), channel_id=1, source_target_pairs={{0,2},{1,3},{2,0},{3,1},{4,6},{5,7},{6,4},{7,5},{8,10},{9,11},{10,... | collective-permute-start | bytes 1179656 | tf_op jit(solution)/shard_map/ppermute | solution.py:591
  59.7 0.9 down_grad.1
  60.6 1.1 in_grad.1
  61.7 1.8 %collective-permute-start.22 = (bf16[4,96,768]{2,1,0:T(8,128)(2,1)S(1)}, bf16[4,96,768]{2,1,0:T(8,128)(2,1)S(1)}, u32[]{:S(2)}, u32[]{:S(2)}) collective-permute-start(bf16[4,96,768]{2,1,0:T(8,128)(2,1)S(1)} %get-tuple-element.182), channel_id=1, source_target_pairs={{0,8},{4,12},{8,0},{12,4},{16,24},{20,28},{24,16},{28,20},{1,9},{5... | collective-permute-start | bytes 1769480 | tf_op jit(solution)/shard_map/ppermute | solution.py:588
  64.0 1.6 %ffn_out.1 = (bf16[256,768]{1,0:T(8,128)(2,1)S(1)}, bf16[256,768]{1,0:T(8,128)(2,1)S(1)}) custom-call(bf16[512,768]{1,0:T(8,128)(2,1)S(1)} %get-tuple-element.168.right.hidden, bf16[768,768]{1,0:T(8,128)(2,1)S(1)} %get-tuple-element.169.down), custom_call_target="tpu_custom_call" | custom-call | tf_op jit(solution)/shard_map/ffn_out/pallas_call | solution.py:60
  65.7 3.7 %collective-permute-done.20.two = bf16[256,768]{1,0:T(8,128)(2,1)S(1)} collective-permute-done((bf16[256,768]{1,0:T(8,128)(2,1)S(1)}, bf16[256,768]{1,0:T(8,128)(2,1)S(1)}, u32[]{:S(2)}, u32[]{:S(2)}) %collective-permute-start.20) | collective-permute-done | bytes 393248 | tf_op jit(solution)/shard_map/ppermute | solution.py:591
  69.5 1.7 %collective-permute-done.21.other = bf16[256,768]{1,0:T(8,128)(2,1)S(1)} collective-permute-done((bf16[256,768]{1,0:T(8,128)(2,1)S(1)}, bf16[256,768]{1,0:T(8,128)(2,1)S(1)}, u32[]{:S(2)}, u32[]{:S(2)}) %collective-permute-start.21) | collective-permute-done | bytes 393248 | tf_op jit(solution)/shard_map/ppermute | solution.py:591
  71.2 5.9 %attend_back.1 = (bf16[4,96,768]{2,1,0:T(8,128)(2,1)S(1)}, bf16[2,96,768]{2,1,0:T(8,128)(2,1)S(1)}, f32[128,768]{1,0:T(8,128)S(1)}, bf16[208,768]{1,0:T(8,128)(2,1)S(1)}, bf16[512,576]{1,0:T(8,128)(2,1)S(1)}) custom-call(f32[512,768]{1,0:T(8,128)S(1)} %get-tuple-element.213.resid, bf16[512,768]{1,0:T(8,128)(2,1)S(1)} %get-tuple-element.139.dy.left, ...), custom_call_target="tpu_custom_call" | custom-call | tf_op jit(solution)/shard_map/attend_back/pallas_call | solution.py:60
  77.3 1.0 collective-permute-done.23.got
  79.1 1.4 %act_grad.1 = (bf16[256,768]{1,0:T(8,128)(2,1)S(1)}, bf16[128,768]{1,0:T(8,128)(2,1)S(1)}, bf16[128,768]{1,0:T(8,128)(2,1)S(1)}) custom-call(bf16[512,576]{1,0:T(8,128)(2,1)S(1)} %get-tuple-element.189.proj_grad, bf16[768,768]{1,0:T(8,128)(2,1)S(1)} %get-tuple-element.172.weights), custom_call_target="tpu_custom_call" | custom-call | tf_op jit(solution)/shard_map/act_grad/pallas_call | solution.py:60
  81.8 3.5 %collective-permute-start.29 = (bf16[2,96,768]{2,1,0:T(8,128)(2,1)S(1)}, bf16[2,96,768]{2,1,0:T(8,128)(2,1)S(1)}, u32[]{:S(2)}, u32[]{:S(2)}) collective-permute-start(bf16[2,96,768]{2,1,0:T(8,128)(2,1)S(1)} %get-tuple-element.184), channel_id=1, source_target_pairs={{0,16},{4,20},{8,24},{12,28},{16,0},{20,4},{24,8},{28,12},{1,17},{... | collective-permute-start | bytes 884744 | tf_op jit(solution)/shard_map/ppermute | solution.py:588
  85.2 1.9 %collective-permute-done.24.got = bf16[208,768]{1,0:T(8,128)(2,1)S(1)} collective-permute-done((bf16[208,768]{1,0:T(8,128)(2,1)S(1)}, bf16[208,768]{1,0:T(8,128)(2,1)S(1)}, u32[]{:S(2)}, u32[]{:S(2)}) %collective-permute-start.24) | collective-permute-done | bytes 319520 | tf_op jit(solution)/shard_map/ppermute | solution.py:588
  87.2 1.8 %collective-permute-start.33 = (bf16[208,768]{1,0:T(8,128)(2,1)S(1)}, bf16[208,768]{1,0:T(8,128)(2,1)S(1)}, u32[]{:S(2)}, u32[]{:S(2)}) collective-permute-start(bf16[208,768]{1,0:T(8,128)(2,1)S(1)} %last_high.1.sent), channel_id=1, source_target_pairs={{0,8},{4,12},{8,0},{12,4},{16,24},{20,28},{24,16},{28,20},{1,9},{5... | collective-permute-start | bytes 958472 | tf_op jit(solution)/shard_map/ppermute | solution.py:588
  89.9 1.6 %collective-permute-start.34 = (bf16[256,768]{1,0:T(8,128)(2,1)S(1)}, bf16[256,768]{1,0:T(8,128)(2,1)S(1)}, u32[]{:S(2)}, u32[]{:S(2)}) collective-permute-start(bf16[256,768]{1,0:T(8,128)(2,1)S(1)} %get-tuple-element.215), channel_id=1, source_target_pairs={{0,2},{1,3},{2,0},{3,1},{4,6},{5,7},{6,4},{7,5},{8,10},{9,11},{10,... | collective-permute-start | bytes 1179656 | tf_op jit(solution)/shard_map/ppermute | solution.py:591
  91.5 5.8 %collective-permute-done.28.got = bf16[2,96,768]{2,1,0:T(8,128)(2,1)S(1)} collective-permute-done((bf16[2,96,768]{2,1,0:T(8,128)(2,1)S(1)}, bf16[2,96,768]{2,1,0:T(8,128)(2,1)S(1)}, u32[]{:S(2)}, u32[]{:S(2)}) %collective-permute-start.28) | collective-permute-done | bytes 294944 | tf_op jit(solution)/shard_map/ppermute | solution.py:588
  97.5 1.6 %collective-permute-start.31 = (bf16[96,768]{1,0:T(8,128)(2,1)S(1)}, bf16[96,768]{1,0:T(8,128)(2,1)S(1)}, u32[]{:S(2)}, u32[]{:S(2)}) collective-permute-start(bf16[96,768]{1,0:T(8,128)(2,1)S(1)} %get-tuple-element.204), channel_id=1, source_target_pairs={{0,4},{4,0},{8,12},{12,8},{16,20},{20,16},{24,28},{28,24},{1,5},{5... | collective-permute-start | bytes 442376 | tf_op jit(solution)/shard_map/ppermute | solution.py:588
  99.0 5.7 %collective-permute-done.30.rest_1_ = bf16[96,768]{1,0:T(8,128)(2,1)S(1)} collective-permute-done((bf16[96,768]{1,0:T(8,128)(2,1)S(1)}, bf16[96,768]{1,0:T(8,128)(2,1)S(1)}, u32[]{:S(2)}, u32[]{:S(2)}) %collective-permute-start.30) | collective-permute-done | bytes 147488 | tf_op jit(solution)/shard_map/ppermute | solution.py:588
  104.8 1.5 %collective-permute-done.33.got = bf16[208,768]{1,0:T(8,128)(2,1)S(1)} collective-permute-done((bf16[208,768]{1,0:T(8,128)(2,1)S(1)}, bf16[208,768]{1,0:T(8,128)(2,1)S(1)}, u32[]{:S(2)}, u32[]{:S(2)}) %collective-permute-start.33) | collective-permute-done | bytes 319520 | tf_op jit(solution)/shard_map/ppermute | solution.py:588
  106.5 1.9 %collective-permute-start.35 = (bf16[112,768]{1,0:T(8,128)(2,1)S(1)}, bf16[112,768]{1,0:T(8,128)(2,1)S(1)}, u32[]{:S(2)}, u32[]{:S(2)}) collective-permute-start(bf16[112,768]{1,0:T(8,128)(2,1)S(1)} %get-tuple-element.212.rest_1_), channel_id=1, source_target_pairs={{0,16},{4,20},{8,24},{12,28},{16,0},{20,4},{24,8},{28,12},{1,17},{... | collective-permute-start | bytes 516104 | tf_op jit(solution)/shard_map/ppermute | solution.py:588
  108.4 1.0 share_out.1
  109.4 7.2 %collective-permute-done.35.rest_2_ = bf16[112,768]{1,0:T(8,128)(2,1)S(1)} collective-permute-done((bf16[112,768]{1,0:T(8,128)(2,1)S(1)}, bf16[112,768]{1,0:T(8,128)(2,1)S(1)}, u32[]{:S(2)}, u32[]{:S(2)}) %collective-permute-start.35) | collective-permute-done | bytes 172064 | tf_op jit(solution)/shard_map/ppermute | solution.py:588
  117.4 12.0 %all_to_all.5.refs_0_ = f32[32,1,384]{2,1,0:T(1,128)S(1)} all-to-all(f32[32,1,384]{2,1,0:T(1,128)} %get-tuple-element.222), channel_id=1, replica_groups=mesh['dp'=8,'tp'=4] {'dp','tp'}, dimensions={0} | all-to-all | bytes 98304 | tf_op jit(solution)/shard_map/all_to_all | solution.py:820
  129.4 4.0 %adam.1 = (f32[1,1]{1,0:T(1,128)}, f32[3,96,192]{2,1,0:T(8,128)}, f32[3,96,192]{2,1,0:T(8,128)}, f32[3,96,192]{2,1,0:T(8,128)}, bf16[3,96,192]{2,1,0:T(8,128)(2,...) custom-call(f32[32,1,384]{2,1,0:T(1,128)S(1)} %all_to_all.5.refs_0_,, ...), custom_call_target="tpu_custom_call" | custom-call | tf_op jit(solution)/shard_map/adam/pallas_call | solution.py:60
  (51 shorter events, 9.3 us)
Async XLA Ops:
  1.9 11.2 %collective-permute-start.1 = (bf16[96,768]{1,0:T(8,128)(2,1)S(1)}, bf16[96,768]{1,0:T(8,128)(2,1)S(1)}, u32[]{:S(2)}, u32[]{:S(2)}) collective-permute-start(bf16[96,768]{1,0:T(8,128)(2,1)S(1)} %get-tuple-element.147.rest_0_), channel_id=1, source_target_pairs={{0,16},{4,20},{8,24},{12,28},{16,0},{20,4},{24,8},{28,12},{1,17},{... | collective-permute-start | bytes 442376 | tf_op jit(solution)/shard_map/ppermute | solution.py:588
  6.0 12.6 %collective-permute-start.4 = (bf16[96,768]{1,0:T(8,128)(2,1)S(1)}, bf16[96,768]{1,0:T(8,128)(2,1)S(1)}, u32[]{:S(2)}, u32[]{:S(2)}) collective-permute-start(bf16[96,768]{1,0:T(8,128)(2,1)S(1)} %get-tuple-element.147.rest_0_), channel_id=1, source_target_pairs={{0,8},{4,12},{8,0},{12,4},{16,24},{20,28},{24,16},{28,20},{1,9},{5... | collective-permute-start | bytes 442376 | tf_op jit(solution)/shard_map/ppermute | solution.py:588
  9.8 17.2 %collective-permute-start = (bf16[96,1536]{1,0:T(8,128)(2,1)S(1)}, bf16[96,1536]{1,0:T(8,128)(2,1)S(1)}, u32[]{:S(2)}, u32[]{:S(2)}) collective-permute-start(bf16[96,1536]{1,0:T(8,128)(2,1)S(1)} %get-tuple-element.151.rest_0_), channel_id=1, source_target_pairs={{0,4},{4,0},{8,12},{12,8},{16,20},{20,16},{24,28},{28,24},{1,5},{5... | collective-permute-start | bytes 884744 | tf_op jit(solution)/shard_map/ppermute | solution.py:588
  13.1 15.4 %collective-permute-start.2 = (bf16[96,1536]{1,0:T(8,128)(2,1)S(1)}, bf16[96,1536]{1,0:T(8,128)(2,1)S(1)}, u32[]{:S(2)}, u32[]{:S(2)}) collective-permute-start(bf16[96,1536]{1,0:T(8,128)(2,1)S(1)} %get-tuple-element.151.rest_0_), channel_id=1, source_target_pairs={{0,16},{4,20},{8,24},{12,28},{16,0},{20,4},{24,8},{28,12},{1,17},{... | collective-permute-start | bytes 884744 | tf_op jit(solution)/shard_map/ppermute | solution.py:588
  13.7 8.3 %collective-permute-start.3 = (bf16[96,768]{1,0:T(8,128)(2,1)S(1)}, bf16[96,768]{1,0:T(8,128)(2,1)S(1)}, u32[]{:S(2)}, u32[]{:S(2)}) collective-permute-start(bf16[96,768]{1,0:T(8,128)(2,1)S(1)} %get-tuple-element.147.rest_0_), channel_id=1, source_target_pairs={{0,4},{4,0},{8,12},{12,8},{16,20},{20,16},{24,28},{28,24},{1,5},{5... | collective-permute-start | bytes 442376 | tf_op jit(solution)/shard_map/ppermute | solution.py:588
  15.2 9.3 %collective-permute-start.7 = (bf16[96,768]{1,0:T(8,128)(2,1)S(1)}, bf16[96,768]{1,0:T(8,128)(2,1)S(1)}, u32[]{:S(2)}, u32[]{:S(2)}) collective-permute-start(bf16[96,768]{1,0:T(8,128)(2,1)S(1)} %collective-permute-done.1.rest_4_), channel_id=1, source_target_pairs={{0,8},{4,12},{8,0},{12,4},{16,24},{20,28},{24,16},{28,20},{1,9},{5... | collective-permute-start | bytes 442376 | tf_op jit(solution)/shard_map/ppermute | solution.py:588
  18.6 6.8 %collective-permute-start.5 = (bf16[96,768]{1,0:T(8,128)(2,1)S(1)}, bf16[96,768]{1,0:T(8,128)(2,1)S(1)}, u32[]{:S(2)}, u32[]{:S(2)}) collective-permute-start(bf16[96,768]{1,0:T(8,128)(2,1)S(1)} %collective-permute-done.4.rest_2_), channel_id=1, source_target_pairs={{0,4},{4,0},{8,12},{12,8},{16,20},{20,16},{24,28},{28,24},{1,5},{5... | collective-permute-start | bytes 442376 | tf_op jit(solution)/shard_map/ppermute | solution.py:588
  22.0 7.1 %collective-permute-start.6 = (bf16[96,768]{1,0:T(8,128)(2,1)S(1)}, bf16[96,768]{1,0:T(8,128)(2,1)S(1)}, u32[]{:S(2)}, u32[]{:S(2)}) collective-permute-start(bf16[96,768]{1,0:T(8,128)(2,1)S(1)} %collective-permute-done.1.rest_4_), channel_id=1, source_target_pairs={{0,4},{4,0},{8,12},{12,8},{16,20},{20,16},{24,28},{28,24},{1,5},{5... | collective-permute-start | bytes 442376 | tf_op jit(solution)/shard_map/ppermute | solution.py:588
  24.5 6.2 %collective-permute-start.8 = (bf16[96,768]{1,0:T(8,128)(2,1)S(1)}, bf16[96,768]{1,0:T(8,128)(2,1)S(1)}, u32[]{:S(2)}, u32[]{:S(2)}) collective-permute-start(bf16[96,768]{1,0:T(8,128)(2,1)S(1)} %collective-permute-done.7.rest_6_), channel_id=1, source_target_pairs={{0,4},{4,0},{8,12},{12,8},{16,20},{20,16},{24,28},{28,24},{1,5},{5... | collective-permute-start | bytes 442376 | tf_op jit(solution)/shard_map/ppermute | solution.py:588
  25.4 9.3 %collective-permute-start.11 = (bf16[96,1536]{1,0:T(8,128)(2,1)S(1)}, bf16[96,1536]{1,0:T(8,128)(2,1)S(1)}, u32[]{:S(2)}, u32[]{:S(2)}) collective-permute-start(bf16[96,1536]{1,0:T(8,128)(2,1)S(1)} %get-tuple-element.151.rest_0_), channel_id=1, source_target_pairs={{0,8},{4,12},{8,0},{12,4},{16,24},{20,28},{24,16},{28,20},{1,9},{5... | collective-permute-start | bytes 884744 | tf_op jit(solution)/shard_map/ppermute | solution.py:588
  33.8 3.1 %collective-permute-start.9 = (bf16[256,768]{1,0:T(8,128)(2,1)S(1)}, bf16[256,768]{1,0:T(8,128)(2,1)S(1)}, u32[]{:S(2)}, u32[]{:S(2)}) collective-permute-start(bf16[256,768]{1,0:T(8,128)(2,1)S(1)} %get-tuple-element.149), channel_id=1, source_target_pairs={{0,1},{1,0},{2,3},{3,2},{4,5},{5,4},{6,7},{7,6},{8,9},{9,8},{10,11... | collective-permute-start | bytes 1179656 | tf_op jit(solution)/shard_map/ppermute | solution.py:591
  34.8 8.5 %collective-permute-start.12 = (bf16[96,1536]{1,0:T(8,128)(2,1)S(1)}, bf16[96,1536]{1,0:T(8,128)(2,1)S(1)}, u32[]{:S(2)}, u32[]{:S(2)}) collective-permute-start(bf16[96,1536]{1,0:T(8,128)(2,1)S(1)} %collective-permute-done.2.rest_4_), channel_id=1, source_target_pairs={{0,8},{4,12},{8,0},{12,4},{16,24},{20,28},{24,16},{28,20},{1,9},{5... | collective-permute-start | bytes 884744 | tf_op jit(solution)/shard_map/ppermute | solution.py:588
  35.3 10.8 %collective-permute-start.10 = (bf16[96,1536]{1,0:T(8,128)(2,1)S(1)}, bf16[96,1536]{1,0:T(8,128)(2,1)S(1)}, u32[]{:S(2)}, u32[]{:S(2)}) collective-permute-start(bf16[96,1536]{1,0:T(8,128)(2,1)S(1)} %collective-permute-done.2.rest_4_), channel_id=1, source_target_pairs={{0,4},{4,0},{8,12},{12,8},{16,20},{20,16},{24,28},{28,24},{1,5},{5... | collective-permute-start | bytes 884744 | tf_op jit(solution)/shard_map/ppermute | solution.py:588
  36.9 9.3 %collective-permute-start.13 = (bf16[128,768]{1,0:T(8,128)(2,1)S(1)}, bf16[128,768]{1,0:T(8,128)(2,1)S(1)}, u32[]{:S(2)}, u32[]{:S(2)}) collective-permute-start(bf16[128,768]{1,0:T(8,128)(2,1)S(1)} %get-tuple-element.153.one), channel_id=1, source_target_pairs={{0,2},{1,3},{2,0},{3,1},{4,6},{5,7},{6,4},{7,5},{8,10},{9,11},{10,... | collective-permute-start | bytes 589832 | tf_op jit(solution)/shard_map/ppermute | solution.py:591
  38.5 9.4 %collective-permute-start.14 = (bf16[128,768]{1,0:T(8,128)(2,1)S(1)}, bf16[128,768]{1,0:T(8,128)(2,1)S(1)}, u32[]{:S(2)}, u32[]{:S(2)}) collective-permute-start(bf16[128,768]{1,0:T(8,128)(2,1)S(1)} %get-tuple-element.155.one), channel_id=1, source_target_pairs={{0,2},{1,3},{2,0},{3,1},{4,6},{5,7},{6,4},{7,5},{8,10},{9,11},{10,... | collective-permute-start | bytes 589832 | tf_op jit(solution)/shard_map/ppermute | solution.py:591
  43.3 7.8 %collective-permute-start.18 = (bf16[96,1536]{1,0:T(8,128)(2,1)S(1)}, bf16[96,1536]{1,0:T(8,128)(2,1)S(1)}, u32[]{:S(2)}, u32[]{:S(2)}) collective-permute-start(bf16[96,1536]{1,0:T(8,128)(2,1)S(1)} %collective-permute-done.12.rest_6_), channel_id=1, source_target_pairs={{0,4},{4,0},{8,12},{12,8},{16,20},{20,16},{24,28},{28,24},{1,5},{5... | collective-permute-start | bytes 884744 | tf_op jit(solution)/shard_map/ppermute | solution.py:588
  44.7 8.0 %collective-permute-start.17 = (bf16[96,1536]{1,0:T(8,128)(2,1)S(1)}, bf16[96,1536]{1,0:T(8,128)(2,1)S(1)}, u32[]{:S(2)}, u32[]{:S(2)}) collective-permute-start(bf16[96,1536]{1,0:T(8,128)(2,1)S(1)} %collective-permute-done.rest_1_), channel_id=1, source_target_pairs={{0,8},{4,12},{8,0},{12,4},{16,24},{20,28},{24,16},{28,20},{1,9},{5... | collective-permute-start | bytes 884744 | tf_op jit(solution)/shard_map/ppermute | solution.py:588
  46.2 6.5 %collective-permute-start.15 = (bf16[128,768]{1,0:T(8,128)(2,1)S(1)}, bf16[128,768]{1,0:T(8,128)(2,1)S(1)}, u32[]{:S(2)}, u32[]{:S(2)}) collective-permute-start(bf16[128,768]{1,0:T(8,128)(2,1)S(1)} %add.4.own_a), channel_id=1, source_target_pairs={{0,1},{1,0},{2,3},{3,2},{4,5},{5,4},{6,7},{7,6},{8,9},{9,8},{10,11... | collective-permute-start | bytes 589832 | tf_op jit(solution)/shard_map/ppermute | solution.py:591
  47.9 4.8 %collective-permute-start.16 = (bf16[128,768]{1,0:T(8,128)(2,1)S(1)}, bf16[128,768]{1,0:T(8,128)(2,1)S(1)}, u32[]{:S(2)}, u32[]{:S(2)}) collective-permute-start(bf16[128,768]{1,0:T(8,128)(2,1)S(1)} %add.5.own_b), channel_id=1, source_target_pairs={{0,1},{1,0},{2,3},{3,2},{4,5},{5,4},{6,7},{7,6},{8,9},{9,8},{10,11... | collective-permute-start | bytes 589832 | tf_op jit(solution)/shard_map/ppermute | solution.py:591
  56.2 1.8 %collective-permute-start.19 = (bf16[256,768]{1,0:T(8,128)(2,1)S(1)}, bf16[256,768]{1,0:T(8,128)(2,1)S(1)}, u32[]{:S(2)}, u32[]{:S(2)}) collective-permute-start(bf16[256,768]{1,0:T(8,128)(2,1)S(1)} %get-tuple-element.159), channel_id=1, source_target_pairs={{0,1},{1,0},{2,3},{3,2},{4,5},{5,4},{6,7},{7,6},{8,9},{9,8},{10,11... | collective-permute-start | bytes 1179656 | tf_op jit(solution)/shard_map/ppermute | solution.py:591
  58.1 11.2 %collective-permute-start.20 = (bf16[256,768]{1,0:T(8,128)(2,1)S(1)}, bf16[256,768]{1,0:T(8,128)(2,1)S(1)}, u32[]{:S(2)}, u32[]{:S(2)}) collective-permute-start(bf16[256,768]{1,0:T(8,128)(2,1)S(1)} %add.6.one), channel_id=1, source_target_pairs={{0,2},{1,3},{2,0},{3,1},{4,6},{5,7},{6,4},{7,5},{8,10},{9,11},{10,... | collective-permute-start | bytes 1179656 | tf_op jit(solution)/shard_map/ppermute | solution.py:591
  61.7 15.5 %collective-permute-start.22 = (bf16[4,96,768]{2,1,0:T(8,128)(2,1)S(1)}, bf16[4,96,768]{2,1,0:T(8,128)(2,1)S(1)}, u32[]{:S(2)}, u32[]{:S(2)}) collective-permute-start(bf16[4,96,768]{2,1,0:T(8,128)(2,1)S(1)} %get-tuple-element.182), channel_id=1, source_target_pairs={{0,8},{4,12},{8,0},{12,4},{16,24},{20,28},{24,16},{28,20},{1,9},{5... | collective-permute-start | bytes 1769480 | tf_op jit(solution)/shard_map/ppermute | solution.py:588
  63.5 14.8 %collective-permute-start.23 = (bf16[4,96,768]{2,1,0:T(8,128)(2,1)S(1)}, bf16[4,96,768]{2,1,0:T(8,128)(2,1)S(1)}, u32[]{:S(2)}, u32[]{:S(2)}) collective-permute-start(bf16[4,96,768]{2,1,0:T(8,128)(2,1)S(1)} %get-tuple-element.186), channel_id=1, source_target_pairs={{0,4},{4,0},{8,12},{12,8},{16,20},{20,16},{24,28},{28,24},{1,5},{5... | collective-permute-start | bytes 1769480 | tf_op jit(solution)/shard_map/ppermute | solution.py:588
  69.4 1.8 %collective-permute-start.21 = (bf16[256,768]{1,0:T(8,128)(2,1)S(1)}, bf16[256,768]{1,0:T(8,128)(2,1)S(1)}, u32[]{:S(2)}, u32[]{:S(2)}) collective-permute-start(bf16[256,768]{1,0:T(8,128)(2,1)S(1)} %add.7.own), channel_id=1, source_target_pairs={{0,1},{1,0},{2,3},{3,2},{4,5},{5,4},{6,7},{7,6},{8,9},{9,8},{10,11... | collective-permute-start | bytes 1179656 | tf_op jit(solution)/shard_map/ppermute | solution.py:591
  78.5 8.6 %collective-permute-start.24 = (bf16[208,768]{1,0:T(8,128)(2,1)S(1)}, bf16[208,768]{1,0:T(8,128)(2,1)S(1)}, u32[]{:S(2)}, u32[]{:S(2)}) collective-permute-start(bf16[208,768]{1,0:T(8,128)(2,1)S(1)} %get-tuple-element.193.sent), channel_id=1, source_target_pairs={{0,4},{4,0},{8,12},{12,8},{16,20},{20,16},{24,28},{28,24},{1,5},{5... | collective-permute-start | bytes 958472 | tf_op jit(solution)/shard_map/ppermute | solution.py:588
  79.1 8.1 %collective-permute-start.25 = (bf16[256,768]{1,0:T(8,128)(2,1)S(1)}, bf16[256,768]{1,0:T(8,128)(2,1)S(1)}, u32[]{:S(2)}, u32[]{:S(2)}) collective-permute-start(bf16[256,768]{1,0:T(8,128)(2,1)S(1)} %get-tuple-element.195), channel_id=1, source_target_pairs={{0,1},{1,0},{2,3},{3,2},{4,5},{5,4},{6,7},{7,6},{8,9},{9,8},{10,11... | collective-permute-start | bytes 1179656 | tf_op jit(solution)/shard_map/ppermute | solution.py:591
  80.5 8.5 %collective-permute-start.26 = (bf16[128,768]{1,0:T(8,128)(2,1)S(1)}, bf16[128,768]{1,0:T(8,128)(2,1)S(1)}, u32[]{:S(2)}, u32[]{:S(2)}) collective-permute-start(bf16[128,768]{1,0:T(8,128)(2,1)S(1)} %get-tuple-element.196), channel_id=1, source_target_pairs={{0,1},{1,0},{2,3},{3,2},{4,5},{5,4},{6,7},{7,6},{8,9},{9,8},{10,11... | collective-permute-start | bytes 589832 | tf_op jit(solution)/shard_map/ppermute | solution.py:591
  81.0 16.2 %collective-permute-start.28 = (bf16[2,96,768]{2,1,0:T(8,128)(2,1)S(1)}, bf16[2,96,768]{2,1,0:T(8,128)(2,1)S(1)}, u32[]{:S(2)}, u32[]{:S(2)}) collective-permute-start(bf16[2,96,768]{2,1,0:T(8,128)(2,1)S(1)} %get-tuple-element.188), channel_id=1, source_target_pairs={{0,8},{4,12},{8,0},{12,4},{16,24},{20,28},{24,16},{28,20},{1,9},{5... | collective-permute-start | bytes 884744 | tf_op jit(solution)/shard_map/ppermute | solution.py:588
  81.8 15.6 %collective-permute-start.29 = (bf16[2,96,768]{2,1,0:T(8,128)(2,1)S(1)}, bf16[2,96,768]{2,1,0:T(8,128)(2,1)S(1)}, u32[]{:S(2)}, u32[]{:S(2)}) collective-permute-start(bf16[2,96,768]{2,1,0:T(8,128)(2,1)S(1)} %get-tuple-element.184), channel_id=1, source_target_pairs={{0,16},{4,20},{8,24},{12,28},{16,0},{20,4},{24,8},{28,12},{1,17},{... | collective-permute-start | bytes 884744 | tf_op jit(solution)/shard_map/ppermute | solution.py:588
  87.1 2.5 %collective-permute-start.27 = (bf16[128,768]{1,0:T(8,128)(2,1)S(1)}, bf16[128,768]{1,0:T(8,128)(2,1)S(1)}, u32[]{:S(2)}, u32[]{:S(2)}) collective-permute-start(bf16[128,768]{1,0:T(8,128)(2,1)S(1)} %get-tuple-element.197), channel_id=1, source_target_pairs={{0,1},{1,0},{2,3},{3,2},{4,5},{5,4},{6,7},{7,6},{8,9},{9,8},{10,11... | collective-permute-start | bytes 589832 | tf_op jit(solution)/shard_map/ppermute | solution.py:591
  87.2 19.2 %collective-permute-start.33 = (bf16[208,768]{1,0:T(8,128)(2,1)S(1)}, bf16[208,768]{1,0:T(8,128)(2,1)S(1)}, u32[]{:S(2)}, u32[]{:S(2)}) collective-permute-start(bf16[208,768]{1,0:T(8,128)(2,1)S(1)} %last_high.1.sent), channel_id=1, source_target_pairs={{0,8},{4,12},{8,0},{12,4},{16,24},{20,28},{24,16},{28,20},{1,9},{5... | collective-permute-start | bytes 958472 | tf_op jit(solution)/shard_map/ppermute | solution.py:588
  89.0 15.8 %collective-permute-start.32 = (bf16[2,96,768]{2,1,0:T(8,128)(2,1)S(1)}, bf16[2,96,768]{2,1,0:T(8,128)(2,1)S(1)}, u32[]{:S(2)}, u32[]{:S(2)}) collective-permute-start(bf16[2,96,768]{2,1,0:T(8,128)(2,1)S(1)} %get-tuple-element.211), channel_id=1, source_target_pairs={{0,4},{4,0},{8,12},{12,8},{16,20},{20,16},{24,28},{28,24},{1,5},{5... | collective-permute-start | bytes 884744 | tf_op jit(solution)/shard_map/ppermute | solution.py:588
  89.9 18.5 %collective-permute-start.34 = (bf16[256,768]{1,0:T(8,128)(2,1)S(1)}, bf16[256,768]{1,0:T(8,128)(2,1)S(1)}, u32[]{:S(2)}, u32[]{:S(2)}) collective-permute-start(bf16[256,768]{1,0:T(8,128)(2,1)S(1)} %get-tuple-element.215), channel_id=1, source_target_pairs={{0,2},{1,3},{2,0},{3,1},{4,6},{5,7},{6,4},{7,5},{8,10},{9,11},{10,... | collective-permute-start | bytes 1179656 | tf_op jit(solution)/shard_map/ppermute | solution.py:591
  97.3 7.4 %collective-permute-start.30 = (bf16[96,768]{1,0:T(8,128)(2,1)S(1)}, bf16[96,768]{1,0:T(8,128)(2,1)S(1)}, u32[]{:S(2)}, u32[]{:S(2)}) collective-permute-start(bf16[96,768]{1,0:T(8,128)(2,1)S(1)} %get-tuple-element.201), channel_id=1, source_target_pairs={{0,16},{4,20},{8,24},{12,28},{16,0},{20,4},{24,8},{28,12},{1,17},{... | collective-permute-start | bytes 442376 | tf_op jit(solution)/shard_map/ppermute | solution.py:588
  97.5 7.3 %collective-permute-start.31 = (bf16[96,768]{1,0:T(8,128)(2,1)S(1)}, bf16[96,768]{1,0:T(8,128)(2,1)S(1)}, u32[]{:S(2)}, u32[]{:S(2)}) collective-permute-start(bf16[96,768]{1,0:T(8,128)(2,1)S(1)} %get-tuple-element.204), channel_id=1, source_target_pairs={{0,4},{4,0},{8,12},{12,8},{16,20},{20,16},{24,28},{28,24},{1,5},{5... | collective-permute-start | bytes 442376 | tf_op jit(solution)/shard_map/ppermute | solution.py:588
  106.5 10.2 %collective-permute-start.35 = (bf16[112,768]{1,0:T(8,128)(2,1)S(1)}, bf16[112,768]{1,0:T(8,128)(2,1)S(1)}, u32[]{:S(2)}, u32[]{:S(2)}) collective-permute-start(bf16[112,768]{1,0:T(8,128)(2,1)S(1)} %get-tuple-element.212.rest_1_), channel_id=1, source_target_pairs={{0,16},{4,20},{8,24},{12,28},{16,0},{20,4},{24,8},{28,12},{1,17},{... | collective-permute-start | bytes 516104 | tf_op jit(solution)/shard_map/ppermute | solution.py:588

commit v4 on v3

--- a/solution.py
+++ b/solution.py
@@ -14,7 +14,8 @@
 LEN = 512
 BLK = 128
 WIN = LEN + BLK
-SMALL = 16
+SMALL = 8
+LINES = 16
 
 
 eps_norm = 1e-06
@@ -446,11 +447,11 @@
     grad[...] = total
     per_row = total.shape[1] // BLK
     lines[...] = jnp.zeros_like(lines)
-    for line in range(SMALL):
+    for line in range(LINES):
         row, at = divmod(line, per_row)
         lines[line : line + 1, :] = small[row : row + 1, at * BLK : (at + 1) * BLK]
     me = lax.axis_index("dp")
-    start = pl.multiple_of(jnp.minimum(2 * me, SMALL), 2)
+    start = pl.multiple_of(jnp.minimum(2 * me, LINES), 2)
     squares = fold(total) + extra_a[...] + extra_b[...]
     two = lines[pl.ds(start, 2), :]
     told = jnp.concatenate((squares, two[0:1, :], two[1:2, :]), axis=1)
@@ -461,23 +462,28 @@
 def adamw(weight, gradient, moment_one, moment_two, rate):
     one_new = beta_one * moment_one + (1.0 - beta_one) * gradient
     two_new = beta_two * moment_two + (1.0 - beta_two) * gradient * gradient
-    one_hat = one_new / (1.0 - beta_one**adam_step)
-    two_hat = two_new / (1.0 - beta_two**adam_step)
-    weight_new = weight - rate * (one_hat / (jnp.sqrt(two_hat) + adam_eps) + decay_rate * weight)
-    return (weight_new, one_new, two_new)
+    root = math.sqrt(1.0 - beta_two**adam_step)
+    scale = rate * root / (1.0 - beta_one**adam_step)
+    step = scale * one_new / (jnp.sqrt(two_new) + adam_eps * root)
+    return (weight * (1.0 - rate * decay_rate) - step, one_new, two_new)
+
+
+def fetch_kernel(*refs):
+    count = len(refs) // 2
+    copies = [pltpu.make_async_copy(refs[i], refs[count + i], refs[-1].at[i]) for i in range(count)]
+    for copy in copies:
+        copy.start()
+    for copy in copies:
+        copy.wait()
 
 
 def adam_kernel(*refs):
-    told, grad_qkvo, grad_in, grad_down, *state_in = refs[:22]
+    told, grad_qkvo, grad_in, grad_down, *state = refs[:22]
     norm_ref, *matrices, gains_a, gains_b, gains_c, gains_grad, table_a, table_b, table_c = refs[22:46]
-    state, staged = refs[46:64], refs[64:80]
-    gains_sum, table_grad, sems_in, sems = refs[80:]
-    fetches = [pltpu.make_async_copy(state_in[i], state[i], sems_in.at[i]) for i in range(18)]
-    for i in (*range(6, 12), *range(6), *range(12, 18)):
-        fetches[i].start()
+    gains_sum, table_grad = refs[46:]
     gains_o, table_o = (gains_a, gains_b, gains_c), (table_a, table_b, table_c)
     qkv, out, ffn_in, ffn_down, gains, table = (state[i : i + 3] for i in range(0, 18, 3))
-    qkv_o, out_o, in_o, down_o = (staged[i : i + 4] for i in range(0, 16, 4))
+    qkv_o, out_o, in_o, down_o = (matrices[i : i + 4] for i in range(0, 16, 4))
     tp = lax.axis_size("tp")
     squares = told[0, :, :BLK]
     for i in range(1, told.shape[0]):
@@ -517,38 +523,15 @@
         if len(to) == 4:
             to[3][at] = new[0].astype(bf16)
 
-    copies = []
-
-    def arrived(first):
-        for i in range(first, first + 3):
-            fetches[i].wait()
-
-    def send(first):
-        for i in range(first, first + 4):
-            copies.append(pltpu.make_async_copy(staged[i], matrices[i], sems.at[i]))
-            copies[-1].start()
-
-    arrived(6)
     update(ffn_in, grad_in[...], in_o, rate_small)
-    send(8)
-    arrived(9)
     update(ffn_down, grad_down[...], down_o, rate_small)
-    send(12)
-    arrived(0)
     width = qkv[0].shape[2]
     for part in range(3):
         update(qkv, grad_qkvo[:, part * width : (part + 1) * width], qkv_o, rate_small, part)
-    send(0)
-    arrived(3)
     update(out, grad_qkvo[:, 3 * width :], out_o, rate_large)
-    send(4)
-    arrived(12)
     update(gains, gains_sum[...], gains_o, rate_large)
     gains_grad[...] = gains_sum[...] * factor
-    arrived(15)
     update(table, table_grad[...], table_o, rate_large)
-    for copy in copies:
-        copy.wait()
 
 
 def on_device(
@@ -805,19 +788,6 @@
         "share_out",
         behind=share_behind,
     )
-    qkvo_grad, payload = call(
-        functools.partial(last_sum_kernel, direct),
-        [sds((rows, packed_cols), f32), pltpu.HBM((everyone, 1, 3 * BLK), f32)],
-        (down_squares, in_squares, *last_parts),
-        "last_sum",
-        scratch=[
-            pltpu.VMEM((everyone, 1, 3 * BLK), f32),
-            pltpu.VMEM((SMALL + 8, BLK), f32),
-            pltpu.SemaphoreType.DMA,
-        ],
-        behind=(block_out,),
-    )
-    told = lax.all_to_all(payload, ("dp", "tp"), 0, 0)
     matrices = (
         qkv_weight,
         qkv_first,
@@ -834,26 +804,41 @@
     )
     vectors = (norm_gains, gains_first, gains_second, bias_table.T, table_first.T, table_second.T)
     state = matrices + vectors
+    fetched = call(
+        fetch_kernel,
+        [sds(m.shape, f32) for m in state],
+        state,
+        "fetch",
+        hbm=range(18),
+        scratch=[pltpu.SemaphoreType.DMA((18,))],
+        limit=4,
+        behind=(block_out,),
+    )
+    qkvo_grad, payload = call(
+        functools.partial(last_sum_kernel, direct),
+        [sds((rows, packed_cols), f32), pltpu.HBM((everyone, 1, 3 * BLK), f32)],
+        (down_squares, in_squares, *last_parts),
+        "last_sum",
+        scratch=[
+            pltpu.VMEM((everyone, 1, 3 * BLK), f32),
+            pltpu.VMEM((LINES + 8, BLK), f32),
+            pltpu.SemaphoreType.DMA,
+        ],
+        behind=(fetched[0],),
+    )
+    told = lax.all_to_all(payload, ("dp", "tp"), 0, 0)
     shapes = [(m.shape, kind) for m in matrices[::3] for kind in (f32, f32, f32, bf16)]
     norm, *updated = call(
         adam_kernel,
         [
             sds((1, 1), f32),
-            *(pltpu.HBM(shape, kind) for shape, kind in shapes),
+            *(sds(shape, kind) for shape, kind in shapes),
             *[sds(norm_gains.shape, f32)] * 4,
             *[sds((heads_here, BUCKETS), f32)] * 3,
         ],
-        (told, qkvo_grad, in_grad, down_grad, *state),
+        (told, qkvo_grad, in_grad, down_grad, *fetched),
         "adam",
-        hbm=range(4, 22),
-        scratch=[
-            *(pltpu.VMEM(m.shape, f32) for m in state),
-            *(pltpu.VMEM(shape, kind) for shape, kind in shapes),
-            pltpu.VMEM(norm_gains.shape, f32),
-            pltpu.VMEM((heads_here, BUCKETS), f32),
-            pltpu.SemaphoreType.DMA((18,)),
-            pltpu.SemaphoreType.DMA((16,)),
-        ],
+        scratch=[pltpu.VMEM(norm_gains.shape, f32), pltpu.VMEM((heads_here, BUCKETS), f32)],
     )
     return (block_out, input_grad, norm.reshape(()), *updated[:-3], *(t.T for t in updated[-3:]))
 

time: 134 us -> 131 us (0.978)
  waiting for transfers between devices: 50.7 us -> 48 us
    ppermute x24, waiting for transfers between devices: 42.1 us -> 39.4 us  [swap_dp(): return lax.ppermute(value, 'dp', [(i, i ^ distance) for i in range(dp)])]
    pallas_call x26 -> x27, Pallas kernels: 28.2 us -> 28.4 us  [call(): pl.pallas_call(body, out_shape=tuple(outs), in_specs=[pl.BlockSpec(memory...]
  transfers between devices with their start and end apart: 36 -> 36, of which waited for: 20 -> 20; matrix products, arithmetic and copies ran while one was open for 0% -> 0% of each run, Pallas kernels for 14% -> 16%
where the time goes in v4:
time: 131 us
  waiting for transfers between devices  48 us (37%)
  starting transfers between devices  41.6 us (32%)
  Pallas kernels  28.4 us (22%)
  blocking collectives  12 us (9%)
    ppermute x24, waiting for transfers between devices, swap_dp(): return lax.ppermute(value, 'dp', [(i, i ^ distance) for i in range(dp)])  39.4 us
    ppermute x24, starting transfers between devices, swap_dp(): return lax.ppermute(value, 'dp', [(i, i ^ distance) for i in range(dp)])  35.4 us
    pallas_call x27, Pallas kernels, call(): pl.pallas_call(body, out_shape=tuple(outs), in_specs=[pl.BlockSpec(memory...  28.4 us
    all_to_all x1, blocking collectives, on_device(): told = lax.all_to_all(payload, ('dp', 'tp'), 0, 0)  12 us
    ppermute x12, waiting for transfers between devices, swap_tp(): return lax.ppermute(value, 'tp', [(i, i ^ distance) for i in range(tp)])  8.66 us
    ppermute x12, starting transfers between devices, swap_tp(): return lax.ppermute(value, 'tp', [(i, i ^ distance) for i in range(tp)])  6.19 us
  transfers between devices with their start and end apart: 36, of which 20 were waited for; matrix products, arithmetic and copies ran while one was open for 0% of the time, Pallas kernels for 16%

profile of v4, /device:TPU:0, one launch (start us, length us, event | category | flops | bytes accessed | tf_op | source)
XLA Modules:
  0.0 131.1 jit_solution(6989593243976530543)
XLA Ops:
  0.7 1.2 pack.1
  1.9 4.1 %collective-permute-start.1 = (bf16[96,768]{1,0:T(8,128)(2,1)S(1)}, bf16[96,768]{1,0:T(8,128)(2,1)S(1)}, u32[]{:S(2)}, u32[]{:S(2)}) collective-permute-start(bf16[96,768]{1,0:T(8,128)(2,1)S(1)} %get-tuple-element.166.rest_0_), channel_id=1, source_target_pairs={{0,16},{4,20},{8,24},{12,28},{16,0},{20,4},{24,8},{28,12},{1,17},{... | collective-permute-start | bytes 442376 | tf_op jit(solution)/shard_map/ppermute | solution.py:571
  6.0 1.6 %collective-permute-start.4 = (bf16[96,768]{1,0:T(8,128)(2,1)S(1)}, bf16[96,768]{1,0:T(8,128)(2,1)S(1)}, u32[]{:S(2)}, u32[]{:S(2)}) collective-permute-start(bf16[96,768]{1,0:T(8,128)(2,1)S(1)} %get-tuple-element.166.rest_0_), channel_id=1, source_target_pairs={{0,8},{4,12},{8,0},{12,4},{16,24},{20,28},{24,16},{28,20},{1,9},{5... | collective-permute-start | bytes 442376 | tf_op jit(solution)/shard_map/ppermute | solution.py:571
  7.6 2.2 %prep.1 = (bf16[512,768]{1,0:T(8,128)(2,1)S(1)}, bf16[768,512]{1,0:T(8,128)(2,1)S(1)}, f32[3,512,512]{2,1,0:T(8,128)S(1)}, s32[1,1024]{1,0:T(1,128)S(1)}, bf16[5...) custom-call(s32[1,4]{1,0:T(1,128)} %seg_in.1, f32[3,32]{1,0:T(4,128)} %bitcast.8, ...), custom_call_target="tpu_custom_call" | custom-call | tf_op jit(solution)/shard_map/prep/pallas_call | solution.py:61
  9.8 1.6 %collective-permute-start = (bf16[96,1536]{1,0:T(8,128)(2,1)S(1)}, bf16[96,1536]{1,0:T(8,128)(2,1)S(1)}, u32[]{:S(2)}, u32[]{:S(2)}) collective-permute-start(bf16[96,1536]{1,0:T(8,128)(2,1)S(1)} %get-tuple-element.170.rest_0_), channel_id=1, source_target_pairs={{0,4},{4,0},{8,12},{12,8},{16,20},{20,16},{24,28},{28,24},{1,5},{5... | collective-permute-start | bytes 884744 | tf_op jit(solution)/shard_map/ppermute | solution.py:571
  11.4 1.8 %collective-permute-done.1.rest_4_ = bf16[96,768]{1,0:T(8,128)(2,1)S(1)} collective-permute-done((bf16[96,768]{1,0:T(8,128)(2,1)S(1)}, bf16[96,768]{1,0:T(8,128)(2,1)S(1)}, u32[]{:S(2)}, u32[]{:S(2)}) %collective-permute-start.1) | collective-permute-done | bytes 147488 | tf_op jit(solution)/shard_map/ppermute | solution.py:571
  13.7 1.5 %collective-permute-start.3 = (bf16[96,768]{1,0:T(8,128)(2,1)S(1)}, bf16[96,768]{1,0:T(8,128)(2,1)S(1)}, u32[]{:S(2)}, u32[]{:S(2)}) collective-permute-start(bf16[96,768]{1,0:T(8,128)(2,1)S(1)} %get-tuple-element.166.rest_0_), channel_id=1, source_target_pairs={{0,4},{4,0},{8,12},{12,8},{16,20},{20,16},{24,28},{28,24},{1,5},{5... | collective-permute-start | bytes 442376 | tf_op jit(solution)/shard_map/ppermute | solution.py:571
  15.2 3.4 %collective-permute-start.7 = (bf16[96,768]{1,0:T(8,128)(2,1)S(1)}, bf16[96,768]{1,0:T(8,128)(2,1)S(1)}, u32[]{:S(2)}, u32[]{:S(2)}) collective-permute-start(bf16[96,768]{1,0:T(8,128)(2,1)S(1)} %collective-permute-done.1.rest_4_), channel_id=1, source_target_pairs={{0,8},{4,12},{8,0},{12,4},{16,24},{20,28},{24,16},{28,20},{1,9},{5... | collective-permute-start | bytes 442376 | tf_op jit(solution)/shard_map/ppermute | solution.py:571
  19.2 2.8 %collective-permute-done.3.rest_1_ = bf16[96,768]{1,0:T(8,128)(2,1)S(1)} collective-permute-done((bf16[96,768]{1,0:T(8,128)(2,1)S(1)}, bf16[96,768]{1,0:T(8,128)(2,1)S(1)}, u32[]{:S(2)}, u32[]{:S(2)}) %collective-permute-start.3) | collective-permute-done | bytes 147488 | tf_op jit(solution)/shard_map/ppermute | solution.py:571
  22.0 2.5 %collective-permute-start.6 = (bf16[96,768]{1,0:T(8,128)(2,1)S(1)}, bf16[96,768]{1,0:T(8,128)(2,1)S(1)}, u32[]{:S(2)}, u32[]{:S(2)}) collective-permute-start(bf16[96,768]{1,0:T(8,128)(2,1)S(1)} %collective-permute-done.1.rest_4_), channel_id=1, source_target_pairs={{0,4},{4,0},{8,12},{12,8},{16,20},{20,16},{24,28},{28,24},{1,5},{5... | collective-permute-start | bytes 442376 | tf_op jit(solution)/shard_map/ppermute | solution.py:571
  25.4 1.6 %collective-permute-start.11 = (bf16[96,1536]{1,0:T(8,128)(2,1)S(1)}, bf16[96,1536]{1,0:T(8,128)(2,1)S(1)}, u32[]{:S(2)}, u32[]{:S(2)}) collective-permute-start(bf16[96,1536]{1,0:T(8,128)(2,1)S(1)} %get-tuple-element.170.rest_0_), channel_id=1, source_target_pairs={{0,8},{4,12},{8,0},{12,4},{16,24},{20,28},{24,16},{28,20},{1,9},{5... | collective-permute-start | bytes 884744 | tf_op jit(solution)/shard_map/ppermute | solution.py:571
  27.0 1.5 %collective-permute-done.2.rest_4_ = bf16[96,1536]{1,0:T(8,128)(2,1)S(1)} collective-permute-done((bf16[96,1536]{1,0:T(8,128)(2,1)S(1)}, bf16[96,1536]{1,0:T(8,128)(2,1)S(1)}, u32[]{:S(2)}, u32[]{:S(2)}) %collective-permute-start.2) | collective-permute-done | bytes 294944 | tf_op jit(solution)/shard_map/ppermute | solution.py:571
  29.1 1.6 %collective-permute-done.8.rest_7_ = bf16[96,768]{1,0:T(8,128)(2,1)S(1)} collective-permute-done((bf16[96,768]{1,0:T(8,128)(2,1)S(1)}, bf16[96,768]{1,0:T(8,128)(2,1)S(1)}, u32[]{:S(2)}, u32[]{:S(2)}) %collective-permute-start.8) | collective-permute-done | bytes 147488 | tf_op jit(solution)/shard_map/ppermute | solution.py:571
  30.7 3.1 %attend.1 = (bf16[768,768]{1,0:T(8,128)(2,1)S(1)}, bf16[512,576]{1,0:T(8,128)(2,1)S(1)}, bf16[3,512,512]{2,1,0:T(8,128)(2,1)S(1)}, bf16[512,192]{1,0:T(8,128)(2,...) custom-call(bf16[512,768]{1,0:T(8,128)(2,1)S(1)} %get-tuple-element.159.act, ...), custom_call_target="tpu_custom_call" | custom-call | tf_op jit(solution)/shard_map/attend/pallas_call | solution.py:61
  35.3 1.5 %collective-permute-start.10 = (bf16[96,1536]{1,0:T(8,128)(2,1)S(1)}, bf16[96,1536]{1,0:T(8,128)(2,1)S(1)}, u32[]{:S(2)}, u32[]{:S(2)}) collective-permute-start(bf16[96,1536]{1,0:T(8,128)(2,1)S(1)} %collective-permute-done.2.rest_4_), channel_id=1, source_target_pairs={{0,4},{4,0},{8,12},{12,8},{16,20},{20,16},{24,28},{28,24},{1,5},{5... | collective-permute-start | bytes 884744 | tf_op jit(solution)/shard_map/ppermute | solution.py:571
  36.9 1.6 %collective-permute-start.13 = (bf16[128,768]{1,0:T(8,128)(2,1)S(1)}, bf16[128,768]{1,0:T(8,128)(2,1)S(1)}, u32[]{:S(2)}, u32[]{:S(2)}) collective-permute-start(bf16[128,768]{1,0:T(8,128)(2,1)S(1)} %get-tuple-element.172.one), channel_id=1, source_target_pairs={{0,2},{1,3},{2,0},{3,1},{4,6},{5,7},{6,4},{7,5},{8,10},{9,11},{10,... | collective-permute-start | bytes 589832 | tf_op jit(solution)/shard_map/ppermute | solution.py:574
  39.0 4.2 %collective-permute-done.12.rest_6_ = bf16[96,1536]{1,0:T(8,128)(2,1)S(1)} collective-permute-done((bf16[96,1536]{1,0:T(8,128)(2,1)S(1)}, bf16[96,1536]{1,0:T(8,128)(2,1)S(1)}, u32[]{:S(2)}, u32[]{:S(2)}) %collective-permute-start.12) | collective-permute-done | bytes 294944 | tf_op jit(solution)/shard_map/ppermute | solution.py:571
  43.3 1.5 %collective-permute-start.18 = (bf16[96,1536]{1,0:T(8,128)(2,1)S(1)}, bf16[96,1536]{1,0:T(8,128)(2,1)S(1)}, u32[]{:S(2)}, u32[]{:S(2)}) collective-permute-start(bf16[96,1536]{1,0:T(8,128)(2,1)S(1)} %collective-permute-done.12.rest_6_), channel_id=1, source_target_pairs={{0,4},{4,0},{8,12},{12,8},{16,20},{20,16},{24,28},{28,24},{1,5},{5... | collective-permute-start | bytes 884744 | tf_op jit(solution)/shard_map/ppermute | solution.py:571
  44.7 1.4 %collective-permute-start.17 = (bf16[96,1536]{1,0:T(8,128)(2,1)S(1)}, bf16[96,1536]{1,0:T(8,128)(2,1)S(1)}, u32[]{:S(2)}, u32[]{:S(2)}) collective-permute-start(bf16[96,1536]{1,0:T(8,128)(2,1)S(1)} %collective-permute-done.rest_1_), channel_id=1, source_target_pairs={{0,8},{4,12},{8,0},{12,4},{16,24},{20,28},{24,16},{28,20},{1,9},{5... | collective-permute-start | bytes 884744 | tf_op jit(solution)/shard_map/ppermute | solution.py:571
  46.3 1.6 %collective-permute-done.14.two = bf16[128,768]{1,0:T(8,128)(2,1)S(1)} collective-permute-done((bf16[128,768]{1,0:T(8,128)(2,1)S(1)}, bf16[128,768]{1,0:T(8,128)(2,1)S(1)}, u32[]{:S(2)}, u32[]{:S(2)}) %collective-permute-start.14) | collective-permute-done | bytes 196640 | tf_op jit(solution)/shard_map/ppermute | solution.py:574
  48.0 3.0 %collective-permute-done.18.rest_7_ = bf16[96,1536]{1,0:T(8,128)(2,1)S(1)} collective-permute-done((bf16[96,1536]{1,0:T(8,128)(2,1)S(1)}, bf16[96,1536]{1,0:T(8,128)(2,1)S(1)}, u32[]{:S(2)}, u32[]{:S(2)}) %collective-permute-start.18) | collective-permute-done | bytes 294944 | tf_op jit(solution)/shard_map/ppermute | solution.py:571
  51.0 1.7 %collective-permute-done.17.rest_3_ = bf16[96,1536]{1,0:T(8,128)(2,1)S(1)} collective-permute-done((bf16[96,1536]{1,0:T(8,128)(2,1)S(1)}, bf16[96,1536]{1,0:T(8,128)(2,1)S(1)}, u32[]{:S(2)}, u32[]{:S(2)}) %collective-permute-start.17) | collective-permute-done | bytes 294944 | tf_op jit(solution)/shard_map/ppermute | solution.py:571
  52.7 3.5 %ffn.1 = (f32[512,768]{1,0:T(8,128)S(1)}, bf16[512,768]{1,0:T(8,128)(2,1)S(1)}, bf16[512,768]{1,0:T(8,128)(2,1)S(1)}, bf16[512,768]{1,0:T(8,128)(2,1)S(1)}, bf16...) custom-call(bf16[512,768]{1,0:T(8,128)(2,1)S(1)} %get-tuple-element., ...), custom_call_target="tpu_custom_call" | custom-call | tf_op jit(solution)/shard_map/ffn/pallas_call | solution.py:61
  56.3 1.7 %collective-permute-done.19.two = bf16[256,768]{1,0:T(8,128)(2,1)S(1)} collective-permute-done((bf16[256,768]{1,0:T(8,128)(2,1)S(1)}, bf16[256,768]{1,0:T(8,128)(2,1)S(1)}, u32[]{:S(2)}, u32[]{:S(2)}) %collective-permute-start.19) | collective-permute-done | bytes 393248 | tf_op jit(solution)/shard_map/ppermute | solution.py:574
  58.1 1.6 %collective-permute-start.20 = (bf16[256,768]{1,0:T(8,128)(2,1)S(1)}, bf16[256,768]{1,0:T(8,128)(2,1)S(1)}, u32[]{:S(2)}, u32[]{:S(2)}) collective-permute-start(bf16[256,768]{1,0:T(8,128)(2,1)S(1)} %add.6.one), channel_id=1, source_target_pairs={{0,2},{1,3},{2,0},{3,1},{4,6},{5,7},{6,4},{7,5},{8,10},{9,11},{10,... | collective-permute-start | bytes 1179656 | tf_op jit(solution)/shard_map/ppermute | solution.py:574
  59.7 0.9 down_grad.1
  60.6 1.1 in_grad.1
  61.7 1.8 %collective-permute-start.22 = (bf16[4,96,768]{2,1,0:T(8,128)(2,1)S(1)}, bf16[4,96,768]{2,1,0:T(8,128)(2,1)S(1)}, u32[]{:S(2)}, u32[]{:S(2)}) collective-permute-start(bf16[4,96,768]{2,1,0:T(8,128)(2,1)S(1)} %get-tuple-element.201), channel_id=1, source_target_pairs={{0,8},{4,12},{8,0},{12,4},{16,24},{20,28},{24,16},{28,20},{1,9},{5... | collective-permute-start | bytes 1769480 | tf_op jit(solution)/shard_map/ppermute | solution.py:571
  64.0 1.6 %ffn_out.1 = (bf16[256,768]{1,0:T(8,128)(2,1)S(1)}, bf16[256,768]{1,0:T(8,128)(2,1)S(1)}) custom-call(bf16[512,768]{1,0:T(8,128)(2,1)S(1)} %get-tuple-element.187.right.hidden, bf16[768,768]{1,0:T(8,128)(2,1)S(1)} %get-tuple-element.188.down), custom_call_target="tpu_custom_call" | custom-call | tf_op jit(solution)/shard_map/ffn_out/pallas_call | solution.py:61
  65.7 3.7 %collective-permute-done.20.two = bf16[256,768]{1,0:T(8,128)(2,1)S(1)} collective-permute-done((bf16[256,768]{1,0:T(8,128)(2,1)S(1)}, bf16[256,768]{1,0:T(8,128)(2,1)S(1)}, u32[]{:S(2)}, u32[]{:S(2)}) %collective-permute-start.20) | collective-permute-done | bytes 393248 | tf_op jit(solution)/shard_map/ppermute | solution.py:574
  69.5 1.7 %collective-permute-done.21.other = bf16[256,768]{1,0:T(8,128)(2,1)S(1)} collective-permute-done((bf16[256,768]{1,0:T(8,128)(2,1)S(1)}, bf16[256,768]{1,0:T(8,128)(2,1)S(1)}, u32[]{:S(2)}, u32[]{:S(2)}) %collective-permute-start.21) | collective-permute-done | bytes 393248 | tf_op jit(solution)/shard_map/ppermute | solution.py:574
  71.2 5.9 %attend_back.1 = (bf16[4,96,768]{2,1,0:T(8,128)(2,1)S(1)}, bf16[2,96,768]{2,1,0:T(8,128)(2,1)S(1)}, f32[128,768]{1,0:T(8,128)S(1)}, bf16[200,768]{1,0:T(8,128)(2,1)S(1)}, bf16[512,576]{1,0:T(8,128)(2,1)S(1)}) custom-call(f32[512,768]{1,0:T(8,128)S(1)} %get-tuple-element.232.resid, bf16[512,768]{1,0:T(8,128)(2,1)S(1)} %get-tuple-element.158.dy.left, ...), custom_call_target="tpu_custom_call" | custom-call | tf_op jit(solution)/shard_map/attend_back/pallas_call | solution.py:61
  77.3 1.0 collective-permute-done.23.got
  79.1 1.4 %act_grad.1 = (bf16[256,768]{1,0:T(8,128)(2,1)S(1)}, bf16[128,768]{1,0:T(8,128)(2,1)S(1)}, bf16[128,768]{1,0:T(8,128)(2,1)S(1)}) custom-call(bf16[512,576]{1,0:T(8,128)(2,1)S(1)} %get-tuple-element.208.proj_grad, bf16[768,768]{1,0:T(8,128)(2,1)S(1)} %get-tuple-element.191.weights), custom_call_target="tpu_custom_call" | custom-call | tf_op jit(solution)/shard_map/act_grad/pallas_call | solution.py:61
  81.8 3.5 %collective-permute-start.29 = (bf16[2,96,768]{2,1,0:T(8,128)(2,1)S(1)}, bf16[2,96,768]{2,1,0:T(8,128)(2,1)S(1)}, u32[]{:S(2)}, u32[]{:S(2)}) collective-permute-start(bf16[2,96,768]{2,1,0:T(8,128)(2,1)S(1)} %get-tuple-element.203), channel_id=1, source_target_pairs={{0,16},{4,20},{8,24},{12,28},{16,0},{20,4},{24,8},{28,12},{1,17},{... | collective-permute-start | bytes 884744 | tf_op jit(solution)/shard_map/ppermute | solution.py:571
  85.2 1.6 %collective-permute-done.24.got = bf16[200,768]{1,0:T(8,128)(2,1)S(1)} collective-permute-done((bf16[200,768]{1,0:T(8,128)(2,1)S(1)}, bf16[200,768]{1,0:T(8,128)(2,1)S(1)}, u32[]{:S(2)}, u32[]{:S(2)}) %collective-permute-start.24) | collective-permute-done | bytes 307232 | tf_op jit(solution)/shard_map/ppermute | solution.py:571
  86.9 1.8 %collective-permute-start.33 = (bf16[200,768]{1,0:T(8,128)(2,1)S(1)}, bf16[200,768]{1,0:T(8,128)(2,1)S(1)}, u32[]{:S(2)}, u32[]{:S(2)}) collective-permute-start(bf16[200,768]{1,0:T(8,128)(2,1)S(1)} %last_high.1.sent), channel_id=1, source_target_pairs={{0,8},{4,12},{8,0},{12,4},{16,24},{20,28},{24,16},{28,20},{1,9},{5... | collective-permute-start | bytes 921608 | tf_op jit(solution)/shard_map/ppermute | solution.py:571
  89.6 1.6 %collective-permute-start.34 = (bf16[256,768]{1,0:T(8,128)(2,1)S(1)}, bf16[256,768]{1,0:T(8,128)(2,1)S(1)}, u32[]{:S(2)}, u32[]{:S(2)}) collective-permute-start(bf16[256,768]{1,0:T(8,128)(2,1)S(1)} %get-tuple-element.234), channel_id=1, source_target_pairs={{0,2},{1,3},{2,0},{3,1},{4,6},{5,7},{6,4},{7,5},{8,10},{9,11},{10,... | collective-permute-start | bytes 1179656 | tf_op jit(solution)/shard_map/ppermute | solution.py:574
  91.2 6.0 %collective-permute-done.28.got = bf16[2,96,768]{2,1,0:T(8,128)(2,1)S(1)} collective-permute-done((bf16[2,96,768]{2,1,0:T(8,128)(2,1)S(1)}, bf16[2,96,768]{2,1,0:T(8,128)(2,1)S(1)}, u32[]{:S(2)}, u32[]{:S(2)}) %collective-permute-start.28) | collective-permute-done | bytes 294944 | tf_op jit(solution)/shard_map/ppermute | solution.py:571
  97.5 1.6 %collective-permute-start.31 = (bf16[96,768]{1,0:T(8,128)(2,1)S(1)}, bf16[96,768]{1,0:T(8,128)(2,1)S(1)}, u32[]{:S(2)}, u32[]{:S(2)}) collective-permute-start(bf16[96,768]{1,0:T(8,128)(2,1)S(1)} %get-tuple-element.223), channel_id=1, source_target_pairs={{0,4},{4,0},{8,12},{12,8},{16,20},{20,16},{24,28},{28,24},{1,5},{5... | collective-permute-start | bytes 442376 | tf_op jit(solution)/shard_map/ppermute | solution.py:571
  99.0 5.4 %collective-permute-done.30.rest_1_ = bf16[96,768]{1,0:T(8,128)(2,1)S(1)} collective-permute-done((bf16[96,768]{1,0:T(8,128)(2,1)S(1)}, bf16[96,768]{1,0:T(8,128)(2,1)S(1)}, u32[]{:S(2)}, u32[]{:S(2)}) %collective-permute-start.30) | collective-permute-done | bytes 147488 | tf_op jit(solution)/shard_map/ppermute | solution.py:571
  104.6 1.5 %collective-permute-done.33.got = bf16[200,768]{1,0:T(8,128)(2,1)S(1)} collective-permute-done((bf16[200,768]{1,0:T(8,128)(2,1)S(1)}, bf16[200,768]{1,0:T(8,128)(2,1)S(1)}, u32[]{:S(2)}, u32[]{:S(2)}) %collective-permute-start.33) | collective-permute-done | bytes 307232 | tf_op jit(solution)/shard_map/ppermute | solution.py:571
  106.2 1.9 %collective-permute-start.35 = (bf16[104,768]{1,0:T(8,128)(2,1)S(1)}, bf16[104,768]{1,0:T(8,128)(2,1)S(1)}, u32[]{:S(2)}, u32[]{:S(2)}) collective-permute-start(bf16[104,768]{1,0:T(8,128)(2,1)S(1)} %get-tuple-element.231.rest_1_), channel_id=1, source_target_pairs={{0,16},{4,20},{8,24},{12,28},{16,0},{20,4},{24,8},{28,12},{1,17},{... | collective-permute-start | bytes 479240 | tf_op jit(solution)/shard_map/ppermute | solution.py:571
  108.1 1.0 share_out.1
  109.2 1.9 %fetch.1 = (f32[3,96,192]{2,1,0:T(8,128)S(1)}, f32[3,96,192]{2,1,0:T(8,128)S(1)}, f32[3,96,192]{2,1,0:T(8,128)S(1)}, f32[96,192]{1,0:T(8,128)S(1)}, f32[96,192]{...) custom-call(f32[3,96,192]{2,1,0:T(8,128)} %refs_0_, ...), custom_call_target="tpu_custom_call" | custom-call | tf_op jit(solution)/shard_map/fetch/pallas_call | solution.py:61
  111.1 4.8 %collective-permute-done.35.rest_2_ = bf16[104,768]{1,0:T(8,128)(2,1)S(1)} collective-permute-done((bf16[104,768]{1,0:T(8,128)(2,1)S(1)}, bf16[104,768]{1,0:T(8,128)(2,1)S(1)}, u32[]{:S(2)}, u32[]{:S(2)}) %collective-permute-start.35) | collective-permute-done | bytes 159776 | tf_op jit(solution)/shard_map/ppermute | solution.py:571
  116.6 12.0 %all_to_all.5.refs_0_ = f32[32,1,384]{2,1,0:T(1,128)S(1)} all-to-all(f32[32,1,384]{2,1,0:T(1,128)} %get-tuple-element.243), channel_id=1, replica_groups=mesh['dp'=8,'tp'=4] {'dp','tp'}, dimensions={0} | all-to-all | bytes 98304 | tf_op jit(solution)/shard_map/all_to_all | solution.py:829
  128.6 2.4 %adam.1 = (f32[1,1]{1,0:T(1,128)}, f32[3,96,192]{2,1,0:T(8,128)}, f32[3,96,192]{2,1,0:T(8,128)}, f32[3,96,192]{2,1,0:T(8,128)}, bf16[3,96,192]{2,1,0:T(8,128)(2,...) custom-call(f32[32,1,384]{2,1,0:T(1,128)S(1)} %all_to_all.5.refs_0_,, ...), custom_call_target="tpu_custom_call" | custom-call | tf_op jit(solution)/shard_map/adam/pallas_call | solution.py:61
  (52 shorter events, 10.2 us)
Async XLA Ops:
  1.9 11.2 %collective-permute-start.1 = (bf16[96,768]{1,0:T(8,128)(2,1)S(1)}, bf16[96,768]{1,0:T(8,128)(2,1)S(1)}, u32[]{:S(2)}, u32[]{:S(2)}) collective-permute-start(bf16[96,768]{1,0:T(8,128)(2,1)S(1)} %get-tuple-element.166.rest_0_), channel_id=1, source_target_pairs={{0,16},{4,20},{8,24},{12,28},{16,0},{20,4},{24,8},{28,12},{1,17},{... | collective-permute-start | bytes 442376 | tf_op jit(solution)/shard_map/ppermute | solution.py:571
  6.0 12.6 %collective-permute-start.4 = (bf16[96,768]{1,0:T(8,128)(2,1)S(1)}, bf16[96,768]{1,0:T(8,128)(2,1)S(1)}, u32[]{:S(2)}, u32[]{:S(2)}) collective-permute-start(bf16[96,768]{1,0:T(8,128)(2,1)S(1)} %get-tuple-element.166.rest_0_), channel_id=1, source_target_pairs={{0,8},{4,12},{8,0},{12,4},{16,24},{20,28},{24,16},{28,20},{1,9},{5... | collective-permute-start | bytes 442376 | tf_op jit(solution)/shard_map/ppermute | solution.py:571
  9.8 17.2 %collective-permute-start = (bf16[96,1536]{1,0:T(8,128)(2,1)S(1)}, bf16[96,1536]{1,0:T(8,128)(2,1)S(1)}, u32[]{:S(2)}, u32[]{:S(2)}) collective-permute-start(bf16[96,1536]{1,0:T(8,128)(2,1)S(1)} %get-tuple-element.170.rest_0_), channel_id=1, source_target_pairs={{0,4},{4,0},{8,12},{12,8},{16,20},{20,16},{24,28},{28,24},{1,5},{5... | collective-permute-start | bytes 884744 | tf_op jit(solution)/shard_map/ppermute | solution.py:571
  13.1 15.4 %collective-permute-start.2 = (bf16[96,1536]{1,0:T(8,128)(2,1)S(1)}, bf16[96,1536]{1,0:T(8,128)(2,1)S(1)}, u32[]{:S(2)}, u32[]{:S(2)}) collective-permute-start(bf16[96,1536]{1,0:T(8,128)(2,1)S(1)} %get-tuple-element.170.rest_0_), channel_id=1, source_target_pairs={{0,16},{4,20},{8,24},{12,28},{16,0},{20,4},{24,8},{28,12},{1,17},{... | collective-permute-start | bytes 884744 | tf_op jit(solution)/shard_map/ppermute | solution.py:571
  13.7 8.3 %collective-permute-start.3 = (bf16[96,768]{1,0:T(8,128)(2,1)S(1)}, bf16[96,768]{1,0:T(8,128)(2,1)S(1)}, u32[]{:S(2)}, u32[]{:S(2)}) collective-permute-start(bf16[96,768]{1,0:T(8,128)(2,1)S(1)} %get-tuple-element.166.rest_0_), channel_id=1, source_target_pairs={{0,4},{4,0},{8,12},{12,8},{16,20},{20,16},{24,28},{28,24},{1,5},{5... | collective-permute-start | bytes 442376 | tf_op jit(solution)/shard_map/ppermute | solution.py:571
  15.2 9.3 %collective-permute-start.7 = (bf16[96,768]{1,0:T(8,128)(2,1)S(1)}, bf16[96,768]{1,0:T(8,128)(2,1)S(1)}, u32[]{:S(2)}, u32[]{:S(2)}) collective-permute-start(bf16[96,768]{1,0:T(8,128)(2,1)S(1)} %collective-permute-done.1.rest_4_), channel_id=1, source_target_pairs={{0,8},{4,12},{8,0},{12,4},{16,24},{20,28},{24,16},{28,20},{1,9},{5... | collective-permute-start | bytes 442376 | tf_op jit(solution)/shard_map/ppermute | solution.py:571
  18.6 6.8 %collective-permute-start.5 = (bf16[96,768]{1,0:T(8,128)(2,1)S(1)}, bf16[96,768]{1,0:T(8,128)(2,1)S(1)}, u32[]{:S(2)}, u32[]{:S(2)}) collective-permute-start(bf16[96,768]{1,0:T(8,128)(2,1)S(1)} %collective-permute-done.4.rest_2_), channel_id=1, source_target_pairs={{0,4},{4,0},{8,12},{12,8},{16,20},{20,16},{24,28},{28,24},{1,5},{5... | collective-permute-start | bytes 442376 | tf_op jit(solution)/shard_map/ppermute | solution.py:571
  22.0 7.1 %collective-permute-start.6 = (bf16[96,768]{1,0:T(8,128)(2,1)S(1)}, bf16[96,768]{1,0:T(8,128)(2,1)S(1)}, u32[]{:S(2)}, u32[]{:S(2)}) collective-permute-start(bf16[96,768]{1,0:T(8,128)(2,1)S(1)} %collective-permute-done.1.rest_4_), channel_id=1, source_target_pairs={{0,4},{4,0},{8,12},{12,8},{16,20},{20,16},{24,28},{28,24},{1,5},{5... | collective-permute-start | bytes 442376 | tf_op jit(solution)/shard_map/ppermute | solution.py:571
  24.5 6.2 %collective-permute-start.8 = (bf16[96,768]{1,0:T(8,128)(2,1)S(1)}, bf16[96,768]{1,0:T(8,128)(2,1)S(1)}, u32[]{:S(2)}, u32[]{:S(2)}) collective-permute-start(bf16[96,768]{1,0:T(8,128)(2,1)S(1)} %collective-permute-done.7.rest_6_), channel_id=1, source_target_pairs={{0,4},{4,0},{8,12},{12,8},{16,20},{20,16},{24,28},{28,24},{1,5},{5... | collective-permute-start | bytes 442376 | tf_op jit(solution)/shard_map/ppermute | solution.py:571
  25.4 9.3 %collective-permute-start.11 = (bf16[96,1536]{1,0:T(8,128)(2,1)S(1)}, bf16[96,1536]{1,0:T(8,128)(2,1)S(1)}, u32[]{:S(2)}, u32[]{:S(2)}) collective-permute-start(bf16[96,1536]{1,0:T(8,128)(2,1)S(1)} %get-tuple-element.170.rest_0_), channel_id=1, source_target_pairs={{0,8},{4,12},{8,0},{12,4},{16,24},{20,28},{24,16},{28,20},{1,9},{5... | collective-permute-start | bytes 884744 | tf_op jit(solution)/shard_map/ppermute | solution.py:571
  33.8 3.1 %collective-permute-start.9 = (bf16[256,768]{1,0:T(8,128)(2,1)S(1)}, bf16[256,768]{1,0:T(8,128)(2,1)S(1)}, u32[]{:S(2)}, u32[]{:S(2)}) collective-permute-start(bf16[256,768]{1,0:T(8,128)(2,1)S(1)} %get-tuple-element.168), channel_id=1, source_target_pairs={{0,1},{1,0},{2,3},{3,2},{4,5},{5,4},{6,7},{7,6},{8,9},{9,8},{10,11... | collective-permute-start | bytes 1179656 | tf_op jit(solution)/shard_map/ppermute | solution.py:574
  34.8 8.5 %collective-permute-start.12 = (bf16[96,1536]{1,0:T(8,128)(2,1)S(1)}, bf16[96,1536]{1,0:T(8,128)(2,1)S(1)}, u32[]{:S(2)}, u32[]{:S(2)}) collective-permute-start(bf16[96,1536]{1,0:T(8,128)(2,1)S(1)} %collective-permute-done.2.rest_4_), channel_id=1, source_target_pairs={{0,8},{4,12},{8,0},{12,4},{16,24},{20,28},{24,16},{28,20},{1,9},{5... | collective-permute-start | bytes 884744 | tf_op jit(solution)/shard_map/ppermute | solution.py:571
  35.3 10.8 %collective-permute-start.10 = (bf16[96,1536]{1,0:T(8,128)(2,1)S(1)}, bf16[96,1536]{1,0:T(8,128)(2,1)S(1)}, u32[]{:S(2)}, u32[]{:S(2)}) collective-permute-start(bf16[96,1536]{1,0:T(8,128)(2,1)S(1)} %collective-permute-done.2.rest_4_), channel_id=1, source_target_pairs={{0,4},{4,0},{8,12},{12,8},{16,20},{20,16},{24,28},{28,24},{1,5},{5... | collective-permute-start | bytes 884744 | tf_op jit(solution)/shard_map/ppermute | solution.py:571
  36.9 9.3 %collective-permute-start.13 = (bf16[128,768]{1,0:T(8,128)(2,1)S(1)}, bf16[128,768]{1,0:T(8,128)(2,1)S(1)}, u32[]{:S(2)}, u32[]{:S(2)}) collective-permute-start(bf16[128,768]{1,0:T(8,128)(2,1)S(1)} %get-tuple-element.172.one), channel_id=1, source_target_pairs={{0,2},{1,3},{2,0},{3,1},{4,6},{5,7},{6,4},{7,5},{8,10},{9,11},{10,... | collective-permute-start | bytes 589832 | tf_op jit(solution)/shard_map/ppermute | solution.py:574
  38.5 9.4 %collective-permute-start.14 = (bf16[128,768]{1,0:T(8,128)(2,1)S(1)}, bf16[128,768]{1,0:T(8,128)(2,1)S(1)}, u32[]{:S(2)}, u32[]{:S(2)}) collective-permute-start(bf16[128,768]{1,0:T(8,128)(2,1)S(1)} %get-tuple-element.174.one), channel_id=1, source_target_pairs={{0,2},{1,3},{2,0},{3,1},{4,6},{5,7},{6,4},{7,5},{8,10},{9,11},{10,... | collective-permute-start | bytes 589832 | tf_op jit(solution)/shard_map/ppermute | solution.py:574
  43.3 7.8 %collective-permute-start.18 = (bf16[96,1536]{1,0:T(8,128)(2,1)S(1)}, bf16[96,1536]{1,0:T(8,128)(2,1)S(1)}, u32[]{:S(2)}, u32[]{:S(2)}) collective-permute-start(bf16[96,1536]{1,0:T(8,128)(2,1)S(1)} %collective-permute-done.12.rest_6_), channel_id=1, source_target_pairs={{0,4},{4,0},{8,12},{12,8},{16,20},{20,16},{24,28},{28,24},{1,5},{5... | collective-permute-start | bytes 884744 | tf_op jit(solution)/shard_map/ppermute | solution.py:571
  44.7 8.0 %collective-permute-start.17 = (bf16[96,1536]{1,0:T(8,128)(2,1)S(1)}, bf16[96,1536]{1,0:T(8,128)(2,1)S(1)}, u32[]{:S(2)}, u32[]{:S(2)}) collective-permute-start(bf16[96,1536]{1,0:T(8,128)(2,1)S(1)} %collective-permute-done.rest_1_), channel_id=1, source_target_pairs={{0,8},{4,12},{8,0},{12,4},{16,24},{20,28},{24,16},{28,20},{1,9},{5... | collective-permute-start | bytes 884744 | tf_op jit(solution)/shard_map/ppermute | solution.py:571
  46.2 6.5 %collective-permute-start.15 = (bf16[128,768]{1,0:T(8,128)(2,1)S(1)}, bf16[128,768]{1,0:T(8,128)(2,1)S(1)}, u32[]{:S(2)}, u32[]{:S(2)}) collective-permute-start(bf16[128,768]{1,0:T(8,128)(2,1)S(1)} %add.4.own_a), channel_id=1, source_target_pairs={{0,1},{1,0},{2,3},{3,2},{4,5},{5,4},{6,7},{7,6},{8,9},{9,8},{10,11... | collective-permute-start | bytes 589832 | tf_op jit(solution)/shard_map/ppermute | solution.py:574
  47.9 4.8 %collective-permute-start.16 = (bf16[128,768]{1,0:T(8,128)(2,1)S(1)}, bf16[128,768]{1,0:T(8,128)(2,1)S(1)}, u32[]{:S(2)}, u32[]{:S(2)}) collective-permute-start(bf16[128,768]{1,0:T(8,128)(2,1)S(1)} %add.5.own_b), channel_id=1, source_target_pairs={{0,1},{1,0},{2,3},{3,2},{4,5},{5,4},{6,7},{7,6},{8,9},{9,8},{10,11... | collective-permute-start | bytes 589832 | tf_op jit(solution)/shard_map/ppermute | solution.py:574
  56.2 1.8 %collective-permute-start.19 = (bf16[256,768]{1,0:T(8,128)(2,1)S(1)}, bf16[256,768]{1,0:T(8,128)(2,1)S(1)}, u32[]{:S(2)}, u32[]{:S(2)}) collective-permute-start(bf16[256,768]{1,0:T(8,128)(2,1)S(1)} %get-tuple-element.178), channel_id=1, source_target_pairs={{0,1},{1,0},{2,3},{3,2},{4,5},{5,4},{6,7},{7,6},{8,9},{9,8},{10,11... | collective-permute-start | bytes 1179656 | tf_op jit(solution)/shard_map/ppermute | solution.py:574
  58.1 11.2 %collective-permute-start.20 = (bf16[256,768]{1,0:T(8,128)(2,1)S(1)}, bf16[256,768]{1,0:T(8,128)(2,1)S(1)}, u32[]{:S(2)}, u32[]{:S(2)}) collective-permute-start(bf16[256,768]{1,0:T(8,128)(2,1)S(1)} %add.6.one), channel_id=1, source_target_pairs={{0,2},{1,3},{2,0},{3,1},{4,6},{5,7},{6,4},{7,5},{8,10},{9,11},{10,... | collective-permute-start | bytes 1179656 | tf_op jit(solution)/shard_map/ppermute | solution.py:574
  61.7 15.5 %collective-permute-start.22 = (bf16[4,96,768]{2,1,0:T(8,128)(2,1)S(1)}, bf16[4,96,768]{2,1,0:T(8,128)(2,1)S(1)}, u32[]{:S(2)}, u32[]{:S(2)}) collective-permute-start(bf16[4,96,768]{2,1,0:T(8,128)(2,1)S(1)} %get-tuple-element.201), channel_id=1, source_target_pairs={{0,8},{4,12},{8,0},{12,4},{16,24},{20,28},{24,16},{28,20},{1,9},{5... | collective-permute-start | bytes 1769480 | tf_op jit(solution)/shard_map/ppermute | solution.py:571
  63.5 14.8 %collective-permute-start.23 = (bf16[4,96,768]{2,1,0:T(8,128)(2,1)S(1)}, bf16[4,96,768]{2,1,0:T(8,128)(2,1)S(1)}, u32[]{:S(2)}, u32[]{:S(2)}) collective-permute-start(bf16[4,96,768]{2,1,0:T(8,128)(2,1)S(1)} %get-tuple-element.205), channel_id=1, source_target_pairs={{0,4},{4,0},{8,12},{12,8},{16,20},{20,16},{24,28},{28,24},{1,5},{5... | collective-permute-start | bytes 1769480 | tf_op jit(solution)/shard_map/ppermute | solution.py:571
  69.4 1.8 %collective-permute-start.21 = (bf16[256,768]{1,0:T(8,128)(2,1)S(1)}, bf16[256,768]{1,0:T(8,128)(2,1)S(1)}, u32[]{:S(2)}, u32[]{:S(2)}) collective-permute-start(bf16[256,768]{1,0:T(8,128)(2,1)S(1)} %add.7.own), channel_id=1, source_target_pairs={{0,1},{1,0},{2,3},{3,2},{4,5},{5,4},{6,7},{7,6},{8,9},{9,8},{10,11... | collective-permute-start | bytes 1179656 | tf_op jit(solution)/shard_map/ppermute | solution.py:574
  78.5 8.4 %collective-permute-start.24 = (bf16[200,768]{1,0:T(8,128)(2,1)S(1)}, bf16[200,768]{1,0:T(8,128)(2,1)S(1)}, u32[]{:S(2)}, u32[]{:S(2)}) collective-permute-start(bf16[200,768]{1,0:T(8,128)(2,1)S(1)} %get-tuple-element.212.sent), channel_id=1, source_target_pairs={{0,4},{4,0},{8,12},{12,8},{16,20},{20,16},{24,28},{28,24},{1,5},{5... | collective-permute-start | bytes 921608 | tf_op jit(solution)/shard_map/ppermute | solution.py:571
  79.1 7.9 %collective-permute-start.25 = (bf16[256,768]{1,0:T(8,128)(2,1)S(1)}, bf16[256,768]{1,0:T(8,128)(2,1)S(1)}, u32[]{:S(2)}, u32[]{:S(2)}) collective-permute-start(bf16[256,768]{1,0:T(8,128)(2,1)S(1)} %get-tuple-element.214), channel_id=1, source_target_pairs={{0,1},{1,0},{2,3},{3,2},{4,5},{5,4},{6,7},{7,6},{8,9},{9,8},{10,11... | collective-permute-start | bytes 1179656 | tf_op jit(solution)/shard_map/ppermute | solution.py:574
  80.5 8.3 %collective-permute-start.26 = (bf16[128,768]{1,0:T(8,128)(2,1)S(1)}, bf16[128,768]{1,0:T(8,128)(2,1)S(1)}, u32[]{:S(2)}, u32[]{:S(2)}) collective-permute-start(bf16[128,768]{1,0:T(8,128)(2,1)S(1)} %get-tuple-element.215), channel_id=1, source_target_pairs={{0,1},{1,0},{2,3},{3,2},{4,5},{5,4},{6,7},{7,6},{8,9},{9,8},{10,11... | collective-permute-start | bytes 589832 | tf_op jit(solution)/shard_map/ppermute | solution.py:574
  81.0 16.2 %collective-permute-start.28 = (bf16[2,96,768]{2,1,0:T(8,128)(2,1)S(1)}, bf16[2,96,768]{2,1,0:T(8,128)(2,1)S(1)}, u32[]{:S(2)}, u32[]{:S(2)}) collective-permute-start(bf16[2,96,768]{2,1,0:T(8,128)(2,1)S(1)} %get-tuple-element.207), channel_id=1, source_target_pairs={{0,8},{4,12},{8,0},{12,4},{16,24},{20,28},{24,16},{28,20},{1,9},{5... | collective-permute-start | bytes 884744 | tf_op jit(solution)/shard_map/ppermute | solution.py:571
  81.8 15.6 %collective-permute-start.29 = (bf16[2,96,768]{2,1,0:T(8,128)(2,1)S(1)}, bf16[2,96,768]{2,1,0:T(8,128)(2,1)S(1)}, u32[]{:S(2)}, u32[]{:S(2)}) collective-permute-start(bf16[2,96,768]{2,1,0:T(8,128)(2,1)S(1)} %get-tuple-element.203), channel_id=1, source_target_pairs={{0,16},{4,20},{8,24},{12,28},{16,0},{20,4},{24,8},{28,12},{1,17},{... | collective-permute-start | bytes 884744 | tf_op jit(solution)/shard_map/ppermute | solution.py:571
  86.8 2.4 %collective-permute-start.27 = (bf16[128,768]{1,0:T(8,128)(2,1)S(1)}, bf16[128,768]{1,0:T(8,128)(2,1)S(1)}, u32[]{:S(2)}, u32[]{:S(2)}) collective-permute-start(bf16[128,768]{1,0:T(8,128)(2,1)S(1)} %get-tuple-element.216), channel_id=1, source_target_pairs={{0,1},{1,0},{2,3},{3,2},{4,5},{5,4},{6,7},{7,6},{8,9},{9,8},{10,11... | collective-permute-start | bytes 589832 | tf_op jit(solution)/shard_map/ppermute | solution.py:574
  86.9 19.2 %collective-permute-start.33 = (bf16[200,768]{1,0:T(8,128)(2,1)S(1)}, bf16[200,768]{1,0:T(8,128)(2,1)S(1)}, u32[]{:S(2)}, u32[]{:S(2)}) collective-permute-start(bf16[200,768]{1,0:T(8,128)(2,1)S(1)} %last_high.1.sent), channel_id=1, source_target_pairs={{0,8},{4,12},{8,0},{12,4},{16,24},{20,28},{24,16},{28,20},{1,9},{5... | collective-permute-start | bytes 921608 | tf_op jit(solution)/shard_map/ppermute | solution.py:571
  88.7 15.8 %collective-permute-start.32 = (bf16[2,96,768]{2,1,0:T(8,128)(2,1)S(1)}, bf16[2,96,768]{2,1,0:T(8,128)(2,1)S(1)}, u32[]{:S(2)}, u32[]{:S(2)}) collective-permute-start(bf16[2,96,768]{2,1,0:T(8,128)(2,1)S(1)} %get-tuple-element.230), channel_id=1, source_target_pairs={{0,4},{4,0},{8,12},{12,8},{16,20},{20,16},{24,28},{28,24},{1,5},{5... | collective-permute-start | bytes 884744 | tf_op jit(solution)/shard_map/ppermute | solution.py:571
  89.6 18.5 %collective-permute-start.34 = (bf16[256,768]{1,0:T(8,128)(2,1)S(1)}, bf16[256,768]{1,0:T(8,128)(2,1)S(1)}, u32[]{:S(2)}, u32[]{:S(2)}) collective-permute-start(bf16[256,768]{1,0:T(8,128)(2,1)S(1)} %get-tuple-element.234), channel_id=1, source_target_pairs={{0,2},{1,3},{2,0},{3,1},{4,6},{5,7},{6,4},{7,5},{8,10},{9,11},{10,... | collective-permute-start | bytes 1179656 | tf_op jit(solution)/shard_map/ppermute | solution.py:574
  97.3 7.1 %collective-permute-start.30 = (bf16[96,768]{1,0:T(8,128)(2,1)S(1)}, bf16[96,768]{1,0:T(8,128)(2,1)S(1)}, u32[]{:S(2)}, u32[]{:S(2)}) collective-permute-start(bf16[96,768]{1,0:T(8,128)(2,1)S(1)} %get-tuple-element.220), channel_id=1, source_target_pairs={{0,16},{4,20},{8,24},{12,28},{16,0},{20,4},{24,8},{28,12},{1,17},{... | collective-permute-start | bytes 442376 | tf_op jit(solution)/shard_map/ppermute | solution.py:571
  97.5 7.0 %collective-permute-start.31 = (bf16[96,768]{1,0:T(8,128)(2,1)S(1)}, bf16[96,768]{1,0:T(8,128)(2,1)S(1)}, u32[]{:S(2)}, u32[]{:S(2)}) collective-permute-start(bf16[96,768]{1,0:T(8,128)(2,1)S(1)} %get-tuple-element.223), channel_id=1, source_target_pairs={{0,4},{4,0},{8,12},{12,8},{16,20},{20,16},{24,28},{28,24},{1,5},{5... | collective-permute-start | bytes 442376 | tf_op jit(solution)/shard_map/ppermute | solution.py:571
  106.2 9.7 %collective-permute-start.35 = (bf16[104,768]{1,0:T(8,128)(2,1)S(1)}, bf16[104,768]{1,0:T(8,128)(2,1)S(1)}, u32[]{:S(2)}, u32[]{:S(2)}) collective-permute-start(bf16[104,768]{1,0:T(8,128)(2,1)S(1)} %get-tuple-element.231.rest_1_), channel_id=1, source_target_pairs={{0,16},{4,20},{8,24},{12,28},{16,0},{20,4},{24,8},{28,12},{1,17},{... | collective-permute-start | bytes 479240 | tf_op jit(solution)/shard_map/ppermute | solution.py:571

commit v5 on v4

--- a/solution.py
+++ b/solution.py
@@ -334,10 +334,13 @@
     small[2 * rows :, :] = whole.astype(bf16)
 
 
-def ffn_out_kernel(hidden, down, keep, send):
+def ffn_out_kernel(hidden, down, keep, *send):
     for half, at, rows in half_rows():
-        to = send if half else keep
-        to[at * BLK : (at + 1) * BLK, :] = dot_nt(hidden[rows, :], down[...]).astype(bf16)
+        block = dot_nt(hidden[rows, :], down[...]).astype(bf16)
+        if half:
+            send[at][...] = block
+        else:
+            keep[at * BLK : (at + 1) * BLK, :] = block
 
 
 def act_grad_kernel(proj_grad, weights, keep, *send):
@@ -350,23 +353,23 @@
             keep[at * BLK : (at + 1) * BLK, :] = block
 
 
-def core_add_kernel(ffn_keep, ffn_got, act_keep, act_got_a, act_got_b, mine, theirs):
+def core_add_kernel(*refs):
+    *before, keep, got_a, got_b, mine, theirs = refs
     chip = lax.axis_index("tp") >> 1
-    for at in range(2):
+    first = mine.shape[0] - BLK
+    for to, block in zip((mine, theirs), before):
+        to[:BLK, :] = block[...]
+    for at, got in enumerate((got_a, got_b)):
         here = slice(at * BLK, (at + 1) * BLK)
-        ffn = (ffn_keep[here, :].astype(f32) + ffn_got[here, :].astype(f32)).astype(bf16)
-        got = (act_got_a, act_got_b)[at]
-        act = (act_keep[here, :].astype(f32) + got[...].astype(f32)).astype(bf16)
+        value = (keep[here, :].astype(f32) + got[...].astype(f32)).astype(bf16)
 
         @pl.when(chip == at)
         def _():
-            mine[:BLK, :] = ffn
-            mine[BLK:, :] = act
+            mine[first:, :] = value
 
         @pl.when(chip != at)
         def _():
-            theirs[:BLK, :] = ffn
-            theirs[BLK:, :] = act
+            theirs[first:, :] = value
 
 
 def share_out_kernel(resid, x, gains, share_grad, mine, got, block_out, input_grad):
@@ -670,28 +673,36 @@
         "ffn",
         scratch=[pltpu.VMEM((tokens, hidden), f32)],
     )
-    back_first = add(back_keep, swap_tp(back_send, 1))
-    back_got = swap_tp(back_first, 2)
-    down_order, in_order = (1, 2, 4), (2, 4, 1)
+    down_order, in_order = (2, 1, 4), (1, 2, 4)
     grad_scratch = [pltpu.VMEM((model, hidden), f32)]
     down_parts = call(
         functools.partial(down_grad_kernel, down_order),
         spread_shapes(dp, model, hidden, (4, 4)),
-        (cotangent, after(hidden_act, back_first)),
+        (cotangent, hidden_act),
         "down_grad",
         scratch=grad_scratch,
     )
+    back_first = add(back_keep, swap_tp(back_send, 1), down_parts[:1])
+    back_got = swap_tp(back_first, 2)
     *in_parts, gain_two_part = call(
         functools.partial(in_grad_kernel, in_order),
         [*spread_shapes(dp, model, hidden, (4, 4)), sds((1, model), f32)],
-        (act_two, after(pre_grad, down_parts[0]), in_full, norm_gains_here),
+        (act_two, after(pre_grad, back_first), in_full, norm_gains_here),
         "in_grad",
         scratch=grad_scratch,
     )
-    ffn_keep, ffn_send = call(
-        ffn_out_kernel, half_shape, (hidden_act, down_full), "ffn_out", behind=(gain_two_part,)
-    )
-    back_sum = add(back_first, back_got, (ffn_keep,))
+    share_shapes = [half_shape[0], *half_blocks]
+    ffn_keep, *ffn_send = call(
+        ffn_out_kernel, share_shapes, (hidden_act, down_full), "ffn_out", behind=(gain_two_part,)
+    )
+    ffn_got = [swap_tp(part, 1) for part in ffn_send]
+    ffn_sums = call(core_add_kernel, half_blocks, (ffn_keep, *ffn_got), "ffn_add", limit=4)
+    back_sum = add(back_first, back_got, ffn_sums[:1])
+    attend_behind = ()
+    if direct:
+        down_keep, down_send = down_parts
+        down_one = pair_add(down_keep, swap_dp(down_send, down_order[0]), (back_sum,))
+        attend_behind = down_one
     everyone = dp * tp
     qkvo_shapes = spread_shapes(dp, model, packed_cols, (4, 2))
     small_shape = sds((2 * rows + SMALL, model), bf16) if direct else sds((SMALL, model), f32)
@@ -718,6 +729,7 @@
             pltpu.VMEM((model, packed_cols), f32),
             pltpu.VMEM((8, 2 * LEN), f32),
         ],
+        behind=attend_behind,
     )
     def summed(parts, behind):
         return call(
@@ -731,36 +743,29 @@
 
     def act_shares(behind):
         keep, *send = call(
-            act_grad_kernel,
-            [half_shape[0], *half_blocks],
-            (proj_grad, weights_one),
-            "act_grad",
-            behind=behind,
+            act_grad_kernel, share_shapes, (proj_grad, weights_one), "act_grad", behind=behind
         )
-        return keep, [swap_tp(part, 1) for part in send]
-
-    def share_sums(keep, got, behind):
+        return (keep, *(swap_tp(part, 1) for part in send))
+
+    def share_sums(shares, behind):
         outs = [sds((2 * BLK, model), bf16)] * 2
-        args = (ffn_keep, swap_tp(ffn_send, 1), keep, *got)
-        return call(core_add_kernel, outs, args, "core_add", limit=4, behind=behind)
+        return call(core_add_kernel, outs, (*ffn_sums, *shares), "core_add", limit=4, behind=behind)
 
     if direct:
         keep, send_low = qkvo_parts
-        down_keep, down_send = down_parts
         in_keep, in_send = in_parts
         in_one = pair_add(in_keep, swap_dp(in_send, in_order[0]), (proj_grad,))
-        down_one = pair_add(down_keep, swap_dp(down_send, down_order[0]), in_one)
-        got_high = swap_dp(after(small, *down_one), 1)
-        share_own, share_got = act_shares(down_one)
+        got_high = swap_dp(after(small, *in_one), 1)
+        act_parts = act_shares(in_one)
+        down_two = next_add(down_one[0], swap_dp(down_one[1], down_order[1]), act_parts[:1])
         (high,) = call(
-            last_high_kernel, [small_shape], (keep, small, got_high), "last_high", limit=4, behind=(share_own,)
+            last_high_kernel, [small_shape], (keep, small, got_high), "last_high", limit=4, behind=down_two
         )
         got_low = swap_dp(after(send_low, high), 1)
-        mine, theirs = share_sums(share_own, share_got, (high,))
-        down_two = next_add(down_one[0], swap_dp(down_one[1], down_order[1]), (mine,))
-        in_two = next_add(in_one[0], swap_dp(in_one[1], in_order[1]), down_two)
-        down_grad, down_squares = summed((down_two[0], swap_dp(down_two[1], down_order[2])), in_two)
-        in_grad, in_squares = summed((in_two[0], swap_dp(in_two[1], in_order[2])), (down_grad,))
+        down_grad, down_squares = summed((down_two[0], swap_dp(down_two[1], down_order[2])), (high,))
+        in_two = next_add(in_one[0], swap_dp(in_one[1], in_order[1]), (down_grad,))
+        mine, theirs = share_sums(act_parts, in_two)
+        in_grad, in_squares = summed((in_two[0], swap_dp(in_two[1], in_order[2])), (mine,))
         last, late = call(
             last_late_kernel,
             [sds((rows, packed_cols), f32), sds((rows + SMALL, packed_cols), bf16)],
@@ -779,7 +784,7 @@
         last_parts = (*qkvo_sums, lax.psum(small, "dp"))
         down_grad, down_squares = summed(down_sums, ())
         in_grad, in_squares = summed(in_sums, ())
-        mine, theirs = share_sums(*act_shares(()), ())
+        mine, theirs = share_sums(act_shares(()), ())
         share_behind = ()
     block_out, input_grad = call(
         share_out_kernel,

time: 131 us -> 128 us (0.977)
  waiting for transfers between devices: 48 us -> 46.2 us
    ppermute x12 -> x13, waiting for transfers between devices: 8.66 us -> 6.1 us  [swap_tp(): return lax.ppermute(value, 'tp', [(i, i ^ distance) for i in range(tp)])]
    ppermute x12 -> x13, starting transfers between devices: 6.19 us -> 5.68 us  [swap_tp(): return lax.ppermute(value, 'tp', [(i, i ^ distance) for i in range(tp)])]
    pallas_call x27 -> x28, Pallas kernels: 28.4 us -> 28.5 us  [call(): pl.pallas_call(body, out_shape=tuple(outs), in_specs=[pl.BlockSpec(memory...]
  transfers between devices with their start and end apart: 36 -> 37, of which waited for: 20 -> 22; matrix products, arithmetic and copies ran while one was open for 0% -> 0% of each run, Pallas kernels for 16% -> 16%
where the time goes in v5:
time: 128 us
  waiting for transfers between devices  46.2 us (36%)
  starting transfers between devices  40.8 us (32%)
  Pallas kernels  28.5 us (22%)
  blocking collectives  11.3 us (9%)
    ppermute x24, waiting for transfers between devices, swap_dp(): return lax.ppermute(value, 'dp', [(i, i ^ distance) for i in range(dp)])  40.1 us
    ppermute x24, starting transfers between devices, swap_dp(): return lax.ppermute(value, 'dp', [(i, i ^ distance) for i in range(dp)])  35.1 us
    pallas_call x28, Pallas kernels, call(): pl.pallas_call(body, out_shape=tuple(outs), in_specs=[pl.BlockSpec(memory...  28.5 us
    all_to_all x1, blocking collectives, on_device(): told = lax.all_to_all(payload, ('dp', 'tp'), 0, 0)  11.3 us
    ppermute x13, waiting for transfers between devices, swap_tp(): return lax.ppermute(value, 'tp', [(i, i ^ distance) for i in range(tp)])  6.1 us
    ppermute x13, starting transfers between devices, swap_tp(): return lax.ppermute(value, 'tp', [(i, i ^ distance) for i in range(tp)])  5.68 us
  transfers between devices with their start and end apart: 37, of which 22 were waited for; matrix products, arithmetic and copies ran while one was open for 0% of the time, Pallas kernels for 16%

profile of v5, /device:TPU:0, one launch (start us, length us, event | category | flops | bytes accessed | tf_op | source)
XLA Modules:
  0.0 127.9 jit_solution(10527147509162945862)
XLA Ops:
  0.7 1.2 pack.1
  1.9 4.1 %collective-permute-start.1 = (bf16[96,768]{1,0:T(8,128)(2,1)S(1)}, bf16[96,768]{1,0:T(8,128)(2,1)S(1)}, u32[]{:S(2)}, u32[]{:S(2)}) collective-permute-start(bf16[96,768]{1,0:T(8,128)(2,1)S(1)} %get-tuple-element.170.rest_0_), channel_id=1, source_target_pairs={{0,16},{4,20},{8,24},{12,28},{16,0},{20,4},{24,8},{28,12},{1,17},{... | collective-permute-start | bytes 442376 | tf_op jit(solution)/shard_map/ppermute | solution.py:574
  6.0 1.6 %collective-permute-start.4 = (bf16[96,768]{1,0:T(8,128)(2,1)S(1)}, bf16[96,768]{1,0:T(8,128)(2,1)S(1)}, u32[]{:S(2)}, u32[]{:S(2)}) collective-permute-start(bf16[96,768]{1,0:T(8,128)(2,1)S(1)} %get-tuple-element.170.rest_0_), channel_id=1, source_target_pairs={{0,8},{4,12},{8,0},{12,4},{16,24},{20,28},{24,16},{28,20},{1,9},{5... | collective-permute-start | bytes 442376 | tf_op jit(solution)/shard_map/ppermute | solution.py:574
  7.6 2.2 %prep.1 = (bf16[512,768]{1,0:T(8,128)(2,1)S(1)}, bf16[768,512]{1,0:T(8,128)(2,1)S(1)}, f32[3,512,512]{2,1,0:T(8,128)S(1)}, s32[1,1024]{1,0:T(1,128)S(1)}, bf16[5...) custom-call(s32[1,4]{1,0:T(1,128)} %seg_in.1, f32[3,32]{1,0:T(4,128)} %bitcast.8, ...), custom_call_target="tpu_custom_call" | custom-call | tf_op jit(solution)/shard_map/prep/pallas_call | solution.py:61
  9.8 1.6 %collective-permute-start = (bf16[96,1536]{1,0:T(8,128)(2,1)S(1)}, bf16[96,1536]{1,0:T(8,128)(2,1)S(1)}, u32[]{:S(2)}, u32[]{:S(2)}) collective-permute-start(bf16[96,1536]{1,0:T(8,128)(2,1)S(1)} %get-tuple-element.174.rest_0_), channel_id=1, source_target_pairs={{0,4},{4,0},{8,12},{12,8},{16,20},{20,16},{24,28},{28,24},{1,5},{5... | collective-permute-start | bytes 884744 | tf_op jit(solution)/shard_map/ppermute | solution.py:574
  11.3 1.8 %collective-permute-done.1.rest_4_ = bf16[96,768]{1,0:T(8,128)(2,1)S(1)} collective-permute-done((bf16[96,768]{1,0:T(8,128)(2,1)S(1)}, bf16[96,768]{1,0:T(8,128)(2,1)S(1)}, u32[]{:S(2)}, u32[]{:S(2)}) %collective-permute-start.1) | collective-permute-done | bytes 147488 | tf_op jit(solution)/shard_map/ppermute | solution.py:574
  13.7 1.5 %collective-permute-start.3 = (bf16[96,768]{1,0:T(8,128)(2,1)S(1)}, bf16[96,768]{1,0:T(8,128)(2,1)S(1)}, u32[]{:S(2)}, u32[]{:S(2)}) collective-permute-start(bf16[96,768]{1,0:T(8,128)(2,1)S(1)} %get-tuple-element.170.rest_0_), channel_id=1, source_target_pairs={{0,4},{4,0},{8,12},{12,8},{16,20},{20,16},{24,28},{28,24},{1,5},{5... | collective-permute-start | bytes 442376 | tf_op jit(solution)/shard_map/ppermute | solution.py:574
  15.2 3.4 %collective-permute-start.7 = (bf16[96,768]{1,0:T(8,128)(2,1)S(1)}, bf16[96,768]{1,0:T(8,128)(2,1)S(1)}, u32[]{:S(2)}, u32[]{:S(2)}) collective-permute-start(bf16[96,768]{1,0:T(8,128)(2,1)S(1)} %collective-permute-done.1.rest_4_), channel_id=1, source_target_pairs={{0,8},{4,12},{8,0},{12,4},{16,24},{20,28},{24,16},{28,20},{1,9},{5... | collective-permute-start | bytes 442376 | tf_op jit(solution)/shard_map/ppermute | solution.py:574
  19.2 2.8 %collective-permute-done.3.rest_1_ = bf16[96,768]{1,0:T(8,128)(2,1)S(1)} collective-permute-done((bf16[96,768]{1,0:T(8,128)(2,1)S(1)}, bf16[96,768]{1,0:T(8,128)(2,1)S(1)}, u32[]{:S(2)}, u32[]{:S(2)}) %collective-permute-start.3) | collective-permute-done | bytes 147488 | tf_op jit(solution)/shard_map/ppermute | solution.py:574
  22.0 2.5 %collective-permute-start.6 = (bf16[96,768]{1,0:T(8,128)(2,1)S(1)}, bf16[96,768]{1,0:T(8,128)(2,1)S(1)}, u32[]{:S(2)}, u32[]{:S(2)}) collective-permute-start(bf16[96,768]{1,0:T(8,128)(2,1)S(1)} %collective-permute-done.1.rest_4_), channel_id=1, source_target_pairs={{0,4},{4,0},{8,12},{12,8},{16,20},{20,16},{24,28},{28,24},{1,5},{5... | collective-permute-start | bytes 442376 | tf_op jit(solution)/shard_map/ppermute | solution.py:574
  24.5 0.9 collective-permute-done.5.rest_3_
  25.4 1.6 %collective-permute-start.11 = (bf16[96,1536]{1,0:T(8,128)(2,1)S(1)}, bf16[96,1536]{1,0:T(8,128)(2,1)S(1)}, u32[]{:S(2)}, u32[]{:S(2)}) collective-permute-start(bf16[96,1536]{1,0:T(8,128)(2,1)S(1)} %get-tuple-element.174.rest_0_), channel_id=1, source_target_pairs={{0,8},{4,12},{8,0},{12,4},{16,24},{20,28},{24,16},{28,20},{1,9},{5... | collective-permute-start | bytes 884744 | tf_op jit(solution)/shard_map/ppermute | solution.py:574
  27.0 1.5 %collective-permute-done.2.rest_4_ = bf16[96,1536]{1,0:T(8,128)(2,1)S(1)} collective-permute-done((bf16[96,1536]{1,0:T(8,128)(2,1)S(1)}, bf16[96,1536]{1,0:T(8,128)(2,1)S(1)}, u32[]{:S(2)}, u32[]{:S(2)}) %collective-permute-start.2) | collective-permute-done | bytes 294944 | tf_op jit(solution)/shard_map/ppermute | solution.py:574
  29.1 1.6 %collective-permute-done.8.rest_7_ = bf16[96,768]{1,0:T(8,128)(2,1)S(1)} collective-permute-done((bf16[96,768]{1,0:T(8,128)(2,1)S(1)}, bf16[96,768]{1,0:T(8,128)(2,1)S(1)}, u32[]{:S(2)}, u32[]{:S(2)}) %collective-permute-start.8) | collective-permute-done | bytes 147488 | tf_op jit(solution)/shard_map/ppermute | solution.py:574
  30.7 3.1 %attend.1 = (bf16[768,768]{1,0:T(8,128)(2,1)S(1)}, bf16[512,576]{1,0:T(8,128)(2,1)S(1)}, bf16[3,512,512]{2,1,0:T(8,128)(2,1)S(1)}, bf16[512,192]{1,0:T(8,128)(2,...) custom-call(bf16[512,768]{1,0:T(8,128)(2,1)S(1)} %get-tuple-element.163.act, ...), custom_call_target="tpu_custom_call" | custom-call | tf_op jit(solution)/shard_map/attend/pallas_call | solution.py:61
  33.8 0.9 collective-permute-done.11.rest_2_
  35.3 1.5 %collective-permute-start.10 = (bf16[96,1536]{1,0:T(8,128)(2,1)S(1)}, bf16[96,1536]{1,0:T(8,128)(2,1)S(1)}, u32[]{:S(2)}, u32[]{:S(2)}) collective-permute-start(bf16[96,1536]{1,0:T(8,128)(2,1)S(1)} %collective-permute-done.2.rest_4_), channel_id=1, source_target_pairs={{0,4},{4,0},{8,12},{12,8},{16,20},{20,16},{24,28},{28,24},{1,5},{5... | collective-permute-start | bytes 884744 | tf_op jit(solution)/shard_map/ppermute | solution.py:574
  36.9 1.6 %collective-permute-start.13 = (bf16[128,768]{1,0:T(8,128)(2,1)S(1)}, bf16[128,768]{1,0:T(8,128)(2,1)S(1)}, u32[]{:S(2)}, u32[]{:S(2)}) collective-permute-start(bf16[128,768]{1,0:T(8,128)(2,1)S(1)} %get-tuple-element.176.one), channel_id=1, source_target_pairs={{0,2},{1,3},{2,0},{3,1},{4,6},{5,7},{6,4},{7,5},{8,10},{9,11},{10,... | collective-permute-start | bytes 589832 | tf_op jit(solution)/shard_map/ppermute | solution.py:577
  39.0 4.2 %collective-permute-done.12.rest_6_ = bf16[96,1536]{1,0:T(8,128)(2,1)S(1)} collective-permute-done((bf16[96,1536]{1,0:T(8,128)(2,1)S(1)}, bf16[96,1536]{1,0:T(8,128)(2,1)S(1)}, u32[]{:S(2)}, u32[]{:S(2)}) %collective-permute-start.12) | collective-permute-done | bytes 294944 | tf_op jit(solution)/shard_map/ppermute | solution.py:574
  43.3 1.5 %collective-permute-start.18 = (bf16[96,1536]{1,0:T(8,128)(2,1)S(1)}, bf16[96,1536]{1,0:T(8,128)(2,1)S(1)}, u32[]{:S(2)}, u32[]{:S(2)}) collective-permute-start(bf16[96,1536]{1,0:T(8,128)(2,1)S(1)} %collective-permute-done.12.rest_6_), channel_id=1, source_target_pairs={{0,4},{4,0},{8,12},{12,8},{16,20},{20,16},{24,28},{28,24},{1,5},{5... | collective-permute-start | bytes 884744 | tf_op jit(solution)/shard_map/ppermute | solution.py:574
  44.7 1.4 %collective-permute-start.17 = (bf16[96,1536]{1,0:T(8,128)(2,1)S(1)}, bf16[96,1536]{1,0:T(8,128)(2,1)S(1)}, u32[]{:S(2)}, u32[]{:S(2)}) collective-permute-start(bf16[96,1536]{1,0:T(8,128)(2,1)S(1)} %collective-permute-done.rest_1_), channel_id=1, source_target_pairs={{0,8},{4,12},{8,0},{12,4},{16,24},{20,28},{24,16},{28,20},{1,9},{5... | collective-permute-start | bytes 884744 | tf_op jit(solution)/shard_map/ppermute | solution.py:574
  46.3 1.6 %collective-permute-done.14.two = bf16[128,768]{1,0:T(8,128)(2,1)S(1)} collective-permute-done((bf16[128,768]{1,0:T(8,128)(2,1)S(1)}, bf16[128,768]{1,0:T(8,128)(2,1)S(1)}, u32[]{:S(2)}, u32[]{:S(2)}) %collective-permute-start.14) | collective-permute-done | bytes 196640 | tf_op jit(solution)/shard_map/ppermute | solution.py:577
  48.0 3.0 %collective-permute-done.18.rest_7_ = bf16[96,1536]{1,0:T(8,128)(2,1)S(1)} collective-permute-done((bf16[96,1536]{1,0:T(8,128)(2,1)S(1)}, bf16[96,1536]{1,0:T(8,128)(2,1)S(1)}, u32[]{:S(2)}, u32[]{:S(2)}) %collective-permute-start.18) | collective-permute-done | bytes 294944 | tf_op jit(solution)/shard_map/ppermute | solution.py:574
  51.0 1.7 %collective-permute-done.17.rest_3_ = bf16[96,1536]{1,0:T(8,128)(2,1)S(1)} collective-permute-done((bf16[96,1536]{1,0:T(8,128)(2,1)S(1)}, bf16[96,1536]{1,0:T(8,128)(2,1)S(1)}, u32[]{:S(2)}, u32[]{:S(2)}) %collective-permute-start.17) | collective-permute-done | bytes 294944 | tf_op jit(solution)/shard_map/ppermute | solution.py:574
  52.7 3.5 %ffn.1 = (f32[512,768]{1,0:T(8,128)S(1)}, bf16[512,768]{1,0:T(8,128)(2,1)S(1)}, bf16[512,768]{1,0:T(8,128)(2,1)S(1)}, bf16[512,768]{1,0:T(8,128)(2,1)S(1)}, bf16...) custom-call(bf16[512,768]{1,0:T(8,128)(2,1)S(1)} %get-tuple-element., ...), custom_call_target="tpu_custom_call" | custom-call | tf_op jit(solution)/shard_map/ffn/pallas_call | solution.py:61
  56.3 0.9 down_grad.1
  58.1 1.6 %collective-permute-start.22 = (bf16[256,768]{1,0:T(8,128)(2,1)S(1)}, bf16[256,768]{1,0:T(8,128)(2,1)S(1)}, u32[]{:S(2)}, u32[]{:S(2)}) collective-permute-start(bf16[256,768]{1,0:T(8,128)(2,1)S(1)} %add.6.one), channel_id=1, source_target_pairs={{0,2},{1,3},{2,0},{3,1},{4,6},{5,7},{6,4},{7,5},{8,10},{9,11},{10,... | collective-permute-start | bytes 1179656 | tf_op jit(solution)/shard_map/ppermute | solution.py:577
  59.7 1.7 %collective-permute-start.23 = (bf16[4,96,768]{2,1,0:T(8,128)(2,1)S(1)}, bf16[4,96,768]{2,1,0:T(8,128)(2,1)S(1)}, u32[]{:S(2)}, u32[]{:S(2)}) collective-permute-start(bf16[4,96,768]{2,1,0:T(8,128)(2,1)S(1)} %get-tuple-element.199), channel_id=1, source_target_pairs={{0,8},{4,12},{8,0},{12,4},{16,24},{20,28},{24,16},{28,20},{1,9},{5... | collective-permute-start | bytes 1769480 | tf_op jit(solution)/shard_map/ppermute | solution.py:574
  61.4 1.0 in_grad.1
  62.5 1.6 %ffn_out.1 = (bf16[256,768]{1,0:T(8,128)(2,1)S(1)}, bf16[128,768]{1,0:T(8,128)(2,1)S(1)}, bf16[128,768]{1,0:T(8,128)(2,1)S(1)}) custom-call(bf16[512,768]{1,0:T(8,128)(2,1)S(1)} %get-tuple-element.191.right.hidden, bf16[768,768]{1,0:T(8,128)(2,1)S(1)} %get-tuple-element.192.down), custom_call_target="tpu_custom_call" | custom-call | tf_op jit(solution)/shard_map/ffn_out/pallas_call | solution.py:61
  66.3 3.1 %collective-permute-done.22.two = bf16[256,768]{1,0:T(8,128)(2,1)S(1)} collective-permute-done((bf16[256,768]{1,0:T(8,128)(2,1)S(1)}, bf16[256,768]{1,0:T(8,128)(2,1)S(1)}, u32[]{:S(2)}, u32[]{:S(2)}) %collective-permute-start.22) | collective-permute-done | bytes 393248 | tf_op jit(solution)/shard_map/ppermute | solution.py:577
  69.5 5.3 %collective-permute-done.23.got = bf16[4,96,768]{2,1,0:T(8,128)(2,1)S(1)} collective-permute-done((bf16[4,96,768]{2,1,0:T(8,128)(2,1)S(1)}, bf16[4,96,768]{2,1,0:T(8,128)(2,1)S(1)}, u32[]{:S(2)}, u32[]{:S(2)}) %collective-permute-start.23) | collective-permute-done | bytes 589856 | tf_op jit(solution)/shard_map/ppermute | solution.py:574
  75.5 5.7 %attend_back.1 = (bf16[4,96,768]{2,1,0:T(8,128)(2,1)S(1)}, bf16[2,96,768]{2,1,0:T(8,128)(2,1)S(1)}, f32[128,768]{1,0:T(8,128)S(1)}, bf16[200,768]{1,0:T(8,128)(2,1)S(1)}, bf16[512,576]{1,0:T(8,128)(2,1)S(1)}) custom-call(f32[512,768]{1,0:T(8,128)S(1)} %get-tuple-element.240.resid, bf16[512,768]{1,0:T(8,128)(2,1)S(1)} %get-tuple-element.162.dy.left, ...), custom_call_target="tpu_custom_call" | custom-call | tf_op jit(solution)/shard_map/attend_back/pallas_call | solution.py:61
  81.4 1.6 %collective-permute-start.27 = (bf16[200,768]{1,0:T(8,128)(2,1)S(1)}, bf16[200,768]{1,0:T(8,128)(2,1)S(1)}, u32[]{:S(2)}, u32[]{:S(2)}) collective-permute-start(bf16[200,768]{1,0:T(8,128)(2,1)S(1)} %get-tuple-element.223.sent), channel_id=1, source_target_pairs={{0,4},{4,0},{8,12},{12,8},{16,20},{20,16},{24,28},{28,24},{1,5},{5... | collective-permute-start | bytes 921608 | tf_op jit(solution)/shard_map/ppermute | solution.py:574
  83.0 1.7 %collective-permute-start.29 = (bf16[2,96,768]{2,1,0:T(8,128)(2,1)S(1)}, bf16[2,96,768]{2,1,0:T(8,128)(2,1)S(1)}, u32[]{:S(2)}, u32[]{:S(2)}) collective-permute-start(bf16[2,96,768]{2,1,0:T(8,128)(2,1)S(1)} %get-tuple-element.215), channel_id=1, source_target_pairs={{0,8},{4,12},{8,0},{12,4},{16,24},{20,28},{24,16},{28,20},{1,9},{5... | collective-permute-start | bytes 884744 | tf_op jit(solution)/shard_map/ppermute | solution.py:574
  84.7 1.4 %act_grad.1 = (bf16[256,768]{1,0:T(8,128)(2,1)S(1)}, bf16[128,768]{1,0:T(8,128)(2,1)S(1)}, bf16[128,768]{1,0:T(8,128)(2,1)S(1)}) custom-call(bf16[512,576]{1,0:T(8,128)(2,1)S(1)} %get-tuple-element.216.proj_grad, bf16[768,768]{1,0:T(8,128)(2,1)S(1)} %get-tuple-element.203.weights), custom_call_target="tpu_custom_call" | custom-call | tf_op jit(solution)/shard_map/act_grad/pallas_call | solution.py:61
  86.1 1.1 collective-permute-done.26.got
  87.3 2.3 %collective-permute-start.28 = (bf16[96,768]{1,0:T(8,128)(2,1)S(1)}, bf16[96,768]{1,0:T(8,128)(2,1)S(1)}, u32[]{:S(2)}, u32[]{:S(2)}) collective-permute-start(bf16[96,768]{1,0:T(8,128)(2,1)S(1)} %get-tuple-element.220), channel_id=1, source_target_pairs={{0,16},{4,20},{8,24},{12,28},{16,0},{20,4},{24,8},{28,12},{1,17},{... | collective-permute-start | bytes 442376 | tf_op jit(solution)/shard_map/ppermute | solution.py:574
  90.1 2.8 %collective-permute-done.27.got = bf16[200,768]{1,0:T(8,128)(2,1)S(1)} collective-permute-done((bf16[200,768]{1,0:T(8,128)(2,1)S(1)}, bf16[200,768]{1,0:T(8,128)(2,1)S(1)}, u32[]{:S(2)}, u32[]{:S(2)}) %collective-permute-start.27) | collective-permute-done | bytes 307232 | tf_op jit(solution)/shard_map/ppermute | solution.py:574
  93.4 2.3 %collective-permute-done.28.rest_1_ = bf16[96,768]{1,0:T(8,128)(2,1)S(1)} collective-permute-done((bf16[96,768]{1,0:T(8,128)(2,1)S(1)}, bf16[96,768]{1,0:T(8,128)(2,1)S(1)}, u32[]{:S(2)}, u32[]{:S(2)}) %collective-permute-start.28) | collective-permute-done | bytes 147488 | tf_op jit(solution)/shard_map/ppermute | solution.py:574
  96.6 2.5 %collective-permute-start.32 = (bf16[96,768]{1,0:T(8,128)(2,1)S(1)}, bf16[96,768]{1,0:T(8,128)(2,1)S(1)}, u32[]{:S(2)}, u32[]{:S(2)}) collective-permute-start(bf16[96,768]{1,0:T(8,128)(2,1)S(1)} %get-tuple-element.228), channel_id=1, source_target_pairs={{0,16},{4,20},{8,24},{12,28},{16,0},{20,4},{24,8},{28,12},{1,17},{... | collective-permute-start | bytes 442376 | tf_op jit(solution)/shard_map/ppermute | solution.py:574
  99.1 4.7 %collective-permute-done.32.rest_1_ = bf16[96,768]{1,0:T(8,128)(2,1)S(1)} collective-permute-done((bf16[96,768]{1,0:T(8,128)(2,1)S(1)}, bf16[96,768]{1,0:T(8,128)(2,1)S(1)}, u32[]{:S(2)}, u32[]{:S(2)}) %collective-permute-start.32) | collective-permute-done | bytes 147488 | tf_op jit(solution)/shard_map/ppermute | solution.py:574
  105.0 1.3 %collective-permute-start.36 = (bf16[104,768]{1,0:T(8,128)(2,1)S(1)}, bf16[104,768]{1,0:T(8,128)(2,1)S(1)}, u32[]{:S(2)}, u32[]{:S(2)}) collective-permute-start(bf16[104,768]{1,0:T(8,128)(2,1)S(1)} %get-tuple-element.239.rest_1_), channel_id=1, source_target_pairs={{0,16},{4,20},{8,24},{12,28},{16,0},{20,4},{24,8},{28,12},{1,17},{... | collective-permute-start | bytes 479240 | tf_op jit(solution)/shard_map/ppermute | solution.py:574
  106.3 1.0 share_out.1
  107.3 1.9 %fetch.1 = (f32[3,96,192]{2,1,0:T(8,128)S(1)}, f32[3,96,192]{2,1,0:T(8,128)S(1)}, f32[3,96,192]{2,1,0:T(8,128)S(1)}, f32[96,192]{1,0:T(8,128)S(1)}, f32[96,192]{...) custom-call(f32[3,96,192]{2,1,0:T(8,128)} %refs_0_, ...), custom_call_target="tpu_custom_call" | custom-call | tf_op jit(solution)/shard_map/fetch/pallas_call | solution.py:61
  109.3 4.0 %collective-permute-done.36.rest_2_ = bf16[104,768]{1,0:T(8,128)(2,1)S(1)} collective-permute-done((bf16[104,768]{1,0:T(8,128)(2,1)S(1)}, bf16[104,768]{1,0:T(8,128)(2,1)S(1)}, u32[]{:S(2)}, u32[]{:S(2)}) %collective-permute-start.36) | collective-permute-done | bytes 159776 | tf_op jit(solution)/shard_map/ppermute | solution.py:574
  114.0 11.3 %all_to_all.5.refs_0_ = f32[32,1,384]{2,1,0:T(1,128)S(1)} all-to-all(f32[32,1,384]{2,1,0:T(1,128)} %get-tuple-element.251), channel_id=1, replica_groups=mesh['dp'=8,'tp'=4] {'dp','tp'}, dimensions={0} | all-to-all | bytes 98304 | tf_op jit(solution)/shard_map/all_to_all | solution.py:834
  125.3 2.4 %adam.1 = (f32[1,1]{1,0:T(1,128)}, f32[3,96,192]{2,1,0:T(8,128)}, f32[3,96,192]{2,1,0:T(8,128)}, f32[3,96,192]{2,1,0:T(8,128)}, bf16[3,96,192]{2,1,0:T(8,128)(2,...) custom-call(f32[32,1,384]{2,1,0:T(1,128)S(1)} %all_to_all.5.refs_0_,, ...), custom_call_target="tpu_custom_call" | custom-call | tf_op jit(solution)/shard_map/adam/pallas_call | solution.py:61
  (55 shorter events, 11.0 us)
Async XLA Ops:
  1.9 11.2 %collective-permute-start.1 = (bf16[96,768]{1,0:T(8,128)(2,1)S(1)}, bf16[96,768]{1,0:T(8,128)(2,1)S(1)}, u32[]{:S(2)}, u32[]{:S(2)}) collective-permute-start(bf16[96,768]{1,0:T(8,128)(2,1)S(1)} %get-tuple-element.170.rest_0_), channel_id=1, source_target_pairs={{0,16},{4,20},{8,24},{12,28},{16,0},{20,4},{24,8},{28,12},{1,17},{... | collective-permute-start | bytes 442376 | tf_op jit(solution)/shard_map/ppermute | solution.py:574
  6.0 12.6 %collective-permute-start.4 = (bf16[96,768]{1,0:T(8,128)(2,1)S(1)}, bf16[96,768]{1,0:T(8,128)(2,1)S(1)}, u32[]{:S(2)}, u32[]{:S(2)}) collective-permute-start(bf16[96,768]{1,0:T(8,128)(2,1)S(1)} %get-tuple-element.170.rest_0_), channel_id=1, source_target_pairs={{0,8},{4,12},{8,0},{12,4},{16,24},{20,28},{24,16},{28,20},{1,9},{5... | collective-permute-start | bytes 442376 | tf_op jit(solution)/shard_map/ppermute | solution.py:574
  9.8 17.3 %collective-permute-start = (bf16[96,1536]{1,0:T(8,128)(2,1)S(1)}, bf16[96,1536]{1,0:T(8,128)(2,1)S(1)}, u32[]{:S(2)}, u32[]{:S(2)}) collective-permute-start(bf16[96,1536]{1,0:T(8,128)(2,1)S(1)} %get-tuple-element.174.rest_0_), channel_id=1, source_target_pairs={{0,4},{4,0},{8,12},{12,8},{16,20},{20,16},{24,28},{28,24},{1,5},{5... | collective-permute-start | bytes 884744 | tf_op jit(solution)/shard_map/ppermute | solution.py:574
  13.1 15.4 %collective-permute-start.2 = (bf16[96,1536]{1,0:T(8,128)(2,1)S(1)}, bf16[96,1536]{1,0:T(8,128)(2,1)S(1)}, u32[]{:S(2)}, u32[]{:S(2)}) collective-permute-start(bf16[96,1536]{1,0:T(8,128)(2,1)S(1)} %get-tuple-element.174.rest_0_), channel_id=1, source_target_pairs={{0,16},{4,20},{8,24},{12,28},{16,0},{20,4},{24,8},{28,12},{1,17},{... | collective-permute-start | bytes 884744 | tf_op jit(solution)/shard_map/ppermute | solution.py:574
  13.7 8.3 %collective-permute-start.3 = (bf16[96,768]{1,0:T(8,128)(2,1)S(1)}, bf16[96,768]{1,0:T(8,128)(2,1)S(1)}, u32[]{:S(2)}, u32[]{:S(2)}) collective-permute-start(bf16[96,768]{1,0:T(8,128)(2,1)S(1)} %get-tuple-element.170.rest_0_), channel_id=1, source_target_pairs={{0,4},{4,0},{8,12},{12,8},{16,20},{20,16},{24,28},{28,24},{1,5},{5... | collective-permute-start | bytes 442376 | tf_op jit(solution)/shard_map/ppermute | solution.py:574
  15.2 9.3 %collective-permute-start.7 = (bf16[96,768]{1,0:T(8,128)(2,1)S(1)}, bf16[96,768]{1,0:T(8,128)(2,1)S(1)}, u32[]{:S(2)}, u32[]{:S(2)}) collective-permute-start(bf16[96,768]{1,0:T(8,128)(2,1)S(1)} %collective-permute-done.1.rest_4_), channel_id=1, source_target_pairs={{0,8},{4,12},{8,0},{12,4},{16,24},{20,28},{24,16},{28,20},{1,9},{5... | collective-permute-start | bytes 442376 | tf_op jit(solution)/shard_map/ppermute | solution.py:574
  18.6 6.8 %collective-permute-start.5 = (bf16[96,768]{1,0:T(8,128)(2,1)S(1)}, bf16[96,768]{1,0:T(8,128)(2,1)S(1)}, u32[]{:S(2)}, u32[]{:S(2)}) collective-permute-start(bf16[96,768]{1,0:T(8,128)(2,1)S(1)} %collective-permute-done.4.rest_2_), channel_id=1, source_target_pairs={{0,4},{4,0},{8,12},{12,8},{16,20},{20,16},{24,28},{28,24},{1,5},{5... | collective-permute-start | bytes 442376 | tf_op jit(solution)/shard_map/ppermute | solution.py:574
  22.0 7.1 %collective-permute-start.6 = (bf16[96,768]{1,0:T(8,128)(2,1)S(1)}, bf16[96,768]{1,0:T(8,128)(2,1)S(1)}, u32[]{:S(2)}, u32[]{:S(2)}) collective-permute-start(bf16[96,768]{1,0:T(8,128)(2,1)S(1)} %collective-permute-done.1.rest_4_), channel_id=1, source_target_pairs={{0,4},{4,0},{8,12},{12,8},{16,20},{20,16},{24,28},{28,24},{1,5},{5... | collective-permute-start | bytes 442376 | tf_op jit(solution)/shard_map/ppermute | solution.py:574
  24.5 6.2 %collective-permute-start.8 = (bf16[96,768]{1,0:T(8,128)(2,1)S(1)}, bf16[96,768]{1,0:T(8,128)(2,1)S(1)}, u32[]{:S(2)}, u32[]{:S(2)}) collective-permute-start(bf16[96,768]{1,0:T(8,128)(2,1)S(1)} %collective-permute-done.7.rest_6_), channel_id=1, source_target_pairs={{0,4},{4,0},{8,12},{12,8},{16,20},{20,16},{24,28},{28,24},{1,5},{5... | collective-permute-start | bytes 442376 | tf_op jit(solution)/shard_map/ppermute | solution.py:574
  25.4 9.3 %collective-permute-start.11 = (bf16[96,1536]{1,0:T(8,128)(2,1)S(1)}, bf16[96,1536]{1,0:T(8,128)(2,1)S(1)}, u32[]{:S(2)}, u32[]{:S(2)}) collective-permute-start(bf16[96,1536]{1,0:T(8,128)(2,1)S(1)} %get-tuple-element.174.rest_0_), channel_id=1, source_target_pairs={{0,8},{4,12},{8,0},{12,4},{16,24},{20,28},{24,16},{28,20},{1,9},{5... | collective-permute-start | bytes 884744 | tf_op jit(solution)/shard_map/ppermute | solution.py:574
  33.8 3.1 %collective-permute-start.9 = (bf16[256,768]{1,0:T(8,128)(2,1)S(1)}, bf16[256,768]{1,0:T(8,128)(2,1)S(1)}, u32[]{:S(2)}, u32[]{:S(2)}) collective-permute-start(bf16[256,768]{1,0:T(8,128)(2,1)S(1)} %get-tuple-element.172), channel_id=1, source_target_pairs={{0,1},{1,0},{2,3},{3,2},{4,5},{5,4},{6,7},{7,6},{8,9},{9,8},{10,11... | collective-permute-start | bytes 1179656 | tf_op jit(solution)/shard_map/ppermute | solution.py:577
  34.8 8.5 %collective-permute-start.12 = (bf16[96,1536]{1,0:T(8,128)(2,1)S(1)}, bf16[96,1536]{1,0:T(8,128)(2,1)S(1)}, u32[]{:S(2)}, u32[]{:S(2)}) collective-permute-start(bf16[96,1536]{1,0:T(8,128)(2,1)S(1)} %collective-permute-done.2.rest_4_), channel_id=1, source_target_pairs={{0,8},{4,12},{8,0},{12,4},{16,24},{20,28},{24,16},{28,20},{1,9},{5... | collective-permute-start | bytes 884744 | tf_op jit(solution)/shard_map/ppermute | solution.py:574
  35.3 10.8 %collective-permute-start.10 = (bf16[96,1536]{1,0:T(8,128)(2,1)S(1)}, bf16[96,1536]{1,0:T(8,128)(2,1)S(1)}, u32[]{:S(2)}, u32[]{:S(2)}) collective-permute-start(bf16[96,1536]{1,0:T(8,128)(2,1)S(1)} %collective-permute-done.2.rest_4_), channel_id=1, source_target_pairs={{0,4},{4,0},{8,12},{12,8},{16,20},{20,16},{24,28},{28,24},{1,5},{5... | collective-permute-start | bytes 884744 | tf_op jit(solution)/shard_map/ppermute | solution.py:574
  36.9 9.3 %collective-permute-start.13 = (bf16[128,768]{1,0:T(8,128)(2,1)S(1)}, bf16[128,768]{1,0:T(8,128)(2,1)S(1)}, u32[]{:S(2)}, u32[]{:S(2)}) collective-permute-start(bf16[128,768]{1,0:T(8,128)(2,1)S(1)} %get-tuple-element.176.one), channel_id=1, source_target_pairs={{0,2},{1,3},{2,0},{3,1},{4,6},{5,7},{6,4},{7,5},{8,10},{9,11},{10,... | collective-permute-start | bytes 589832 | tf_op jit(solution)/shard_map/ppermute | solution.py:577
  38.5 9.4 %collective-permute-start.14 = (bf16[128,768]{1,0:T(8,128)(2,1)S(1)}, bf16[128,768]{1,0:T(8,128)(2,1)S(1)}, u32[]{:S(2)}, u32[]{:S(2)}) collective-permute-start(bf16[128,768]{1,0:T(8,128)(2,1)S(1)} %get-tuple-element.178.one), channel_id=1, source_target_pairs={{0,2},{1,3},{2,0},{3,1},{4,6},{5,7},{6,4},{7,5},{8,10},{9,11},{10,... | collective-permute-start | bytes 589832 | tf_op jit(solution)/shard_map/ppermute | solution.py:577
  43.3 7.8 %collective-permute-start.18 = (bf16[96,1536]{1,0:T(8,128)(2,1)S(1)}, bf16[96,1536]{1,0:T(8,128)(2,1)S(1)}, u32[]{:S(2)}, u32[]{:S(2)}) collective-permute-start(bf16[96,1536]{1,0:T(8,128)(2,1)S(1)} %collective-permute-done.12.rest_6_), channel_id=1, source_target_pairs={{0,4},{4,0},{8,12},{12,8},{16,20},{20,16},{24,28},{28,24},{1,5},{5... | collective-permute-start | bytes 884744 | tf_op jit(solution)/shard_map/ppermute | solution.py:574
  44.7 8.0 %collective-permute-start.17 = (bf16[96,1536]{1,0:T(8,128)(2,1)S(1)}, bf16[96,1536]{1,0:T(8,128)(2,1)S(1)}, u32[]{:S(2)}, u32[]{:S(2)}) collective-permute-start(bf16[96,1536]{1,0:T(8,128)(2,1)S(1)} %collective-permute-done.rest_1_), channel_id=1, source_target_pairs={{0,8},{4,12},{8,0},{12,4},{16,24},{20,28},{24,16},{28,20},{1,9},{5... | collective-permute-start | bytes 884744 | tf_op jit(solution)/shard_map/ppermute | solution.py:574
  46.2 6.5 %collective-permute-start.15 = (bf16[128,768]{1,0:T(8,128)(2,1)S(1)}, bf16[128,768]{1,0:T(8,128)(2,1)S(1)}, u32[]{:S(2)}, u32[]{:S(2)}) collective-permute-start(bf16[128,768]{1,0:T(8,128)(2,1)S(1)} %add.4.own_a), channel_id=1, source_target_pairs={{0,1},{1,0},{2,3},{3,2},{4,5},{5,4},{6,7},{7,6},{8,9},{9,8},{10,11... | collective-permute-start | bytes 589832 | tf_op jit(solution)/shard_map/ppermute | solution.py:577
  47.9 4.8 %collective-permute-start.16 = (bf16[128,768]{1,0:T(8,128)(2,1)S(1)}, bf16[128,768]{1,0:T(8,128)(2,1)S(1)}, u32[]{:S(2)}, u32[]{:S(2)}) collective-permute-start(bf16[128,768]{1,0:T(8,128)(2,1)S(1)} %add.5.own_b), channel_id=1, source_target_pairs={{0,1},{1,0},{2,3},{3,2},{4,5},{5,4},{6,7},{7,6},{8,9},{9,8},{10,11... | collective-permute-start | bytes 589832 | tf_op jit(solution)/shard_map/ppermute | solution.py:577
  56.2 1.8 %collective-permute-start.19 = (bf16[256,768]{1,0:T(8,128)(2,1)S(1)}, bf16[256,768]{1,0:T(8,128)(2,1)S(1)}, u32[]{:S(2)}, u32[]{:S(2)}) collective-permute-start(bf16[256,768]{1,0:T(8,128)(2,1)S(1)} %get-tuple-element.185), channel_id=1, source_target_pairs={{0,1},{1,0},{2,3},{3,2},{4,5},{5,4},{6,7},{7,6},{8,9},{9,8},{10,11... | collective-permute-start | bytes 1179656 | tf_op jit(solution)/shard_map/ppermute | solution.py:577
  58.1 11.2 %collective-permute-start.22 = (bf16[256,768]{1,0:T(8,128)(2,1)S(1)}, bf16[256,768]{1,0:T(8,128)(2,1)S(1)}, u32[]{:S(2)}, u32[]{:S(2)}) collective-permute-start(bf16[256,768]{1,0:T(8,128)(2,1)S(1)} %add.6.one), channel_id=1, source_target_pairs={{0,2},{1,3},{2,0},{3,1},{4,6},{5,7},{6,4},{7,5},{8,10},{9,11},{10,... | collective-permute-start | bytes 1179656 | tf_op jit(solution)/shard_map/ppermute | solution.py:577
  59.7 15.1 %collective-permute-start.23 = (bf16[4,96,768]{2,1,0:T(8,128)(2,1)S(1)}, bf16[4,96,768]{2,1,0:T(8,128)(2,1)S(1)}, u32[]{:S(2)}, u32[]{:S(2)}) collective-permute-start(bf16[4,96,768]{2,1,0:T(8,128)(2,1)S(1)} %get-tuple-element.199), channel_id=1, source_target_pairs={{0,8},{4,12},{8,0},{12,4},{16,24},{20,28},{24,16},{28,20},{1,9},{5... | collective-permute-start | bytes 1769480 | tf_op jit(solution)/shard_map/ppermute | solution.py:574
  64.1 1.5 %collective-permute-start.20 = (bf16[128,768]{1,0:T(8,128)(2,1)S(1)}, bf16[128,768]{1,0:T(8,128)(2,1)S(1)}, u32[]{:S(2)}, u32[]{:S(2)}) collective-permute-start(bf16[128,768]{1,0:T(8,128)(2,1)S(1)} %get-tuple-element.194), channel_id=1, source_target_pairs={{0,1},{1,0},{2,3},{3,2},{4,5},{5,4},{6,7},{7,6},{8,9},{9,8},{10,11... | collective-permute-start | bytes 589832 | tf_op jit(solution)/shard_map/ppermute | solution.py:577
  64.2 1.7 %collective-permute-start.21 = (bf16[128,768]{1,0:T(8,128)(2,1)S(1)}, bf16[128,768]{1,0:T(8,128)(2,1)S(1)}, u32[]{:S(2)}, u32[]{:S(2)}) collective-permute-start(bf16[128,768]{1,0:T(8,128)(2,1)S(1)} %get-tuple-element.195), channel_id=1, source_target_pairs={{0,1},{1,0},{2,3},{3,2},{4,5},{5,4},{6,7},{7,6},{8,9},{9,8},{10,11... | collective-permute-start | bytes 589832 | tf_op jit(solution)/shard_map/ppermute | solution.py:577
  64.7 16.6 %collective-permute-start.25 = (bf16[4,96,768]{2,1,0:T(8,128)(2,1)S(1)}, bf16[4,96,768]{2,1,0:T(8,128)(2,1)S(1)}, u32[]{:S(2)}, u32[]{:S(2)}) collective-permute-start(bf16[4,96,768]{2,1,0:T(8,128)(2,1)S(1)} %get-tuple-element.213), channel_id=1, source_target_pairs={{0,4},{4,0},{8,12},{12,8},{16,20},{20,16},{24,28},{28,24},{1,5},{5... | collective-permute-start | bytes 1769480 | tf_op jit(solution)/shard_map/ppermute | solution.py:574
  69.4 6.1 %collective-permute-start.24 = (bf16[256,768]{1,0:T(8,128)(2,1)S(1)}, bf16[256,768]{1,0:T(8,128)(2,1)S(1)}, u32[]{:S(2)}, u32[]{:S(2)}) collective-permute-start(bf16[256,768]{1,0:T(8,128)(2,1)S(1)} %add.7.own), channel_id=1, source_target_pairs={{0,1},{1,0},{2,3},{3,2},{4,5},{5,4},{6,7},{7,6},{8,9},{9,8},{10,11... | collective-permute-start | bytes 1179656 | tf_op jit(solution)/shard_map/ppermute | solution.py:577
  74.9 12.3 %collective-permute-start.26 = (bf16[2,96,768]{2,1,0:T(8,128)(2,1)S(1)}, bf16[2,96,768]{2,1,0:T(8,128)(2,1)S(1)}, u32[]{:S(2)}, u32[]{:S(2)}) collective-permute-start(bf16[2,96,768]{2,1,0:T(8,128)(2,1)S(1)} %get-tuple-element.201), channel_id=1, source_target_pairs={{0,4},{4,0},{8,12},{12,8},{16,20},{20,16},{24,28},{28,24},{1,5},{5... | collective-permute-start | bytes 884744 | tf_op jit(solution)/shard_map/ppermute | solution.py:574
  81.4 11.5 %collective-permute-start.27 = (bf16[200,768]{1,0:T(8,128)(2,1)S(1)}, bf16[200,768]{1,0:T(8,128)(2,1)S(1)}, u32[]{:S(2)}, u32[]{:S(2)}) collective-permute-start(bf16[200,768]{1,0:T(8,128)(2,1)S(1)} %get-tuple-element.223.sent), channel_id=1, source_target_pairs={{0,4},{4,0},{8,12},{12,8},{16,20},{20,16},{24,28},{28,24},{1,5},{5... | collective-permute-start | bytes 921608 | tf_op jit(solution)/shard_map/ppermute | solution.py:574
  83.0 12.7 %collective-permute-start.29 = (bf16[2,96,768]{2,1,0:T(8,128)(2,1)S(1)}, bf16[2,96,768]{2,1,0:T(8,128)(2,1)S(1)}, u32[]{:S(2)}, u32[]{:S(2)}) collective-permute-start(bf16[2,96,768]{2,1,0:T(8,128)(2,1)S(1)} %get-tuple-element.215), channel_id=1, source_target_pairs={{0,8},{4,12},{8,0},{12,4},{16,24},{20,28},{24,16},{28,20},{1,9},{5... | collective-permute-start | bytes 884744 | tf_op jit(solution)/shard_map/ppermute | solution.py:574
  87.3 8.4 %collective-permute-start.28 = (bf16[96,768]{1,0:T(8,128)(2,1)S(1)}, bf16[96,768]{1,0:T(8,128)(2,1)S(1)}, u32[]{:S(2)}, u32[]{:S(2)}) collective-permute-start(bf16[96,768]{1,0:T(8,128)(2,1)S(1)} %get-tuple-element.220), channel_id=1, source_target_pairs={{0,16},{4,20},{8,24},{12,28},{16,0},{20,4},{24,8},{28,12},{1,17},{... | collective-permute-start | bytes 442376 | tf_op jit(solution)/shard_map/ppermute | solution.py:574
  89.6 6.2 %collective-permute-start.30 = (bf16[128,768]{1,0:T(8,128)(2,1)S(1)}, bf16[128,768]{1,0:T(8,128)(2,1)S(1)}, u32[]{:S(2)}, u32[]{:S(2)}) collective-permute-start(bf16[128,768]{1,0:T(8,128)(2,1)S(1)} %get-tuple-element.231), channel_id=1, source_target_pairs={{0,1},{1,0},{2,3},{3,2},{4,5},{5,4},{6,7},{7,6},{8,9},{9,8},{10,11... | collective-permute-start | bytes 589832 | tf_op jit(solution)/shard_map/ppermute | solution.py:577
  89.6 6.2 %collective-permute-start.31 = (bf16[128,768]{1,0:T(8,128)(2,1)S(1)}, bf16[128,768]{1,0:T(8,128)(2,1)S(1)}, u32[]{:S(2)}, u32[]{:S(2)}) collective-permute-start(bf16[128,768]{1,0:T(8,128)(2,1)S(1)} %get-tuple-element.232), channel_id=1, source_target_pairs={{0,1},{1,0},{2,3},{3,2},{4,5},{5,4},{6,7},{7,6},{8,9},{9,8},{10,11... | collective-permute-start | bytes 589832 | tf_op jit(solution)/shard_map/ppermute | solution.py:577
  93.0 11.8 %collective-permute-start.34 = (bf16[200,768]{1,0:T(8,128)(2,1)S(1)}, bf16[200,768]{1,0:T(8,128)(2,1)S(1)}, u32[]{:S(2)}, u32[]{:S(2)}) collective-permute-start(bf16[200,768]{1,0:T(8,128)(2,1)S(1)} %last_high.1.sent), channel_id=1, source_target_pairs={{0,8},{4,12},{8,0},{12,4},{16,24},{20,28},{24,16},{28,20},{1,9},{5... | collective-permute-start | bytes 921608 | tf_op jit(solution)/shard_map/ppermute | solution.py:574
  95.6 8.3 %collective-permute-start.33 = (bf16[2,96,768]{2,1,0:T(8,128)(2,1)S(1)}, bf16[2,96,768]{2,1,0:T(8,128)(2,1)S(1)}, u32[]{:S(2)}, u32[]{:S(2)}) collective-permute-start(bf16[2,96,768]{2,1,0:T(8,128)(2,1)S(1)} %get-tuple-element.238), channel_id=1, source_target_pairs={{0,4},{4,0},{8,12},{12,8},{16,20},{20,16},{24,28},{28,24},{1,5},{5... | collective-permute-start | bytes 884744 | tf_op jit(solution)/shard_map/ppermute | solution.py:574
  96.0 10.3 %collective-permute-start.35 = (bf16[256,768]{1,0:T(8,128)(2,1)S(1)}, bf16[256,768]{1,0:T(8,128)(2,1)S(1)}, u32[]{:S(2)}, u32[]{:S(2)}) collective-permute-start(bf16[256,768]{1,0:T(8,128)(2,1)S(1)} %get-tuple-element.242), channel_id=1, source_target_pairs={{0,2},{1,3},{2,0},{3,1},{4,6},{5,7},{6,4},{7,5},{8,10},{9,11},{10,... | collective-permute-start | bytes 1179656 | tf_op jit(solution)/shard_map/ppermute | solution.py:577
  96.6 7.3 %collective-permute-start.32 = (bf16[96,768]{1,0:T(8,128)(2,1)S(1)}, bf16[96,768]{1,0:T(8,128)(2,1)S(1)}, u32[]{:S(2)}, u32[]{:S(2)}) collective-permute-start(bf16[96,768]{1,0:T(8,128)(2,1)S(1)} %get-tuple-element.228), channel_id=1, source_target_pairs={{0,16},{4,20},{8,24},{12,28},{16,0},{20,4},{24,8},{28,12},{1,17},{... | collective-permute-start | bytes 442376 | tf_op jit(solution)/shard_map/ppermute | solution.py:574
  105.0 8.3 %collective-permute-start.36 = (bf16[104,768]{1,0:T(8,128)(2,1)S(1)}, bf16[104,768]{1,0:T(8,128)(2,1)S(1)}, u32[]{:S(2)}, u32[]{:S(2)}) collective-permute-start(bf16[104,768]{1,0:T(8,128)(2,1)S(1)} %get-tuple-element.239.rest_1_), channel_id=1, source_target_pairs={{0,16},{4,20},{8,24},{12,28},{16,0},{20,4},{24,8},{28,12},{1,17},{... | collective-permute-start | bytes 479240 | tf_op jit(solution)/shard_map/ppermute | solution.py:574

commit v6 on v5

--- a/solution.py
+++ b/solution.py
@@ -399,6 +399,16 @@
     for k in range(4):
         to = theirs if k >= 2 else mine
         to[k % 2] = (keep[k].astype(f32) + got[k].astype(f32)).astype(bf16)
+
+
+def high_add_kernel(keep, got, theirs):
+    for k in range(2):
+        theirs[k] = (keep[k + 2].astype(f32) + got[k].astype(f32)).astype(bf16)
+
+
+def late_add_kernel(keep, got_low, got, mine, theirs):
+    for k, to in enumerate((mine, theirs)):
+        to[...] = (keep[k].astype(f32) + got_low[k].astype(f32) + got[k].astype(f32)).astype(bf16)
 
 
 def next_add_kernel(keep, got, mine, theirs):
@@ -584,6 +594,15 @@
         outs = [sds((2, *keep.shape[1:]), bf16)] * 2
         return call(pair_add_kernel, outs, (keep, got), "pair_add", limit=4, behind=behind)
 
+    def high_add(keep, got, behind):
+        outs = [sds((2, *keep.shape[1:]), bf16)]
+        (out,) = call(high_add_kernel, outs, (keep, got), "high_add", limit=4, behind=behind)
+        return out
+
+    def late_add(keep, got_low, got, behind):
+        outs = [sds(keep.shape[1:], bf16)] * 2
+        return call(late_add_kernel, outs, (keep, got_low, got), "late_add", limit=4, behind=behind)
+
     def next_add(keep, got, behind):
         outs = [sds(keep.shape[1:], bf16)] * 2
         return call(next_add_kernel, outs, (keep, got), "next_add", limit=4, behind=behind)
@@ -631,7 +650,7 @@
         three_across = swap_dp(three, 1)
         qkvo_blocks = [packed, own, one, one_across, two, two_across, three, three_across]
         ffn_three = swap_dp(after(ffn_two, ffn_one), 2)
-        ffn_blocks = [packed_ffn, ffn_own, ffn_one, swap_dp(after(ffn_own, ffn_three), 2)]
+        ffn_blocks = [packed_ffn, ffn_own, ffn_one, swap_dp(after(ffn_own, ffn_one), 2)]
         for block in (ffn_two, ffn_three):
             ffn_blocks += [block, swap_dp(block, 1)]
         bias = after(bias, ffn_own, ffn_two)
@@ -673,11 +692,11 @@
         "ffn",
         scratch=[pltpu.VMEM((tokens, hidden), f32)],
     )
-    down_order, in_order = (2, 1, 4), (1, 2, 4)
+    down_order, in_order = (2, 4, 1), (1, 2, 4)
     grad_scratch = [pltpu.VMEM((model, hidden), f32)]
     down_parts = call(
         functools.partial(down_grad_kernel, down_order),
-        spread_shapes(dp, model, hidden, (4, 4)),
+        spread_shapes(dp, model, hidden, (4, 2, 2)),
         (cotangent, hidden_act),
         "down_grad",
         scratch=grad_scratch,
@@ -697,12 +716,16 @@
     )
     ffn_got = [swap_tp(part, 1) for part in ffn_send]
     ffn_sums = call(core_add_kernel, half_blocks, (ffn_keep, *ffn_got), "ffn_add", limit=4)
-    back_sum = add(back_first, back_got, ffn_sums[:1])
     attend_behind = ()
+    back_behind = ffn_sums[:1]
     if direct:
-        down_keep, down_send = down_parts
-        down_one = pair_add(down_keep, swap_dp(down_send, down_order[0]), (back_sum,))
-        attend_behind = down_one
+        down_keep, down_high, down_low = down_parts
+        down_got = swap_dp(down_high, down_order[0])
+        back_behind = (*back_behind, down_got)
+    back_sum = add(back_first, back_got, back_behind)
+    if direct:
+        down_one = high_add(down_keep, down_got, (back_sum,))
+        attend_behind = (down_one,)
     everyone = dp * tp
     qkvo_shapes = spread_shapes(dp, model, packed_cols, (4, 2))
     small_shape = sds((2 * rows + SMALL, model), bf16) if direct else sds((SMALL, model), f32)
@@ -757,7 +780,8 @@
         in_one = pair_add(in_keep, swap_dp(in_send, in_order[0]), (proj_grad,))
         got_high = swap_dp(after(small, *in_one), 1)
         act_parts = act_shares(in_one)
-        down_two = next_add(down_one[0], swap_dp(down_one[1], down_order[1]), act_parts[:1])
+        down_rest = (swap_dp(down_low, down_order[0]), swap_dp(down_one, down_order[1]))
+        down_two = late_add(down_keep, *down_rest, act_parts[:1])
         (high,) = call(
             last_high_kernel, [small_shape], (keep, small, got_high), "last_high", limit=4, behind=down_two
         )

time: 128 us -> 126 us (0.984)
    ppermute x13, waiting for transfers between devices: 6.1 us -> 3.56 us  [swap_tp(): return lax.ppermute(value, 'tp', [(i, i ^ distance) for i in range(tp)])]
    ppermute x24 -> x25, starting transfers between devices: 35.1 us -> 33.6 us  [swap_dp(): return lax.ppermute(value, 'dp', [(i, i ^ distance) for i in range(dp)])]
    ppermute x24 -> x25, waiting for transfers between devices: 40.1 us -> 41.5 us  [swap_dp(): return lax.ppermute(value, 'dp', [(i, i ^ distance) for i in range(dp)])]
  transfers between devices with their start and end apart: 37 -> 38, of which waited for: 22 -> 20; matrix products, arithmetic and copies ran while one was open for 0% -> 0% of each run, Pallas kernels for 16% -> 16%
where the time goes in v6:
time: 126 us
  waiting for transfers between devices  45.1 us (36%)
  starting transfers between devices  40.1 us (32%)
  Pallas kernels  28.4 us (23%)
  blocking collectives  11 us (9%)
    ppermute x25, waiting for transfers between devices, swap_dp(): return lax.ppermute(value, 'dp', [(i, i ^ distance) for i in range(dp)])  41.5 us
    ppermute x25, starting transfers between devices, swap_dp(): return lax.ppermute(value, 'dp', [(i, i ^ distance) for i in range(dp)])  33.6 us
    pallas_call x28, Pallas kernels, call(): pl.pallas_call(body, out_shape=tuple(outs), in_specs=[pl.BlockSpec(memory...  28.4 us
    all_to_all x1, blocking collectives, on_device(): told = lax.all_to_all(payload, ('dp', 'tp'), 0, 0)  11 us
    ppermute x13, starting transfers between devices, swap_tp(): return lax.ppermute(value, 'tp', [(i, i ^ distance) for i in range(tp)])  6.54 us
    ppermute x13, waiting for transfers between devices, swap_tp(): return lax.ppermute(value, 'tp', [(i, i ^ distance) for i in range(tp)])  3.56 us
  transfers between devices with their start and end apart: 38, of which 20 were waited for; matrix products, arithmetic and copies ran while one was open for 0% of the time, Pallas kernels for 16%

profile of v6, /device:TPU:0, one launch (start us, length us, event | category | flops | bytes accessed | tf_op | source)
XLA Modules:
  0.0 125.7 jit_solution(15643923686871846539)
XLA Ops:
  0.7 1.2 pack.1
  1.9 4.1 %collective-permute-start.1 = (bf16[96,768]{1,0:T(8,128)(2,1)S(1)}, bf16[96,768]{1,0:T(8,128)(2,1)S(1)}, u32[]{:S(2)}, u32[]{:S(2)}) collective-permute-start(bf16[96,768]{1,0:T(8,128)(2,1)S(1)} %get-tuple-element.169.rest_0_), channel_id=1, source_target_pairs={{0,16},{4,20},{8,24},{12,28},{16,0},{20,4},{24,8},{28,12},{1,17},{... | collective-permute-start | bytes 442376 | tf_op jit(solution)/shard_map/ppermute | solution.py:584
  6.0 1.6 %collective-permute-start.4 = (bf16[96,768]{1,0:T(8,128)(2,1)S(1)}, bf16[96,768]{1,0:T(8,128)(2,1)S(1)}, u32[]{:S(2)}, u32[]{:S(2)}) collective-permute-start(bf16[96,768]{1,0:T(8,128)(2,1)S(1)} %get-tuple-element.169.rest_0_), channel_id=1, source_target_pairs={{0,8},{4,12},{8,0},{12,4},{16,24},{20,28},{24,16},{28,20},{1,9},{5... | collective-permute-start | bytes 442376 | tf_op jit(solution)/shard_map/ppermute | solution.py:584
  7.6 2.2 %prep.1 = (bf16[512,768]{1,0:T(8,128)(2,1)S(1)}, bf16[768,512]{1,0:T(8,128)(2,1)S(1)}, f32[3,512,512]{2,1,0:T(8,128)S(1)}, s32[1,1024]{1,0:T(1,128)S(1)}, bf16[5...) custom-call(s32[1,4]{1,0:T(1,128)} %seg_in.1, f32[3,32]{1,0:T(4,128)} %bitcast.8, ...), custom_call_target="tpu_custom_call" | custom-call | tf_op jit(solution)/shard_map/prep/pallas_call | solution.py:61
  9.8 1.6 %collective-permute-start = (bf16[96,1536]{1,0:T(8,128)(2,1)S(1)}, bf16[96,1536]{1,0:T(8,128)(2,1)S(1)}, u32[]{:S(2)}, u32[]{:S(2)}) collective-permute-start(bf16[96,1536]{1,0:T(8,128)(2,1)S(1)} %get-tuple-element.173.rest_0_), channel_id=1, source_target_pairs={{0,4},{4,0},{8,12},{12,8},{16,20},{20,16},{24,28},{28,24},{1,5},{5... | collective-permute-start | bytes 884744 | tf_op jit(solution)/shard_map/ppermute | solution.py:584
  11.3 1.8 %collective-permute-done.1.rest_4_ = bf16[96,768]{1,0:T(8,128)(2,1)S(1)} collective-permute-done((bf16[96,768]{1,0:T(8,128)(2,1)S(1)}, bf16[96,768]{1,0:T(8,128)(2,1)S(1)}, u32[]{:S(2)}, u32[]{:S(2)}) %collective-permute-start.1) | collective-permute-done | bytes 147488 | tf_op jit(solution)/shard_map/ppermute | solution.py:584
  13.7 1.5 %collective-permute-start.3 = (bf16[96,768]{1,0:T(8,128)(2,1)S(1)}, bf16[96,768]{1,0:T(8,128)(2,1)S(1)}, u32[]{:S(2)}, u32[]{:S(2)}) collective-permute-start(bf16[96,768]{1,0:T(8,128)(2,1)S(1)} %get-tuple-element.169.rest_0_), channel_id=1, source_target_pairs={{0,4},{4,0},{8,12},{12,8},{16,20},{20,16},{24,28},{28,24},{1,5},{5... | collective-permute-start | bytes 442376 | tf_op jit(solution)/shard_map/ppermute | solution.py:584
  15.2 3.4 %collective-permute-start.7 = (bf16[96,768]{1,0:T(8,128)(2,1)S(1)}, bf16[96,768]{1,0:T(8,128)(2,1)S(1)}, u32[]{:S(2)}, u32[]{:S(2)}) collective-permute-start(bf16[96,768]{1,0:T(8,128)(2,1)S(1)} %collective-permute-done.1.rest_4_), channel_id=1, source_target_pairs={{0,8},{4,12},{8,0},{12,4},{16,24},{20,28},{24,16},{28,20},{1,9},{5... | collective-permute-start | bytes 442376 | tf_op jit(solution)/shard_map/ppermute | solution.py:584
  19.2 2.8 %collective-permute-done.3.rest_1_ = bf16[96,768]{1,0:T(8,128)(2,1)S(1)} collective-permute-done((bf16[96,768]{1,0:T(8,128)(2,1)S(1)}, bf16[96,768]{1,0:T(8,128)(2,1)S(1)}, u32[]{:S(2)}, u32[]{:S(2)}) %collective-permute-start.3) | collective-permute-done | bytes 147488 | tf_op jit(solution)/shard_map/ppermute | solution.py:584
  22.0 2.5 %collective-permute-start.6 = (bf16[96,768]{1,0:T(8,128)(2,1)S(1)}, bf16[96,768]{1,0:T(8,128)(2,1)S(1)}, u32[]{:S(2)}, u32[]{:S(2)}) collective-permute-start(bf16[96,768]{1,0:T(8,128)(2,1)S(1)} %collective-permute-done.1.rest_4_), channel_id=1, source_target_pairs={{0,4},{4,0},{8,12},{12,8},{16,20},{20,16},{24,28},{28,24},{1,5},{5... | collective-permute-start | bytes 442376 | tf_op jit(solution)/shard_map/ppermute | solution.py:584
  24.5 0.9 collective-permute-done.5.rest_3_
  25.4 1.6 %collective-permute-start.11 = (bf16[96,1536]{1,0:T(8,128)(2,1)S(1)}, bf16[96,1536]{1,0:T(8,128)(2,1)S(1)}, u32[]{:S(2)}, u32[]{:S(2)}) collective-permute-start(bf16[96,1536]{1,0:T(8,128)(2,1)S(1)} %get-tuple-element.173.rest_0_), channel_id=1, source_target_pairs={{0,8},{4,12},{8,0},{12,4},{16,24},{20,28},{24,16},{28,20},{1,9},{5... | collective-permute-start | bytes 884744 | tf_op jit(solution)/shard_map/ppermute | solution.py:584
  27.0 1.5 %collective-permute-done.2.rest_4_ = bf16[96,1536]{1,0:T(8,128)(2,1)S(1)} collective-permute-done((bf16[96,1536]{1,0:T(8,128)(2,1)S(1)}, bf16[96,1536]{1,0:T(8,128)(2,1)S(1)}, u32[]{:S(2)}, u32[]{:S(2)}) %collective-permute-start.2) | collective-permute-done | bytes 294944 | tf_op jit(solution)/shard_map/ppermute | solution.py:584
  29.1 1.6 %collective-permute-done.8.rest_7_ = bf16[96,768]{1,0:T(8,128)(2,1)S(1)} collective-permute-done((bf16[96,768]{1,0:T(8,128)(2,1)S(1)}, bf16[96,768]{1,0:T(8,128)(2,1)S(1)}, u32[]{:S(2)}, u32[]{:S(2)}) %collective-permute-start.8) | collective-permute-done | bytes 147488 | tf_op jit(solution)/shard_map/ppermute | solution.py:584
  30.7 3.1 %attend.1 = (bf16[768,768]{1,0:T(8,128)(2,1)S(1)}, bf16[512,576]{1,0:T(8,128)(2,1)S(1)}, bf16[3,512,512]{2,1,0:T(8,128)(2,1)S(1)}, bf16[512,192]{1,0:T(8,128)(2,...) custom-call(bf16[512,768]{1,0:T(8,128)(2,1)S(1)} %get-tuple-element.162.act, ...), custom_call_target="tpu_custom_call" | custom-call | tf_op jit(solution)/shard_map/attend/pallas_call | solution.py:61
  33.8 0.9 collective-permute-done.11.rest_2_
  35.3 1.5 %collective-permute-start.10 = (bf16[96,1536]{1,0:T(8,128)(2,1)S(1)}, bf16[96,1536]{1,0:T(8,128)(2,1)S(1)}, u32[]{:S(2)}, u32[]{:S(2)}) collective-permute-start(bf16[96,1536]{1,0:T(8,128)(2,1)S(1)} %collective-permute-done.2.rest_4_), channel_id=1, source_target_pairs={{0,4},{4,0},{8,12},{12,8},{16,20},{20,16},{24,28},{28,24},{1,5},{5... | collective-permute-start | bytes 884744 | tf_op jit(solution)/shard_map/ppermute | solution.py:584
  36.9 1.6 %collective-permute-start.13 = (bf16[128,768]{1,0:T(8,128)(2,1)S(1)}, bf16[128,768]{1,0:T(8,128)(2,1)S(1)}, u32[]{:S(2)}, u32[]{:S(2)}) collective-permute-start(bf16[128,768]{1,0:T(8,128)(2,1)S(1)} %get-tuple-element.175.one), channel_id=1, source_target_pairs={{0,2},{1,3},{2,0},{3,1},{4,6},{5,7},{6,4},{7,5},{8,10},{9,11},{10,... | collective-permute-start | bytes 589832 | tf_op jit(solution)/shard_map/ppermute | solution.py:587
  39.0 1.1 collective-permute-start.17
  40.1 4.6 %collective-permute-done.12.rest_6_ = bf16[96,1536]{1,0:T(8,128)(2,1)S(1)} collective-permute-done((bf16[96,1536]{1,0:T(8,128)(2,1)S(1)}, bf16[96,1536]{1,0:T(8,128)(2,1)S(1)}, u32[]{:S(2)}, u32[]{:S(2)}) %collective-permute-start.12) | collective-permute-done | bytes 294944 | tf_op jit(solution)/shard_map/ppermute | solution.py:584
  44.7 1.1 collective-permute-start.18
  45.9 2.0 %collective-permute-done.14.two = bf16[128,768]{1,0:T(8,128)(2,1)S(1)} collective-permute-done((bf16[128,768]{1,0:T(8,128)(2,1)S(1)}, bf16[128,768]{1,0:T(8,128)(2,1)S(1)}, u32[]{:S(2)}, u32[]{:S(2)}) %collective-permute-start.14) | collective-permute-done | bytes 196640 | tf_op jit(solution)/shard_map/ppermute | solution.py:587
  48.0 1.6 %collective-permute-done.17.rest_3_ = bf16[96,1536]{1,0:T(8,128)(2,1)S(1)} collective-permute-done((bf16[96,1536]{1,0:T(8,128)(2,1)S(1)}, bf16[96,1536]{1,0:T(8,128)(2,1)S(1)}, u32[]{:S(2)}, u32[]{:S(2)}) %collective-permute-start.17) | collective-permute-done | bytes 294944 | tf_op jit(solution)/shard_map/ppermute | solution.py:584
  49.6 1.8 %collective-permute-done.18.rest_7_ = bf16[96,1536]{1,0:T(8,128)(2,1)S(1)} collective-permute-done((bf16[96,1536]{1,0:T(8,128)(2,1)S(1)}, bf16[96,1536]{1,0:T(8,128)(2,1)S(1)}, u32[]{:S(2)}, u32[]{:S(2)}) %collective-permute-start.18) | collective-permute-done | bytes 294944 | tf_op jit(solution)/shard_map/ppermute | solution.py:584
  51.4 3.5 %ffn.1 = (f32[512,768]{1,0:T(8,128)S(1)}, bf16[512,768]{1,0:T(8,128)(2,1)S(1)}, bf16[512,768]{1,0:T(8,128)(2,1)S(1)}, bf16[512,768]{1,0:T(8,128)(2,1)S(1)}, bf16...) custom-call(bf16[512,768]{1,0:T(8,128)(2,1)S(1)} %get-tuple-element., ...), custom_call_target="tpu_custom_call" | custom-call | tf_op jit(solution)/shard_map/ffn/pallas_call | solution.py:61
  55.0 0.9 down_grad.1
  56.8 1.4 %collective-permute-start.23 = (bf16[256,768]{1,0:T(8,128)(2,1)S(1)}, bf16[256,768]{1,0:T(8,128)(2,1)S(1)}, u32[]{:S(2)}, u32[]{:S(2)}) collective-permute-start(bf16[256,768]{1,0:T(8,128)(2,1)S(1)} %add.6.one), channel_id=1, source_target_pairs={{0,2},{1,3},{2,0},{3,1},{4,6},{5,7},{6,4},{7,5},{8,10},{9,11},{10,... | collective-permute-start | bytes 1179656 | tf_op jit(solution)/shard_map/ppermute | solution.py:587
  58.3 2.0 %collective-permute-start.22 = (bf16[2,96,768]{2,1,0:T(8,128)(2,1)S(1)}, bf16[2,96,768]{2,1,0:T(8,128)(2,1)S(1)}, u32[]{:S(2)}, u32[]{:S(2)}) collective-permute-start(bf16[2,96,768]{2,1,0:T(8,128)(2,1)S(1)} %get-tuple-element.196), channel_id=1, source_target_pairs={{0,8},{4,12},{8,0},{12,4},{16,24},{20,28},{24,16},{28,20},{1,9},{5... | collective-permute-start | bytes 884744 | tf_op jit(solution)/shard_map/ppermute | solution.py:584
  60.2 1.0 in_grad.1
  61.3 1.6 %ffn_out.1 = (bf16[256,768]{1,0:T(8,128)(2,1)S(1)}, bf16[128,768]{1,0:T(8,128)(2,1)S(1)}, bf16[128,768]{1,0:T(8,128)(2,1)S(1)}) custom-call(bf16[512,768]{1,0:T(8,128)(2,1)S(1)} %get-tuple-element.190.right.hidden, bf16[768,768]{1,0:T(8,128)(2,1)S(1)} %get-tuple-element.191.down), custom_call_target="tpu_custom_call" | custom-call | tf_op jit(solution)/shard_map/ffn_out/pallas_call | solution.py:61
  63.5 1.5 %collective-permute-start.25 = (bf16[4,96,768]{2,1,0:T(8,128)(2,1)S(1)}, bf16[4,96,768]{2,1,0:T(8,128)(2,1)S(1)}, u32[]{:S(2)}, u32[]{:S(2)}) collective-permute-start(bf16[4,96,768]{2,1,0:T(8,128)(2,1)S(1)} %get-tuple-element.210), channel_id=1, source_target_pairs={{0,4},{4,0},{8,12},{12,8},{16,20},{20,16},{24,28},{28,24},{1,5},{5... | collective-permute-start | bytes 1769480 | tf_op jit(solution)/shard_map/ppermute | solution.py:584
  65.4 1.9 %collective-permute-done.22.got = bf16[2,96,768]{2,1,0:T(8,128)(2,1)S(1)} collective-permute-done((bf16[2,96,768]{2,1,0:T(8,128)(2,1)S(1)}, bf16[2,96,768]{2,1,0:T(8,128)(2,1)S(1)}, u32[]{:S(2)}, u32[]{:S(2)}) %collective-permute-start.22) | collective-permute-done | bytes 294944 | tf_op jit(solution)/shard_map/ppermute | solution.py:584
  68.2 1.9 %collective-permute-start.26 = (bf16[2,96,768]{2,1,0:T(8,128)(2,1)S(1)}, bf16[2,96,768]{2,1,0:T(8,128)(2,1)S(1)}, u32[]{:S(2)}, u32[]{:S(2)}) collective-permute-start(bf16[2,96,768]{2,1,0:T(8,128)(2,1)S(1)} %get-tuple-element.216), channel_id=1, source_target_pairs={{0,8},{4,12},{8,0},{12,4},{16,24},{20,28},{24,16},{28,20},{1,9},{5... | collective-permute-start | bytes 884744 | tf_op jit(solution)/shard_map/ppermute | solution.py:584
  70.2 3.5 %collective-permute-start.27 = (bf16[2,96,768]{2,1,0:T(8,128)(2,1)S(1)}, bf16[2,96,768]{2,1,0:T(8,128)(2,1)S(1)}, u32[]{:S(2)}, u32[]{:S(2)}) collective-permute-start(bf16[2,96,768]{2,1,0:T(8,128)(2,1)S(1)} %high_add.1), channel_id=1, source_target_pairs={{0,16},{4,20},{8,24},{12,28},{16,0},{20,4},{24,8},{28,12},{1,17},{... | collective-permute-start | bytes 884744 | tf_op jit(solution)/shard_map/ppermute | solution.py:584
  73.7 5.7 %attend_back.1 = (bf16[4,96,768]{2,1,0:T(8,128)(2,1)S(1)}, bf16[2,96,768]{2,1,0:T(8,128)(2,1)S(1)}, f32[128,768]{1,0:T(8,128)S(1)}, bf16[200,768]{1,0:T(8,128)(2,1)S(1)}, bf16[512,576]{1,0:T(8,128)(2,1)S(1)}) custom-call(f32[512,768]{1,0:T(8,128)S(1)} %get-tuple-element.238.resid, bf16[512,768]{1,0:T(8,128)(2,1)S(1)} %get-tuple-element.161.dy.left, ...), custom_call_target="tpu_custom_call" | custom-call | tf_op jit(solution)/shard_map/attend_back/pallas_call | solution.py:61
  79.6 0.9 collective-permute-start.28
  80.6 1.4 %act_grad.1 = (bf16[256,768]{1,0:T(8,128)(2,1)S(1)}, bf16[128,768]{1,0:T(8,128)(2,1)S(1)}, bf16[128,768]{1,0:T(8,128)(2,1)S(1)}) custom-call(bf16[512,576]{1,0:T(8,128)(2,1)S(1)} %get-tuple-element.213.proj_grad, bf16[768,768]{1,0:T(8,128)(2,1)S(1)} %get-tuple-element.200.weights), custom_call_target="tpu_custom_call" | custom-call | tf_op jit(solution)/shard_map/act_grad/pallas_call | solution.py:61
  82.0 2.0 %collective-permute-done.26.got_low = bf16[2,96,768]{2,1,0:T(8,128)(2,1)S(1)} collective-permute-done((bf16[2,96,768]{2,1,0:T(8,128)(2,1)S(1)}, bf16[2,96,768]{2,1,0:T(8,128)(2,1)S(1)}, u32[]{:S(2)}, u32[]{:S(2)}) %collective-permute-start.26) | collective-permute-done | bytes 294944 | tf_op jit(solution)/shard_map/ppermute | solution.py:584
  84.0 3.5 %collective-permute-done.27.got = bf16[2,96,768]{2,1,0:T(8,128)(2,1)S(1)} collective-permute-done((bf16[2,96,768]{2,1,0:T(8,128)(2,1)S(1)}, bf16[2,96,768]{2,1,0:T(8,128)(2,1)S(1)}, u32[]{:S(2)}, u32[]{:S(2)}) %collective-permute-start.27) | collective-permute-done | bytes 294944 | tf_op jit(solution)/shard_map/ppermute | solution.py:584
  88.9 0.9 collective-permute-done.28.got
  90.0 2.9 %collective-permute-done.29.rest_1_ = bf16[96,768]{1,0:T(8,128)(2,1)S(1)} collective-permute-done((bf16[96,768]{1,0:T(8,128)(2,1)S(1)}, bf16[96,768]{1,0:T(8,128)(2,1)S(1)}, u32[]{:S(2)}, u32[]{:S(2)}) %collective-permute-start.29) | collective-permute-done | bytes 147488 | tf_op jit(solution)/shard_map/ppermute | solution.py:584
  94.1 1.6 %collective-permute-start.36 = (bf16[256,768]{1,0:T(8,128)(2,1)S(1)}, bf16[256,768]{1,0:T(8,128)(2,1)S(1)}, u32[]{:S(2)}, u32[]{:S(2)}) collective-permute-start(bf16[256,768]{1,0:T(8,128)(2,1)S(1)} %get-tuple-element.240), channel_id=1, source_target_pairs={{0,2},{1,3},{2,0},{3,1},{4,6},{5,7},{6,4},{7,5},{8,10},{9,11},{10,... | collective-permute-start | bytes 1179656 | tf_op jit(solution)/shard_map/ppermute | solution.py:587
  96.0 7.8 %collective-permute-done.33.rest_1_ = bf16[96,768]{1,0:T(8,128)(2,1)S(1)} collective-permute-done((bf16[96,768]{1,0:T(8,128)(2,1)S(1)}, bf16[96,768]{1,0:T(8,128)(2,1)S(1)}, u32[]{:S(2)}, u32[]{:S(2)}) %collective-permute-start.33) | collective-permute-done | bytes 147488 | tf_op jit(solution)/shard_map/ppermute | solution.py:584
  104.2 1.1 share_out.1
  105.2 1.9 %fetch.1 = (f32[3,96,192]{2,1,0:T(8,128)S(1)}, f32[3,96,192]{2,1,0:T(8,128)S(1)}, f32[3,96,192]{2,1,0:T(8,128)S(1)}, f32[96,192]{1,0:T(8,128)S(1)}, f32[96,192]{...) custom-call(f32[3,96,192]{2,1,0:T(8,128)} %refs_0_, ...), custom_call_target="tpu_custom_call" | custom-call | tf_op jit(solution)/shard_map/fetch/pallas_call | solution.py:61
  107.2 4.3 %collective-permute-done.37.rest_2_ = bf16[104,768]{1,0:T(8,128)(2,1)S(1)} collective-permute-done((bf16[104,768]{1,0:T(8,128)(2,1)S(1)}, bf16[104,768]{1,0:T(8,128)(2,1)S(1)}, u32[]{:S(2)}, u32[]{:S(2)}) %collective-permute-start.37) | collective-permute-done | bytes 159776 | tf_op jit(solution)/shard_map/ppermute | solution.py:584
  112.2 11.0 %all_to_all.5.refs_0_ = f32[32,1,384]{2,1,0:T(1,128)S(1)} all-to-all(f32[32,1,384]{2,1,0:T(1,128)} %get-tuple-element.249), channel_id=1, replica_groups=mesh['dp'=8,'tp'=4] {'dp','tp'}, dimensions={0} | all-to-all | bytes 98304 | tf_op jit(solution)/shard_map/all_to_all | solution.py:858
  123.2 2.4 %adam.1 = (f32[1,1]{1,0:T(1,128)}, f32[3,96,192]{2,1,0:T(8,128)}, f32[3,96,192]{2,1,0:T(8,128)}, f32[3,96,192]{2,1,0:T(8,128)}, bf16[3,96,192]{2,1,0:T(8,128)(2,...) custom-call(f32[32,1,384]{2,1,0:T(1,128)S(1)} %all_to_all.5.refs_0_,, ...), custom_call_target="tpu_custom_call" | custom-call | tf_op jit(solution)/shard_map/adam/pallas_call | solution.py:61
  (57 shorter events, 10.3 us)
Async XLA Ops:
  1.9 11.2 %collective-permute-start.1 = (bf16[96,768]{1,0:T(8,128)(2,1)S(1)}, bf16[96,768]{1,0:T(8,128)(2,1)S(1)}, u32[]{:S(2)}, u32[]{:S(2)}) collective-permute-start(bf16[96,768]{1,0:T(8,128)(2,1)S(1)} %get-tuple-element.169.rest_0_), channel_id=1, source_target_pairs={{0,16},{4,20},{8,24},{12,28},{16,0},{20,4},{24,8},{28,12},{1,17},{... | collective-permute-start | bytes 442376 | tf_op jit(solution)/shard_map/ppermute | solution.py:584
  6.0 12.6 %collective-permute-start.4 = (bf16[96,768]{1,0:T(8,128)(2,1)S(1)}, bf16[96,768]{1,0:T(8,128)(2,1)S(1)}, u32[]{:S(2)}, u32[]{:S(2)}) collective-permute-start(bf16[96,768]{1,0:T(8,128)(2,1)S(1)} %get-tuple-element.169.rest_0_), channel_id=1, source_target_pairs={{0,8},{4,12},{8,0},{12,4},{16,24},{20,28},{24,16},{28,20},{1,9},{5... | collective-permute-start | bytes 442376 | tf_op jit(solution)/shard_map/ppermute | solution.py:584
  9.8 17.3 %collective-permute-start = (bf16[96,1536]{1,0:T(8,128)(2,1)S(1)}, bf16[96,1536]{1,0:T(8,128)(2,1)S(1)}, u32[]{:S(2)}, u32[]{:S(2)}) collective-permute-start(bf16[96,1536]{1,0:T(8,128)(2,1)S(1)} %get-tuple-element.173.rest_0_), channel_id=1, source_target_pairs={{0,4},{4,0},{8,12},{12,8},{16,20},{20,16},{24,28},{28,24},{1,5},{5... | collective-permute-start | bytes 884744 | tf_op jit(solution)/shard_map/ppermute | solution.py:584
  13.1 15.4 %collective-permute-start.2 = (bf16[96,1536]{1,0:T(8,128)(2,1)S(1)}, bf16[96,1536]{1,0:T(8,128)(2,1)S(1)}, u32[]{:S(2)}, u32[]{:S(2)}) collective-permute-start(bf16[96,1536]{1,0:T(8,128)(2,1)S(1)} %get-tuple-element.173.rest_0_), channel_id=1, source_target_pairs={{0,16},{4,20},{8,24},{12,28},{16,0},{20,4},{24,8},{28,12},{1,17},{... | collective-permute-start | bytes 884744 | tf_op jit(solution)/shard_map/ppermute | solution.py:584
  13.7 8.3 %collective-permute-start.3 = (bf16[96,768]{1,0:T(8,128)(2,1)S(1)}, bf16[96,768]{1,0:T(8,128)(2,1)S(1)}, u32[]{:S(2)}, u32[]{:S(2)}) collective-permute-start(bf16[96,768]{1,0:T(8,128)(2,1)S(1)} %get-tuple-element.169.rest_0_), channel_id=1, source_target_pairs={{0,4},{4,0},{8,12},{12,8},{16,20},{20,16},{24,28},{28,24},{1,5},{5... | collective-permute-start | bytes 442376 | tf_op jit(solution)/shard_map/ppermute | solution.py:584
  15.2 9.3 %collective-permute-start.7 = (bf16[96,768]{1,0:T(8,128)(2,1)S(1)}, bf16[96,768]{1,0:T(8,128)(2,1)S(1)}, u32[]{:S(2)}, u32[]{:S(2)}) collective-permute-start(bf16[96,768]{1,0:T(8,128)(2,1)S(1)} %collective-permute-done.1.rest_4_), channel_id=1, source_target_pairs={{0,8},{4,12},{8,0},{12,4},{16,24},{20,28},{24,16},{28,20},{1,9},{5... | collective-permute-start | bytes 442376 | tf_op jit(solution)/shard_map/ppermute | solution.py:584
  18.6 6.8 %collective-permute-start.5 = (bf16[96,768]{1,0:T(8,128)(2,1)S(1)}, bf16[96,768]{1,0:T(8,128)(2,1)S(1)}, u32[]{:S(2)}, u32[]{:S(2)}) collective-permute-start(bf16[96,768]{1,0:T(8,128)(2,1)S(1)} %collective-permute-done.4.rest_2_), channel_id=1, source_target_pairs={{0,4},{4,0},{8,12},{12,8},{16,20},{20,16},{24,28},{28,24},{1,5},{5... | collective-permute-start | bytes 442376 | tf_op jit(solution)/shard_map/ppermute | solution.py:584
  22.0 7.1 %collective-permute-start.6 = (bf16[96,768]{1,0:T(8,128)(2,1)S(1)}, bf16[96,768]{1,0:T(8,128)(2,1)S(1)}, u32[]{:S(2)}, u32[]{:S(2)}) collective-permute-start(bf16[96,768]{1,0:T(8,128)(2,1)S(1)} %collective-permute-done.1.rest_4_), channel_id=1, source_target_pairs={{0,4},{4,0},{8,12},{12,8},{16,20},{20,16},{24,28},{28,24},{1,5},{5... | collective-permute-start | bytes 442376 | tf_op jit(solution)/shard_map/ppermute | solution.py:584
  24.5 6.2 %collective-permute-start.8 = (bf16[96,768]{1,0:T(8,128)(2,1)S(1)}, bf16[96,768]{1,0:T(8,128)(2,1)S(1)}, u32[]{:S(2)}, u32[]{:S(2)}) collective-permute-start(bf16[96,768]{1,0:T(8,128)(2,1)S(1)} %collective-permute-done.7.rest_6_), channel_id=1, source_target_pairs={{0,4},{4,0},{8,12},{12,8},{16,20},{20,16},{24,28},{28,24},{1,5},{5... | collective-permute-start | bytes 442376 | tf_op jit(solution)/shard_map/ppermute | solution.py:584
  25.4 9.3 %collective-permute-start.11 = (bf16[96,1536]{1,0:T(8,128)(2,1)S(1)}, bf16[96,1536]{1,0:T(8,128)(2,1)S(1)}, u32[]{:S(2)}, u32[]{:S(2)}) collective-permute-start(bf16[96,1536]{1,0:T(8,128)(2,1)S(1)} %get-tuple-element.173.rest_0_), channel_id=1, source_target_pairs={{0,8},{4,12},{8,0},{12,4},{16,24},{20,28},{24,16},{28,20},{1,9},{5... | collective-permute-start | bytes 884744 | tf_op jit(solution)/shard_map/ppermute | solution.py:584
  33.8 3.1 %collective-permute-start.9 = (bf16[256,768]{1,0:T(8,128)(2,1)S(1)}, bf16[256,768]{1,0:T(8,128)(2,1)S(1)}, u32[]{:S(2)}, u32[]{:S(2)}) collective-permute-start(bf16[256,768]{1,0:T(8,128)(2,1)S(1)} %get-tuple-element.171), channel_id=1, source_target_pairs={{0,1},{1,0},{2,3},{3,2},{4,5},{5,4},{6,7},{7,6},{8,9},{9,8},{10,11... | collective-permute-start | bytes 1179656 | tf_op jit(solution)/shard_map/ppermute | solution.py:587
  34.8 9.9 %collective-permute-start.12 = (bf16[96,1536]{1,0:T(8,128)(2,1)S(1)}, bf16[96,1536]{1,0:T(8,128)(2,1)S(1)}, u32[]{:S(2)}, u32[]{:S(2)}) collective-permute-start(bf16[96,1536]{1,0:T(8,128)(2,1)S(1)} %collective-permute-done.2.rest_4_), channel_id=1, source_target_pairs={{0,8},{4,12},{8,0},{12,4},{16,24},{20,28},{24,16},{28,20},{1,9},{5... | collective-permute-start | bytes 884744 | tf_op jit(solution)/shard_map/ppermute | solution.py:584
  35.3 10.4 %collective-permute-start.10 = (bf16[96,1536]{1,0:T(8,128)(2,1)S(1)}, bf16[96,1536]{1,0:T(8,128)(2,1)S(1)}, u32[]{:S(2)}, u32[]{:S(2)}) collective-permute-start(bf16[96,1536]{1,0:T(8,128)(2,1)S(1)} %collective-permute-done.2.rest_4_), channel_id=1, source_target_pairs={{0,4},{4,0},{8,12},{12,8},{16,20},{20,16},{24,28},{28,24},{1,5},{5... | collective-permute-start | bytes 884744 | tf_op jit(solution)/shard_map/ppermute | solution.py:584
  36.9 8.8 %collective-permute-start.13 = (bf16[128,768]{1,0:T(8,128)(2,1)S(1)}, bf16[128,768]{1,0:T(8,128)(2,1)S(1)}, u32[]{:S(2)}, u32[]{:S(2)}) collective-permute-start(bf16[128,768]{1,0:T(8,128)(2,1)S(1)} %get-tuple-element.175.one), channel_id=1, source_target_pairs={{0,2},{1,3},{2,0},{3,1},{4,6},{5,7},{6,4},{7,5},{8,10},{9,11},{10,... | collective-permute-start | bytes 589832 | tf_op jit(solution)/shard_map/ppermute | solution.py:587
  38.5 9.4 %collective-permute-start.14 = (bf16[128,768]{1,0:T(8,128)(2,1)S(1)}, bf16[128,768]{1,0:T(8,128)(2,1)S(1)}, u32[]{:S(2)}, u32[]{:S(2)}) collective-permute-start(bf16[128,768]{1,0:T(8,128)(2,1)S(1)} %get-tuple-element.177.one), channel_id=1, source_target_pairs={{0,2},{1,3},{2,0},{3,1},{4,6},{5,7},{6,4},{7,5},{8,10},{9,11},{10,... | collective-permute-start | bytes 589832 | tf_op jit(solution)/shard_map/ppermute | solution.py:587
  39.0 10.6 %collective-permute-start.17 = (bf16[96,1536]{1,0:T(8,128)(2,1)S(1)}, bf16[96,1536]{1,0:T(8,128)(2,1)S(1)}, u32[]{:S(2)}, u32[]{:S(2)}) collective-permute-start(bf16[96,1536]{1,0:T(8,128)(2,1)S(1)} %collective-permute-done.rest_1_), channel_id=1, source_target_pairs={{0,8},{4,12},{8,0},{12,4},{16,24},{20,28},{24,16},{28,20},{1,9},{5... | collective-permute-start | bytes 884744 | tf_op jit(solution)/shard_map/ppermute | solution.py:584
  44.7 6.7 %collective-permute-start.18 = (bf16[96,1536]{1,0:T(8,128)(2,1)S(1)}, bf16[96,1536]{1,0:T(8,128)(2,1)S(1)}, u32[]{:S(2)}, u32[]{:S(2)}) collective-permute-start(bf16[96,1536]{1,0:T(8,128)(2,1)S(1)} %collective-permute-done.12.rest_6_), channel_id=1, source_target_pairs={{0,4},{4,0},{8,12},{12,8},{16,20},{20,16},{24,28},{28,24},{1,5},{5... | collective-permute-start | bytes 884744 | tf_op jit(solution)/shard_map/ppermute | solution.py:584
  45.8 5.6 %collective-permute-start.15 = (bf16[128,768]{1,0:T(8,128)(2,1)S(1)}, bf16[128,768]{1,0:T(8,128)(2,1)S(1)}, u32[]{:S(2)}, u32[]{:S(2)}) collective-permute-start(bf16[128,768]{1,0:T(8,128)(2,1)S(1)} %add.4.own_a), channel_id=1, source_target_pairs={{0,1},{1,0},{2,3},{3,2},{4,5},{5,4},{6,7},{7,6},{8,9},{9,8},{10,11... | collective-permute-start | bytes 589832 | tf_op jit(solution)/shard_map/ppermute | solution.py:587
  47.9 3.5 %collective-permute-start.16 = (bf16[128,768]{1,0:T(8,128)(2,1)S(1)}, bf16[128,768]{1,0:T(8,128)(2,1)S(1)}, u32[]{:S(2)}, u32[]{:S(2)}) collective-permute-start(bf16[128,768]{1,0:T(8,128)(2,1)S(1)} %add.5.own_b), channel_id=1, source_target_pairs={{0,1},{1,0},{2,3},{3,2},{4,5},{5,4},{6,7},{7,6},{8,9},{9,8},{10,11... | collective-permute-start | bytes 589832 | tf_op jit(solution)/shard_map/ppermute | solution.py:587
  54.9 1.8 %collective-permute-start.19 = (bf16[256,768]{1,0:T(8,128)(2,1)S(1)}, bf16[256,768]{1,0:T(8,128)(2,1)S(1)}, u32[]{:S(2)}, u32[]{:S(2)}) collective-permute-start(bf16[256,768]{1,0:T(8,128)(2,1)S(1)} %get-tuple-element.184), channel_id=1, source_target_pairs={{0,1},{1,0},{2,3},{3,2},{4,5},{5,4},{6,7},{7,6},{8,9},{9,8},{10,11... | collective-permute-start | bytes 1179656 | tf_op jit(solution)/shard_map/ppermute | solution.py:587
  56.8 11.2 %collective-permute-start.23 = (bf16[256,768]{1,0:T(8,128)(2,1)S(1)}, bf16[256,768]{1,0:T(8,128)(2,1)S(1)}, u32[]{:S(2)}, u32[]{:S(2)}) collective-permute-start(bf16[256,768]{1,0:T(8,128)(2,1)S(1)} %add.6.one), channel_id=1, source_target_pairs={{0,2},{1,3},{2,0},{3,1},{4,6},{5,7},{6,4},{7,5},{8,10},{9,11},{10,... | collective-permute-start | bytes 1179656 | tf_op jit(solution)/shard_map/ppermute | solution.py:587
  58.3 9.0 %collective-permute-start.22 = (bf16[2,96,768]{2,1,0:T(8,128)(2,1)S(1)}, bf16[2,96,768]{2,1,0:T(8,128)(2,1)S(1)}, u32[]{:S(2)}, u32[]{:S(2)}) collective-permute-start(bf16[2,96,768]{2,1,0:T(8,128)(2,1)S(1)} %get-tuple-element.196), channel_id=1, source_target_pairs={{0,8},{4,12},{8,0},{12,4},{16,24},{20,28},{24,16},{28,20},{1,9},{5... | collective-permute-start | bytes 884744 | tf_op jit(solution)/shard_map/ppermute | solution.py:584
  62.9 2.1 %collective-permute-start.20 = (bf16[128,768]{1,0:T(8,128)(2,1)S(1)}, bf16[128,768]{1,0:T(8,128)(2,1)S(1)}, u32[]{:S(2)}, u32[]{:S(2)}) collective-permute-start(bf16[128,768]{1,0:T(8,128)(2,1)S(1)} %get-tuple-element.193), channel_id=1, source_target_pairs={{0,1},{1,0},{2,3},{3,2},{4,5},{5,4},{6,7},{7,6},{8,9},{9,8},{10,11... | collective-permute-start | bytes 589832 | tf_op jit(solution)/shard_map/ppermute | solution.py:587
  63.0 2.0 %collective-permute-start.21 = (bf16[128,768]{1,0:T(8,128)(2,1)S(1)}, bf16[128,768]{1,0:T(8,128)(2,1)S(1)}, u32[]{:S(2)}, u32[]{:S(2)}) collective-permute-start(bf16[128,768]{1,0:T(8,128)(2,1)S(1)} %get-tuple-element.194), channel_id=1, source_target_pairs={{0,1},{1,0},{2,3},{3,2},{4,5},{5,4},{6,7},{7,6},{8,9},{9,8},{10,11... | collective-permute-start | bytes 589832 | tf_op jit(solution)/shard_map/ppermute | solution.py:587
  63.5 15.9 %collective-permute-start.25 = (bf16[4,96,768]{2,1,0:T(8,128)(2,1)S(1)}, bf16[4,96,768]{2,1,0:T(8,128)(2,1)S(1)}, u32[]{:S(2)}, u32[]{:S(2)}) collective-permute-start(bf16[4,96,768]{2,1,0:T(8,128)(2,1)S(1)} %get-tuple-element.210), channel_id=1, source_target_pairs={{0,4},{4,0},{8,12},{12,8},{16,20},{20,16},{24,28},{28,24},{1,5},{5... | collective-permute-start | bytes 1769480 | tf_op jit(solution)/shard_map/ppermute | solution.py:584
  68.1 5.6 %collective-permute-start.24 = (bf16[256,768]{1,0:T(8,128)(2,1)S(1)}, bf16[256,768]{1,0:T(8,128)(2,1)S(1)}, u32[]{:S(2)}, u32[]{:S(2)}) collective-permute-start(bf16[256,768]{1,0:T(8,128)(2,1)S(1)} %add.7.own), channel_id=1, source_target_pairs={{0,1},{1,0},{2,3},{3,2},{4,5},{5,4},{6,7},{7,6},{8,9},{9,8},{10,11... | collective-permute-start | bytes 1179656 | tf_op jit(solution)/shard_map/ppermute | solution.py:587
  68.2 15.8 %collective-permute-start.26 = (bf16[2,96,768]{2,1,0:T(8,128)(2,1)S(1)}, bf16[2,96,768]{2,1,0:T(8,128)(2,1)S(1)}, u32[]{:S(2)}, u32[]{:S(2)}) collective-permute-start(bf16[2,96,768]{2,1,0:T(8,128)(2,1)S(1)} %get-tuple-element.216), channel_id=1, source_target_pairs={{0,8},{4,12},{8,0},{12,4},{16,24},{20,28},{24,16},{28,20},{1,9},{5... | collective-permute-start | bytes 884744 | tf_op jit(solution)/shard_map/ppermute | solution.py:584
  70.2 17.3 %collective-permute-start.27 = (bf16[2,96,768]{2,1,0:T(8,128)(2,1)S(1)}, bf16[2,96,768]{2,1,0:T(8,128)(2,1)S(1)}, u32[]{:S(2)}, u32[]{:S(2)}) collective-permute-start(bf16[2,96,768]{2,1,0:T(8,128)(2,1)S(1)} %high_add.1), channel_id=1, source_target_pairs={{0,16},{4,20},{8,24},{12,28},{16,0},{20,4},{24,8},{28,12},{1,17},{... | collective-permute-start | bytes 884744 | tf_op jit(solution)/shard_map/ppermute | solution.py:584
  79.6 10.2 %collective-permute-start.28 = (bf16[200,768]{1,0:T(8,128)(2,1)S(1)}, bf16[200,768]{1,0:T(8,128)(2,1)S(1)}, u32[]{:S(2)}, u32[]{:S(2)}) collective-permute-start(bf16[200,768]{1,0:T(8,128)(2,1)S(1)} %get-tuple-element.221.sent), channel_id=1, source_target_pairs={{0,4},{4,0},{8,12},{12,8},{16,20},{20,16},{24,28},{28,24},{1,5},{5... | collective-permute-start | bytes 921608 | tf_op jit(solution)/shard_map/ppermute | solution.py:584
  80.5 13.3 %collective-permute-start.30 = (bf16[2,96,768]{2,1,0:T(8,128)(2,1)S(1)}, bf16[2,96,768]{2,1,0:T(8,128)(2,1)S(1)}, u32[]{:S(2)}, u32[]{:S(2)}) collective-permute-start(bf16[2,96,768]{2,1,0:T(8,128)(2,1)S(1)} %get-tuple-element.212), channel_id=1, source_target_pairs={{0,8},{4,12},{8,0},{12,4},{16,24},{20,28},{24,16},{28,20},{1,9},{5... | collective-permute-start | bytes 884744 | tf_op jit(solution)/shard_map/ppermute | solution.py:584
  87.6 5.2 %collective-permute-start.29 = (bf16[96,768]{1,0:T(8,128)(2,1)S(1)}, bf16[96,768]{1,0:T(8,128)(2,1)S(1)}, u32[]{:S(2)}, u32[]{:S(2)}) collective-permute-start(bf16[96,768]{1,0:T(8,128)(2,1)S(1)} %get-tuple-element.218), channel_id=1, source_target_pairs={{0,4},{4,0},{8,12},{12,8},{16,20},{20,16},{24,28},{28,24},{1,5},{5... | collective-permute-start | bytes 442376 | tf_op jit(solution)/shard_map/ppermute | solution.py:584
  88.4 5.5 %collective-permute-start.31 = (bf16[128,768]{1,0:T(8,128)(2,1)S(1)}, bf16[128,768]{1,0:T(8,128)(2,1)S(1)}, u32[]{:S(2)}, u32[]{:S(2)}) collective-permute-start(bf16[128,768]{1,0:T(8,128)(2,1)S(1)} %get-tuple-element.229), channel_id=1, source_target_pairs={{0,1},{1,0},{2,3},{3,2},{4,5},{5,4},{6,7},{7,6},{8,9},{9,8},{10,11... | collective-permute-start | bytes 589832 | tf_op jit(solution)/shard_map/ppermute | solution.py:587
  88.4 5.5 %collective-permute-start.32 = (bf16[128,768]{1,0:T(8,128)(2,1)S(1)}, bf16[128,768]{1,0:T(8,128)(2,1)S(1)}, u32[]{:S(2)}, u32[]{:S(2)}) collective-permute-start(bf16[128,768]{1,0:T(8,128)(2,1)S(1)} %get-tuple-element.230), channel_id=1, source_target_pairs={{0,1},{1,0},{2,3},{3,2},{4,5},{5,4},{6,7},{7,6},{8,9},{9,8},{10,11... | collective-permute-start | bytes 589832 | tf_op jit(solution)/shard_map/ppermute | solution.py:587
  89.9 14.0 %collective-permute-start.35 = (bf16[200,768]{1,0:T(8,128)(2,1)S(1)}, bf16[200,768]{1,0:T(8,128)(2,1)S(1)}, u32[]{:S(2)}, u32[]{:S(2)}) collective-permute-start(bf16[200,768]{1,0:T(8,128)(2,1)S(1)} %last_high.1.sent), channel_id=1, source_target_pairs={{0,8},{4,12},{8,0},{12,4},{16,24},{20,28},{24,16},{28,20},{1,9},{5... | collective-permute-start | bytes 921608 | tf_op jit(solution)/shard_map/ppermute | solution.py:584
  92.8 11.1 %collective-permute-start.34 = (bf16[2,96,768]{2,1,0:T(8,128)(2,1)S(1)}, bf16[2,96,768]{2,1,0:T(8,128)(2,1)S(1)}, u32[]{:S(2)}, u32[]{:S(2)}) collective-permute-start(bf16[2,96,768]{2,1,0:T(8,128)(2,1)S(1)} %get-tuple-element.236), channel_id=1, source_target_pairs={{0,4},{4,0},{8,12},{12,8},{16,20},{20,16},{24,28},{28,24},{1,5},{5... | collective-permute-start | bytes 884744 | tf_op jit(solution)/shard_map/ppermute | solution.py:584
  94.1 10.1 %collective-permute-start.36 = (bf16[256,768]{1,0:T(8,128)(2,1)S(1)}, bf16[256,768]{1,0:T(8,128)(2,1)S(1)}, u32[]{:S(2)}, u32[]{:S(2)}) collective-permute-start(bf16[256,768]{1,0:T(8,128)(2,1)S(1)} %get-tuple-element.240), channel_id=1, source_target_pairs={{0,2},{1,3},{2,0},{3,1},{4,6},{5,7},{6,4},{7,5},{8,10},{9,11},{10,... | collective-permute-start | bytes 1179656 | tf_op jit(solution)/shard_map/ppermute | solution.py:587
  95.7 8.2 %collective-permute-start.33 = (bf16[96,768]{1,0:T(8,128)(2,1)S(1)}, bf16[96,768]{1,0:T(8,128)(2,1)S(1)}, u32[]{:S(2)}, u32[]{:S(2)}) collective-permute-start(bf16[96,768]{1,0:T(8,128)(2,1)S(1)} %get-tuple-element.226), channel_id=1, source_target_pairs={{0,16},{4,20},{8,24},{12,28},{16,0},{20,4},{24,8},{28,12},{1,17},{... | collective-permute-start | bytes 442376 | tf_op jit(solution)/shard_map/ppermute | solution.py:584
  104.1 7.4 %collective-permute-start.37 = (bf16[104,768]{1,0:T(8,128)(2,1)S(1)}, bf16[104,768]{1,0:T(8,128)(2,1)S(1)}, u32[]{:S(2)}, u32[]{:S(2)}) collective-permute-start(bf16[104,768]{1,0:T(8,128)(2,1)S(1)} %get-tuple-element.237.rest_1_), channel_id=1, source_target_pairs={{0,16},{4,20},{8,24},{12,28},{16,0},{20,4},{24,8},{28,12},{1,17},{... | collective-permute-start | bytes 479240 | tf_op jit(solution)/shard_map/ppermute | solution.py:584

commit v7 on v6

--- a/solution.py
+++ b/solution.py
@@ -260,8 +260,13 @@
     gain_part[...] = row_products(weights[...], grad[...]) / gains[1:2, :]
 
 
+def turn_kernel(prob, out):
+    for h in range(prob.shape[0]):
+        out[h] = prob[h].T
+
+
 def attend_back_kernel(
-    n_outs, resid, dy, gains, own, other, weights, qkv, prob, mixed, act_t, bucket, gain_two, *rest
+    n_outs, resid, dy, gains, own, other, weights, qkv, prob, prob_t, mixed, act_t, bucket, gain_two, *rest
 ):
     outs = rest[:n_outs]
     share_grad, small, proj_grad, resid_low, grad, diag = rest[n_outs:]
@@ -302,7 +307,7 @@
             turned = pltpu.roll(wide, 0, 1, stride=1, stride_axis=0)
             low_at = LEN - BLK - r * BLK
             diag[h : h + 1, low_at : low_at + WIN] += jnp.sum(turned, axis=0, keepdims=True)
-        for s, part in enumerate((dot_nn(low, key), dot_tn(low, query), dot_tn(prob[h], grad_rows))):
+        for s, part in enumerate((dot_nn(low, key), dot_tn(low, query), dot_nn(prob_t[h], grad_rows))):
             proj_grad[:, s * width + h * HDIM : s * width + (h + 1) * HDIM] = part.astype(bf16)
     grad[:, : 3 * width] = dot_nn(act_t[...], proj_grad[...])
     grad[:, 3 * width :] = dot_tn(resid_low[...], mixed[...])
@@ -646,18 +651,18 @@
         three = swap_dp(two, 2)
         ffn_two = swap_dp(after(packed_ffn, two), 4)
         two_across = swap_dp(two, 1)
-        ffn_one = swap_dp(after(packed_ffn, three, own, one_across), 2)
+        ffn_one = swap_dp(after(packed_ffn, three, own), 2)
         three_across = swap_dp(three, 1)
         qkvo_blocks = [packed, own, one, one_across, two, two_across, three, three_across]
         ffn_three = swap_dp(after(ffn_two, ffn_one), 2)
         ffn_blocks = [packed_ffn, ffn_own, ffn_one, swap_dp(after(ffn_own, ffn_one), 2)]
         for block in (ffn_two, ffn_three):
             ffn_blocks += [block, swap_dp(block, 1)]
-        bias = after(bias, ffn_own, ffn_two)
-        ffn_early = (ffn_blocks[5], ffn_three)
+        bias = after(bias, ffn_own, one_across)
+        ffn_first, ffn_early = (ffn_two,), (ffn_blocks[5], ffn_three)
     else:
         qkvo_blocks = [lax.all_gather(packed, "dp", axis=0, tiled=True)]
-        ffn_blocks = ffn_early = [lax.all_gather(packed_ffn, "dp", axis=0, tiled=True)]
+        ffn_first = ffn_blocks = ffn_early = [lax.all_gather(packed_ffn, "dp", axis=0, tiled=True)]
     n_blocks = len(qkvo_blocks)
 
     weights_one, qkv, prob, mixed, attn_keep, attn_send = call(
@@ -674,7 +679,7 @@
     )
     half_blocks = [sds((BLK, model), bf16)] * 2
     attn_first = call(
-        split_add_kernel, half_blocks, (attn_keep, swap_tp(attn_send, 1)), "split_add", limit=4
+        split_add_kernel, half_blocks, (attn_keep, swap_tp(after(attn_send, *ffn_first), 1)), "split_add", limit=4
     )
     attn_own = [add(first, swap_tp(first, 2), ffn_early) for first in attn_first]
     attn_sums = (*attn_own, *(swap_tp(own, 1) for own in attn_own))
@@ -722,7 +727,8 @@
         down_keep, down_high, down_low = down_parts
         down_got = swap_dp(down_high, down_order[0])
         back_behind = (*back_behind, down_got)
-    back_sum = add(back_first, back_got, back_behind)
+    (prob_t,) = call(turn_kernel, [sds(prob.shape, bf16)], (prob,), "turn", behind=ffn_sums[:1])
+    back_sum = add(back_first, back_got, (*back_behind, prob_t))
     if direct:
         down_one = high_add(down_keep, down_got, (back_sum,))
         attend_behind = (down_one,)
@@ -741,6 +747,7 @@
             weights_one,
             qkv,
             prob,
+            prob_t,
             mixed,
             act_one_t,
             bucket_row,

time: 126 us -> 124 us (0.984)
  starting transfers between devices: 40.1 us -> 38.3 us
    ppermute x25, starting transfers between devices: 33.6 us -> 31.4 us  [swap_dp(): return lax.ppermute(value, 'dp', [(i, i ^ distance) for i in range(dp)])]
    ppermute x13, waiting for transfers between devices: 3.56 us -> 1.98 us  [swap_tp(): return lax.ppermute(value, 'tp', [(i, i ^ distance) for i in range(tp)])]
    pallas_call x28 -> x29, Pallas kernels: 28.4 us -> 29 us  [call(): pl.pallas_call(body, out_shape=tuple(outs), in_specs=[pl.BlockSpec(memory...]
  transfers between devices with their start and end apart: 38 -> 38, of which waited for: 20 -> 18; matrix products, arithmetic and copies ran while one was open for 0% -> 0% of each run, Pallas kernels for 16% -> 17%
where the time goes in v7:
time: 124 us
  waiting for transfers between devices  44.6 us (36%)
  starting transfers between devices  38.3 us (31%)
  Pallas kernels  29 us (23%)
  blocking collectives  11.2 us (9%)
    ppermute x25, waiting for transfers between devices, swap_dp(): return lax.ppermute(value, 'dp', [(i, i ^ distance) for i in range(dp)])  42.6 us
    ppermute x25, starting transfers between devices, swap_dp(): return lax.ppermute(value, 'dp', [(i, i ^ distance) for i in range(dp)])  31.4 us
    pallas_call x29, Pallas kernels, call(): pl.pallas_call(body, out_shape=tuple(outs), in_specs=[pl.BlockSpec(memory...  29 us
    all_to_all x1, blocking collectives, on_device(): told = lax.all_to_all(payload, ('dp', 'tp'), 0, 0)  11.2 us
    ppermute x13, starting transfers between devices, swap_tp(): return lax.ppermute(value, 'tp', [(i, i ^ distance) for i in range(tp)])  6.86 us
  transfers between devices with their start and end apart: 38, of which 18 were waited for; matrix products, arithmetic and copies ran while one was open for 0% of the time, Pallas kernels for 17%

profile of v7, /device:TPU:0, one launch (start us, length us, event | category | flops | bytes accessed | tf_op | source)
XLA Modules:
  0.0 124.2 jit_solution(5209016033842891290)
XLA Ops:
  0.7 1.2 pack.1
  1.9 4.1 %collective-permute-start.4 = (bf16[96,768]{1,0:T(8,128)(2,1)S(1)}, bf16[96,768]{1,0:T(8,128)(2,1)S(1)}, u32[]{:S(2)}, u32[]{:S(2)}) collective-permute-start(bf16[96,768]{1,0:T(8,128)(2,1)S(1)} %get-tuple-element.170.rest_0_), channel_id=1, source_target_pairs={{0,16},{4,20},{8,24},{12,28},{16,0},{20,4},{24,8},{28,12},{1,17},{... | collective-permute-start | bytes 442376 | tf_op jit(solution)/shard_map/ppermute | solution.py:589
  6.0 1.6 %collective-permute-start.1 = (bf16[96,768]{1,0:T(8,128)(2,1)S(1)}, bf16[96,768]{1,0:T(8,128)(2,1)S(1)}, u32[]{:S(2)}, u32[]{:S(2)}) collective-permute-start(bf16[96,768]{1,0:T(8,128)(2,1)S(1)} %get-tuple-element.170.rest_0_), channel_id=1, source_target_pairs={{0,8},{4,12},{8,0},{12,4},{16,24},{20,28},{24,16},{28,20},{1,9},{5... | collective-permute-start | bytes 442376 | tf_op jit(solution)/shard_map/ppermute | solution.py:589
  7.6 2.2 %prep.1 = (bf16[512,768]{1,0:T(8,128)(2,1)S(1)}, bf16[768,512]{1,0:T(8,128)(2,1)S(1)}, f32[3,512,512]{2,1,0:T(8,128)S(1)}, s32[1,1024]{1,0:T(1,128)S(1)}, bf16[5...) custom-call(s32[1,4]{1,0:T(1,128)} %seg_in.1, f32[3,32]{1,0:T(4,128)} %bitcast.8, ...), custom_call_target="tpu_custom_call" | custom-call | tf_op jit(solution)/shard_map/prep/pallas_call | solution.py:61
  9.8 1.6 %collective-permute-start = (bf16[96,1536]{1,0:T(8,128)(2,1)S(1)}, bf16[96,1536]{1,0:T(8,128)(2,1)S(1)}, u32[]{:S(2)}, u32[]{:S(2)}) collective-permute-start(bf16[96,1536]{1,0:T(8,128)(2,1)S(1)} %get-tuple-element.176.rest_0_), channel_id=1, source_target_pairs={{0,4},{4,0},{8,12},{12,8},{16,20},{20,16},{24,28},{28,24},{1,5},{5... | collective-permute-start | bytes 884744 | tf_op jit(solution)/shard_map/ppermute | solution.py:589
  11.9 1.2 %collective-permute-done.4.rest_4_ = bf16[96,768]{1,0:T(8,128)(2,1)S(1)} collective-permute-done((bf16[96,768]{1,0:T(8,128)(2,1)S(1)}, bf16[96,768]{1,0:T(8,128)(2,1)S(1)}, u32[]{:S(2)}, u32[]{:S(2)}) %collective-permute-start.4) | collective-permute-done | bytes 147488 | tf_op jit(solution)/shard_map/ppermute | solution.py:589
  13.7 3.4 %collective-permute-start.8 = (bf16[96,1536]{1,0:T(8,128)(2,1)S(1)}, bf16[96,1536]{1,0:T(8,128)(2,1)S(1)}, u32[]{:S(2)}, u32[]{:S(2)}) collective-permute-start(bf16[96,1536]{1,0:T(8,128)(2,1)S(1)} %get-tuple-element.176.rest_0_), channel_id=1, source_target_pairs={{0,16},{4,20},{8,24},{12,28},{16,0},{20,4},{24,8},{28,12},{1,17},{... | collective-permute-start | bytes 884744 | tf_op jit(solution)/shard_map/ppermute | solution.py:589
  17.1 1.5 %collective-permute-start.2 = (bf16[96,768]{1,0:T(8,128)(2,1)S(1)}, bf16[96,768]{1,0:T(8,128)(2,1)S(1)}, u32[]{:S(2)}, u32[]{:S(2)}) collective-permute-start(bf16[96,768]{1,0:T(8,128)(2,1)S(1)} %collective-permute-done.1.rest_2_), channel_id=1, source_target_pairs={{0,4},{4,0},{8,12},{12,8},{16,20},{20,16},{24,28},{28,24},{1,5},{5... | collective-permute-start | bytes 442376 | tf_op jit(solution)/shard_map/ppermute | solution.py:589
  18.6 4.3 %collective-permute-done.3.rest_1_ = bf16[96,768]{1,0:T(8,128)(2,1)S(1)} collective-permute-done((bf16[96,768]{1,0:T(8,128)(2,1)S(1)}, bf16[96,768]{1,0:T(8,128)(2,1)S(1)}, u32[]{:S(2)}, u32[]{:S(2)}) %collective-permute-start.3) | collective-permute-done | bytes 147488 | tf_op jit(solution)/shard_map/ppermute | solution.py:589
  23.0 1.5 %collective-permute-start.5 = (bf16[96,768]{1,0:T(8,128)(2,1)S(1)}, bf16[96,768]{1,0:T(8,128)(2,1)S(1)}, u32[]{:S(2)}, u32[]{:S(2)}) collective-permute-start(bf16[96,768]{1,0:T(8,128)(2,1)S(1)} %collective-permute-done.4.rest_4_), channel_id=1, source_target_pairs={{0,4},{4,0},{8,12},{12,8},{16,20},{20,16},{24,28},{28,24},{1,5},{5... | collective-permute-start | bytes 442376 | tf_op jit(solution)/shard_map/ppermute | solution.py:589
  25.0 1.1 collective-permute-done.2.rest_3_
  26.6 2.5 %collective-permute-done.5.rest_5_ = bf16[96,768]{1,0:T(8,128)(2,1)S(1)} collective-permute-done((bf16[96,768]{1,0:T(8,128)(2,1)S(1)}, bf16[96,768]{1,0:T(8,128)(2,1)S(1)}, u32[]{:S(2)}, u32[]{:S(2)}) %collective-permute-start.5) | collective-permute-done | bytes 147488 | tf_op jit(solution)/shard_map/ppermute | solution.py:589
  29.1 1.6 %collective-permute-done.7.rest_7_ = bf16[96,768]{1,0:T(8,128)(2,1)S(1)} collective-permute-done((bf16[96,768]{1,0:T(8,128)(2,1)S(1)}, bf16[96,768]{1,0:T(8,128)(2,1)S(1)}, u32[]{:S(2)}, u32[]{:S(2)}) %collective-permute-start.7) | collective-permute-done | bytes 147488 | tf_op jit(solution)/shard_map/ppermute | solution.py:589
  30.7 3.1 %attend.1 = (bf16[768,768]{1,0:T(8,128)(2,1)S(1)}, bf16[512,576]{1,0:T(8,128)(2,1)S(1)}, bf16[3,512,512]{2,1,0:T(8,128)(2,1)S(1)}, bf16[512,192]{1,0:T(8,128)(2,...) custom-call(bf16[512,768]{1,0:T(8,128)(2,1)S(1)} %get-tuple-element.164.act, ...), custom_call_target="tpu_custom_call" | custom-call | tf_op jit(solution)/shard_map/attend/pallas_call | solution.py:61
  33.9 1.2 collective-permute-done.11.rest_2_
  35.0 1.5 %collective-permute-start.10 = (bf16[96,1536]{1,0:T(8,128)(2,1)S(1)}, bf16[96,1536]{1,0:T(8,128)(2,1)S(1)}, u32[]{:S(2)}, u32[]{:S(2)}) collective-permute-start(bf16[96,1536]{1,0:T(8,128)(2,1)S(1)} %collective-permute-done.8.rest_4_), channel_id=1, source_target_pairs={{0,4},{4,0},{8,12},{12,8},{16,20},{20,16},{24,28},{28,24},{1,5},{5... | collective-permute-start | bytes 884744 | tf_op jit(solution)/shard_map/ppermute | solution.py:589
  36.6 1.6 %collective-permute-start.13 = (bf16[128,768]{1,0:T(8,128)(2,1)S(1)}, bf16[128,768]{1,0:T(8,128)(2,1)S(1)}, u32[]{:S(2)}, u32[]{:S(2)}) collective-permute-start(bf16[128,768]{1,0:T(8,128)(2,1)S(1)} %get-tuple-element.178.one), channel_id=1, source_target_pairs={{0,2},{1,3},{2,0},{3,1},{4,6},{5,7},{6,4},{7,5},{8,10},{9,11},{10,... | collective-permute-start | bytes 589832 | tf_op jit(solution)/shard_map/ppermute | solution.py:592
  38.7 2.0 %collective-permute-start.17 = (bf16[96,1536]{1,0:T(8,128)(2,1)S(1)}, bf16[96,1536]{1,0:T(8,128)(2,1)S(1)}, u32[]{:S(2)}, u32[]{:S(2)}) collective-permute-start(bf16[96,1536]{1,0:T(8,128)(2,1)S(1)} %collective-permute-done.rest_1_), channel_id=1, source_target_pairs={{0,8},{4,12},{8,0},{12,4},{16,24},{20,28},{24,16},{28,20},{1,9},{5... | collective-permute-start | bytes 884744 | tf_op jit(solution)/shard_map/ppermute | solution.py:589
  40.7 4.2 %collective-permute-done.12.rest_6_ = bf16[96,1536]{1,0:T(8,128)(2,1)S(1)} collective-permute-done((bf16[96,1536]{1,0:T(8,128)(2,1)S(1)}, bf16[96,1536]{1,0:T(8,128)(2,1)S(1)}, u32[]{:S(2)}, u32[]{:S(2)}) %collective-permute-start.12) | collective-permute-done | bytes 294944 | tf_op jit(solution)/shard_map/ppermute | solution.py:589
  45.0 1.5 %collective-permute-start.18 = (bf16[96,1536]{1,0:T(8,128)(2,1)S(1)}, bf16[96,1536]{1,0:T(8,128)(2,1)S(1)}, u32[]{:S(2)}, u32[]{:S(2)}) collective-permute-start(bf16[96,1536]{1,0:T(8,128)(2,1)S(1)} %collective-permute-done.12.rest_6_), channel_id=1, source_target_pairs={{0,4},{4,0},{8,12},{12,8},{16,20},{20,16},{24,28},{28,24},{1,5},{5... | collective-permute-start | bytes 884744 | tf_op jit(solution)/shard_map/ppermute | solution.py:589
  47.2 2.4 %collective-permute-done.17.rest_3_ = bf16[96,1536]{1,0:T(8,128)(2,1)S(1)} collective-permute-done((bf16[96,1536]{1,0:T(8,128)(2,1)S(1)}, bf16[96,1536]{1,0:T(8,128)(2,1)S(1)}, u32[]{:S(2)}, u32[]{:S(2)}) %collective-permute-start.17) | collective-permute-done | bytes 294944 | tf_op jit(solution)/shard_map/ppermute | solution.py:589
  49.6 2.1 %collective-permute-done.18.rest_7_ = bf16[96,1536]{1,0:T(8,128)(2,1)S(1)} collective-permute-done((bf16[96,1536]{1,0:T(8,128)(2,1)S(1)}, bf16[96,1536]{1,0:T(8,128)(2,1)S(1)}, u32[]{:S(2)}, u32[]{:S(2)}) %collective-permute-start.18) | collective-permute-done | bytes 294944 | tf_op jit(solution)/shard_map/ppermute | solution.py:589
  51.7 3.5 %ffn.1 = (f32[512,768]{1,0:T(8,128)S(1)}, bf16[512,768]{1,0:T(8,128)(2,1)S(1)}, bf16[512,768]{1,0:T(8,128)(2,1)S(1)}, bf16[512,768]{1,0:T(8,128)(2,1)S(1)}, bf16...) custom-call(bf16[512,768]{1,0:T(8,128)(2,1)S(1)} %get-tuple-element., ...), custom_call_target="tpu_custom_call" | custom-call | tf_op jit(solution)/shard_map/ffn/pallas_call | solution.py:61
  55.3 0.9 down_grad.1
  56.2 0.8 collective-permute-done.19.two
  57.1 1.6 %collective-permute-start.23 = (bf16[256,768]{1,0:T(8,128)(2,1)S(1)}, bf16[256,768]{1,0:T(8,128)(2,1)S(1)}, u32[]{:S(2)}, u32[]{:S(2)}) collective-permute-start(bf16[256,768]{1,0:T(8,128)(2,1)S(1)} %add.6.one), channel_id=1, source_target_pairs={{0,2},{1,3},{2,0},{3,1},{4,6},{5,7},{6,4},{7,5},{8,10},{9,11},{10,... | collective-permute-start | bytes 1179656 | tf_op jit(solution)/shard_map/ppermute | solution.py:592
  58.7 1.0 in_grad.1
  59.7 1.6 %ffn_out.1 = (bf16[256,768]{1,0:T(8,128)(2,1)S(1)}, bf16[128,768]{1,0:T(8,128)(2,1)S(1)}, bf16[128,768]{1,0:T(8,128)(2,1)S(1)}) custom-call(bf16[512,768]{1,0:T(8,128)(2,1)S(1)} %get-tuple-element.193.right.hidden, bf16[768,768]{1,0:T(8,128)(2,1)S(1)} %get-tuple-element.194.down), custom_call_target="tpu_custom_call" | custom-call | tf_op jit(solution)/shard_map/ffn_out/pallas_call | solution.py:61
  62.0 1.5 %collective-permute-start.25 = (bf16[4,96,768]{2,1,0:T(8,128)(2,1)S(1)}, bf16[4,96,768]{2,1,0:T(8,128)(2,1)S(1)}, u32[]{:S(2)}, u32[]{:S(2)}) collective-permute-start(bf16[4,96,768]{2,1,0:T(8,128)(2,1)S(1)} %get-tuple-element.214), channel_id=1, source_target_pairs={{0,4},{4,0},{8,12},{12,8},{16,20},{20,16},{24,28},{28,24},{1,5},{5... | collective-permute-start | bytes 1769480 | tf_op jit(solution)/shard_map/ppermute | solution.py:589
  64.3 3.2 %collective-permute-done.22.got = bf16[2,96,768]{2,1,0:T(8,128)(2,1)S(1)} collective-permute-done((bf16[2,96,768]{2,1,0:T(8,128)(2,1)S(1)}, bf16[2,96,768]{2,1,0:T(8,128)(2,1)S(1)}, u32[]{:S(2)}, u32[]{:S(2)}) %collective-permute-start.22) | collective-permute-done | bytes 294944 | tf_op jit(solution)/shard_map/ppermute | solution.py:589
  67.4 0.9 collective-permute-done.23.two
  68.6 3.6 %collective-permute-start.27 = (bf16[2,96,768]{2,1,0:T(8,128)(2,1)S(1)}, bf16[2,96,768]{2,1,0:T(8,128)(2,1)S(1)}, u32[]{:S(2)}, u32[]{:S(2)}) collective-permute-start(bf16[2,96,768]{2,1,0:T(8,128)(2,1)S(1)} %high_add.1), channel_id=1, source_target_pairs={{0,16},{4,20},{8,24},{12,28},{16,0},{20,4},{24,8},{28,12},{1,17},{... | collective-permute-start | bytes 884744 | tf_op jit(solution)/shard_map/ppermute | solution.py:589
  72.2 5.8 %attend_back.1 = (bf16[4,96,768]{2,1,0:T(8,128)(2,1)S(1)}, bf16[2,96,768]{2,1,0:T(8,128)(2,1)S(1)}, f32[128,768]{1,0:T(8,128)S(1)}, bf16[200,768]{1,0:T(8,128)(2,1)S(1)}, bf16[512,576]{1,0:T(8,128)(2,1)S(1)}) custom-call(f32[512,768]{1,0:T(8,128)S(1)} %get-tuple-element.242.resid, bf16[512,768]{1,0:T(8,128)(2,1)S(1)} %get-tuple-element.163.dy.left, ...), custom_call_target="tpu_custom_call" | custom-call | tf_op jit(solution)/shard_map/attend_back/pallas_call | solution.py:61
  78.2 0.8 collective-permute-start.28
  79.0 2.0 %collective-permute-start.30 = (bf16[2,96,768]{2,1,0:T(8,128)(2,1)S(1)}, bf16[2,96,768]{2,1,0:T(8,128)(2,1)S(1)}, u32[]{:S(2)}, u32[]{:S(2)}) collective-permute-start(bf16[2,96,768]{2,1,0:T(8,128)(2,1)S(1)} %get-tuple-element.216), channel_id=1, source_target_pairs={{0,8},{4,12},{8,0},{12,4},{16,24},{20,28},{24,16},{28,20},{1,9},{5... | collective-permute-start | bytes 884744 | tf_op jit(solution)/shard_map/ppermute | solution.py:589
  81.0 1.4 %act_grad.1 = (bf16[256,768]{1,0:T(8,128)(2,1)S(1)}, bf16[128,768]{1,0:T(8,128)(2,1)S(1)}, bf16[128,768]{1,0:T(8,128)(2,1)S(1)}) custom-call(bf16[512,576]{1,0:T(8,128)(2,1)S(1)} %get-tuple-element.217.proj_grad, bf16[768,768]{1,0:T(8,128)(2,1)S(1)} %get-tuple-element.205.weights), custom_call_target="tpu_custom_call" | custom-call | tf_op jit(solution)/shard_map/act_grad/pallas_call | solution.py:61
  82.4 1.9 %collective-permute-done.26.got_low = bf16[2,96,768]{2,1,0:T(8,128)(2,1)S(1)} collective-permute-done((bf16[2,96,768]{2,1,0:T(8,128)(2,1)S(1)}, bf16[2,96,768]{2,1,0:T(8,128)(2,1)S(1)}, u32[]{:S(2)}, u32[]{:S(2)}) %collective-permute-start.26) | collective-permute-done | bytes 294944 | tf_op jit(solution)/shard_map/ppermute | solution.py:589
  84.3 1.7 %collective-permute-done.27.got = bf16[2,96,768]{2,1,0:T(8,128)(2,1)S(1)} collective-permute-done((bf16[2,96,768]{2,1,0:T(8,128)(2,1)S(1)}, bf16[2,96,768]{2,1,0:T(8,128)(2,1)S(1)}, u32[]{:S(2)}, u32[]{:S(2)}) %collective-permute-start.27) | collective-permute-done | bytes 294944 | tf_op jit(solution)/shard_map/ppermute | solution.py:589
  86.1 1.0 collective-permute-start.29
  88.0 3.3 %collective-permute-done.29.rest_1_ = bf16[96,768]{1,0:T(8,128)(2,1)S(1)} collective-permute-done((bf16[96,768]{1,0:T(8,128)(2,1)S(1)}, bf16[96,768]{1,0:T(8,128)(2,1)S(1)}, u32[]{:S(2)}, u32[]{:S(2)}) %collective-permute-start.29) | collective-permute-done | bytes 147488 | tf_op jit(solution)/shard_map/ppermute | solution.py:589
  91.3 1.0 collective-permute-start.34
  92.8 1.6 %collective-permute-start.36 = (bf16[256,768]{1,0:T(8,128)(2,1)S(1)}, bf16[256,768]{1,0:T(8,128)(2,1)S(1)}, u32[]{:S(2)}, u32[]{:S(2)}) collective-permute-start(bf16[256,768]{1,0:T(8,128)(2,1)S(1)} %get-tuple-element.244), channel_id=1, source_target_pairs={{0,2},{1,3},{2,0},{3,1},{4,6},{5,7},{6,4},{7,5},{8,10},{9,11},{10,... | collective-permute-start | bytes 1179656 | tf_op jit(solution)/shard_map/ppermute | solution.py:592
  94.7 7.6 %collective-permute-done.33.rest_1_ = bf16[96,768]{1,0:T(8,128)(2,1)S(1)} collective-permute-done((bf16[96,768]{1,0:T(8,128)(2,1)S(1)}, bf16[96,768]{1,0:T(8,128)(2,1)S(1)}, u32[]{:S(2)}, u32[]{:S(2)}) %collective-permute-start.33) | collective-permute-done | bytes 147488 | tf_op jit(solution)/shard_map/ppermute | solution.py:589
  102.6 1.1 share_out.1
  103.7 1.9 %fetch.1 = (f32[3,96,192]{2,1,0:T(8,128)S(1)}, f32[3,96,192]{2,1,0:T(8,128)S(1)}, f32[3,96,192]{2,1,0:T(8,128)S(1)}, f32[96,192]{1,0:T(8,128)S(1)}, f32[96,192]{...) custom-call(f32[3,96,192]{2,1,0:T(8,128)} %refs_0_, ...), custom_call_target="tpu_custom_call" | custom-call | tf_op jit(solution)/shard_map/fetch/pallas_call | solution.py:61
  105.6 4.2 %collective-permute-done.37.rest_2_ = bf16[104,768]{1,0:T(8,128)(2,1)S(1)} collective-permute-done((bf16[104,768]{1,0:T(8,128)(2,1)S(1)}, bf16[104,768]{1,0:T(8,128)(2,1)S(1)}, u32[]{:S(2)}, u32[]{:S(2)}) %collective-permute-start.37) | collective-permute-done | bytes 159776 | tf_op jit(solution)/shard_map/ppermute | solution.py:589
  110.5 11.2 %all_to_all.5.refs_0_ = f32[32,1,384]{2,1,0:T(1,128)S(1)} all-to-all(f32[32,1,384]{2,1,0:T(1,128)} %get-tuple-element.253), channel_id=1, replica_groups=mesh['dp'=8,'tp'=4] {'dp','tp'}, dimensions={0} | all-to-all | bytes 98304 | tf_op jit(solution)/shard_map/all_to_all | solution.py:865
  121.7 2.4 %adam.1 = (f32[1,1]{1,0:T(1,128)}, f32[3,96,192]{2,1,0:T(8,128)}, f32[3,96,192]{2,1,0:T(8,128)}, f32[3,96,192]{2,1,0:T(8,128)}, bf16[3,96,192]{2,1,0:T(8,128)(2,...) custom-call(f32[32,1,384]{2,1,0:T(1,128)S(1)} %all_to_all.5.refs_0_,, ...), custom_call_target="tpu_custom_call" | custom-call | tf_op jit(solution)/shard_map/adam/pallas_call | solution.py:61
  (58 shorter events, 8.2 us)
Async XLA Ops:
  1.9 11.2 %collective-permute-start.4 = (bf16[96,768]{1,0:T(8,128)(2,1)S(1)}, bf16[96,768]{1,0:T(8,128)(2,1)S(1)}, u32[]{:S(2)}, u32[]{:S(2)}) collective-permute-start(bf16[96,768]{1,0:T(8,128)(2,1)S(1)} %get-tuple-element.170.rest_0_), channel_id=1, source_target_pairs={{0,16},{4,20},{8,24},{12,28},{16,0},{20,4},{24,8},{28,12},{1,17},{... | collective-permute-start | bytes 442376 | tf_op jit(solution)/shard_map/ppermute | solution.py:589
  6.0 11.1 %collective-permute-start.1 = (bf16[96,768]{1,0:T(8,128)(2,1)S(1)}, bf16[96,768]{1,0:T(8,128)(2,1)S(1)}, u32[]{:S(2)}, u32[]{:S(2)}) collective-permute-start(bf16[96,768]{1,0:T(8,128)(2,1)S(1)} %get-tuple-element.170.rest_0_), channel_id=1, source_target_pairs={{0,8},{4,12},{8,0},{12,4},{16,24},{20,28},{24,16},{28,20},{1,9},{5... | collective-permute-start | bytes 442376 | tf_op jit(solution)/shard_map/ppermute | solution.py:589
  9.8 16.8 %collective-permute-start = (bf16[96,1536]{1,0:T(8,128)(2,1)S(1)}, bf16[96,1536]{1,0:T(8,128)(2,1)S(1)}, u32[]{:S(2)}, u32[]{:S(2)}) collective-permute-start(bf16[96,1536]{1,0:T(8,128)(2,1)S(1)} %get-tuple-element.176.rest_0_), channel_id=1, source_target_pairs={{0,4},{4,0},{8,12},{12,8},{16,20},{20,16},{24,28},{28,24},{1,5},{5... | collective-permute-start | bytes 884744 | tf_op jit(solution)/shard_map/ppermute | solution.py:589
  11.4 11.6 %collective-permute-start.3 = (bf16[96,768]{1,0:T(8,128)(2,1)S(1)}, bf16[96,768]{1,0:T(8,128)(2,1)S(1)}, u32[]{:S(2)}, u32[]{:S(2)}) collective-permute-start(bf16[96,768]{1,0:T(8,128)(2,1)S(1)} %get-tuple-element.170.rest_0_), channel_id=1, source_target_pairs={{0,4},{4,0},{8,12},{12,8},{16,20},{20,16},{24,28},{28,24},{1,5},{5... | collective-permute-start | bytes 442376 | tf_op jit(solution)/shard_map/ppermute | solution.py:589
  13.1 11.3 %collective-permute-start.6 = (bf16[96,768]{1,0:T(8,128)(2,1)S(1)}, bf16[96,768]{1,0:T(8,128)(2,1)S(1)}, u32[]{:S(2)}, u32[]{:S(2)}) collective-permute-start(bf16[96,768]{1,0:T(8,128)(2,1)S(1)} %collective-permute-done.4.rest_4_), channel_id=1, source_target_pairs={{0,8},{4,12},{8,0},{12,4},{16,24},{20,28},{24,16},{28,20},{1,9},{5... | collective-permute-start | bytes 442376 | tf_op jit(solution)/shard_map/ppermute | solution.py:589
  13.7 20.0 %collective-permute-start.8 = (bf16[96,1536]{1,0:T(8,128)(2,1)S(1)}, bf16[96,1536]{1,0:T(8,128)(2,1)S(1)}, u32[]{:S(2)}, u32[]{:S(2)}) collective-permute-start(bf16[96,1536]{1,0:T(8,128)(2,1)S(1)} %get-tuple-element.176.rest_0_), channel_id=1, source_target_pairs={{0,16},{4,20},{8,24},{12,28},{16,0},{20,4},{24,8},{28,12},{1,17},{... | collective-permute-start | bytes 884744 | tf_op jit(solution)/shard_map/ppermute | solution.py:589
  17.1 9.0 %collective-permute-start.2 = (bf16[96,768]{1,0:T(8,128)(2,1)S(1)}, bf16[96,768]{1,0:T(8,128)(2,1)S(1)}, u32[]{:S(2)}, u32[]{:S(2)}) collective-permute-start(bf16[96,768]{1,0:T(8,128)(2,1)S(1)} %collective-permute-done.1.rest_2_), channel_id=1, source_target_pairs={{0,4},{4,0},{8,12},{12,8},{16,20},{20,16},{24,28},{28,24},{1,5},{5... | collective-permute-start | bytes 442376 | tf_op jit(solution)/shard_map/ppermute | solution.py:589
  23.0 6.1 %collective-permute-start.5 = (bf16[96,768]{1,0:T(8,128)(2,1)S(1)}, bf16[96,768]{1,0:T(8,128)(2,1)S(1)}, u32[]{:S(2)}, u32[]{:S(2)}) collective-permute-start(bf16[96,768]{1,0:T(8,128)(2,1)S(1)} %collective-permute-done.4.rest_4_), channel_id=1, source_target_pairs={{0,4},{4,0},{8,12},{12,8},{16,20},{20,16},{24,28},{28,24},{1,5},{5... | collective-permute-start | bytes 442376 | tf_op jit(solution)/shard_map/ppermute | solution.py:589
  24.5 6.2 %collective-permute-start.7 = (bf16[96,768]{1,0:T(8,128)(2,1)S(1)}, bf16[96,768]{1,0:T(8,128)(2,1)S(1)}, u32[]{:S(2)}, u32[]{:S(2)}) collective-permute-start(bf16[96,768]{1,0:T(8,128)(2,1)S(1)} %collective-permute-done.6.rest_6_), channel_id=1, source_target_pairs={{0,4},{4,0},{8,12},{12,8},{16,20},{20,16},{24,28},{28,24},{1,5},{5... | collective-permute-start | bytes 442376 | tf_op jit(solution)/shard_map/ppermute | solution.py:589
  26.1 8.9 %collective-permute-start.11 = (bf16[96,1536]{1,0:T(8,128)(2,1)S(1)}, bf16[96,1536]{1,0:T(8,128)(2,1)S(1)}, u32[]{:S(2)}, u32[]{:S(2)}) collective-permute-start(bf16[96,1536]{1,0:T(8,128)(2,1)S(1)} %get-tuple-element.176.rest_0_), channel_id=1, source_target_pairs={{0,8},{4,12},{8,0},{12,4},{16,24},{20,28},{24,16},{28,20},{1,9},{5... | collective-permute-start | bytes 884744 | tf_op jit(solution)/shard_map/ppermute | solution.py:589
  33.8 2.7 %collective-permute-start.9 = (bf16[256,768]{1,0:T(8,128)(2,1)S(1)}, bf16[256,768]{1,0:T(8,128)(2,1)S(1)}, u32[]{:S(2)}, u32[]{:S(2)}) collective-permute-start(bf16[256,768]{1,0:T(8,128)(2,1)S(1)} %get-tuple-element.174), channel_id=1, source_target_pairs={{0,1},{1,0},{2,3},{3,2},{4,5},{5,4},{6,7},{7,6},{8,9},{9,8},{10,11... | collective-permute-start | bytes 1179656 | tf_op jit(solution)/shard_map/ppermute | solution.py:592
  35.0 9.9 %collective-permute-start.12 = (bf16[96,1536]{1,0:T(8,128)(2,1)S(1)}, bf16[96,1536]{1,0:T(8,128)(2,1)S(1)}, u32[]{:S(2)}, u32[]{:S(2)}) collective-permute-start(bf16[96,1536]{1,0:T(8,128)(2,1)S(1)} %collective-permute-done.8.rest_4_), channel_id=1, source_target_pairs={{0,8},{4,12},{8,0},{12,4},{16,24},{20,28},{24,16},{28,20},{1,9},{5... | collective-permute-start | bytes 884744 | tf_op jit(solution)/shard_map/ppermute | solution.py:589
  35.0 11.4 %collective-permute-start.10 = (bf16[96,1536]{1,0:T(8,128)(2,1)S(1)}, bf16[96,1536]{1,0:T(8,128)(2,1)S(1)}, u32[]{:S(2)}, u32[]{:S(2)}) collective-permute-start(bf16[96,1536]{1,0:T(8,128)(2,1)S(1)} %collective-permute-done.8.rest_4_), channel_id=1, source_target_pairs={{0,4},{4,0},{8,12},{12,8},{16,20},{20,16},{24,28},{28,24},{1,5},{5... | collective-permute-start | bytes 884744 | tf_op jit(solution)/shard_map/ppermute | solution.py:589
  36.6 9.9 %collective-permute-start.13 = (bf16[128,768]{1,0:T(8,128)(2,1)S(1)}, bf16[128,768]{1,0:T(8,128)(2,1)S(1)}, u32[]{:S(2)}, u32[]{:S(2)}) collective-permute-start(bf16[128,768]{1,0:T(8,128)(2,1)S(1)} %get-tuple-element.178.one), channel_id=1, source_target_pairs={{0,2},{1,3},{2,0},{3,1},{4,6},{5,7},{6,4},{7,5},{8,10},{9,11},{10,... | collective-permute-start | bytes 589832 | tf_op jit(solution)/shard_map/ppermute | solution.py:592
  38.2 8.7 %collective-permute-start.14 = (bf16[128,768]{1,0:T(8,128)(2,1)S(1)}, bf16[128,768]{1,0:T(8,128)(2,1)S(1)}, u32[]{:S(2)}, u32[]{:S(2)}) collective-permute-start(bf16[128,768]{1,0:T(8,128)(2,1)S(1)} %get-tuple-element.180.one), channel_id=1, source_target_pairs={{0,2},{1,3},{2,0},{3,1},{4,6},{5,7},{6,4},{7,5},{8,10},{9,11},{10,... | collective-permute-start | bytes 589832 | tf_op jit(solution)/shard_map/ppermute | solution.py:592
  38.7 10.9 %collective-permute-start.17 = (bf16[96,1536]{1,0:T(8,128)(2,1)S(1)}, bf16[96,1536]{1,0:T(8,128)(2,1)S(1)}, u32[]{:S(2)}, u32[]{:S(2)}) collective-permute-start(bf16[96,1536]{1,0:T(8,128)(2,1)S(1)} %collective-permute-done.rest_1_), channel_id=1, source_target_pairs={{0,8},{4,12},{8,0},{12,4},{16,24},{20,28},{24,16},{28,20},{1,9},{5... | collective-permute-start | bytes 884744 | tf_op jit(solution)/shard_map/ppermute | solution.py:589
  45.0 6.7 %collective-permute-start.18 = (bf16[96,1536]{1,0:T(8,128)(2,1)S(1)}, bf16[96,1536]{1,0:T(8,128)(2,1)S(1)}, u32[]{:S(2)}, u32[]{:S(2)}) collective-permute-start(bf16[96,1536]{1,0:T(8,128)(2,1)S(1)} %collective-permute-done.12.rest_6_), channel_id=1, source_target_pairs={{0,4},{4,0},{8,12},{12,8},{16,20},{20,16},{24,28},{28,24},{1,5},{5... | collective-permute-start | bytes 884744 | tf_op jit(solution)/shard_map/ppermute | solution.py:589
  46.5 5.2 %collective-permute-start.15 = (bf16[128,768]{1,0:T(8,128)(2,1)S(1)}, bf16[128,768]{1,0:T(8,128)(2,1)S(1)}, u32[]{:S(2)}, u32[]{:S(2)}) collective-permute-start(bf16[128,768]{1,0:T(8,128)(2,1)S(1)} %add.4.own_a), channel_id=1, source_target_pairs={{0,1},{1,0},{2,3},{3,2},{4,5},{5,4},{6,7},{7,6},{8,9},{9,8},{10,11... | collective-permute-start | bytes 589832 | tf_op jit(solution)/shard_map/ppermute | solution.py:592
  47.0 4.7 %collective-permute-start.16 = (bf16[128,768]{1,0:T(8,128)(2,1)S(1)}, bf16[128,768]{1,0:T(8,128)(2,1)S(1)}, u32[]{:S(2)}, u32[]{:S(2)}) collective-permute-start(bf16[128,768]{1,0:T(8,128)(2,1)S(1)} %add.5.own_b), channel_id=1, source_target_pairs={{0,1},{1,0},{2,3},{3,2},{4,5},{5,4},{6,7},{7,6},{8,9},{9,8},{10,11... | collective-permute-start | bytes 589832 | tf_op jit(solution)/shard_map/ppermute | solution.py:592
  55.2 1.8 %collective-permute-start.19 = (bf16[256,768]{1,0:T(8,128)(2,1)S(1)}, bf16[256,768]{1,0:T(8,128)(2,1)S(1)}, u32[]{:S(2)}, u32[]{:S(2)}) collective-permute-start(bf16[256,768]{1,0:T(8,128)(2,1)S(1)} %get-tuple-element.187), channel_id=1, source_target_pairs={{0,1},{1,0},{2,3},{3,2},{4,5},{5,4},{6,7},{7,6},{8,9},{9,8},{10,11... | collective-permute-start | bytes 1179656 | tf_op jit(solution)/shard_map/ppermute | solution.py:592
  57.1 11.2 %collective-permute-start.23 = (bf16[256,768]{1,0:T(8,128)(2,1)S(1)}, bf16[256,768]{1,0:T(8,128)(2,1)S(1)}, u32[]{:S(2)}, u32[]{:S(2)}) collective-permute-start(bf16[256,768]{1,0:T(8,128)(2,1)S(1)} %add.6.one), channel_id=1, source_target_pairs={{0,2},{1,3},{2,0},{3,1},{4,6},{5,7},{6,4},{7,5},{8,10},{9,11},{10,... | collective-permute-start | bytes 1179656 | tf_op jit(solution)/shard_map/ppermute | solution.py:592
  58.7 8.8 %collective-permute-start.22 = (bf16[2,96,768]{2,1,0:T(8,128)(2,1)S(1)}, bf16[2,96,768]{2,1,0:T(8,128)(2,1)S(1)}, u32[]{:S(2)}, u32[]{:S(2)}) collective-permute-start(bf16[2,96,768]{2,1,0:T(8,128)(2,1)S(1)} %get-tuple-element.199), channel_id=1, source_target_pairs={{0,8},{4,12},{8,0},{12,4},{16,24},{20,28},{24,16},{28,20},{1,9},{5... | collective-permute-start | bytes 884744 | tf_op jit(solution)/shard_map/ppermute | solution.py:589
  61.4 2.1 %collective-permute-start.20 = (bf16[128,768]{1,0:T(8,128)(2,1)S(1)}, bf16[128,768]{1,0:T(8,128)(2,1)S(1)}, u32[]{:S(2)}, u32[]{:S(2)}) collective-permute-start(bf16[128,768]{1,0:T(8,128)(2,1)S(1)} %get-tuple-element.196), channel_id=1, source_target_pairs={{0,1},{1,0},{2,3},{3,2},{4,5},{5,4},{6,7},{7,6},{8,9},{9,8},{10,11... | collective-permute-start | bytes 589832 | tf_op jit(solution)/shard_map/ppermute | solution.py:592
  61.5 2.0 %collective-permute-start.21 = (bf16[128,768]{1,0:T(8,128)(2,1)S(1)}, bf16[128,768]{1,0:T(8,128)(2,1)S(1)}, u32[]{:S(2)}, u32[]{:S(2)}) collective-permute-start(bf16[128,768]{1,0:T(8,128)(2,1)S(1)} %get-tuple-element.197), channel_id=1, source_target_pairs={{0,1},{1,0},{2,3},{3,2},{4,5},{5,4},{6,7},{7,6},{8,9},{9,8},{10,11... | collective-permute-start | bytes 589832 | tf_op jit(solution)/shard_map/ppermute | solution.py:592
  62.0 16.1 %collective-permute-start.25 = (bf16[4,96,768]{2,1,0:T(8,128)(2,1)S(1)}, bf16[4,96,768]{2,1,0:T(8,128)(2,1)S(1)}, u32[]{:S(2)}, u32[]{:S(2)}) collective-permute-start(bf16[4,96,768]{2,1,0:T(8,128)(2,1)S(1)} %get-tuple-element.214), channel_id=1, source_target_pairs={{0,4},{4,0},{8,12},{12,8},{16,20},{20,16},{24,28},{28,24},{1,5},{5... | collective-permute-start | bytes 1769480 | tf_op jit(solution)/shard_map/ppermute | solution.py:589
  68.4 3.8 %collective-permute-start.24 = (bf16[256,768]{1,0:T(8,128)(2,1)S(1)}, bf16[256,768]{1,0:T(8,128)(2,1)S(1)}, u32[]{:S(2)}, u32[]{:S(2)}) collective-permute-start(bf16[256,768]{1,0:T(8,128)(2,1)S(1)} %add.7.own), channel_id=1, source_target_pairs={{0,1},{1,0},{2,3},{3,2},{4,5},{5,4},{6,7},{7,6},{8,9},{9,8},{10,11... | collective-permute-start | bytes 1179656 | tf_op jit(solution)/shard_map/ppermute | solution.py:592
  68.5 15.8 %collective-permute-start.26 = (bf16[2,96,768]{2,1,0:T(8,128)(2,1)S(1)}, bf16[2,96,768]{2,1,0:T(8,128)(2,1)S(1)}, u32[]{:S(2)}, u32[]{:S(2)}) collective-permute-start(bf16[2,96,768]{2,1,0:T(8,128)(2,1)S(1)} %get-tuple-element.220), channel_id=1, source_target_pairs={{0,8},{4,12},{8,0},{12,4},{16,24},{20,28},{24,16},{28,20},{1,9},{5... | collective-permute-start | bytes 884744 | tf_op jit(solution)/shard_map/ppermute | solution.py:589
  68.6 17.4 %collective-permute-start.27 = (bf16[2,96,768]{2,1,0:T(8,128)(2,1)S(1)}, bf16[2,96,768]{2,1,0:T(8,128)(2,1)S(1)}, u32[]{:S(2)}, u32[]{:S(2)}) collective-permute-start(bf16[2,96,768]{2,1,0:T(8,128)(2,1)S(1)} %high_add.1), channel_id=1, source_target_pairs={{0,16},{4,20},{8,24},{12,28},{16,0},{20,4},{24,8},{28,12},{1,17},{... | collective-permute-start | bytes 884744 | tf_op jit(solution)/shard_map/ppermute | solution.py:589
  78.2 9.4 %collective-permute-start.28 = (bf16[200,768]{1,0:T(8,128)(2,1)S(1)}, bf16[200,768]{1,0:T(8,128)(2,1)S(1)}, u32[]{:S(2)}, u32[]{:S(2)}) collective-permute-start(bf16[200,768]{1,0:T(8,128)(2,1)S(1)} %get-tuple-element.225.sent), channel_id=1, source_target_pairs={{0,4},{4,0},{8,12},{12,8},{16,20},{20,16},{24,28},{28,24},{1,5},{5... | collective-permute-start | bytes 921608 | tf_op jit(solution)/shard_map/ppermute | solution.py:589
  79.0 13.5 %collective-permute-start.30 = (bf16[2,96,768]{2,1,0:T(8,128)(2,1)S(1)}, bf16[2,96,768]{2,1,0:T(8,128)(2,1)S(1)}, u32[]{:S(2)}, u32[]{:S(2)}) collective-permute-start(bf16[2,96,768]{2,1,0:T(8,128)(2,1)S(1)} %get-tuple-element.216), channel_id=1, source_target_pairs={{0,8},{4,12},{8,0},{12,4},{16,24},{20,28},{24,16},{28,20},{1,9},{5... | collective-permute-start | bytes 884744 | tf_op jit(solution)/shard_map/ppermute | solution.py:589
  86.1 5.2 %collective-permute-start.29 = (bf16[96,768]{1,0:T(8,128)(2,1)S(1)}, bf16[96,768]{1,0:T(8,128)(2,1)S(1)}, u32[]{:S(2)}, u32[]{:S(2)}) collective-permute-start(bf16[96,768]{1,0:T(8,128)(2,1)S(1)} %get-tuple-element.222), channel_id=1, source_target_pairs={{0,4},{4,0},{8,12},{12,8},{16,20},{20,16},{24,28},{28,24},{1,5},{5... | collective-permute-start | bytes 442376 | tf_op jit(solution)/shard_map/ppermute | solution.py:589
  87.1 5.4 %collective-permute-start.31 = (bf16[128,768]{1,0:T(8,128)(2,1)S(1)}, bf16[128,768]{1,0:T(8,128)(2,1)S(1)}, u32[]{:S(2)}, u32[]{:S(2)}) collective-permute-start(bf16[128,768]{1,0:T(8,128)(2,1)S(1)} %get-tuple-element.233), channel_id=1, source_target_pairs={{0,1},{1,0},{2,3},{3,2},{4,5},{5,4},{6,7},{7,6},{8,9},{9,8},{10,11... | collective-permute-start | bytes 589832 | tf_op jit(solution)/shard_map/ppermute | solution.py:592
  87.1 5.4 %collective-permute-start.32 = (bf16[128,768]{1,0:T(8,128)(2,1)S(1)}, bf16[128,768]{1,0:T(8,128)(2,1)S(1)}, u32[]{:S(2)}, u32[]{:S(2)}) collective-permute-start(bf16[128,768]{1,0:T(8,128)(2,1)S(1)} %get-tuple-element.234), channel_id=1, source_target_pairs={{0,1},{1,0},{2,3},{3,2},{4,5},{5,4},{6,7},{7,6},{8,9},{9,8},{10,11... | collective-permute-start | bytes 589832 | tf_op jit(solution)/shard_map/ppermute | solution.py:592
  87.7 14.7 %collective-permute-start.35 = (bf16[200,768]{1,0:T(8,128)(2,1)S(1)}, bf16[200,768]{1,0:T(8,128)(2,1)S(1)}, u32[]{:S(2)}, u32[]{:S(2)}) collective-permute-start(bf16[200,768]{1,0:T(8,128)(2,1)S(1)} %last_high.1.sent), channel_id=1, source_target_pairs={{0,8},{4,12},{8,0},{12,4},{16,24},{20,28},{24,16},{28,20},{1,9},{5... | collective-permute-start | bytes 921608 | tf_op jit(solution)/shard_map/ppermute | solution.py:589
  91.3 11.0 %collective-permute-start.34 = (bf16[2,96,768]{2,1,0:T(8,128)(2,1)S(1)}, bf16[2,96,768]{2,1,0:T(8,128)(2,1)S(1)}, u32[]{:S(2)}, u32[]{:S(2)}) collective-permute-start(bf16[2,96,768]{2,1,0:T(8,128)(2,1)S(1)} %get-tuple-element.240), channel_id=1, source_target_pairs={{0,4},{4,0},{8,12},{12,8},{16,20},{20,16},{24,28},{28,24},{1,5},{5... | collective-permute-start | bytes 884744 | tf_op jit(solution)/shard_map/ppermute | solution.py:589
  92.8 9.8 %collective-permute-start.36 = (bf16[256,768]{1,0:T(8,128)(2,1)S(1)}, bf16[256,768]{1,0:T(8,128)(2,1)S(1)}, u32[]{:S(2)}, u32[]{:S(2)}) collective-permute-start(bf16[256,768]{1,0:T(8,128)(2,1)S(1)} %get-tuple-element.244), channel_id=1, source_target_pairs={{0,2},{1,3},{2,0},{3,1},{4,6},{5,7},{6,4},{7,5},{8,10},{9,11},{10,... | collective-permute-start | bytes 1179656 | tf_op jit(solution)/shard_map/ppermute | solution.py:592
  94.4 8.0 %collective-permute-start.33 = (bf16[96,768]{1,0:T(8,128)(2,1)S(1)}, bf16[96,768]{1,0:T(8,128)(2,1)S(1)}, u32[]{:S(2)}, u32[]{:S(2)}) collective-permute-start(bf16[96,768]{1,0:T(8,128)(2,1)S(1)} %get-tuple-element.230), channel_id=1, source_target_pairs={{0,16},{4,20},{8,24},{12,28},{16,0},{20,4},{24,8},{28,12},{1,17},{... | collective-permute-start | bytes 442376 | tf_op jit(solution)/shard_map/ppermute | solution.py:589
  102.5 7.3 %collective-permute-start.37 = (bf16[104,768]{1,0:T(8,128)(2,1)S(1)}, bf16[104,768]{1,0:T(8,128)(2,1)S(1)}, u32[]{:S(2)}, u32[]{:S(2)}) collective-permute-start(bf16[104,768]{1,0:T(8,128)(2,1)S(1)} %get-tuple-element.241.rest_1_), channel_id=1, source_target_pairs={{0,16},{4,20},{8,24},{12,28},{16,0},{20,4},{24,8},{28,12},{1,17},{... | collective-permute-start | bytes 479240 | tf_op jit(solution)/shard_map/ppermute | solution.py:589

commit v8 on v7

--- a/solution.py
+++ b/solution.py
@@ -191,7 +191,7 @@
 
 def attend_kernel(n_blocks, act, bias, *rest):
     blocks = rest[:n_blocks]
-    weights, qkv, prob, mixed, keep, send = rest[n_blocks:]
+    weights, qkv, prob, mixed, *halves = rest[n_blocks:]
     assemble(weights, blocks)
     width = qkv.shape[1] // 3
     qkv[...] = dot_nn(act[...], weights[:, : 3 * width]).astype(bf16)
@@ -207,8 +207,7 @@
         mixed[:, cols] = dot_nn(low, value).astype(bf16)
     out_cols = weights[:, 3 * width :]
     for half, at, rows in half_rows():
-        to = send if half else keep
-        to[at * BLK : (at + 1) * BLK, :] = dot_nt(mixed[rows, :], out_cols).astype(bf16)
+        halves[2 * half + at][...] = dot_nt(mixed[rows, :], out_cols).astype(bf16)
 
 
 def ffn_kernel(n_blocks, x, gains, dy, own_a, own_b, other_a, other_b, *rest):
@@ -392,12 +391,6 @@
 
 def add_kernel(one, two, out):
     out[...] = (one[...].astype(f32) + two[...].astype(f32)).astype(bf16)
-
-
-def split_add_kernel(one, two, *outs):
-    for i, out in enumerate(outs):
-        rows = slice(i * BLK, (i + 1) * BLK)
-        out[...] = (one[rows, :].astype(f32) + two[rows, :].astype(f32)).astype(bf16)
 
 
 def pair_add_kernel(keep, got, mine, theirs):
@@ -651,7 +644,7 @@
         three = swap_dp(two, 2)
         ffn_two = swap_dp(after(packed_ffn, two), 4)
         two_across = swap_dp(two, 1)
-        ffn_one = swap_dp(after(packed_ffn, three, own), 2)
+        ffn_one = swap_dp(after(packed_ffn, two, own), 2)
         three_across = swap_dp(three, 1)
         qkvo_blocks = [packed, own, one, one_across, two, two_across, three, three_across]
         ffn_three = swap_dp(after(ffn_two, ffn_one), 2)
@@ -665,22 +658,21 @@
         ffn_first = ffn_blocks = ffn_early = [lax.all_gather(packed_ffn, "dp", axis=0, tiled=True)]
     n_blocks = len(qkvo_blocks)
 
-    weights_one, qkv, prob, mixed, attn_keep, attn_send = call(
+    weights_one, qkv, prob, mixed, *attn_parts = call(
         functools.partial(attend_kernel, n_blocks),
         [
             sds((model, packed_cols), bf16),
             sds((tokens, 3 * local), bf16),
             sds((heads_here, LEN, LEN), bf16),
             sds((tokens, local), bf16),
-            *half_shape,
+            *[sds((BLK, model), bf16)] * 4,
         ],
         (act_one, bias, *qkvo_blocks),
         "attend",
     )
     half_blocks = [sds((BLK, model), bf16)] * 2
-    attn_first = call(
-        split_add_kernel, half_blocks, (attn_keep, swap_tp(after(attn_send, *ffn_first), 1)), "split_add", limit=4
-    )
+    attn_got = [swap_tp(after(part, *ffn_first), 1) for part in attn_parts[2:]]
+    attn_first = [add(part, got) for part, got in zip(attn_parts, attn_got)]
     attn_own = [add(first, swap_tp(first, 2), ffn_early) for first in attn_first]
     attn_sums = (*attn_own, *(swap_tp(own, 1) for own in attn_own))
     resid, act_two, hidden_act, pre_grad, back_keep, back_send, down_full, in_full = call(

time: 124 us -> 124 us (level)
  starting transfers between devices: 38.3 us -> 41.6 us
  waiting for transfers between devices: 44.6 us -> 41.9 us
    ppermute x25, waiting for transfers between devices: 42.6 us -> 38.3 us  [swap_dp(): return lax.ppermute(value, 'dp', [(i, i ^ distance) for i in range(dp)])]
    ppermute x25, starting transfers between devices: 31.4 us -> 34.4 us  [swap_dp(): return lax.ppermute(value, 'dp', [(i, i ^ distance) for i in range(dp)])]
    ppermute x13 -> x14, waiting for transfers between devices: 1.98 us -> 3.57 us  [swap_tp(): return lax.ppermute(value, 'tp', [(i, i ^ distance) for i in range(tp)])]
    ppermute x13 -> x14, starting transfers between devices: 6.86 us -> 7.25 us  [swap_tp(): return lax.ppermute(value, 'tp', [(i, i ^ distance) for i in range(tp)])]
    pallas_call x29 -> x30, Pallas kernels: 29 us -> 29 us  [call(): pl.pallas_call(body, out_shape=tuple(outs), in_specs=[pl.BlockSpec(memory...]
  transfers between devices with their start and end apart: 38 -> 39, of which waited for: 18 -> 18; matrix products, arithmetic and copies ran while one was open for 0% -> 0% of each run, Pallas kernels for 17% -> 17%
where the time goes in v8:
time: 124 us
  waiting for transfers between devices  41.9 us (34%)
  starting transfers between devices  41.6 us (34%)
  Pallas kernels  29 us (23%)
  blocking collectives  10.1 us (8%)
    ppermute x25, waiting for transfers between devices, swap_dp(): return lax.ppermute(value, 'dp', [(i, i ^ distance) for i in range(dp)])  38.3 us
    ppermute x25, starting transfers between devices, swap_dp(): return lax.ppermute(value, 'dp', [(i, i ^ distance) for i in range(dp)])  34.4 us
    pallas_call x30, Pallas kernels, call(): pl.pallas_call(body, out_shape=tuple(outs), in_specs=[pl.BlockSpec(memory...  29 us
    all_to_all x1, blocking collectives, on_device(): told = lax.all_to_all(payload, ('dp', 'tp'), 0, 0)  10.1 us
    ppermute x14, starting transfers between devices, swap_tp(): return lax.ppermute(value, 'tp', [(i, i ^ distance) for i in range(tp)])  7.25 us
    ppermute x14, waiting for transfers between devices, swap_tp(): return lax.ppermute(value, 'tp', [(i, i ^ distance) for i in range(tp)])  3.57 us
  transfers between devices with their start and end apart: 39, of which 18 were waited for; matrix products, arithmetic and copies ran while one was open for 0% of the time, Pallas kernels for 17%

profile of v8, /device:TPU:0, one launch (start us, length us, event | category | flops | bytes accessed | tf_op | source)
XLA Modules:
  0.0 123.7 jit_solution(918032638625946881)
XLA Ops:
  0.7 1.2 %pack.1 = (bf16[96,768]{1,0:T(8,128)(2,1)S(1)}, bf16[96,1536]{1,0:T(8,128)(2,1)S(1)}) custom-call(f32[3,96,192]{2,1,0:T(8,128)} %refs_0_, f32[96,192]{1,0:T(8,128)} %refs_3_.1, f32[96,768]{1,0:T(8,128)} %refs_9_.1, f32[96,768]{1,0:T(8,128)} %refs_6_.1), custom_call_target="tpu_custom_call" | custom-call | tf_op jit(solution)/shard_map/pack/pallas_call | solution.py:61
  1.9 4.1 %collective-permute-start.4 = (bf16[96,768]{1,0:T(8,128)(2,1)S(1)}, bf16[96,768]{1,0:T(8,128)(2,1)S(1)}, u32[]{:S(2)}, u32[]{:S(2)}) collective-permute-start(bf16[96,768]{1,0:T(8,128)(2,1)S(1)} %get-tuple-element.171.rest_0_), channel_id=1, source_target_pairs={{0,16},{4,20},{8,24},{12,28},{16,0},{20,4},{24,8},{28,12},{1,17},{... | collective-permute-start | bytes 442376 | tf_op jit(solution)/shard_map/ppermute | solution.py:582
  6.0 1.6 %collective-permute-start.1 = (bf16[96,768]{1,0:T(8,128)(2,1)S(1)}, bf16[96,768]{1,0:T(8,128)(2,1)S(1)}, u32[]{:S(2)}, u32[]{:S(2)}) collective-permute-start(bf16[96,768]{1,0:T(8,128)(2,1)S(1)} %get-tuple-element.171.rest_0_), channel_id=1, source_target_pairs={{0,8},{4,12},{8,0},{12,4},{16,24},{20,28},{24,16},{28,20},{1,9},{5... | collective-permute-start | bytes 442376 | tf_op jit(solution)/shard_map/ppermute | solution.py:582
  7.6 2.2 %prep.1 = (bf16[512,768]{1,0:T(8,128)(2,1)S(1)}, bf16[768,512]{1,0:T(8,128)(2,1)S(1)}, f32[3,512,512]{2,1,0:T(8,128)S(1)}, s32[1,1024]{1,0:T(1,128)S(1)}, bf16[5...) custom-call(s32[1,4]{1,0:T(1,128)} %seg_in.1, f32[3,32]{1,0:T(4,128)} %bitcast.8, ...), custom_call_target="tpu_custom_call" | custom-call | tf_op jit(solution)/shard_map/prep/pallas_call | solution.py:61
  9.8 1.6 %collective-permute-start.3 = (bf16[96,768]{1,0:T(8,128)(2,1)S(1)}, bf16[96,768]{1,0:T(8,128)(2,1)S(1)}, u32[]{:S(2)}, u32[]{:S(2)}) collective-permute-start(bf16[96,768]{1,0:T(8,128)(2,1)S(1)} %get-tuple-element.171.rest_0_), channel_id=1, source_target_pairs={{0,4},{4,0},{8,12},{12,8},{16,20},{20,16},{24,28},{28,24},{1,5},{5... | collective-permute-start | bytes 442376 | tf_op jit(solution)/shard_map/ppermute | solution.py:582
  11.9 1.2 %collective-permute-done.4.rest_4_ = bf16[96,768]{1,0:T(8,128)(2,1)S(1)} collective-permute-done((bf16[96,768]{1,0:T(8,128)(2,1)S(1)}, bf16[96,768]{1,0:T(8,128)(2,1)S(1)}, u32[]{:S(2)}, u32[]{:S(2)}) %collective-permute-start.4) | collective-permute-done | bytes 147488 | tf_op jit(solution)/shard_map/ppermute | solution.py:582
  13.8 1.5 %collective-permute-start.2 = (bf16[96,768]{1,0:T(8,128)(2,1)S(1)}, bf16[96,768]{1,0:T(8,128)(2,1)S(1)}, u32[]{:S(2)}, u32[]{:S(2)}) collective-permute-start(bf16[96,768]{1,0:T(8,128)(2,1)S(1)} %collective-permute-done.1.rest_2_), channel_id=1, source_target_pairs={{0,4},{4,0},{8,12},{12,8},{16,20},{20,16},{24,28},{28,24},{1,5},{5... | collective-permute-start | bytes 442376 | tf_op jit(solution)/shard_map/ppermute | solution.py:582
  15.2 3.4 %collective-permute-start.8 = (bf16[96,1536]{1,0:T(8,128)(2,1)S(1)}, bf16[96,1536]{1,0:T(8,128)(2,1)S(1)}, u32[]{:S(2)}, u32[]{:S(2)}) collective-permute-start(bf16[96,1536]{1,0:T(8,128)(2,1)S(1)} %get-tuple-element.176.rest_0_), channel_id=1, source_target_pairs={{0,16},{4,20},{8,24},{12,28},{16,0},{20,4},{24,8},{28,12},{1,17},{... | collective-permute-start | bytes 884744 | tf_op jit(solution)/shard_map/ppermute | solution.py:582
  18.6 3.8 %collective-permute-start.5 = (bf16[96,768]{1,0:T(8,128)(2,1)S(1)}, bf16[96,768]{1,0:T(8,128)(2,1)S(1)}, u32[]{:S(2)}, u32[]{:S(2)}) collective-permute-start(bf16[96,768]{1,0:T(8,128)(2,1)S(1)} %collective-permute-done.4.rest_4_), channel_id=1, source_target_pairs={{0,4},{4,0},{8,12},{12,8},{16,20},{20,16},{24,28},{28,24},{1,5},{5... | collective-permute-start | bytes 442376 | tf_op jit(solution)/shard_map/ppermute | solution.py:582
  22.4 3.7 %collective-permute-done.2.rest_3_ = bf16[96,768]{1,0:T(8,128)(2,1)S(1)} collective-permute-done((bf16[96,768]{1,0:T(8,128)(2,1)S(1)}, bf16[96,768]{1,0:T(8,128)(2,1)S(1)}, u32[]{:S(2)}, u32[]{:S(2)}) %collective-permute-start.2) | collective-permute-done | bytes 147488 | tf_op jit(solution)/shard_map/ppermute | solution.py:582
  26.1 1.5 %collective-permute-start.7 = (bf16[96,768]{1,0:T(8,128)(2,1)S(1)}, bf16[96,768]{1,0:T(8,128)(2,1)S(1)}, u32[]{:S(2)}, u32[]{:S(2)}) collective-permute-start(bf16[96,768]{1,0:T(8,128)(2,1)S(1)} %collective-permute-done.6.rest_6_), channel_id=1, source_target_pairs={{0,4},{4,0},{8,12},{12,8},{16,20},{20,16},{24,28},{28,24},{1,5},{5... | collective-permute-start | bytes 442376 | tf_op jit(solution)/shard_map/ppermute | solution.py:582
  27.6 1.5 %collective-permute-done.5.rest_5_ = bf16[96,768]{1,0:T(8,128)(2,1)S(1)} collective-permute-done((bf16[96,768]{1,0:T(8,128)(2,1)S(1)}, bf16[96,768]{1,0:T(8,128)(2,1)S(1)}, u32[]{:S(2)}, u32[]{:S(2)}) %collective-permute-start.5) | collective-permute-done | bytes 147488 | tf_op jit(solution)/shard_map/ppermute | solution.py:582
  29.1 2.2 %collective-permute-done.7.rest_7_ = bf16[96,768]{1,0:T(8,128)(2,1)S(1)} collective-permute-done((bf16[96,768]{1,0:T(8,128)(2,1)S(1)}, bf16[96,768]{1,0:T(8,128)(2,1)S(1)}, u32[]{:S(2)}, u32[]{:S(2)}) %collective-permute-start.7) | collective-permute-done | bytes 147488 | tf_op jit(solution)/shard_map/ppermute | solution.py:582
  31.3 3.1 %attend.1 = (bf16[768,768]{1,0:T(8,128)(2,1)S(1)}, bf16[512,576]{1,0:T(8,128)(2,1)S(1)}, bf16[3,512,512]{2,1,0:T(8,128)(2,1)S(1)}, bf16[512,192]{1,0:T(8,128)(2,...) custom-call(bf16[512,768]{1,0:T(8,128)(2,1)S(1)} %get-tuple-element., ...), custom_call_target="tpu_custom_call" | custom-call | tf_op jit(solution)/shard_map/attend/pallas_call | solution.py:61
  35.4 1.5 %collective-permute-start.10 = (bf16[96,1536]{1,0:T(8,128)(2,1)S(1)}, bf16[96,1536]{1,0:T(8,128)(2,1)S(1)}, u32[]{:S(2)}, u32[]{:S(2)}) collective-permute-start(bf16[96,1536]{1,0:T(8,128)(2,1)S(1)} %collective-permute-done.8.rest_4_), channel_id=1, source_target_pairs={{0,4},{4,0},{8,12},{12,8},{16,20},{20,16},{24,28},{28,24},{1,5},{5... | collective-permute-start | bytes 884744 | tf_op jit(solution)/shard_map/ppermute | solution.py:582
  36.9 1.6 %collective-permute-start.15 = (bf16[128,768]{1,0:T(8,128)(2,1)S(1)}, bf16[128,768]{1,0:T(8,128)(2,1)S(1)}, u32[]{:S(2)}, u32[]{:S(2)}) collective-permute-start(bf16[128,768]{1,0:T(8,128)(2,1)S(1)} %add.8.one), channel_id=1, source_target_pairs={{0,2},{1,3},{2,0},{3,1},{4,6},{5,7},{6,4},{7,5},{8,10},{9,11},{10,... | collective-permute-start | bytes 589832 | tf_op jit(solution)/shard_map/ppermute | solution.py:585
  39.1 1.6 %collective-permute-start.18 = (bf16[96,1536]{1,0:T(8,128)(2,1)S(1)}, bf16[96,1536]{1,0:T(8,128)(2,1)S(1)}, u32[]{:S(2)}, u32[]{:S(2)}) collective-permute-start(bf16[96,1536]{1,0:T(8,128)(2,1)S(1)} %collective-permute-done.rest_1_), channel_id=1, source_target_pairs={{0,8},{4,12},{8,0},{12,4},{16,24},{20,28},{24,16},{28,20},{1,9},{5... | collective-permute-start | bytes 884744 | tf_op jit(solution)/shard_map/ppermute | solution.py:582
  40.7 4.1 %collective-permute-done.12.rest_6_ = bf16[96,1536]{1,0:T(8,128)(2,1)S(1)} collective-permute-done((bf16[96,1536]{1,0:T(8,128)(2,1)S(1)}, bf16[96,1536]{1,0:T(8,128)(2,1)S(1)}, u32[]{:S(2)}, u32[]{:S(2)}) %collective-permute-start.12) | collective-permute-done | bytes 294944 | tf_op jit(solution)/shard_map/ppermute | solution.py:582
  44.8 1.5 %collective-permute-start.19 = (bf16[96,1536]{1,0:T(8,128)(2,1)S(1)}, bf16[96,1536]{1,0:T(8,128)(2,1)S(1)}, u32[]{:S(2)}, u32[]{:S(2)}) collective-permute-start(bf16[96,1536]{1,0:T(8,128)(2,1)S(1)} %collective-permute-done.12.rest_6_), channel_id=1, source_target_pairs={{0,4},{4,0},{8,12},{12,8},{16,20},{20,16},{24,28},{28,24},{1,5},{5... | collective-permute-start | bytes 884744 | tf_op jit(solution)/shard_map/ppermute | solution.py:582
  46.4 1.1 collective-permute-done.13.two
  47.7 2.6 %collective-permute-done.18.rest_3_ = bf16[96,1536]{1,0:T(8,128)(2,1)S(1)} collective-permute-done((bf16[96,1536]{1,0:T(8,128)(2,1)S(1)}, bf16[96,1536]{1,0:T(8,128)(2,1)S(1)}, u32[]{:S(2)}, u32[]{:S(2)}) %collective-permute-start.18) | collective-permute-done | bytes 294944 | tf_op jit(solution)/shard_map/ppermute | solution.py:582
  50.3 1.8 %collective-permute-done.19.rest_7_ = bf16[96,1536]{1,0:T(8,128)(2,1)S(1)} collective-permute-done((bf16[96,1536]{1,0:T(8,128)(2,1)S(1)}, bf16[96,1536]{1,0:T(8,128)(2,1)S(1)}, u32[]{:S(2)}, u32[]{:S(2)}) %collective-permute-start.19) | collective-permute-done | bytes 294944 | tf_op jit(solution)/shard_map/ppermute | solution.py:582
  52.1 3.5 %ffn.1 = (f32[512,768]{1,0:T(8,128)S(1)}, bf16[512,768]{1,0:T(8,128)(2,1)S(1)}, bf16[512,768]{1,0:T(8,128)(2,1)S(1)}, bf16[512,768]{1,0:T(8,128)(2,1)S(1)}, bf16...) custom-call(bf16[512,768]{1,0:T(8,128)(2,1)S(1)} %get-tuple-element., ...), custom_call_target="tpu_custom_call" | custom-call | tf_op jit(solution)/shard_map/ffn/pallas_call | solution.py:61
  55.7 0.9 down_grad.1
  57.5 1.6 %collective-permute-start.24 = (bf16[256,768]{1,0:T(8,128)(2,1)S(1)}, bf16[256,768]{1,0:T(8,128)(2,1)S(1)}, u32[]{:S(2)}, u32[]{:S(2)}) collective-permute-start(bf16[256,768]{1,0:T(8,128)(2,1)S(1)} %add.10.one), channel_id=1, source_target_pairs={{0,2},{1,3},{2,0},{3,1},{4,6},{5,7},{6,4},{7,5},{8,10},{9,11},{10,... | collective-permute-start | bytes 1179656 | tf_op jit(solution)/shard_map/ppermute | solution.py:585
  59.5 1.0 in_grad.1
  60.6 1.6 %ffn_out.1 = (bf16[256,768]{1,0:T(8,128)(2,1)S(1)}, bf16[128,768]{1,0:T(8,128)(2,1)S(1)}, bf16[128,768]{1,0:T(8,128)(2,1)S(1)}) custom-call(bf16[512,768]{1,0:T(8,128)(2,1)S(1)} %get-tuple-element.195.right.hidden, bf16[768,768]{1,0:T(8,128)(2,1)S(1)} %get-tuple-element.196.down), custom_call_target="tpu_custom_call" | custom-call | tf_op jit(solution)/shard_map/ffn_out/pallas_call | solution.py:61
  62.8 1.5 %collective-permute-start.26 = (bf16[4,96,768]{2,1,0:T(8,128)(2,1)S(1)}, bf16[4,96,768]{2,1,0:T(8,128)(2,1)S(1)}, u32[]{:S(2)}, u32[]{:S(2)}) collective-permute-start(bf16[4,96,768]{2,1,0:T(8,128)(2,1)S(1)} %get-tuple-element.216), channel_id=1, source_target_pairs={{0,4},{4,0},{8,12},{12,8},{16,20},{20,16},{24,28},{28,24},{1,5},{5... | collective-permute-start | bytes 1769480 | tf_op jit(solution)/shard_map/ppermute | solution.py:582
  65.1 2.7 %collective-permute-done.23.got = bf16[2,96,768]{2,1,0:T(8,128)(2,1)S(1)} collective-permute-done((bf16[2,96,768]{2,1,0:T(8,128)(2,1)S(1)}, bf16[2,96,768]{2,1,0:T(8,128)(2,1)S(1)}, u32[]{:S(2)}, u32[]{:S(2)}) %collective-permute-start.23) | collective-permute-done | bytes 294944 | tf_op jit(solution)/shard_map/ppermute | solution.py:582
  67.8 0.9 collective-permute-done.24.two
  69.8 0.8 collective-permute-done.25.other
  70.6 5.8 %attend_back.1 = (bf16[4,96,768]{2,1,0:T(8,128)(2,1)S(1)}, bf16[2,96,768]{2,1,0:T(8,128)(2,1)S(1)}, f32[128,768]{1,0:T(8,128)S(1)}, bf16[200,768]{1,0:T(8,128)(2,1)S(1)}, bf16[512,576]{1,0:T(8,128)(2,1)S(1)}) custom-call(f32[512,768]{1,0:T(8,128)S(1)} %get-tuple-element.244.resid, bf16[512,768]{1,0:T(8,128)(2,1)S(1)} %get-tuple-element.164.dy.left, ...), custom_call_target="tpu_custom_call" | custom-call | tf_op jit(solution)/shard_map/attend_back/pallas_call | solution.py:61
  76.4 1.7 %collective-permute-done.26.got = bf16[4,96,768]{2,1,0:T(8,128)(2,1)S(1)} collective-permute-done((bf16[4,96,768]{2,1,0:T(8,128)(2,1)S(1)}, bf16[4,96,768]{2,1,0:T(8,128)(2,1)S(1)}, u32[]{:S(2)}, u32[]{:S(2)}) %collective-permute-start.26) | collective-permute-done | bytes 589856 | tf_op jit(solution)/shard_map/ppermute | solution.py:582
  78.2 1.6 %collective-permute-start.29 = (bf16[200,768]{1,0:T(8,128)(2,1)S(1)}, bf16[200,768]{1,0:T(8,128)(2,1)S(1)}, u32[]{:S(2)}, u32[]{:S(2)}) collective-permute-start(bf16[200,768]{1,0:T(8,128)(2,1)S(1)} %get-tuple-element.227.sent), channel_id=1, source_target_pairs={{0,4},{4,0},{8,12},{12,8},{16,20},{20,16},{24,28},{28,24},{1,5},{5... | collective-permute-start | bytes 921608 | tf_op jit(solution)/shard_map/ppermute | solution.py:582
  79.8 1.6 %collective-permute-start.31 = (bf16[2,96,768]{2,1,0:T(8,128)(2,1)S(1)}, bf16[2,96,768]{2,1,0:T(8,128)(2,1)S(1)}, u32[]{:S(2)}, u32[]{:S(2)}) collective-permute-start(bf16[2,96,768]{2,1,0:T(8,128)(2,1)S(1)} %get-tuple-element.218), channel_id=1, source_target_pairs={{0,8},{4,12},{8,0},{12,4},{16,24},{20,28},{24,16},{28,20},{1,9},{5... | collective-permute-start | bytes 884744 | tf_op jit(solution)/shard_map/ppermute | solution.py:582
  81.4 1.4 %act_grad.1 = (bf16[256,768]{1,0:T(8,128)(2,1)S(1)}, bf16[128,768]{1,0:T(8,128)(2,1)S(1)}, bf16[128,768]{1,0:T(8,128)(2,1)S(1)}) custom-call(bf16[512,576]{1,0:T(8,128)(2,1)S(1)} %get-tuple-element.219.proj_grad, bf16[768,768]{1,0:T(8,128)(2,1)S(1)} %get-tuple-element.207.weights), custom_call_target="tpu_custom_call" | custom-call | tf_op jit(solution)/shard_map/act_grad/pallas_call | solution.py:61
  83.4 2.6 %collective-permute-done.28.got = bf16[2,96,768]{2,1,0:T(8,128)(2,1)S(1)} collective-permute-done((bf16[2,96,768]{2,1,0:T(8,128)(2,1)S(1)}, bf16[2,96,768]{2,1,0:T(8,128)(2,1)S(1)}, u32[]{:S(2)}, u32[]{:S(2)}) %collective-permute-start.28) | collective-permute-done | bytes 294944 | tf_op jit(solution)/shard_map/ppermute | solution.py:582
  86.1 1.6 %collective-permute-start.30 = (bf16[96,768]{1,0:T(8,128)(2,1)S(1)}, bf16[96,768]{1,0:T(8,128)(2,1)S(1)}, u32[]{:S(2)}, u32[]{:S(2)}) collective-permute-start(bf16[96,768]{1,0:T(8,128)(2,1)S(1)} %get-tuple-element.224), channel_id=1, source_target_pairs={{0,4},{4,0},{8,12},{12,8},{16,20},{20,16},{24,28},{28,24},{1,5},{5... | collective-permute-start | bytes 442376 | tf_op jit(solution)/shard_map/ppermute | solution.py:582
  88.2 1.3 %collective-permute-start.36 = (bf16[200,768]{1,0:T(8,128)(2,1)S(1)}, bf16[200,768]{1,0:T(8,128)(2,1)S(1)}, u32[]{:S(2)}, u32[]{:S(2)}) collective-permute-start(bf16[200,768]{1,0:T(8,128)(2,1)S(1)} %last_high.1.sent), channel_id=1, source_target_pairs={{0,8},{4,12},{8,0},{12,4},{16,24},{20,28},{24,16},{28,20},{1,9},{5... | collective-permute-start | bytes 921608 | tf_op jit(solution)/shard_map/ppermute | solution.py:582
  89.5 1.8 %collective-permute-done.30.rest_1_ = bf16[96,768]{1,0:T(8,128)(2,1)S(1)} collective-permute-done((bf16[96,768]{1,0:T(8,128)(2,1)S(1)}, bf16[96,768]{1,0:T(8,128)(2,1)S(1)}, u32[]{:S(2)}, u32[]{:S(2)}) %collective-permute-start.30) | collective-permute-done | bytes 147488 | tf_op jit(solution)/shard_map/ppermute | solution.py:582
  91.3 1.5 %collective-permute-start.35 = (bf16[2,96,768]{2,1,0:T(8,128)(2,1)S(1)}, bf16[2,96,768]{2,1,0:T(8,128)(2,1)S(1)}, u32[]{:S(2)}, u32[]{:S(2)}) collective-permute-start(bf16[2,96,768]{2,1,0:T(8,128)(2,1)S(1)} %get-tuple-element.242), channel_id=1, source_target_pairs={{0,4},{4,0},{8,12},{12,8},{16,20},{20,16},{24,28},{28,24},{1,5},{5... | collective-permute-start | bytes 884744 | tf_op jit(solution)/shard_map/ppermute | solution.py:582
  93.2 1.6 %collective-permute-start.37 = (bf16[256,768]{1,0:T(8,128)(2,1)S(1)}, bf16[256,768]{1,0:T(8,128)(2,1)S(1)}, u32[]{:S(2)}, u32[]{:S(2)}) collective-permute-start(bf16[256,768]{1,0:T(8,128)(2,1)S(1)} %get-tuple-element.246), channel_id=1, source_target_pairs={{0,2},{1,3},{2,0},{3,1},{4,6},{5,7},{6,4},{7,5},{8,10},{9,11},{10,... | collective-permute-start | bytes 1179656 | tf_op jit(solution)/shard_map/ppermute | solution.py:585
  95.2 7.1 %collective-permute-done.34.rest_1_ = bf16[96,768]{1,0:T(8,128)(2,1)S(1)} collective-permute-done((bf16[96,768]{1,0:T(8,128)(2,1)S(1)}, bf16[96,768]{1,0:T(8,128)(2,1)S(1)}, u32[]{:S(2)}, u32[]{:S(2)}) %collective-permute-start.34) | collective-permute-done | bytes 147488 | tf_op jit(solution)/shard_map/ppermute | solution.py:582
  102.7 1.1 share_out.1
  103.7 1.9 %fetch.1 = (f32[3,96,192]{2,1,0:T(8,128)S(1)}, f32[3,96,192]{2,1,0:T(8,128)S(1)}, f32[3,96,192]{2,1,0:T(8,128)S(1)}, f32[96,192]{1,0:T(8,128)S(1)}, f32[96,192]{...) custom-call(f32[3,96,192]{2,1,0:T(8,128)} %refs_0_, ...), custom_call_target="tpu_custom_call" | custom-call | tf_op jit(solution)/shard_map/fetch/pallas_call | solution.py:61
  105.7 4.7 %collective-permute-done.38.rest_2_ = bf16[104,768]{1,0:T(8,128)(2,1)S(1)} collective-permute-done((bf16[104,768]{1,0:T(8,128)(2,1)S(1)}, bf16[104,768]{1,0:T(8,128)(2,1)S(1)}, u32[]{:S(2)}, u32[]{:S(2)}) %collective-permute-start.38) | collective-permute-done | bytes 159776 | tf_op jit(solution)/shard_map/ppermute | solution.py:582
  111.1 10.1 %all_to_all.5.refs_0_ = f32[32,1,384]{2,1,0:T(1,128)S(1)} all-to-all(f32[32,1,384]{2,1,0:T(1,128)} %get-tuple-element.255), channel_id=1, replica_groups=mesh['dp'=8,'tp'=4] {'dp','tp'}, dimensions={0} | all-to-all | bytes 98304 | tf_op jit(solution)/shard_map/all_to_all | solution.py:857
  121.2 2.4 %adam.1 = (f32[1,1]{1,0:T(1,128)}, f32[3,96,192]{2,1,0:T(8,128)}, f32[3,96,192]{2,1,0:T(8,128)}, f32[3,96,192]{2,1,0:T(8,128)}, bf16[3,96,192]{2,1,0:T(8,128)(2,...) custom-call(f32[32,1,384]{2,1,0:T(1,128)S(1)} %all_to_all.5.refs_0_,, ...), custom_call_target="tpu_custom_call" | custom-call | tf_op jit(solution)/shard_map/adam/pallas_call | solution.py:61
  (61 shorter events, 10.2 us)
Async XLA Ops:
  1.9 11.2 %collective-permute-start.4 = (bf16[96,768]{1,0:T(8,128)(2,1)S(1)}, bf16[96,768]{1,0:T(8,128)(2,1)S(1)}, u32[]{:S(2)}, u32[]{:S(2)}) collective-permute-start(bf16[96,768]{1,0:T(8,128)(2,1)S(1)} %get-tuple-element.171.rest_0_), channel_id=1, source_target_pairs={{0,16},{4,20},{8,24},{12,28},{16,0},{20,4},{24,8},{28,12},{1,17},{... | collective-permute-start | bytes 442376 | tf_op jit(solution)/shard_map/ppermute | solution.py:582
  6.0 7.7 %collective-permute-start.1 = (bf16[96,768]{1,0:T(8,128)(2,1)S(1)}, bf16[96,768]{1,0:T(8,128)(2,1)S(1)}, u32[]{:S(2)}, u32[]{:S(2)}) collective-permute-start(bf16[96,768]{1,0:T(8,128)(2,1)S(1)} %get-tuple-element.171.rest_0_), channel_id=1, source_target_pairs={{0,8},{4,12},{8,0},{12,4},{16,24},{20,28},{24,16},{28,20},{1,9},{5... | collective-permute-start | bytes 442376 | tf_op jit(solution)/shard_map/ppermute | solution.py:582
  9.8 8.8 %collective-permute-start.3 = (bf16[96,768]{1,0:T(8,128)(2,1)S(1)}, bf16[96,768]{1,0:T(8,128)(2,1)S(1)}, u32[]{:S(2)}, u32[]{:S(2)}) collective-permute-start(bf16[96,768]{1,0:T(8,128)(2,1)S(1)} %get-tuple-element.171.rest_0_), channel_id=1, source_target_pairs={{0,4},{4,0},{8,12},{12,8},{16,20},{20,16},{24,28},{28,24},{1,5},{5... | collective-permute-start | bytes 442376 | tf_op jit(solution)/shard_map/ppermute | solution.py:582
  11.4 16.3 %collective-permute-start = (bf16[96,1536]{1,0:T(8,128)(2,1)S(1)}, bf16[96,1536]{1,0:T(8,128)(2,1)S(1)}, u32[]{:S(2)}, u32[]{:S(2)}) collective-permute-start(bf16[96,1536]{1,0:T(8,128)(2,1)S(1)} %get-tuple-element.176.rest_0_), channel_id=1, source_target_pairs={{0,4},{4,0},{8,12},{12,8},{16,20},{20,16},{24,28},{28,24},{1,5},{5... | collective-permute-start | bytes 884744 | tf_op jit(solution)/shard_map/ppermute | solution.py:582
  13.1 5.5 %collective-permute-start.6 = (bf16[96,768]{1,0:T(8,128)(2,1)S(1)}, bf16[96,768]{1,0:T(8,128)(2,1)S(1)}, u32[]{:S(2)}, u32[]{:S(2)}) collective-permute-start(bf16[96,768]{1,0:T(8,128)(2,1)S(1)} %collective-permute-done.4.rest_4_), channel_id=1, source_target_pairs={{0,8},{4,12},{8,0},{12,4},{16,24},{20,28},{24,16},{28,20},{1,9},{5... | collective-permute-start | bytes 442376 | tf_op jit(solution)/shard_map/ppermute | solution.py:582
  13.8 12.4 %collective-permute-start.2 = (bf16[96,768]{1,0:T(8,128)(2,1)S(1)}, bf16[96,768]{1,0:T(8,128)(2,1)S(1)}, u32[]{:S(2)}, u32[]{:S(2)}) collective-permute-start(bf16[96,768]{1,0:T(8,128)(2,1)S(1)} %collective-permute-done.1.rest_2_), channel_id=1, source_target_pairs={{0,4},{4,0},{8,12},{12,8},{16,20},{20,16},{24,28},{28,24},{1,5},{5... | collective-permute-start | bytes 442376 | tf_op jit(solution)/shard_map/ppermute | solution.py:582
  15.2 19.1 %collective-permute-start.8 = (bf16[96,1536]{1,0:T(8,128)(2,1)S(1)}, bf16[96,1536]{1,0:T(8,128)(2,1)S(1)}, u32[]{:S(2)}, u32[]{:S(2)}) collective-permute-start(bf16[96,1536]{1,0:T(8,128)(2,1)S(1)} %get-tuple-element.176.rest_0_), channel_id=1, source_target_pairs={{0,16},{4,20},{8,24},{12,28},{16,0},{20,4},{24,8},{28,12},{1,17},{... | collective-permute-start | bytes 884744 | tf_op jit(solution)/shard_map/ppermute | solution.py:582
  18.6 16.3 %collective-permute-start.11 = (bf16[96,1536]{1,0:T(8,128)(2,1)S(1)}, bf16[96,1536]{1,0:T(8,128)(2,1)S(1)}, u32[]{:S(2)}, u32[]{:S(2)}) collective-permute-start(bf16[96,1536]{1,0:T(8,128)(2,1)S(1)} %get-tuple-element.176.rest_0_), channel_id=1, source_target_pairs={{0,8},{4,12},{8,0},{12,4},{16,24},{20,28},{24,16},{28,20},{1,9},{5... | collective-permute-start | bytes 884744 | tf_op jit(solution)/shard_map/ppermute | solution.py:582
  18.6 10.5 %collective-permute-start.5 = (bf16[96,768]{1,0:T(8,128)(2,1)S(1)}, bf16[96,768]{1,0:T(8,128)(2,1)S(1)}, u32[]{:S(2)}, u32[]{:S(2)}) collective-permute-start(bf16[96,768]{1,0:T(8,128)(2,1)S(1)} %collective-permute-done.4.rest_4_), channel_id=1, source_target_pairs={{0,4},{4,0},{8,12},{12,8},{16,20},{20,16},{24,28},{28,24},{1,5},{5... | collective-permute-start | bytes 442376 | tf_op jit(solution)/shard_map/ppermute | solution.py:582
  26.1 5.1 %collective-permute-start.7 = (bf16[96,768]{1,0:T(8,128)(2,1)S(1)}, bf16[96,768]{1,0:T(8,128)(2,1)S(1)}, u32[]{:S(2)}, u32[]{:S(2)}) collective-permute-start(bf16[96,768]{1,0:T(8,128)(2,1)S(1)} %collective-permute-done.6.rest_6_), channel_id=1, source_target_pairs={{0,4},{4,0},{8,12},{12,8},{16,20},{20,16},{24,28},{28,24},{1,5},{5... | collective-permute-start | bytes 442376 | tf_op jit(solution)/shard_map/ppermute | solution.py:582
  34.4 2.5 %collective-permute-start.14 = (bf16[128,768]{1,0:T(8,128)(2,1)S(1)}, bf16[128,768]{1,0:T(8,128)(2,1)S(1)}, u32[]{:S(2)}, u32[]{:S(2)}) collective-permute-start(bf16[128,768]{1,0:T(8,128)(2,1)S(1)} %get-tuple-element.181), channel_id=1, source_target_pairs={{0,1},{1,0},{2,3},{3,2},{4,5},{5,4},{6,7},{7,6},{8,9},{9,8},{10,11... | collective-permute-start | bytes 589832 | tf_op jit(solution)/shard_map/ppermute | solution.py:585
  34.4 4.1 %collective-permute-start.9 = (bf16[128,768]{1,0:T(8,128)(2,1)S(1)}, bf16[128,768]{1,0:T(8,128)(2,1)S(1)}, u32[]{:S(2)}, u32[]{:S(2)}) collective-permute-start(bf16[128,768]{1,0:T(8,128)(2,1)S(1)} %get-tuple-element.175), channel_id=1, source_target_pairs={{0,1},{1,0},{2,3},{3,2},{4,5},{5,4},{6,7},{7,6},{8,9},{9,8},{10,11... | collective-permute-start | bytes 589832 | tf_op jit(solution)/shard_map/ppermute | solution.py:585
  34.9 9.9 %collective-permute-start.12 = (bf16[96,1536]{1,0:T(8,128)(2,1)S(1)}, bf16[96,1536]{1,0:T(8,128)(2,1)S(1)}, u32[]{:S(2)}, u32[]{:S(2)}) collective-permute-start(bf16[96,1536]{1,0:T(8,128)(2,1)S(1)} %collective-permute-done.8.rest_4_), channel_id=1, source_target_pairs={{0,8},{4,12},{8,0},{12,4},{16,24},{20,28},{24,16},{28,20},{1,9},{5... | collective-permute-start | bytes 884744 | tf_op jit(solution)/shard_map/ppermute | solution.py:582
  35.4 10.9 %collective-permute-start.10 = (bf16[96,1536]{1,0:T(8,128)(2,1)S(1)}, bf16[96,1536]{1,0:T(8,128)(2,1)S(1)}, u32[]{:S(2)}, u32[]{:S(2)}) collective-permute-start(bf16[96,1536]{1,0:T(8,128)(2,1)S(1)} %collective-permute-done.8.rest_4_), channel_id=1, source_target_pairs={{0,4},{4,0},{8,12},{12,8},{16,20},{20,16},{24,28},{28,24},{1,5},{5... | collective-permute-start | bytes 884744 | tf_op jit(solution)/shard_map/ppermute | solution.py:582
  36.9 9.4 %collective-permute-start.15 = (bf16[128,768]{1,0:T(8,128)(2,1)S(1)}, bf16[128,768]{1,0:T(8,128)(2,1)S(1)}, u32[]{:S(2)}, u32[]{:S(2)}) collective-permute-start(bf16[128,768]{1,0:T(8,128)(2,1)S(1)} %add.8.one), channel_id=1, source_target_pairs={{0,2},{1,3},{2,0},{3,1},{4,6},{5,7},{6,4},{7,5},{8,10},{9,11},{10,... | collective-permute-start | bytes 589832 | tf_op jit(solution)/shard_map/ppermute | solution.py:585
  38.6 9.0 %collective-permute-start.13 = (bf16[128,768]{1,0:T(8,128)(2,1)S(1)}, bf16[128,768]{1,0:T(8,128)(2,1)S(1)}, u32[]{:S(2)}, u32[]{:S(2)}) collective-permute-start(bf16[128,768]{1,0:T(8,128)(2,1)S(1)} %add.6.one), channel_id=1, source_target_pairs={{0,2},{1,3},{2,0},{3,1},{4,6},{5,7},{6,4},{7,5},{8,10},{9,11},{10,... | collective-permute-start | bytes 589832 | tf_op jit(solution)/shard_map/ppermute | solution.py:585
  39.1 11.1 %collective-permute-start.18 = (bf16[96,1536]{1,0:T(8,128)(2,1)S(1)}, bf16[96,1536]{1,0:T(8,128)(2,1)S(1)}, u32[]{:S(2)}, u32[]{:S(2)}) collective-permute-start(bf16[96,1536]{1,0:T(8,128)(2,1)S(1)} %collective-permute-done.rest_1_), channel_id=1, source_target_pairs={{0,8},{4,12},{8,0},{12,4},{16,24},{20,28},{24,16},{28,20},{1,9},{5... | collective-permute-start | bytes 884744 | tf_op jit(solution)/shard_map/ppermute | solution.py:582
  44.8 7.3 %collective-permute-start.19 = (bf16[96,1536]{1,0:T(8,128)(2,1)S(1)}, bf16[96,1536]{1,0:T(8,128)(2,1)S(1)}, u32[]{:S(2)}, u32[]{:S(2)}) collective-permute-start(bf16[96,1536]{1,0:T(8,128)(2,1)S(1)} %collective-permute-done.12.rest_6_), channel_id=1, source_target_pairs={{0,4},{4,0},{8,12},{12,8},{16,20},{20,16},{24,28},{28,24},{1,5},{5... | collective-permute-start | bytes 884744 | tf_op jit(solution)/shard_map/ppermute | solution.py:582
  46.3 3.9 %collective-permute-start.17 = (bf16[128,768]{1,0:T(8,128)(2,1)S(1)}, bf16[128,768]{1,0:T(8,128)(2,1)S(1)}, u32[]{:S(2)}, u32[]{:S(2)}) collective-permute-start(bf16[128,768]{1,0:T(8,128)(2,1)S(1)} %add.9.own_b), channel_id=1, source_target_pairs={{0,1},{1,0},{2,3},{3,2},{4,5},{5,4},{6,7},{7,6},{8,9},{9,8},{10,11... | collective-permute-start | bytes 589832 | tf_op jit(solution)/shard_map/ppermute | solution.py:585
  47.6 2.7 %collective-permute-start.16 = (bf16[128,768]{1,0:T(8,128)(2,1)S(1)}, bf16[128,768]{1,0:T(8,128)(2,1)S(1)}, u32[]{:S(2)}, u32[]{:S(2)}) collective-permute-start(bf16[128,768]{1,0:T(8,128)(2,1)S(1)} %add.7.own_a), channel_id=1, source_target_pairs={{0,1},{1,0},{2,3},{3,2},{4,5},{5,4},{6,7},{7,6},{8,9},{9,8},{10,11... | collective-permute-start | bytes 589832 | tf_op jit(solution)/shard_map/ppermute | solution.py:585
  55.6 1.8 %collective-permute-start.20 = (bf16[256,768]{1,0:T(8,128)(2,1)S(1)}, bf16[256,768]{1,0:T(8,128)(2,1)S(1)}, u32[]{:S(2)}, u32[]{:S(2)}) collective-permute-start(bf16[256,768]{1,0:T(8,128)(2,1)S(1)} %get-tuple-element.189), channel_id=1, source_target_pairs={{0,1},{1,0},{2,3},{3,2},{4,5},{5,4},{6,7},{7,6},{8,9},{9,8},{10,11... | collective-permute-start | bytes 1179656 | tf_op jit(solution)/shard_map/ppermute | solution.py:585
  57.5 11.2 %collective-permute-start.24 = (bf16[256,768]{1,0:T(8,128)(2,1)S(1)}, bf16[256,768]{1,0:T(8,128)(2,1)S(1)}, u32[]{:S(2)}, u32[]{:S(2)}) collective-permute-start(bf16[256,768]{1,0:T(8,128)(2,1)S(1)} %add.10.one), channel_id=1, source_target_pairs={{0,2},{1,3},{2,0},{3,1},{4,6},{5,7},{6,4},{7,5},{8,10},{9,11},{10,... | collective-permute-start | bytes 1179656 | tf_op jit(solution)/shard_map/ppermute | solution.py:585
  59.1 8.8 %collective-permute-start.23 = (bf16[2,96,768]{2,1,0:T(8,128)(2,1)S(1)}, bf16[2,96,768]{2,1,0:T(8,128)(2,1)S(1)}, u32[]{:S(2)}, u32[]{:S(2)}) collective-permute-start(bf16[2,96,768]{2,1,0:T(8,128)(2,1)S(1)} %get-tuple-element.201), channel_id=1, source_target_pairs={{0,8},{4,12},{8,0},{12,4},{16,24},{20,28},{24,16},{28,20},{1,9},{5... | collective-permute-start | bytes 884744 | tf_op jit(solution)/shard_map/ppermute | solution.py:582
  62.2 2.1 %collective-permute-start.21 = (bf16[128,768]{1,0:T(8,128)(2,1)S(1)}, bf16[128,768]{1,0:T(8,128)(2,1)S(1)}, u32[]{:S(2)}, u32[]{:S(2)}) collective-permute-start(bf16[128,768]{1,0:T(8,128)(2,1)S(1)} %get-tuple-element.198), channel_id=1, source_target_pairs={{0,1},{1,0},{2,3},{3,2},{4,5},{5,4},{6,7},{7,6},{8,9},{9,8},{10,11... | collective-permute-start | bytes 589832 | tf_op jit(solution)/shard_map/ppermute | solution.py:585
  62.3 2.0 %collective-permute-start.22 = (bf16[128,768]{1,0:T(8,128)(2,1)S(1)}, bf16[128,768]{1,0:T(8,128)(2,1)S(1)}, u32[]{:S(2)}, u32[]{:S(2)}) collective-permute-start(bf16[128,768]{1,0:T(8,128)(2,1)S(1)} %get-tuple-element.199), channel_id=1, source_target_pairs={{0,1},{1,0},{2,3},{3,2},{4,5},{5,4},{6,7},{7,6},{8,9},{9,8},{10,11... | collective-permute-start | bytes 589832 | tf_op jit(solution)/shard_map/ppermute | solution.py:585
  62.8 15.3 %collective-permute-start.26 = (bf16[4,96,768]{2,1,0:T(8,128)(2,1)S(1)}, bf16[4,96,768]{2,1,0:T(8,128)(2,1)S(1)}, u32[]{:S(2)}, u32[]{:S(2)}) collective-permute-start(bf16[4,96,768]{2,1,0:T(8,128)(2,1)S(1)} %get-tuple-element.216), channel_id=1, source_target_pairs={{0,4},{4,0},{8,12},{12,8},{16,20},{20,16},{24,28},{28,24},{1,5},{5... | collective-permute-start | bytes 1769480 | tf_op jit(solution)/shard_map/ppermute | solution.py:582
  68.8 1.8 %collective-permute-start.25 = (bf16[256,768]{1,0:T(8,128)(2,1)S(1)}, bf16[256,768]{1,0:T(8,128)(2,1)S(1)}, u32[]{:S(2)}, u32[]{:S(2)}) collective-permute-start(bf16[256,768]{1,0:T(8,128)(2,1)S(1)} %add.11.own), channel_id=1, source_target_pairs={{0,1},{1,0},{2,3},{3,2},{4,5},{5,4},{6,7},{7,6},{8,9},{9,8},{10,11... | collective-permute-start | bytes 1179656 | tf_op jit(solution)/shard_map/ppermute | solution.py:585
  68.9 14.5 %collective-permute-start.27 = (bf16[2,96,768]{2,1,0:T(8,128)(2,1)S(1)}, bf16[2,96,768]{2,1,0:T(8,128)(2,1)S(1)}, u32[]{:S(2)}, u32[]{:S(2)}) collective-permute-start(bf16[2,96,768]{2,1,0:T(8,128)(2,1)S(1)} %get-tuple-element.222), channel_id=1, source_target_pairs={{0,8},{4,12},{8,0},{12,4},{16,24},{20,28},{24,16},{28,20},{1,9},{5... | collective-permute-start | bytes 884744 | tf_op jit(solution)/shard_map/ppermute | solution.py:582
  69.5 16.5 %collective-permute-start.28 = (bf16[2,96,768]{2,1,0:T(8,128)(2,1)S(1)}, bf16[2,96,768]{2,1,0:T(8,128)(2,1)S(1)}, u32[]{:S(2)}, u32[]{:S(2)}) collective-permute-start(bf16[2,96,768]{2,1,0:T(8,128)(2,1)S(1)} %high_add.1), channel_id=1, source_target_pairs={{0,16},{4,20},{8,24},{12,28},{16,0},{20,4},{24,8},{28,12},{1,17},{... | collective-permute-start | bytes 884744 | tf_op jit(solution)/shard_map/ppermute | solution.py:582
  78.2 9.9 %collective-permute-start.29 = (bf16[200,768]{1,0:T(8,128)(2,1)S(1)}, bf16[200,768]{1,0:T(8,128)(2,1)S(1)}, u32[]{:S(2)}, u32[]{:S(2)}) collective-permute-start(bf16[200,768]{1,0:T(8,128)(2,1)S(1)} %get-tuple-element.227.sent), channel_id=1, source_target_pairs={{0,4},{4,0},{8,12},{12,8},{16,20},{20,16},{24,28},{28,24},{1,5},{5... | collective-permute-start | bytes 921608 | tf_op jit(solution)/shard_map/ppermute | solution.py:582
  79.8 13.1 %collective-permute-start.31 = (bf16[2,96,768]{2,1,0:T(8,128)(2,1)S(1)}, bf16[2,96,768]{2,1,0:T(8,128)(2,1)S(1)}, u32[]{:S(2)}, u32[]{:S(2)}) collective-permute-start(bf16[2,96,768]{2,1,0:T(8,128)(2,1)S(1)} %get-tuple-element.218), channel_id=1, source_target_pairs={{0,8},{4,12},{8,0},{12,4},{16,24},{20,28},{24,16},{28,20},{1,9},{5... | collective-permute-start | bytes 884744 | tf_op jit(solution)/shard_map/ppermute | solution.py:582
  86.1 5.2 %collective-permute-start.30 = (bf16[96,768]{1,0:T(8,128)(2,1)S(1)}, bf16[96,768]{1,0:T(8,128)(2,1)S(1)}, u32[]{:S(2)}, u32[]{:S(2)}) collective-permute-start(bf16[96,768]{1,0:T(8,128)(2,1)S(1)} %get-tuple-element.224), channel_id=1, source_target_pairs={{0,4},{4,0},{8,12},{12,8},{16,20},{20,16},{24,28},{28,24},{1,5},{5... | collective-permute-start | bytes 442376 | tf_op jit(solution)/shard_map/ppermute | solution.py:582
  87.6 5.3 %collective-permute-start.32 = (bf16[128,768]{1,0:T(8,128)(2,1)S(1)}, bf16[128,768]{1,0:T(8,128)(2,1)S(1)}, u32[]{:S(2)}, u32[]{:S(2)}) collective-permute-start(bf16[128,768]{1,0:T(8,128)(2,1)S(1)} %get-tuple-element.235), channel_id=1, source_target_pairs={{0,1},{1,0},{2,3},{3,2},{4,5},{5,4},{6,7},{7,6},{8,9},{9,8},{10,11... | collective-permute-start | bytes 589832 | tf_op jit(solution)/shard_map/ppermute | solution.py:585
  87.6 5.3 %collective-permute-start.33 = (bf16[128,768]{1,0:T(8,128)(2,1)S(1)}, bf16[128,768]{1,0:T(8,128)(2,1)S(1)}, u32[]{:S(2)}, u32[]{:S(2)}) collective-permute-start(bf16[128,768]{1,0:T(8,128)(2,1)S(1)} %get-tuple-element.236), channel_id=1, source_target_pairs={{0,1},{1,0},{2,3},{3,2},{4,5},{5,4},{6,7},{7,6},{8,9},{9,8},{10,11... | collective-permute-start | bytes 589832 | tf_op jit(solution)/shard_map/ppermute | solution.py:585
  88.2 14.2 %collective-permute-start.36 = (bf16[200,768]{1,0:T(8,128)(2,1)S(1)}, bf16[200,768]{1,0:T(8,128)(2,1)S(1)}, u32[]{:S(2)}, u32[]{:S(2)}) collective-permute-start(bf16[200,768]{1,0:T(8,128)(2,1)S(1)} %last_high.1.sent), channel_id=1, source_target_pairs={{0,8},{4,12},{8,0},{12,4},{16,24},{20,28},{24,16},{28,20},{1,9},{5... | collective-permute-start | bytes 921608 | tf_op jit(solution)/shard_map/ppermute | solution.py:582
  91.3 11.1 %collective-permute-start.35 = (bf16[2,96,768]{2,1,0:T(8,128)(2,1)S(1)}, bf16[2,96,768]{2,1,0:T(8,128)(2,1)S(1)}, u32[]{:S(2)}, u32[]{:S(2)}) collective-permute-start(bf16[2,96,768]{2,1,0:T(8,128)(2,1)S(1)} %get-tuple-element.242), channel_id=1, source_target_pairs={{0,4},{4,0},{8,12},{12,8},{16,20},{20,16},{24,28},{28,24},{1,5},{5... | collective-permute-start | bytes 884744 | tf_op jit(solution)/shard_map/ppermute | solution.py:582
  93.2 9.5 %collective-permute-start.37 = (bf16[256,768]{1,0:T(8,128)(2,1)S(1)}, bf16[256,768]{1,0:T(8,128)(2,1)S(1)}, u32[]{:S(2)}, u32[]{:S(2)}) collective-permute-start(bf16[256,768]{1,0:T(8,128)(2,1)S(1)} %get-tuple-element.246), channel_id=1, source_target_pairs={{0,2},{1,3},{2,0},{3,1},{4,6},{5,7},{6,4},{7,5},{8,10},{9,11},{10,... | collective-permute-start | bytes 1179656 | tf_op jit(solution)/shard_map/ppermute | solution.py:585
  94.7 7.6 %collective-permute-start.34 = (bf16[96,768]{1,0:T(8,128)(2,1)S(1)}, bf16[96,768]{1,0:T(8,128)(2,1)S(1)}, u32[]{:S(2)}, u32[]{:S(2)}) collective-permute-start(bf16[96,768]{1,0:T(8,128)(2,1)S(1)} %get-tuple-element.232), channel_id=1, source_target_pairs={{0,16},{4,20},{8,24},{12,28},{16,0},{20,4},{24,8},{28,12},{1,17},{... | collective-permute-start | bytes 442376 | tf_op jit(solution)/shard_map/ppermute | solution.py:582
  102.6 7.8 %collective-permute-start.38 = (bf16[104,768]{1,0:T(8,128)(2,1)S(1)}, bf16[104,768]{1,0:T(8,128)(2,1)S(1)}, u32[]{:S(2)}, u32[]{:S(2)}) collective-permute-start(bf16[104,768]{1,0:T(8,128)(2,1)S(1)} %get-tuple-element.243.rest_1_), channel_id=1, source_target_pairs={{0,16},{4,20},{8,24},{12,28},{16,0},{20,4},{24,8},{28,12},{1,17},{... | collective-permute-start | bytes 479240 | tf_op jit(solution)/shard_map/ppermute | solution.py:582

commit v9 on v8

--- a/solution.py
+++ b/solution.py
@@ -777,7 +777,7 @@
         keep, send_low = qkvo_parts
         in_keep, in_send = in_parts
         in_one = pair_add(in_keep, swap_dp(in_send, in_order[0]), (proj_grad,))
-        got_high = swap_dp(after(small, *in_one), 1)
+        got_high = swap_dp(small, 1)
         act_parts = act_shares(in_one)
         down_rest = (swap_dp(down_low, down_order[0]), swap_dp(down_one, down_order[1]))
         down_two = late_add(down_keep, *down_rest, act_parts[:1])

time: 124 us -> 124 us (level)
  no operation moved by 1% of the time
where the time goes in v9:
time: 124 us
  waiting for transfers between devices  43.1 us (35%)
  starting transfers between devices  40.4 us (33%)
  Pallas kernels  29 us (23%)
  blocking collectives  9.98 us (8%)
    ppermute x25, waiting for transfers between devices, swap_dp(): return lax.ppermute(value, 'dp', [(i, i ^ distance) for i in range(dp)])  39.6 us
    ppermute x25, starting transfers between devices, swap_dp(): return lax.ppermute(value, 'dp', [(i, i ^ distance) for i in range(dp)])  33.2 us
    pallas_call x30, Pallas kernels, call(): pl.pallas_call(body, out_shape=tuple(outs), in_specs=[pl.BlockSpec(memory...  29 us
    all_to_all x1, blocking collectives, on_device(): told = lax.all_to_all(payload, ('dp', 'tp'), 0, 0)  9.98 us
    ppermute x14, starting transfers between devices, swap_tp(): return lax.ppermute(value, 'tp', [(i, i ^ distance) for i in range(tp)])  7.25 us
    ppermute x14, waiting for transfers between devices, swap_tp(): return lax.ppermute(value, 'tp', [(i, i ^ distance) for i in range(tp)])  3.57 us
  transfers between devices with their start and end apart: 39, of which 18 were waited for; matrix products, arithmetic and copies ran while one was open for 0% of the time, Pallas kernels for 17%

profile of v9, /device:TPU:0, one launch (start us, length us, event | category | flops | bytes accessed | tf_op | source)
XLA Modules:
  0.0 123.7 jit_solution(8698868120779117514)
XLA Ops:
  0.7 1.2 %pack.1 = (bf16[96,768]{1,0:T(8,128)(2,1)S(1)}, bf16[96,1536]{1,0:T(8,128)(2,1)S(1)}) custom-call(f32[3,96,192]{2,1,0:T(8,128)} %refs_0_, f32[96,192]{1,0:T(8,128)} %refs_3_.1, f32[96,768]{1,0:T(8,128)} %refs_9_.1, f32[96,768]{1,0:T(8,128)} %refs_6_.1), custom_call_target="tpu_custom_call" | custom-call | tf_op jit(solution)/shard_map/pack/pallas_call | solution.py:61
  1.9 4.1 %collective-permute-start.4 = (bf16[96,768]{1,0:T(8,128)(2,1)S(1)}, bf16[96,768]{1,0:T(8,128)(2,1)S(1)}, u32[]{:S(2)}, u32[]{:S(2)}) collective-permute-start(bf16[96,768]{1,0:T(8,128)(2,1)S(1)} %get-tuple-element.170.rest_0_), channel_id=1, source_target_pairs={{0,16},{4,20},{8,24},{12,28},{16,0},{20,4},{24,8},{28,12},{1,17},{... | collective-permute-start | bytes 442376 | tf_op jit(solution)/shard_map/ppermute | solution.py:582
  6.0 1.6 %collective-permute-start.1 = (bf16[96,768]{1,0:T(8,128)(2,1)S(1)}, bf16[96,768]{1,0:T(8,128)(2,1)S(1)}, u32[]{:S(2)}, u32[]{:S(2)}) collective-permute-start(bf16[96,768]{1,0:T(8,128)(2,1)S(1)} %get-tuple-element.170.rest_0_), channel_id=1, source_target_pairs={{0,8},{4,12},{8,0},{12,4},{16,24},{20,28},{24,16},{28,20},{1,9},{5... | collective-permute-start | bytes 442376 | tf_op jit(solution)/shard_map/ppermute | solution.py:582
  7.6 2.2 %prep.1 = (bf16[512,768]{1,0:T(8,128)(2,1)S(1)}, bf16[768,512]{1,0:T(8,128)(2,1)S(1)}, f32[3,512,512]{2,1,0:T(8,128)S(1)}, s32[1,1024]{1,0:T(1,128)S(1)}, bf16[5...) custom-call(s32[1,4]{1,0:T(1,128)} %seg_in.1, f32[3,32]{1,0:T(4,128)} %bitcast.8, ...), custom_call_target="tpu_custom_call" | custom-call | tf_op jit(solution)/shard_map/prep/pallas_call | solution.py:61
  9.8 1.6 %collective-permute-start.3 = (bf16[96,768]{1,0:T(8,128)(2,1)S(1)}, bf16[96,768]{1,0:T(8,128)(2,1)S(1)}, u32[]{:S(2)}, u32[]{:S(2)}) collective-permute-start(bf16[96,768]{1,0:T(8,128)(2,1)S(1)} %get-tuple-element.170.rest_0_), channel_id=1, source_target_pairs={{0,4},{4,0},{8,12},{12,8},{16,20},{20,16},{24,28},{28,24},{1,5},{5... | collective-permute-start | bytes 442376 | tf_op jit(solution)/shard_map/ppermute | solution.py:582
  11.9 1.2 %collective-permute-done.4.rest_4_ = bf16[96,768]{1,0:T(8,128)(2,1)S(1)} collective-permute-done((bf16[96,768]{1,0:T(8,128)(2,1)S(1)}, bf16[96,768]{1,0:T(8,128)(2,1)S(1)}, u32[]{:S(2)}, u32[]{:S(2)}) %collective-permute-start.4) | collective-permute-done | bytes 147488 | tf_op jit(solution)/shard_map/ppermute | solution.py:582
  13.8 1.5 %collective-permute-start.2 = (bf16[96,768]{1,0:T(8,128)(2,1)S(1)}, bf16[96,768]{1,0:T(8,128)(2,1)S(1)}, u32[]{:S(2)}, u32[]{:S(2)}) collective-permute-start(bf16[96,768]{1,0:T(8,128)(2,1)S(1)} %collective-permute-done.1.rest_2_), channel_id=1, source_target_pairs={{0,4},{4,0},{8,12},{12,8},{16,20},{20,16},{24,28},{28,24},{1,5},{5... | collective-permute-start | bytes 442376 | tf_op jit(solution)/shard_map/ppermute | solution.py:582
  15.2 3.4 %collective-permute-start.8 = (bf16[96,1536]{1,0:T(8,128)(2,1)S(1)}, bf16[96,1536]{1,0:T(8,128)(2,1)S(1)}, u32[]{:S(2)}, u32[]{:S(2)}) collective-permute-start(bf16[96,1536]{1,0:T(8,128)(2,1)S(1)} %get-tuple-element.175.rest_0_), channel_id=1, source_target_pairs={{0,16},{4,20},{8,24},{12,28},{16,0},{20,4},{24,8},{28,12},{1,17},{... | collective-permute-start | bytes 884744 | tf_op jit(solution)/shard_map/ppermute | solution.py:582
  18.6 3.8 %collective-permute-start.5 = (bf16[96,768]{1,0:T(8,128)(2,1)S(1)}, bf16[96,768]{1,0:T(8,128)(2,1)S(1)}, u32[]{:S(2)}, u32[]{:S(2)}) collective-permute-start(bf16[96,768]{1,0:T(8,128)(2,1)S(1)} %collective-permute-done.4.rest_4_), channel_id=1, source_target_pairs={{0,4},{4,0},{8,12},{12,8},{16,20},{20,16},{24,28},{28,24},{1,5},{5... | collective-permute-start | bytes 442376 | tf_op jit(solution)/shard_map/ppermute | solution.py:582
  22.4 3.7 %collective-permute-done.2.rest_3_ = bf16[96,768]{1,0:T(8,128)(2,1)S(1)} collective-permute-done((bf16[96,768]{1,0:T(8,128)(2,1)S(1)}, bf16[96,768]{1,0:T(8,128)(2,1)S(1)}, u32[]{:S(2)}, u32[]{:S(2)}) %collective-permute-start.2) | collective-permute-done | bytes 147488 | tf_op jit(solution)/shard_map/ppermute | solution.py:582
  26.1 1.5 %collective-permute-start.7 = (bf16[96,768]{1,0:T(8,128)(2,1)S(1)}, bf16[96,768]{1,0:T(8,128)(2,1)S(1)}, u32[]{:S(2)}, u32[]{:S(2)}) collective-permute-start(bf16[96,768]{1,0:T(8,128)(2,1)S(1)} %collective-permute-done.6.rest_6_), channel_id=1, source_target_pairs={{0,4},{4,0},{8,12},{12,8},{16,20},{20,16},{24,28},{28,24},{1,5},{5... | collective-permute-start | bytes 442376 | tf_op jit(solution)/shard_map/ppermute | solution.py:582
  27.6 1.5 %collective-permute-done.5.rest_5_ = bf16[96,768]{1,0:T(8,128)(2,1)S(1)} collective-permute-done((bf16[96,768]{1,0:T(8,128)(2,1)S(1)}, bf16[96,768]{1,0:T(8,128)(2,1)S(1)}, u32[]{:S(2)}, u32[]{:S(2)}) %collective-permute-start.5) | collective-permute-done | bytes 147488 | tf_op jit(solution)/shard_map/ppermute | solution.py:582
  29.1 2.2 %collective-permute-done.7.rest_7_ = bf16[96,768]{1,0:T(8,128)(2,1)S(1)} collective-permute-done((bf16[96,768]{1,0:T(8,128)(2,1)S(1)}, bf16[96,768]{1,0:T(8,128)(2,1)S(1)}, u32[]{:S(2)}, u32[]{:S(2)}) %collective-permute-start.7) | collective-permute-done | bytes 147488 | tf_op jit(solution)/shard_map/ppermute | solution.py:582
  31.3 3.1 %attend.1 = (bf16[768,768]{1,0:T(8,128)(2,1)S(1)}, bf16[512,576]{1,0:T(8,128)(2,1)S(1)}, bf16[3,512,512]{2,1,0:T(8,128)(2,1)S(1)}, bf16[512,192]{1,0:T(8,128)(2,...) custom-call(bf16[512,768]{1,0:T(8,128)(2,1)S(1)} %get-tuple-element., ...), custom_call_target="tpu_custom_call" | custom-call | tf_op jit(solution)/shard_map/attend/pallas_call | solution.py:61
  35.4 1.5 %collective-permute-start.10 = (bf16[96,1536]{1,0:T(8,128)(2,1)S(1)}, bf16[96,1536]{1,0:T(8,128)(2,1)S(1)}, u32[]{:S(2)}, u32[]{:S(2)}) collective-permute-start(bf16[96,1536]{1,0:T(8,128)(2,1)S(1)} %collective-permute-done.8.rest_4_), channel_id=1, source_target_pairs={{0,4},{4,0},{8,12},{12,8},{16,20},{20,16},{24,28},{28,24},{1,5},{5... | collective-permute-start | bytes 884744 | tf_op jit(solution)/shard_map/ppermute | solution.py:582
  36.9 1.6 %collective-permute-start.15 = (bf16[128,768]{1,0:T(8,128)(2,1)S(1)}, bf16[128,768]{1,0:T(8,128)(2,1)S(1)}, u32[]{:S(2)}, u32[]{:S(2)}) collective-permute-start(bf16[128,768]{1,0:T(8,128)(2,1)S(1)} %add.8.one), channel_id=1, source_target_pairs={{0,2},{1,3},{2,0},{3,1},{4,6},{5,7},{6,4},{7,5},{8,10},{9,11},{10,... | collective-permute-start | bytes 589832 | tf_op jit(solution)/shard_map/ppermute | solution.py:585
  39.1 1.6 %collective-permute-start.18 = (bf16[96,1536]{1,0:T(8,128)(2,1)S(1)}, bf16[96,1536]{1,0:T(8,128)(2,1)S(1)}, u32[]{:S(2)}, u32[]{:S(2)}) collective-permute-start(bf16[96,1536]{1,0:T(8,128)(2,1)S(1)} %collective-permute-done.rest_1_), channel_id=1, source_target_pairs={{0,8},{4,12},{8,0},{12,4},{16,24},{20,28},{24,16},{28,20},{1,9},{5... | collective-permute-start | bytes 884744 | tf_op jit(solution)/shard_map/ppermute | solution.py:582
  40.7 4.1 %collective-permute-done.12.rest_6_ = bf16[96,1536]{1,0:T(8,128)(2,1)S(1)} collective-permute-done((bf16[96,1536]{1,0:T(8,128)(2,1)S(1)}, bf16[96,1536]{1,0:T(8,128)(2,1)S(1)}, u32[]{:S(2)}, u32[]{:S(2)}) %collective-permute-start.12) | collective-permute-done | bytes 294944 | tf_op jit(solution)/shard_map/ppermute | solution.py:582
  44.8 1.5 %collective-permute-start.19 = (bf16[96,1536]{1,0:T(8,128)(2,1)S(1)}, bf16[96,1536]{1,0:T(8,128)(2,1)S(1)}, u32[]{:S(2)}, u32[]{:S(2)}) collective-permute-start(bf16[96,1536]{1,0:T(8,128)(2,1)S(1)} %collective-permute-done.12.rest_6_), channel_id=1, source_target_pairs={{0,4},{4,0},{8,12},{12,8},{16,20},{20,16},{24,28},{28,24},{1,5},{5... | collective-permute-start | bytes 884744 | tf_op jit(solution)/shard_map/ppermute | solution.py:582
  46.4 1.1 collective-permute-done.13.two
  47.7 2.6 %collective-permute-done.18.rest_3_ = bf16[96,1536]{1,0:T(8,128)(2,1)S(1)} collective-permute-done((bf16[96,1536]{1,0:T(8,128)(2,1)S(1)}, bf16[96,1536]{1,0:T(8,128)(2,1)S(1)}, u32[]{:S(2)}, u32[]{:S(2)}) %collective-permute-start.18) | collective-permute-done | bytes 294944 | tf_op jit(solution)/shard_map/ppermute | solution.py:582
  50.3 1.8 %collective-permute-done.19.rest_7_ = bf16[96,1536]{1,0:T(8,128)(2,1)S(1)} collective-permute-done((bf16[96,1536]{1,0:T(8,128)(2,1)S(1)}, bf16[96,1536]{1,0:T(8,128)(2,1)S(1)}, u32[]{:S(2)}, u32[]{:S(2)}) %collective-permute-start.19) | collective-permute-done | bytes 294944 | tf_op jit(solution)/shard_map/ppermute | solution.py:582
  52.1 3.5 %ffn.1 = (f32[512,768]{1,0:T(8,128)S(1)}, bf16[512,768]{1,0:T(8,128)(2,1)S(1)}, bf16[512,768]{1,0:T(8,128)(2,1)S(1)}, bf16[512,768]{1,0:T(8,128)(2,1)S(1)}, bf16...) custom-call(bf16[512,768]{1,0:T(8,128)(2,1)S(1)} %get-tuple-element., ...), custom_call_target="tpu_custom_call" | custom-call | tf_op jit(solution)/shard_map/ffn/pallas_call | solution.py:61
  55.7 0.9 down_grad.1
  56.6 0.8 collective-permute-done.20.two
  57.5 1.6 %collective-permute-start.24 = (bf16[256,768]{1,0:T(8,128)(2,1)S(1)}, bf16[256,768]{1,0:T(8,128)(2,1)S(1)}, u32[]{:S(2)}, u32[]{:S(2)}) collective-permute-start(bf16[256,768]{1,0:T(8,128)(2,1)S(1)} %add.10.one), channel_id=1, source_target_pairs={{0,2},{1,3},{2,0},{3,1},{4,6},{5,7},{6,4},{7,5},{8,10},{9,11},{10,... | collective-permute-start | bytes 1179656 | tf_op jit(solution)/shard_map/ppermute | solution.py:585
  59.5 1.0 in_grad.1
  60.6 1.6 %ffn_out.1 = (bf16[256,768]{1,0:T(8,128)(2,1)S(1)}, bf16[128,768]{1,0:T(8,128)(2,1)S(1)}, bf16[128,768]{1,0:T(8,128)(2,1)S(1)}) custom-call(bf16[512,768]{1,0:T(8,128)(2,1)S(1)} %get-tuple-element.194.right.hidden, bf16[768,768]{1,0:T(8,128)(2,1)S(1)} %get-tuple-element.195.down), custom_call_target="tpu_custom_call" | custom-call | tf_op jit(solution)/shard_map/ffn_out/pallas_call | solution.py:61
  62.8 1.5 %collective-permute-start.26 = (bf16[4,96,768]{2,1,0:T(8,128)(2,1)S(1)}, bf16[4,96,768]{2,1,0:T(8,128)(2,1)S(1)}, u32[]{:S(2)}, u32[]{:S(2)}) collective-permute-start(bf16[4,96,768]{2,1,0:T(8,128)(2,1)S(1)} %get-tuple-element.215), channel_id=1, source_target_pairs={{0,4},{4,0},{8,12},{12,8},{16,20},{20,16},{24,28},{28,24},{1,5},{5... | collective-permute-start | bytes 1769480 | tf_op jit(solution)/shard_map/ppermute | solution.py:582
  65.1 2.7 %collective-permute-done.23.got = bf16[2,96,768]{2,1,0:T(8,128)(2,1)S(1)} collective-permute-done((bf16[2,96,768]{2,1,0:T(8,128)(2,1)S(1)}, bf16[2,96,768]{2,1,0:T(8,128)(2,1)S(1)}, u32[]{:S(2)}, u32[]{:S(2)}) %collective-permute-start.23) | collective-permute-done | bytes 294944 | tf_op jit(solution)/shard_map/ppermute | solution.py:582
  67.8 0.9 collective-permute-done.24.two
  69.8 0.8 collective-permute-done.25.other
  70.6 5.8 %attend_back.1 = (bf16[4,96,768]{2,1,0:T(8,128)(2,1)S(1)}, bf16[2,96,768]{2,1,0:T(8,128)(2,1)S(1)}, f32[128,768]{1,0:T(8,128)S(1)}, bf16[200,768]{1,0:T(8,128)(2,1)S(1)}, bf16[512,576]{1,0:T(8,128)(2,1)S(1)}) custom-call(f32[512,768]{1,0:T(8,128)S(1)} %get-tuple-element.242.resid, bf16[512,768]{1,0:T(8,128)(2,1)S(1)} %get-tuple-element.163.dy.left, ...), custom_call_target="tpu_custom_call" | custom-call | tf_op jit(solution)/shard_map/attend_back/pallas_call | solution.py:61
  76.4 1.6 %collective-permute-start.29 = (bf16[200,768]{1,0:T(8,128)(2,1)S(1)}, bf16[200,768]{1,0:T(8,128)(2,1)S(1)}, u32[]{:S(2)}, u32[]{:S(2)}) collective-permute-start(bf16[200,768]{1,0:T(8,128)(2,1)S(1)} %get-tuple-element.225.sent), channel_id=1, source_target_pairs={{0,4},{4,0},{8,12},{12,8},{16,20},{20,16},{24,28},{28,24},{1,5},{5... | collective-permute-start | bytes 921608 | tf_op jit(solution)/shard_map/ppermute | solution.py:582
  78.2 1.6 %collective-permute-start.31 = (bf16[2,96,768]{2,1,0:T(8,128)(2,1)S(1)}, bf16[2,96,768]{2,1,0:T(8,128)(2,1)S(1)}, u32[]{:S(2)}, u32[]{:S(2)}) collective-permute-start(bf16[2,96,768]{2,1,0:T(8,128)(2,1)S(1)} %get-tuple-element.217), channel_id=1, source_target_pairs={{0,8},{4,12},{8,0},{12,4},{16,24},{20,28},{24,16},{28,20},{1,9},{5... | collective-permute-start | bytes 884744 | tf_op jit(solution)/shard_map/ppermute | solution.py:582
  79.9 1.4 %act_grad.1 = (bf16[256,768]{1,0:T(8,128)(2,1)S(1)}, bf16[128,768]{1,0:T(8,128)(2,1)S(1)}, bf16[128,768]{1,0:T(8,128)(2,1)S(1)}) custom-call(bf16[512,576]{1,0:T(8,128)(2,1)S(1)} %get-tuple-element.218.proj_grad, bf16[768,768]{1,0:T(8,128)(2,1)S(1)} %get-tuple-element.206.weights), custom_call_target="tpu_custom_call" | custom-call | tf_op jit(solution)/shard_map/act_grad/pallas_call | solution.py:61
  81.3 2.1 %collective-permute-done.27.got_low = bf16[2,96,768]{2,1,0:T(8,128)(2,1)S(1)} collective-permute-done((bf16[2,96,768]{2,1,0:T(8,128)(2,1)S(1)}, bf16[2,96,768]{2,1,0:T(8,128)(2,1)S(1)}, u32[]{:S(2)}, u32[]{:S(2)}) %collective-permute-start.27) | collective-permute-done | bytes 294944 | tf_op jit(solution)/shard_map/ppermute | solution.py:582
  83.4 2.6 %collective-permute-done.28.got = bf16[2,96,768]{2,1,0:T(8,128)(2,1)S(1)} collective-permute-done((bf16[2,96,768]{2,1,0:T(8,128)(2,1)S(1)}, bf16[2,96,768]{2,1,0:T(8,128)(2,1)S(1)}, u32[]{:S(2)}, u32[]{:S(2)}) %collective-permute-start.28) | collective-permute-done | bytes 294944 | tf_op jit(solution)/shard_map/ppermute | solution.py:582
  86.1 1.6 %collective-permute-start.30 = (bf16[96,768]{1,0:T(8,128)(2,1)S(1)}, bf16[96,768]{1,0:T(8,128)(2,1)S(1)}, u32[]{:S(2)}, u32[]{:S(2)}) collective-permute-start(bf16[96,768]{1,0:T(8,128)(2,1)S(1)} %get-tuple-element.223), channel_id=1, source_target_pairs={{0,4},{4,0},{8,12},{12,8},{16,20},{20,16},{24,28},{28,24},{1,5},{5... | collective-permute-start | bytes 442376 | tf_op jit(solution)/shard_map/ppermute | solution.py:582
  88.3 3.0 %collective-permute-done.30.rest_1_ = bf16[96,768]{1,0:T(8,128)(2,1)S(1)} collective-permute-done((bf16[96,768]{1,0:T(8,128)(2,1)S(1)}, bf16[96,768]{1,0:T(8,128)(2,1)S(1)}, u32[]{:S(2)}, u32[]{:S(2)}) %collective-permute-start.30) | collective-permute-done | bytes 147488 | tf_op jit(solution)/shard_map/ppermute | solution.py:582
  91.3 1.5 %collective-permute-start.35 = (bf16[2,96,768]{2,1,0:T(8,128)(2,1)S(1)}, bf16[2,96,768]{2,1,0:T(8,128)(2,1)S(1)}, u32[]{:S(2)}, u32[]{:S(2)}) collective-permute-start(bf16[2,96,768]{2,1,0:T(8,128)(2,1)S(1)} %get-tuple-element.240), channel_id=1, source_target_pairs={{0,4},{4,0},{8,12},{12,8},{16,20},{20,16},{24,28},{28,24},{1,5},{5... | collective-permute-start | bytes 884744 | tf_op jit(solution)/shard_map/ppermute | solution.py:582
  93.2 1.6 %collective-permute-start.37 = (bf16[256,768]{1,0:T(8,128)(2,1)S(1)}, bf16[256,768]{1,0:T(8,128)(2,1)S(1)}, u32[]{:S(2)}, u32[]{:S(2)}) collective-permute-start(bf16[256,768]{1,0:T(8,128)(2,1)S(1)} %get-tuple-element.244), channel_id=1, source_target_pairs={{0,2},{1,3},{2,0},{3,1},{4,6},{5,7},{6,4},{7,5},{8,10},{9,11},{10,... | collective-permute-start | bytes 1179656 | tf_op jit(solution)/shard_map/ppermute | solution.py:585
  95.2 7.1 %collective-permute-done.34.rest_1_ = bf16[96,768]{1,0:T(8,128)(2,1)S(1)} collective-permute-done((bf16[96,768]{1,0:T(8,128)(2,1)S(1)}, bf16[96,768]{1,0:T(8,128)(2,1)S(1)}, u32[]{:S(2)}, u32[]{:S(2)}) %collective-permute-start.34) | collective-permute-done | bytes 147488 | tf_op jit(solution)/shard_map/ppermute | solution.py:582
  102.7 1.1 share_out.1
  103.7 1.9 %fetch.1 = (f32[3,96,192]{2,1,0:T(8,128)S(1)}, f32[3,96,192]{2,1,0:T(8,128)S(1)}, f32[3,96,192]{2,1,0:T(8,128)S(1)}, f32[96,192]{1,0:T(8,128)S(1)}, f32[96,192]{...) custom-call(f32[3,96,192]{2,1,0:T(8,128)} %refs_0_, ...), custom_call_target="tpu_custom_call" | custom-call | tf_op jit(solution)/shard_map/fetch/pallas_call | solution.py:61
  105.7 4.8 %collective-permute-done.38.rest_2_ = bf16[104,768]{1,0:T(8,128)(2,1)S(1)} collective-permute-done((bf16[104,768]{1,0:T(8,128)(2,1)S(1)}, bf16[104,768]{1,0:T(8,128)(2,1)S(1)}, u32[]{:S(2)}, u32[]{:S(2)}) %collective-permute-start.38) | collective-permute-done | bytes 159776 | tf_op jit(solution)/shard_map/ppermute | solution.py:582
  111.2 10.0 %all_to_all.5.refs_0_ = f32[32,1,384]{2,1,0:T(1,128)S(1)} all-to-all(f32[32,1,384]{2,1,0:T(1,128)} %get-tuple-element.253), channel_id=1, replica_groups=mesh['dp'=8,'tp'=4] {'dp','tp'}, dimensions={0} | all-to-all | bytes 98304 | tf_op jit(solution)/shard_map/all_to_all | solution.py:857
  121.2 2.4 %adam.1 = (f32[1,1]{1,0:T(1,128)}, f32[3,96,192]{2,1,0:T(8,128)}, f32[3,96,192]{2,1,0:T(8,128)}, f32[3,96,192]{2,1,0:T(8,128)}, bf16[3,96,192]{2,1,0:T(8,128)(2,...) custom-call(f32[32,1,384]{2,1,0:T(1,128)S(1)} %all_to_all.5.refs_0_,, ...), custom_call_target="tpu_custom_call" | custom-call | tf_op jit(solution)/shard_map/adam/pallas_call | solution.py:61
  (61 shorter events, 9.0 us)
Async XLA Ops:
  1.9 11.2 %collective-permute-start.4 = (bf16[96,768]{1,0:T(8,128)(2,1)S(1)}, bf16[96,768]{1,0:T(8,128)(2,1)S(1)}, u32[]{:S(2)}, u32[]{:S(2)}) collective-permute-start(bf16[96,768]{1,0:T(8,128)(2,1)S(1)} %get-tuple-element.170.rest_0_), channel_id=1, source_target_pairs={{0,16},{4,20},{8,24},{12,28},{16,0},{20,4},{24,8},{28,12},{1,17},{... | collective-permute-start | bytes 442376 | tf_op jit(solution)/shard_map/ppermute | solution.py:582
  6.0 7.7 %collective-permute-start.1 = (bf16[96,768]{1,0:T(8,128)(2,1)S(1)}, bf16[96,768]{1,0:T(8,128)(2,1)S(1)}, u32[]{:S(2)}, u32[]{:S(2)}) collective-permute-start(bf16[96,768]{1,0:T(8,128)(2,1)S(1)} %get-tuple-element.170.rest_0_), channel_id=1, source_target_pairs={{0,8},{4,12},{8,0},{12,4},{16,24},{20,28},{24,16},{28,20},{1,9},{5... | collective-permute-start | bytes 442376 | tf_op jit(solution)/shard_map/ppermute | solution.py:582
  9.8 8.8 %collective-permute-start.3 = (bf16[96,768]{1,0:T(8,128)(2,1)S(1)}, bf16[96,768]{1,0:T(8,128)(2,1)S(1)}, u32[]{:S(2)}, u32[]{:S(2)}) collective-permute-start(bf16[96,768]{1,0:T(8,128)(2,1)S(1)} %get-tuple-element.170.rest_0_), channel_id=1, source_target_pairs={{0,4},{4,0},{8,12},{12,8},{16,20},{20,16},{24,28},{28,24},{1,5},{5... | collective-permute-start | bytes 442376 | tf_op jit(solution)/shard_map/ppermute | solution.py:582
  11.4 16.3 %collective-permute-start = (bf16[96,1536]{1,0:T(8,128)(2,1)S(1)}, bf16[96,1536]{1,0:T(8,128)(2,1)S(1)}, u32[]{:S(2)}, u32[]{:S(2)}) collective-permute-start(bf16[96,1536]{1,0:T(8,128)(2,1)S(1)} %get-tuple-element.175.rest_0_), channel_id=1, source_target_pairs={{0,4},{4,0},{8,12},{12,8},{16,20},{20,16},{24,28},{28,24},{1,5},{5... | collective-permute-start | bytes 884744 | tf_op jit(solution)/shard_map/ppermute | solution.py:582
  13.1 5.5 %collective-permute-start.6 = (bf16[96,768]{1,0:T(8,128)(2,1)S(1)}, bf16[96,768]{1,0:T(8,128)(2,1)S(1)}, u32[]{:S(2)}, u32[]{:S(2)}) collective-permute-start(bf16[96,768]{1,0:T(8,128)(2,1)S(1)} %collective-permute-done.4.rest_4_), channel_id=1, source_target_pairs={{0,8},{4,12},{8,0},{12,4},{16,24},{20,28},{24,16},{28,20},{1,9},{5... | collective-permute-start | bytes 442376 | tf_op jit(solution)/shard_map/ppermute | solution.py:582
  13.8 12.4 %collective-permute-start.2 = (bf16[96,768]{1,0:T(8,128)(2,1)S(1)}, bf16[96,768]{1,0:T(8,128)(2,1)S(1)}, u32[]{:S(2)}, u32[]{:S(2)}) collective-permute-start(bf16[96,768]{1,0:T(8,128)(2,1)S(1)} %collective-permute-done.1.rest_2_), channel_id=1, source_target_pairs={{0,4},{4,0},{8,12},{12,8},{16,20},{20,16},{24,28},{28,24},{1,5},{5... | collective-permute-start | bytes 442376 | tf_op jit(solution)/shard_map/ppermute | solution.py:582
  15.2 19.1 %collective-permute-start.8 = (bf16[96,1536]{1,0:T(8,128)(2,1)S(1)}, bf16[96,1536]{1,0:T(8,128)(2,1)S(1)}, u32[]{:S(2)}, u32[]{:S(2)}) collective-permute-start(bf16[96,1536]{1,0:T(8,128)(2,1)S(1)} %get-tuple-element.175.rest_0_), channel_id=1, source_target_pairs={{0,16},{4,20},{8,24},{12,28},{16,0},{20,4},{24,8},{28,12},{1,17},{... | collective-permute-start | bytes 884744 | tf_op jit(solution)/shard_map/ppermute | solution.py:582
  18.6 16.3 %collective-permute-start.11 = (bf16[96,1536]{1,0:T(8,128)(2,1)S(1)}, bf16[96,1536]{1,0:T(8,128)(2,1)S(1)}, u32[]{:S(2)}, u32[]{:S(2)}) collective-permute-start(bf16[96,1536]{1,0:T(8,128)(2,1)S(1)} %get-tuple-element.175.rest_0_), channel_id=1, source_target_pairs={{0,8},{4,12},{8,0},{12,4},{16,24},{20,28},{24,16},{28,20},{1,9},{5... | collective-permute-start | bytes 884744 | tf_op jit(solution)/shard_map/ppermute | solution.py:582
  18.6 10.5 %collective-permute-start.5 = (bf16[96,768]{1,0:T(8,128)(2,1)S(1)}, bf16[96,768]{1,0:T(8,128)(2,1)S(1)}, u32[]{:S(2)}, u32[]{:S(2)}) collective-permute-start(bf16[96,768]{1,0:T(8,128)(2,1)S(1)} %collective-permute-done.4.rest_4_), channel_id=1, source_target_pairs={{0,4},{4,0},{8,12},{12,8},{16,20},{20,16},{24,28},{28,24},{1,5},{5... | collective-permute-start | bytes 442376 | tf_op jit(solution)/shard_map/ppermute | solution.py:582
  26.1 5.1 %collective-permute-start.7 = (bf16[96,768]{1,0:T(8,128)(2,1)S(1)}, bf16[96,768]{1,0:T(8,128)(2,1)S(1)}, u32[]{:S(2)}, u32[]{:S(2)}) collective-permute-start(bf16[96,768]{1,0:T(8,128)(2,1)S(1)} %collective-permute-done.6.rest_6_), channel_id=1, source_target_pairs={{0,4},{4,0},{8,12},{12,8},{16,20},{20,16},{24,28},{28,24},{1,5},{5... | collective-permute-start | bytes 442376 | tf_op jit(solution)/shard_map/ppermute | solution.py:582
  34.4 2.5 %collective-permute-start.14 = (bf16[128,768]{1,0:T(8,128)(2,1)S(1)}, bf16[128,768]{1,0:T(8,128)(2,1)S(1)}, u32[]{:S(2)}, u32[]{:S(2)}) collective-permute-start(bf16[128,768]{1,0:T(8,128)(2,1)S(1)} %get-tuple-element.180), channel_id=1, source_target_pairs={{0,1},{1,0},{2,3},{3,2},{4,5},{5,4},{6,7},{7,6},{8,9},{9,8},{10,11... | collective-permute-start | bytes 589832 | tf_op jit(solution)/shard_map/ppermute | solution.py:585
  34.4 4.1 %collective-permute-start.9 = (bf16[128,768]{1,0:T(8,128)(2,1)S(1)}, bf16[128,768]{1,0:T(8,128)(2,1)S(1)}, u32[]{:S(2)}, u32[]{:S(2)}) collective-permute-start(bf16[128,768]{1,0:T(8,128)(2,1)S(1)} %get-tuple-element.174), channel_id=1, source_target_pairs={{0,1},{1,0},{2,3},{3,2},{4,5},{5,4},{6,7},{7,6},{8,9},{9,8},{10,11... | collective-permute-start | bytes 589832 | tf_op jit(solution)/shard_map/ppermute | solution.py:585
  34.9 9.9 %collective-permute-start.12 = (bf16[96,1536]{1,0:T(8,128)(2,1)S(1)}, bf16[96,1536]{1,0:T(8,128)(2,1)S(1)}, u32[]{:S(2)}, u32[]{:S(2)}) collective-permute-start(bf16[96,1536]{1,0:T(8,128)(2,1)S(1)} %collective-permute-done.8.rest_4_), channel_id=1, source_target_pairs={{0,8},{4,12},{8,0},{12,4},{16,24},{20,28},{24,16},{28,20},{1,9},{5... | collective-permute-start | bytes 884744 | tf_op jit(solution)/shard_map/ppermute | solution.py:582
  35.4 10.9 %collective-permute-start.10 = (bf16[96,1536]{1,0:T(8,128)(2,1)S(1)}, bf16[96,1536]{1,0:T(8,128)(2,1)S(1)}, u32[]{:S(2)}, u32[]{:S(2)}) collective-permute-start(bf16[96,1536]{1,0:T(8,128)(2,1)S(1)} %collective-permute-done.8.rest_4_), channel_id=1, source_target_pairs={{0,4},{4,0},{8,12},{12,8},{16,20},{20,16},{24,28},{28,24},{1,5},{5... | collective-permute-start | bytes 884744 | tf_op jit(solution)/shard_map/ppermute | solution.py:582
  36.9 9.4 %collective-permute-start.15 = (bf16[128,768]{1,0:T(8,128)(2,1)S(1)}, bf16[128,768]{1,0:T(8,128)(2,1)S(1)}, u32[]{:S(2)}, u32[]{:S(2)}) collective-permute-start(bf16[128,768]{1,0:T(8,128)(2,1)S(1)} %add.8.one), channel_id=1, source_target_pairs={{0,2},{1,3},{2,0},{3,1},{4,6},{5,7},{6,4},{7,5},{8,10},{9,11},{10,... | collective-permute-start | bytes 589832 | tf_op jit(solution)/shard_map/ppermute | solution.py:585
  38.6 9.0 %collective-permute-start.13 = (bf16[128,768]{1,0:T(8,128)(2,1)S(1)}, bf16[128,768]{1,0:T(8,128)(2,1)S(1)}, u32[]{:S(2)}, u32[]{:S(2)}) collective-permute-start(bf16[128,768]{1,0:T(8,128)(2,1)S(1)} %add.6.one), channel_id=1, source_target_pairs={{0,2},{1,3},{2,0},{3,1},{4,6},{5,7},{6,4},{7,5},{8,10},{9,11},{10,... | collective-permute-start | bytes 589832 | tf_op jit(solution)/shard_map/ppermute | solution.py:585
  39.1 11.1 %collective-permute-start.18 = (bf16[96,1536]{1,0:T(8,128)(2,1)S(1)}, bf16[96,1536]{1,0:T(8,128)(2,1)S(1)}, u32[]{:S(2)}, u32[]{:S(2)}) collective-permute-start(bf16[96,1536]{1,0:T(8,128)(2,1)S(1)} %collective-permute-done.rest_1_), channel_id=1, source_target_pairs={{0,8},{4,12},{8,0},{12,4},{16,24},{20,28},{24,16},{28,20},{1,9},{5... | collective-permute-start | bytes 884744 | tf_op jit(solution)/shard_map/ppermute | solution.py:582
  44.8 7.3 %collective-permute-start.19 = (bf16[96,1536]{1,0:T(8,128)(2,1)S(1)}, bf16[96,1536]{1,0:T(8,128)(2,1)S(1)}, u32[]{:S(2)}, u32[]{:S(2)}) collective-permute-start(bf16[96,1536]{1,0:T(8,128)(2,1)S(1)} %collective-permute-done.12.rest_6_), channel_id=1, source_target_pairs={{0,4},{4,0},{8,12},{12,8},{16,20},{20,16},{24,28},{28,24},{1,5},{5... | collective-permute-start | bytes 884744 | tf_op jit(solution)/shard_map/ppermute | solution.py:582
  46.3 3.9 %collective-permute-start.17 = (bf16[128,768]{1,0:T(8,128)(2,1)S(1)}, bf16[128,768]{1,0:T(8,128)(2,1)S(1)}, u32[]{:S(2)}, u32[]{:S(2)}) collective-permute-start(bf16[128,768]{1,0:T(8,128)(2,1)S(1)} %add.9.own_b), channel_id=1, source_target_pairs={{0,1},{1,0},{2,3},{3,2},{4,5},{5,4},{6,7},{7,6},{8,9},{9,8},{10,11... | collective-permute-start | bytes 589832 | tf_op jit(solution)/shard_map/ppermute | solution.py:585
  47.6 2.7 %collective-permute-start.16 = (bf16[128,768]{1,0:T(8,128)(2,1)S(1)}, bf16[128,768]{1,0:T(8,128)(2,1)S(1)}, u32[]{:S(2)}, u32[]{:S(2)}) collective-permute-start(bf16[128,768]{1,0:T(8,128)(2,1)S(1)} %add.7.own_a), channel_id=1, source_target_pairs={{0,1},{1,0},{2,3},{3,2},{4,5},{5,4},{6,7},{7,6},{8,9},{9,8},{10,11... | collective-permute-start | bytes 589832 | tf_op jit(solution)/shard_map/ppermute | solution.py:585
  55.6 1.8 %collective-permute-start.20 = (bf16[256,768]{1,0:T(8,128)(2,1)S(1)}, bf16[256,768]{1,0:T(8,128)(2,1)S(1)}, u32[]{:S(2)}, u32[]{:S(2)}) collective-permute-start(bf16[256,768]{1,0:T(8,128)(2,1)S(1)} %get-tuple-element.188), channel_id=1, source_target_pairs={{0,1},{1,0},{2,3},{3,2},{4,5},{5,4},{6,7},{7,6},{8,9},{9,8},{10,11... | collective-permute-start | bytes 1179656 | tf_op jit(solution)/shard_map/ppermute | solution.py:585
  57.5 11.2 %collective-permute-start.24 = (bf16[256,768]{1,0:T(8,128)(2,1)S(1)}, bf16[256,768]{1,0:T(8,128)(2,1)S(1)}, u32[]{:S(2)}, u32[]{:S(2)}) collective-permute-start(bf16[256,768]{1,0:T(8,128)(2,1)S(1)} %add.10.one), channel_id=1, source_target_pairs={{0,2},{1,3},{2,0},{3,1},{4,6},{5,7},{6,4},{7,5},{8,10},{9,11},{10,... | collective-permute-start | bytes 1179656 | tf_op jit(solution)/shard_map/ppermute | solution.py:585
  59.1 8.8 %collective-permute-start.23 = (bf16[2,96,768]{2,1,0:T(8,128)(2,1)S(1)}, bf16[2,96,768]{2,1,0:T(8,128)(2,1)S(1)}, u32[]{:S(2)}, u32[]{:S(2)}) collective-permute-start(bf16[2,96,768]{2,1,0:T(8,128)(2,1)S(1)} %get-tuple-element.200), channel_id=1, source_target_pairs={{0,8},{4,12},{8,0},{12,4},{16,24},{20,28},{24,16},{28,20},{1,9},{5... | collective-permute-start | bytes 884744 | tf_op jit(solution)/shard_map/ppermute | solution.py:582
  62.2 2.1 %collective-permute-start.21 = (bf16[128,768]{1,0:T(8,128)(2,1)S(1)}, bf16[128,768]{1,0:T(8,128)(2,1)S(1)}, u32[]{:S(2)}, u32[]{:S(2)}) collective-permute-start(bf16[128,768]{1,0:T(8,128)(2,1)S(1)} %get-tuple-element.197), channel_id=1, source_target_pairs={{0,1},{1,0},{2,3},{3,2},{4,5},{5,4},{6,7},{7,6},{8,9},{9,8},{10,11... | collective-permute-start | bytes 589832 | tf_op jit(solution)/shard_map/ppermute | solution.py:585
  62.3 2.0 %collective-permute-start.22 = (bf16[128,768]{1,0:T(8,128)(2,1)S(1)}, bf16[128,768]{1,0:T(8,128)(2,1)S(1)}, u32[]{:S(2)}, u32[]{:S(2)}) collective-permute-start(bf16[128,768]{1,0:T(8,128)(2,1)S(1)} %get-tuple-element.198), channel_id=1, source_target_pairs={{0,1},{1,0},{2,3},{3,2},{4,5},{5,4},{6,7},{7,6},{8,9},{9,8},{10,11... | collective-permute-start | bytes 589832 | tf_op jit(solution)/shard_map/ppermute | solution.py:585
  62.8 15.3 %collective-permute-start.26 = (bf16[4,96,768]{2,1,0:T(8,128)(2,1)S(1)}, bf16[4,96,768]{2,1,0:T(8,128)(2,1)S(1)}, u32[]{:S(2)}, u32[]{:S(2)}) collective-permute-start(bf16[4,96,768]{2,1,0:T(8,128)(2,1)S(1)} %get-tuple-element.215), channel_id=1, source_target_pairs={{0,4},{4,0},{8,12},{12,8},{16,20},{20,16},{24,28},{28,24},{1,5},{5... | collective-permute-start | bytes 1769480 | tf_op jit(solution)/shard_map/ppermute | solution.py:582
  68.8 1.8 %collective-permute-start.25 = (bf16[256,768]{1,0:T(8,128)(2,1)S(1)}, bf16[256,768]{1,0:T(8,128)(2,1)S(1)}, u32[]{:S(2)}, u32[]{:S(2)}) collective-permute-start(bf16[256,768]{1,0:T(8,128)(2,1)S(1)} %add.11.own), channel_id=1, source_target_pairs={{0,1},{1,0},{2,3},{3,2},{4,5},{5,4},{6,7},{7,6},{8,9},{9,8},{10,11... | collective-permute-start | bytes 1179656 | tf_op jit(solution)/shard_map/ppermute | solution.py:585
  68.9 14.5 %collective-permute-start.27 = (bf16[2,96,768]{2,1,0:T(8,128)(2,1)S(1)}, bf16[2,96,768]{2,1,0:T(8,128)(2,1)S(1)}, u32[]{:S(2)}, u32[]{:S(2)}) collective-permute-start(bf16[2,96,768]{2,1,0:T(8,128)(2,1)S(1)} %get-tuple-element.221), channel_id=1, source_target_pairs={{0,8},{4,12},{8,0},{12,4},{16,24},{20,28},{24,16},{28,20},{1,9},{5... | collective-permute-start | bytes 884744 | tf_op jit(solution)/shard_map/ppermute | solution.py:582
  69.5 16.5 %collective-permute-start.28 = (bf16[2,96,768]{2,1,0:T(8,128)(2,1)S(1)}, bf16[2,96,768]{2,1,0:T(8,128)(2,1)S(1)}, u32[]{:S(2)}, u32[]{:S(2)}) collective-permute-start(bf16[2,96,768]{2,1,0:T(8,128)(2,1)S(1)} %high_add.1), channel_id=1, source_target_pairs={{0,16},{4,20},{8,24},{12,28},{16,0},{20,4},{24,8},{28,12},{1,17},{... | collective-permute-start | bytes 884744 | tf_op jit(solution)/shard_map/ppermute | solution.py:582
  76.4 11.8 %collective-permute-start.29 = (bf16[200,768]{1,0:T(8,128)(2,1)S(1)}, bf16[200,768]{1,0:T(8,128)(2,1)S(1)}, u32[]{:S(2)}, u32[]{:S(2)}) collective-permute-start(bf16[200,768]{1,0:T(8,128)(2,1)S(1)} %get-tuple-element.225.sent), channel_id=1, source_target_pairs={{0,4},{4,0},{8,12},{12,8},{16,20},{20,16},{24,28},{28,24},{1,5},{5... | collective-permute-start | bytes 921608 | tf_op jit(solution)/shard_map/ppermute | solution.py:582
  78.2 14.6 %collective-permute-start.31 = (bf16[2,96,768]{2,1,0:T(8,128)(2,1)S(1)}, bf16[2,96,768]{2,1,0:T(8,128)(2,1)S(1)}, u32[]{:S(2)}, u32[]{:S(2)}) collective-permute-start(bf16[2,96,768]{2,1,0:T(8,128)(2,1)S(1)} %get-tuple-element.217), channel_id=1, source_target_pairs={{0,8},{4,12},{8,0},{12,4},{16,24},{20,28},{24,16},{28,20},{1,9},{5... | collective-permute-start | bytes 884744 | tf_op jit(solution)/shard_map/ppermute | solution.py:582
  86.1 5.2 %collective-permute-start.30 = (bf16[96,768]{1,0:T(8,128)(2,1)S(1)}, bf16[96,768]{1,0:T(8,128)(2,1)S(1)}, u32[]{:S(2)}, u32[]{:S(2)}) collective-permute-start(bf16[96,768]{1,0:T(8,128)(2,1)S(1)} %get-tuple-element.223), channel_id=1, source_target_pairs={{0,4},{4,0},{8,12},{12,8},{16,20},{20,16},{24,28},{28,24},{1,5},{5... | collective-permute-start | bytes 442376 | tf_op jit(solution)/shard_map/ppermute | solution.py:582
  87.6 5.3 %collective-permute-start.32 = (bf16[128,768]{1,0:T(8,128)(2,1)S(1)}, bf16[128,768]{1,0:T(8,128)(2,1)S(1)}, u32[]{:S(2)}, u32[]{:S(2)}) collective-permute-start(bf16[128,768]{1,0:T(8,128)(2,1)S(1)} %get-tuple-element.233), channel_id=1, source_target_pairs={{0,1},{1,0},{2,3},{3,2},{4,5},{5,4},{6,7},{7,6},{8,9},{9,8},{10,11... | collective-permute-start | bytes 589832 | tf_op jit(solution)/shard_map/ppermute | solution.py:585
  87.6 5.3 %collective-permute-start.33 = (bf16[128,768]{1,0:T(8,128)(2,1)S(1)}, bf16[128,768]{1,0:T(8,128)(2,1)S(1)}, u32[]{:S(2)}, u32[]{:S(2)}) collective-permute-start(bf16[128,768]{1,0:T(8,128)(2,1)S(1)} %get-tuple-element.234), channel_id=1, source_target_pairs={{0,1},{1,0},{2,3},{3,2},{4,5},{5,4},{6,7},{7,6},{8,9},{9,8},{10,11... | collective-permute-start | bytes 589832 | tf_op jit(solution)/shard_map/ppermute | solution.py:585
  88.2 14.2 %collective-permute-start.36 = (bf16[200,768]{1,0:T(8,128)(2,1)S(1)}, bf16[200,768]{1,0:T(8,128)(2,1)S(1)}, u32[]{:S(2)}, u32[]{:S(2)}) collective-permute-start(bf16[200,768]{1,0:T(8,128)(2,1)S(1)} %last_high.1.sent), channel_id=1, source_target_pairs={{0,8},{4,12},{8,0},{12,4},{16,24},{20,28},{24,16},{28,20},{1,9},{5... | collective-permute-start | bytes 921608 | tf_op jit(solution)/shard_map/ppermute | solution.py:582
  91.3 11.1 %collective-permute-start.35 = (bf16[2,96,768]{2,1,0:T(8,128)(2,1)S(1)}, bf16[2,96,768]{2,1,0:T(8,128)(2,1)S(1)}, u32[]{:S(2)}, u32[]{:S(2)}) collective-permute-start(bf16[2,96,768]{2,1,0:T(8,128)(2,1)S(1)} %get-tuple-element.240), channel_id=1, source_target_pairs={{0,4},{4,0},{8,12},{12,8},{16,20},{20,16},{24,28},{28,24},{1,5},{5... | collective-permute-start | bytes 884744 | tf_op jit(solution)/shard_map/ppermute | solution.py:582
  93.2 9.5 %collective-permute-start.37 = (bf16[256,768]{1,0:T(8,128)(2,1)S(1)}, bf16[256,768]{1,0:T(8,128)(2,1)S(1)}, u32[]{:S(2)}, u32[]{:S(2)}) collective-permute-start(bf16[256,768]{1,0:T(8,128)(2,1)S(1)} %get-tuple-element.244), channel_id=1, source_target_pairs={{0,2},{1,3},{2,0},{3,1},{4,6},{5,7},{6,4},{7,5},{8,10},{9,11},{10,... | collective-permute-start | bytes 1179656 | tf_op jit(solution)/shard_map/ppermute | solution.py:585
  94.7 7.6 %collective-permute-start.34 = (bf16[96,768]{1,0:T(8,128)(2,1)S(1)}, bf16[96,768]{1,0:T(8,128)(2,1)S(1)}, u32[]{:S(2)}, u32[]{:S(2)}) collective-permute-start(bf16[96,768]{1,0:T(8,128)(2,1)S(1)} %get-tuple-element.230), channel_id=1, source_target_pairs={{0,16},{4,20},{8,24},{12,28},{16,0},{20,4},{24,8},{28,12},{1,17},{... | collective-permute-start | bytes 442376 | tf_op jit(solution)/shard_map/ppermute | solution.py:582
  102.6 7.9 %collective-permute-start.38 = (bf16[104,768]{1,0:T(8,128)(2,1)S(1)}, bf16[104,768]{1,0:T(8,128)(2,1)S(1)}, u32[]{:S(2)}, u32[]{:S(2)}) collective-permute-start(bf16[104,768]{1,0:T(8,128)(2,1)S(1)} %get-tuple-element.241.rest_1_), channel_id=1, source_target_pairs={{0,16},{4,20},{8,24},{12,28},{16,0},{20,4},{24,8},{28,12},{1,17},{... | collective-permute-start | bytes 479240 | tf_op jit(solution)/shard_map/ppermute | solution.py:582
